TPU v7x, 32 devices: a whole 2x2x4 slice. The times are simulated.
32 devices in a mesh: dp: 8 (over z, x), tensor: 4 (over y, core).
Axes of the slice: x: 2, y: 2, z: 4, core: 2. Of those that a mesh axis runs over, the one named last changes fastest.
Arguments:
- tokens: bfloat16 [8192, 1536], P(('dp', 'tensor')), may hold values from -6 to 6
- cotangent: bfloat16 [8192, 1536], P(('dp', 'tensor')), may hold values from -6 to 6
- prefix: int32 [8], P('dp'), may hold values from 0 to 1024
- routes: int32 [8192, 8], P('dp'), may hold values from 0 to 39, all different within a row; in each aligned block of 1024 rows (0 to 1023, 1024 to 2047, ...) at most 256 rows name the same one
- norm1: bfloat16 [1536], P('dp'), may hold values from 0.5 to 1.5
- w_query: bfloat16 [1536, 1536], P('dp', 'tensor'), may hold values from -0.15625 to 0.15625
- w_key: bfloat16 [1536, 512], P('dp', 'tensor'), may hold values from -0.15625 to 0.15625
- w_value: bfloat16 [1536, 512], P('dp', 'tensor'), may hold values from -0.15625 to 0.15625
- w_out: bfloat16 [1536, 1536], P('tensor', 'dp'), may hold values from -2.5 to 2.5
- norm2: bfloat16 [1536], P('dp'), may hold values from 0.5 to 1.5
- w_router: bfloat16 [1536, 40], P('dp'), may hold values from -0.076171875 to 0.076171875
- w_gate: bfloat16 [40, 1536, 512], P(None, 'dp', 'tensor'), may hold values from -0.15625 to 0.15625
- w_up: bfloat16 [40, 1536, 512], P(None, 'dp', 'tensor'), may hold values from -0.15625 to 0.15625
- w_down: bfloat16 [40, 512, 1536], P(None, 'tensor', 'dp'), may hold values from -1 to 1
Outputs:
- mixed: bfloat16 [8192, 1536], P(('dp', 'tensor'))
- grad_tokens: float32 [8192, 1536], P(('dp', 'tensor'))
- grad_norm1: float32 [1536], P('dp')
- grad_query: float32 [1536, 1536], P('dp', 'tensor')
- grad_key: float32 [1536, 512], P('dp', 'tensor')
- grad_value: float32 [1536, 512], P('dp', 'tensor')
- grad_out: float32 [1536, 1536], P('tensor', 'dp')
- grad_norm2: float32 [1536], P('dp')
- grad_router: float32 [1536, 40], P('dp')
- grad_gate: float32 [40, 1536, 512], P(None, 'dp', 'tensor')
- grad_up: float32 [40, 1536, 512], P(None, 'dp', 'tensor')
- grad_down: float32 [40, 512, 1536], P(None, 'tensor', 'dp')
Inputs may be any that keep to these rules, and one draw needn't show every extreme that they name: `routes`: each row names 8 different experts. Among the 1024 rows of one index of dp no expert is named more than 256 times, and in every draw some expert is named exactly 256 times in some such block.
All inputs are finite; a program needn't handle non-finite values.
Results may differ from a plain program's by a relative error of at most 0.02.
Values may be sent and summed in bfloat16 or wider, within the bound.
No kernel may reach another device: no remote copies, remote signals or barrier semaphores. Data moves between devices by JAX's collectives and lax.ppermute only.
A program may use at most 448 MiB of HBM per device.

v0:
```python
import jax
import jax.numpy as jnp
from jax import lax
from jax.sharding import PartitionSpec as P

HEAD_DIM = 64
CAP = 256


EPSILON = 1e-05
HIGHEST = lax.Precision.HIGHEST


def norm_forward(values, gain):
    scale = lax.rsqrt(jnp.mean(values * values, axis=-1, keepdims=True) + EPSILON)
    return (values * scale * gain, scale)


def norm_backward(values, scale, gain, grad_normed):
    normal_x = values * scale
    grad_hat = grad_normed * gain
    grad_values = scale * (
        grad_hat - normal_x * jnp.mean(grad_hat * normal_x, axis=-1, keepdims=True)
    )
    return (grad_values, jnp.sum(grad_normed * normal_x, axis=0))


def rotary_tables(row_count, seq_len, half):
    position = (jnp.arange(row_count, dtype=jnp.int32) % seq_len).astype(jnp.float32)
    inverse = jnp.power(10000.0, -jnp.arange(half, dtype=jnp.int32).astype(jnp.float32) / half)
    angle = position[:, None] * inverse[None, :]
    return (jnp.cos(angle)[:, None, :], jnp.sin(angle)[:, None, :])


def rotate_forward(tensor, cosine, sine):
    half = tensor.shape[-1] // 2
    first = tensor[..., :half]
    second = tensor[..., half:]
    return jnp.concatenate(
        [first * cosine - second * sine, second * cosine + first * sine], axis=-1
    )


def rotate_backward(tensor, cosine, sine):
    half = tensor.shape[-1] // 2
    first = tensor[..., :half]
    second = tensor[..., half:]
    return jnp.concatenate(
        [first * cosine + second * sine, second * cosine - first * sine], axis=-1
    )


def masked_scores(query, keys, prefix_len):
    seq_len, heads_kv, head_size = keys.shape
    grouped = query.reshape(seq_len, heads_kv, -1, head_size)
    scores = jnp.einsum(
        "qhgd,khd->hgqk", grouped, keys, preferred_element_type=jnp.float32
    ) * head_size ** (-0.5)
    row_ids = jnp.arange(seq_len, dtype=jnp.int32)
    allowed = (row_ids[None, :] <= row_ids[:, None]) | (row_ids[None, :] < prefix_len)
    return (jnp.where(allowed, scores, -1e30), grouped)


def attend_forward(members):
    query, keys, values, prefix_len = members
    scores, grouped = masked_scores(query, keys, prefix_len)
    highest = jnp.max(scores, axis=-1, keepdims=True)
    shifted = jnp.exp(scores - highest)
    summed = jnp.sum(shifted, axis=-1, keepdims=True)
    weights = (shifted / summed).astype(jnp.bfloat16)
    output = jnp.einsum("hgqk,khd->qhgd", weights, values, preferred_element_type=jnp.float32)
    return (output.reshape(query.shape[0], -1).astype(jnp.bfloat16), highest + jnp.log(summed))


def attend_backward(members):
    query, keys, values, grad_mixed, log_total, prefix_len = members
    scores, grouped = masked_scores(query, keys, prefix_len)
    weights = jnp.exp(scores - log_total)
    seq_len, heads_kv, head_size = keys.shape
    grad_grouped = grad_mixed.reshape(seq_len, heads_kv, -1, head_size)
    grad_weights = jnp.einsum(
        "qhgd,khd->hgqk", grad_grouped, values, preferred_element_type=jnp.float32
    )
    grad_scores = (
        weights * (grad_weights - jnp.sum(weights * grad_weights, axis=-1, keepdims=True))
    ).astype(jnp.bfloat16)
    scaling = head_size ** (-0.5)
    grad_query = (
        jnp.einsum("hgqk,khd->qhgd", grad_scores, keys, preferred_element_type=jnp.float32)
        * scaling
    )
    grad_keys = (
        jnp.einsum("hgqk,qhgd->khd", grad_scores, grouped, preferred_element_type=jnp.float32)
        * scaling
    )
    grad_values = jnp.einsum(
        "hgqk,qhgd->khd",
        weights.astype(jnp.bfloat16),
        grad_grouped,
        preferred_element_type=jnp.float32,
    )
    return (grad_query.reshape(seq_len, -1, head_size), grad_keys, grad_values)


def slot_index(group_routes, n_experts, capacity):
    flat_experts = group_routes.reshape(-1)
    hits = (flat_experts[:, None] == jnp.arange(n_experts, dtype=jnp.int32)[None, :]).astype(
        jnp.int32
    )
    earlier = jnp.cumsum(hits, axis=0) - hits
    return flat_experts * capacity + jnp.sum(earlier * hits, axis=1)


def on_device(
    tokens,
    cotangent,
    prefix,
    routes,
    norm1,
    w_query,
    w_key,
    w_value,
    w_out,
    norm2,
    w_router,
    w_gate,
    w_up,
    w_down,
):
    group = routes.shape[0]
    top_count = routes.shape[1]
    n_seq = prefix.shape[0]
    seq_len = group // n_seq
    n_experts = w_gate.shape[0]
    capacity = CAP
    width = tokens.shape[1]
    f32 = jnp.float32
    bf16 = jnp.bfloat16
    gathered = (
        lax.all_gather(norm1, "dp", axis=0, tiled=True),
        lax.all_gather(w_query, "dp", axis=0, tiled=True),
        lax.all_gather(w_key, "dp", axis=0, tiled=True),
        lax.all_gather(w_value, "dp", axis=0, tiled=True),
        lax.all_gather(w_out, "dp", axis=1, tiled=True),
        lax.all_gather(norm2, "dp", axis=0, tiled=True),
        lax.all_gather(w_router, "dp", axis=0, tiled=True),
        lax.all_gather(w_gate, "dp", axis=1, tiled=True),
        lax.all_gather(w_up, "dp", axis=1, tiled=True),
        lax.all_gather(w_down, "dp", axis=2, tiled=True),
    )
    (
        gain_one,
        query_full,
        key_full,
        value_full,
        out_full,
        gain_two,
        router_full,
        gate_full,
        up_full,
        down_full,
    ) = gathered
    gain_one = gain_one.astype(f32)
    gain_two = gain_two.astype(f32)
    values_in = tokens.astype(f32)
    normed_one, scale_one = norm_forward(values_in, gain_one)
    group_one = lax.all_gather(normed_one.astype(bf16), "tensor", axis=0, tiled=True)
    cosine, sine = rotary_tables(group, seq_len, HEAD_DIM // 2)
    query_pre = jnp.dot(group_one, query_full, preferred_element_type=f32).reshape(
        group, -1, HEAD_DIM
    )
    key_pre = jnp.dot(group_one, key_full, preferred_element_type=f32).reshape(group, -1, HEAD_DIM)
    query_rot = (
        rotate_forward(query_pre, cosine, sine).astype(bf16).reshape(n_seq, seq_len, -1, HEAD_DIM)
    )
    key_rot = (
        rotate_forward(key_pre, cosine, sine).astype(bf16).reshape(n_seq, seq_len, -1, HEAD_DIM)
    )
    value_all = (
        jnp.dot(group_one, value_full, preferred_element_type=f32)
        .astype(bf16)
        .reshape(n_seq, seq_len, -1, HEAD_DIM)
    )
    attended, log_total = lax.map(attend_forward, (query_rot, key_rot, value_all, prefix))
    attended = attended.reshape(group, -1)
    middle = values_in + lax.psum_scatter(
        jnp.dot(attended, out_full, preferred_element_type=f32),
        "tensor",
        scatter_dimension=0,
        tiled=True,
    )
    normed_two, scale_two = norm_forward(middle, gain_two)
    group_two = lax.all_gather(normed_two.astype(bf16), "tensor", axis=0, tiled=True)
    cot_group = lax.all_gather(cotangent, "tensor", axis=0, tiled=True)
    logits = jnp.dot(group_two, router_full, preferred_element_type=f32)
    route_hits = (
        routes[:, :, None] == jnp.arange(n_experts, dtype=jnp.int32)[None, None, :]
    ).astype(f32)
    chosen = jnp.sum(route_hits * logits[:, None, :], axis=-1)
    gates = jax.nn.softmax(chosen, axis=-1)
    flat_slots = slot_index(routes, n_experts, capacity)
    owners = (
        jnp.zeros((n_experts * capacity,), jnp.int32)
        .at[flat_slots]
        .set(jnp.arange(group * top_count, dtype=jnp.int32) // top_count)
    )
    slot_gates = jnp.zeros((n_experts * capacity,), f32).at[flat_slots].set(gates.reshape(-1))
    expert_step = 8
    blocks = n_experts // expert_step
    owner_blocks = owners.reshape(blocks, expert_step * capacity)
    gate_blocks = slot_gates.reshape(blocks, expert_step * capacity)

    def expert_forward(running, members):
        owner_ids, block_gates, gate_w, up_w, down_w = members
        stacked = group_two[owner_ids].reshape(expert_step, capacity, width)
        gate_part = jnp.einsum("ecd,edf->ecf", stacked, gate_w, preferred_element_type=f32)
        up_part = jnp.einsum("ecd,edf->ecf", stacked, up_w, preferred_element_type=f32)
        hidden = (jax.nn.silu(gate_part) * up_part).astype(bf16)
        expert_out = jnp.einsum("ecf,efd->ecd", hidden, down_w, preferred_element_type=f32).reshape(
            -1, width
        )
        gate_grad = jnp.sum(cot_group[owner_ids].astype(f32) * expert_out, axis=1)
        running = running.at[owner_ids].add(block_gates[:, None] * expert_out)
        return (running, (gate_part, up_part, gate_grad))

    expert_total, kept = lax.scan(
        expert_forward,
        jnp.zeros((group, width), f32),
        (
            owner_blocks,
            gate_blocks,
            gate_full.reshape(blocks, expert_step, width, -1),
            up_full.reshape(blocks, expert_step, width, -1),
            down_full.reshape(blocks, expert_step, -1, width),
        ),
    )
    gate_parts, up_parts, gate_grads = kept
    expert_share = lax.psum_scatter(
        expert_total.astype(jnp.bfloat16), "tensor", scatter_dimension=0, tiled=True
    ).astype(jnp.float32)
    mixed = (middle + expert_share).astype(bf16)
    query_back, key_back, value_back, out_back, router_back, gate_back, up_back, down_back = (
        lax.all_gather(w_query, "dp", axis=0, tiled=True),
        lax.all_gather(w_key, "dp", axis=0, tiled=True),
        lax.all_gather(w_value, "dp", axis=0, tiled=True),
        lax.all_gather(w_out, "dp", axis=1, tiled=True),
        lax.all_gather(w_router, "dp", axis=0, tiled=True),
        lax.all_gather(w_gate, "dp", axis=1, tiled=True),
        lax.all_gather(w_up, "dp", axis=1, tiled=True),
        lax.all_gather(w_down, "dp", axis=2, tiled=True),
    )

    def expert_backward(running, members):
        owner_ids, block_gates, gate_part, up_part, gate_w, up_w, down_w = members
        stacked = group_two[owner_ids].reshape(expert_step, capacity, width)
        sigmoid_g = jax.nn.sigmoid(gate_part)
        silu_g = gate_part * sigmoid_g
        hidden = (silu_g * up_part).astype(bf16)
        grad_exp = (
            (block_gates[:, None] * cot_group[owner_ids].astype(f32))
            .astype(bf16)
            .reshape(expert_step, capacity, width)
        )
        grad_hidden = jnp.einsum("ecd,efd->ecf", grad_exp, down_w, preferred_element_type=f32)
        grad_down_w = jnp.einsum("ecf,ecd->efd", hidden, grad_exp, preferred_element_type=f32)
        grad_gate_part = (
            grad_hidden * up_part * sigmoid_g * (1.0 + gate_part * (1.0 - sigmoid_g))
        ).astype(bf16)
        grad_up_part = (grad_hidden * silu_g).astype(bf16)
        grad_gate_w = jnp.einsum(
            "ecd,ecf->edf", stacked, grad_gate_part, preferred_element_type=f32
        )
        grad_up_w = jnp.einsum("ecd,ecf->edf", stacked, grad_up_part, preferred_element_type=f32)
        grad_stacked = jnp.einsum(
            "ecf,edf->ecd", grad_gate_part, gate_w, preferred_element_type=f32
        ) + jnp.einsum("ecf,edf->ecd", grad_up_part, up_w, preferred_element_type=f32)
        running = running.at[owner_ids].add(grad_stacked.reshape(-1, width))
        return (running, (grad_gate_w, grad_up_w, grad_down_w))

    grad_group_two, expert_grads = lax.scan(
        expert_backward,
        jnp.zeros((group, width), f32),
        (
            owner_blocks,
            gate_blocks,
            gate_parts,
            up_parts,
            gate_back.reshape(blocks, expert_step, width, -1),
            up_back.reshape(blocks, expert_step, width, -1),
            down_back.reshape(blocks, expert_step, -1, width),
        ),
    )
    grad_gate_w, grad_up_w, grad_down_w = expert_grads
    grad_gate_w = grad_gate_w.reshape(n_experts, width, -1)
    grad_up_w = grad_up_w.reshape(n_experts, width, -1)
    grad_down_w = grad_down_w.reshape(n_experts, -1, width)
    grad_gates = gate_grads.reshape(-1)[flat_slots].reshape(group, top_count)
    grad_chosen = gates * (grad_gates - jnp.sum(gates * grad_gates, axis=-1, keepdims=True))
    grad_logits = jnp.sum(grad_chosen[:, :, None] * route_hits, axis=1)
    router_float = router_back.astype(f32)
    grad_group_two = grad_group_two + jnp.dot(grad_logits, router_float.T, precision=HIGHEST)
    grad_router_part = jnp.dot(group_two.astype(f32).T, grad_logits, precision=HIGHEST)
    grad_normed_two = lax.psum_scatter(
        grad_group_two.astype(jnp.bfloat16), "tensor", scatter_dimension=0, tiled=True
    ).astype(jnp.float32)
    grad_middle_part, grad_gain_two = norm_backward(middle, scale_two, gain_two, grad_normed_two)
    grad_middle = cotangent.astype(f32) + grad_middle_part
    grad_branch = lax.all_gather(grad_middle.astype(bf16), "tensor", axis=0, tiled=True)
    grad_out_w = jnp.dot(attended.T, grad_branch, preferred_element_type=f32)
    grad_attended = (
        jnp.einsum("td,cd->tc", grad_branch, out_back, preferred_element_type=f32)
        .astype(bf16)
        .reshape(n_seq, seq_len, -1)
    )
    grad_query, grad_keys, grad_values = lax.map(
        attend_backward, (query_rot, key_rot, value_all, grad_attended, log_total, prefix)
    )
    grad_query_pre = (
        rotate_backward(grad_query.reshape(group, -1, HEAD_DIM), cosine, sine)
        .astype(bf16)
        .reshape(group, -1)
    )
    grad_key_pre = (
        rotate_backward(grad_keys.reshape(group, -1, HEAD_DIM), cosine, sine)
        .astype(bf16)
        .reshape(group, -1)
    )
    grad_value_pre = grad_values.reshape(group, -1).astype(bf16)
    grad_query_w = jnp.dot(group_one.T, grad_query_pre, preferred_element_type=f32)
    grad_key_w = jnp.dot(group_one.T, grad_key_pre, preferred_element_type=f32)
    grad_value_w = jnp.dot(group_one.T, grad_value_pre, preferred_element_type=f32)
    result = jnp.einsum("tc,dc->td", grad_query_pre, query_back, preferred_element_type=f32)
    result = result + jnp.einsum("tc,dc->td", grad_key_pre, key_back, preferred_element_type=f32)
    grad_normed_one = lax.psum_scatter(
        (
            result + jnp.einsum("tc,dc->td", grad_value_pre, value_back, preferred_element_type=f32)
        ).astype(jnp.bfloat16),
        "tensor",
        scatter_dimension=0,
        tiled=True,
    ).astype(jnp.float32)
    grad_input_part, grad_gain_one = norm_backward(values_in, scale_one, gain_one, grad_normed_one)
    grad_tokens = grad_middle + grad_input_part
    shard_query, shard_key, shard_value, shard_out, shard_gate, shard_up, shard_down = (
        lax.psum_scatter(grad_query_w, "dp", scatter_dimension=0, tiled=True),
        lax.psum_scatter(grad_key_w, "dp", scatter_dimension=0, tiled=True),
        lax.psum_scatter(grad_value_w, "dp", scatter_dimension=0, tiled=True),
        lax.psum_scatter(grad_out_w, "dp", scatter_dimension=1, tiled=True),
        lax.psum_scatter(grad_gate_w, "dp", scatter_dimension=1, tiled=True),
        lax.psum_scatter(grad_up_w, "dp", scatter_dimension=1, tiled=True),
        lax.psum_scatter(grad_down_w, "dp", scatter_dimension=2, tiled=True),
    )
    sum_gain_one, sum_gain_two, sum_router = lax.psum(
        (grad_gain_one, grad_gain_two, grad_router_part), ("dp", "tensor")
    )
    rows_data = norm1.shape[0]
    first_data = lax.axis_index("dp") * rows_data
    grad_norm1 = lax.dynamic_slice_in_dim(sum_gain_one, first_data, rows_data, 0)
    grad_norm2 = lax.dynamic_slice_in_dim(sum_gain_two, first_data, rows_data, 0)
    grad_router = lax.dynamic_slice_in_dim(sum_router, first_data, rows_data, 0)
    return (
        mixed,
        grad_tokens,
        grad_norm1,
        shard_query,
        shard_key,
        shard_value,
        shard_out,
        grad_norm2,
        grad_router,
        shard_gate,
        shard_up,
        shard_down,
    )


def solution(mesh):
    in_specs = (
        P(("dp", "tensor"), None),
        P(("dp", "tensor"), None),
        P("dp"),
        P("dp", None),
        P("dp"),
        P("dp", "tensor"),
        P("dp", "tensor"),
        P("dp", "tensor"),
        P("tensor", "dp"),
        P("dp"),
        P("dp", None),
        P(None, "dp", "tensor"),
        P(None, "dp", "tensor"),
        P(None, "tensor", "dp"),
    )
    out_specs = (
        P(("dp", "tensor"), None),
        P(("dp", "tensor"), None),
        P("dp"),
        P("dp", "tensor"),
        P("dp", "tensor"),
        P("dp", "tensor"),
        P("tensor", "dp"),
        P("dp"),
        P("dp", None),
        P(None, "dp", "tensor"),
        P(None, "dp", "tensor"),
        P(None, "tensor", "dp"),
    )
    return jax.shard_map(
        on_device, mesh=mesh, in_specs=in_specs, out_specs=out_specs, check_vma=False
    )
```

profile of v0, /device:TPU:0, one launch (start us, length us, event | category | flops | bytes accessed | tf_op | source)
XLA Modules:
  0.0 3935.6 jit_solution(10461136271433551710)
XLA Ops:
  12.2 23.4 all-reduce.3
  40.2 31.2 all_gather.53
  71.4 31.8 all_gather.52
  112.4 10.7 fusion.100
  123.1 10.4 fusion.46
  135.4 10.6 fusion.70
  156.8 57.6 %reduce-scatter.12.cloned.1.call-done = f32[256,1536]{1,0:T(8,128)} async-done(((f32[1024,1536]{1,0:T(8,128)}), f32[256,1536]{1,0:T(8,128)}) %reduce-scatter.12.cloned.1.call-update) | async-done | bytes 1572880 | tf_op jit(solution)/shard_map/reduce_scatter | solution.py:186
  221.0 30.9 all-gather
  252.7 11.9 reduce-window.6
  267.6 30.5 scatter_custom_fusion.2
  303.1 30.5 scatter_custom_fusion.3
  333.6 129.0 %all-gather.23.cloned.1.call-done = bf16[40,128,1536]{1,2,0:T(8,128)(2,1)} async-done(((bf16[40,128,192]{1,2,0:T(8,128)(2,1)}), bf16[40,128,1536]{1,2,0:T(8,128)(2,1)}) %all-gather.23.cloned.1.call-update) | async-done | bytes 15728656 | tf_op jit(solution)/shard_map/all_gather | solution.py:149
  462.6 20.8 copy.76
  490.8 216.7 %all-gather.19.cloned.1.call-done = bf16[40,1536,128]{2,1,0:T(8,128)(2,1)} async-done(((bf16[40,192,128]{2,1,0:T(8,128)(2,1)}), bf16[40,1536,128]{2,1,0:T(8,128)(2,1)}) %all-gather.19.cloned.1.call-update) | async-done | bytes 15728656 | tf_op jit(solution)/shard_map/all_gather | solution.py:147
  707.5 214.9 %all-gather.21.cloned.1.call-done = bf16[40,1536,128]{2,1,0:T(8,128)(2,1)} async-done(((bf16[40,192,128]{2,1,0:T(8,128)(2,1)}), bf16[40,1536,128]{2,1,0:T(8,128)(2,1)}) %all-gather.21.cloned.1.call-update) | async-done | bytes 15728656 | tf_op jit(solution)/shard_map/all_gather | solution.py:148
  925.8 408.8 %while.7 = (s32[]{:T(128)}, f32[1024,1536]{1,0:T(8,128)}, f32[5,8,256,128]{3,2,1,0:T(8,128)}, f32[5,8,256,128]{3,2,1,0:T(8,128)}, f32[5,2048]{1,0:T(8,128)S(1)},...) while((s32[]{:T(128)}, f32[1024,1536]{1,0:T(8,128)}, ...), condition=%wide.region_16.17_spmd, body=%wide.region_13.16_spmd.sunk | while | flops 2433226752 | bytes 179431648 | solution.py:226
  926.3 10.1 gather_fusion.1
  936.4 15.6 gather_fusion
  970.9 10.0 bitcast_multiply_fusion.8
  980.9 26.8 scatter_fusion
  1007.9 10.1 gather_fusion.1
  1018.1 15.6 gather_fusion
  1062.5 26.8 scatter_fusion
  1089.6 10.1 gather_fusion.1
  1099.7 15.6 gather_fusion
  1144.2 26.8 scatter_fusion
  1171.2 10.1 gather_fusion.1
  1181.4 15.6 gather_fusion
  1225.9 26.8 scatter_fusion
  1253.0 10.1 gather_fusion.1
  1263.1 15.6 gather_fusion
  1307.7 26.8 scatter_fusion
  1335.4 45.5 %gather_fusion.4 = f32[8192]{0:T(1024)S(1)} fusion(f32[10240]{0:T(1024)S(1)} %reshape.422, s32[8192]{0:T(1024)S(1)} %copy-done.52), kind=kCustom, calls=%fused_computation.4 | custom fusion | bytes 98304 | tf_op jit(solution)/shard_map/gather | solution.py:297
  1387.5 482.3 %while.8 = (s32[]{:T(128)}, f32[1024,1536]{1,0:T(8,128)}, f32[5,8,1536,128]{3,2,1,0:T(8,128)}, f32[5,8,1536,128]{3,2,1,0:T(8,128)}, f32[5,8,128,1536]{2,3,1,0:T(...) while((s32[]{:T(128)}, f32[1024,1536]{1,0:T(8,128)}, ...), condition=%wide.region_20.21_spmd, body=%wide.region_18.20_spmd.sunk | while | flops 4861992960 | bytes 169978160 | solution.py:280
  1388.6 10.2 gather_fusion.3
  1398.7 15.6 gather_fusion.2
  1433.4 26.8 scatter_fusion.1
  1485.0 10.2 gather_fusion.3
  1495.1 15.6 gather_fusion.2
  1529.8 26.8 scatter_fusion.1
  1581.3 10.2 gather_fusion.3
  1591.4 15.6 gather_fusion.2
  1626.1 26.8 scatter_fusion.1
  1677.6 10.2 gather_fusion.3
  1687.8 15.6 gather_fusion.2
  1722.4 26.8 scatter_fusion.1
  1773.9 10.2 gather_fusion.3
  1784.1 15.6 gather_fusion.2
  1818.7 26.8 scatter_fusion.1
  1875.9 36.2 reduce-scatter.16.cloned.1.call-done
  1920.1 26.2 all-gather.27.cloned.1.call-done
  1949.9 10.3 fusion.80
  1960.3 16.1 fusion.43
  1976.4 21.8 fusion.45
  2042.6 34.3 all-reduce.6.cloned.1.call-done
  2078.4 39.2 reduce-scatter.18.cloned.1.call-done
  2119.4 39.8 %all-reduce.2 = (f32[1536]{0:T(1024)S(1)}, f32[1536]{0:T(1024)S(1)}) all-reduce(f32[1536]{0:T(1024)S(1)} %get-tuple-element.213, f32[1536]{0:T(1024)S(1)} %get-tuple-element.211), channel_id=1, replica_groups=mesh['dp'=8,'tensor'=4] {'dp','tensor'}, use_global_device_ids=true, to_apply=%region_29.30 | all-reduce | flops 3072 | bytes 24576 | tf_op jit(solution)/shard_map/psum | solution.py:353
  2164.3 61.1 %reduce-scatter.24.cloned.1.call-done = f32[192,128]{1,0:T(8,128)} async-done(((f32[1536,128]{1,0:T(8,128)}), f32[192,128]{1,0:T(8,128)}) %reduce-scatter.24.cloned.1.call-update) | async-done | bytes 98320 | tf_op jit(solution)/shard_map/reduce_scatter | solution.py:347
  2225.4 66.1 %reduce-scatter.22.cloned.1.call-done = f32[192,128]{1,0:T(8,128)} async-done(((f32[1536,128]{1,0:T(8,128)}), f32[192,128]{1,0:T(8,128)}) %reduce-scatter.22.cloned.1.call-update) | async-done | bytes 98320 | tf_op jit(solution)/shard_map/reduce_scatter | solution.py:346
  2291.5 72.7 %reduce-scatter.26.cloned.1.call-done = f32[384,192]{0,1:T(8,128)} async-done(((f32[384,1536]{0,1:T(8,128)}), f32[384,192]{0,1:T(8,128)}) %reduce-scatter.26.cloned.1.call-update) | async-done | bytes 294928 | tf_op jit(solution)/shard_map/reduce_scatter | solution.py:348
  2364.2 72.8 %reduce-scatter.20.cloned.1.call-done = f32[192,384]{1,0:T(8,128)} async-done(((f32[1536,384]{1,0:T(8,128)}), f32[192,384]{1,0:T(8,128)}) %reduce-scatter.20.cloned.1.call-update) | async-done | bytes 294928 | tf_op jit(solution)/shard_map/reduce_scatter | solution.py:345
  2437.0 497.3 %reduce-scatter.32.cloned.1.call-done = f32[40,128,192]{1,2,0:T(8,128)} async-done(((f32[40,128,1536]{1,2,0:T(8,128)}), f32[40,128,192]{1,2,0:T(8,128)}) %reduce-scatter.32.cloned.1.call-update) | async-done | bytes 3932176 | tf_op jit(solution)/shard_map/reduce_scatter | solution.py:351
  2934.3 497.0 %reduce-scatter.28.cloned.1.call-done = f32[40,192,128]{2,1,0:T(8,128)} async-done(((f32[40,1536,128]{2,1,0:T(8,128)}), f32[40,192,128]{2,1,0:T(8,128)}) %reduce-scatter.28.cloned.1.call-update) | async-done | bytes 3932176 | tf_op jit(solution)/shard_map/reduce_scatter | solution.py:349
  3431.3 497.2 %reduce-scatter.30.cloned.1.call-done = f32[40,192,128]{2,1,0:T(8,128)} async-done(((f32[40,1536,128]{2,1,0:T(8,128)}), f32[40,192,128]{2,1,0:T(8,128)}) %reduce-scatter.30.cloned.1.call-update) | async-done | bytes 3932176 | tf_op jit(solution)/shard_map/reduce_scatter | solution.py:350
  (421 shorter events, 487.8 us)
Async XLA Ops:
  7.2 97.9 %all-gather.11.cloned.1.call-start = ((), (), s32[]{:S(2)}) async-start(), calls=%async_computation.11 | async-start | bytes 3932160 | tf_op jit(solution)/shard_map/all_gather | solution.py:167
  8.6 31.5 copy-start.60
  37.9 70.4 %all-gather.13.cloned.1.call-start = ((), (), s32[]{:S(2)}) async-start(), calls=%async_computation.12 | async-start | bytes 1327104 | tf_op jit(solution)/shard_map/all_gather | solution.py:141
  38.7 112.3 %all-gather.15.cloned.1.call-start = ((), (), s32[]{:S(2)}) async-start(), calls=%async_computation.13 | async-start | bytes 1327104 | tf_op jit(solution)/shard_map/all_gather | solution.py:144
  39.4 175.0 %reduce-scatter.12.cloned.1.call-start = ((), (), s32[]{:S(2)}) async-start(), calls=%async_computation.14 | async-start | bytes 7864320 | tf_op jit(solution)/shard_map/reduce_scatter | solution.py:186
  71.4 40.7 %copy-start.14 = (bf16[1536,128]{1,0:T(8,128)(2,1)}, bf16[1536,128]{1,0:T(8,128)(2,1)S(1)}, u32[]{:S(2)}) copy-start(bf16[1536,128]{1,0:T(8,128)(2,1)S(1)} %all_gather.53) | copy-start | bytes 1179652
  103.2 30.3 copy-start.16
  112.4 10.7 copy-start.23
  112.4 10.7 copy-start.25
  123.1 11.6 copy-start.48
  123.1 10.4 copy-start.2
  146.0 10.7 copy-start.28
  156.7 57.7 %copy-start.10 = (bf16[256,1536]{1,0:T(8,128)(2,1)S(1)}, bf16[256,1536]{1,0:T(8,128)(2,1)}, u32[]{:S(2)}) copy-start(bf16[256,1536]{1,0:T(8,128)(2,1)} %param.18) | copy-start | bytes 2359300
  156.7 142.0 %all-gather.17.cloned.1.call-start = ((), (), s32[]{:S(2)}) async-start(), calls=%async_computation.15 | async-start | bytes 3932160 | tf_op jit(solution)/shard_map/all_gather | solution.py:193
  156.8 62.6 %copy-start.44 = (f32[1536]{0:T(1024)}, f32[1536]{0:T(1024)S(1)}, u32[]{:S(2)}) copy-start(f32[1536]{0:T(1024)S(1)} %convert_element_type.218) | copy-start | bytes 18436
  217.3 245.2 %all-gather.23.cloned.1.call-start = ((), (), s32[]{:S(2)}) async-start(), calls=%async_computation.18 | async-start | bytes 17694720 | tf_op jit(solution)/shard_map/all_gather | solution.py:149
  217.9 273.0 %all-gather.25.cloned.1.call-start = ((), (), s32[]{:S(2)}) async-start(), calls=%async_computation.19 | async-start | bytes 3932160 | tf_op jit(solution)/shard_map/all_gather | solution.py:194
  218.6 488.9 %all-gather.19.cloned.1.call-start = ((), (), s32[]{:S(2)}) async-start(), calls=%async_computation.16 | async-start | bytes 17694720 | tf_op jit(solution)/shard_map/all_gather | solution.py:147
  219.4 703.0 %all-gather.21.cloned.1.call-start = ((), (), s32[]{:S(2)}) async-start(), calls=%async_computation.17 | async-start | bytes 17694720 | tf_op jit(solution)/shard_map/all_gather | solution.py:148
  220.1 1692.0 %reduce-scatter.16.cloned.1.call-start = ((), (), s32[]{:S(2)}) async-start(), calls=%async_computation.21 | async-start | bytes 3932160 | tf_op jit(solution)/shard_map/reduce_scatter | solution.py:303
  252.0 46.7 %copy-start.32 = (bf16[1536,40]{0,1:T(8,128)(2,1)}, bf16[1536,40]{0,1:T(8,128)(2,1)S(1)}, u32[]{:S(2)}) copy-start(bf16[1536,40]{0,1:T(8,128)(2,1)S(1)} %reshape.510) | copy-start | bytes 368644
  483.3 442.5 %copy-start = (bf16[1024,1536]{1,0:T(8,128)(2,1)S(1)}, bf16[1024,1536]{1,0:T(8,128)(2,1)}, u32[]{:S(2)}) copy-start(bf16[1024,1536]{1,0:T(8,128)(2,1)} %all-gather.17.cloned.1.call-done) | copy-start | bytes 9437188
  925.8 409.5 %copy-start.52 = (s32[8192]{0:T(1024)S(1)}, s32[8192]{0:T(1024)}, u32[]{:S(2)}) copy-start(s32[8192]{0:T(1024)} %broadcast_clamp_fusion.2) | copy-start | bytes 98308
  952.0 11.4 slice-start
  1033.7 11.4 slice-start
  1115.3 11.4 slice-start
  1197.0 11.5 slice-start
  1278.7 11.5 slice-start
  1335.3 47.9 %copy-start.31 = (f32[1024,8]{0,1:T(8,128)S(1)}, f32[1024,8]{0,1:T(8,128)}, u32[]{:S(2)}) copy-start(f32[1024,8]{0,1:T(8,128)} %copy-done.30) | copy-start | bytes 98308
  1335.3 47.9 %copy-start.54 = (f32[1024]{0:T(1024)S(1)}, f32[1024]{0:T(1024)}, u32[]{:S(2)}) copy-start(f32[1024]{0:T(1024)} %copy-done.53) | copy-start | bytes 12292
  1335.3 47.9 %copy-start.56 = (f32[1024]{0:T(1024)S(1)}, f32[1024]{0:T(1024)}, u32[]{:S(2)}) copy-start(f32[1024]{0:T(1024)} %copy-done.55) | copy-start | bytes 12292
  1335.3 47.9 %copy-start.42 = (s32[1024,8]{0,1:T(8,128)S(1)}, s32[1024,8]{0,1:T(8,128)}, u32[]{:S(2)}) copy-start(s32[1024,8]{0,1:T(8,128)} %param.21) | copy-start | bytes 98308
  1387.5 482.3 %copy-start.27 = (f32[1024,40]{0,1:T(8,128)S(1)}, f32[1024,40]{0,1:T(8,128)}, u32[]{:S(2)}) copy-start(f32[1024,40]{0,1:T(8,128)} %select_reduce_fusion) | copy-start | bytes 491524
  1387.5 482.3 %copy-start.33 = (bf16[1536,40]{0,1:T(8,128)(2,1)S(1)}, bf16[1536,40]{0,1:T(8,128)(2,1)}, u32[]{:S(2)}) copy-start(bf16[1536,40]{0,1:T(8,128)(2,1)} %copy-done.32) | copy-start | bytes 368644
  1460.1 8.7 copy-start.5
  1556.5 8.7 copy-start.5
  1652.8 8.8 copy-start.5
  1749.2 8.7 copy-start.5
  1845.5 8.7 copy-start.5
  1869.7 42.4 %copy-start.45 = (f32[1536]{0:T(1024)S(1)}, f32[1536]{0:T(1024)}, u32[]{:S(2)}) copy-start(f32[1536]{0:T(1024)} %copy-done.44) | copy-start | bytes 18436
  1869.8 42.4 %copy-start.58 = (f32[256]{0:T(256)S(1)}, f32[256]{0:T(256)}, u32[]{:S(2)}) copy-start(f32[256]{0:T(256)} %copy-done.57) | copy-start | bytes 3076
  1875.8 41.8 %copy-start.49 = (f32[2,3,1024]{2,1,0:T(4,128)S(1)}, f32[2,3,1024]{2,1,0:T(4,128)}, u32[]{:S(2)}) copy-start(f32[2,3,1024]{2,1,0:T(4,128)} %copy-done.48) | copy-start | bytes 73732
  1875.8 41.8 %copy-start.51 = (f32[2,3,1024]{2,1,0:T(4,128)S(1)}, f32[2,3,1024]{2,1,0:T(4,128)}, u32[]{:S(2)}) copy-start(f32[2,3,1024]{2,1,0:T(4,128)} %copy-done.50) | copy-start | bytes 73732
  1875.9 70.4 %all-gather.27.cloned.1.call-start = ((), (), s32[]{:S(2)}) async-start(), calls=%async_computation.22 | async-start | bytes 3932160 | tf_op jit(solution)/shard_map/all_gather | solution.py:308
  1917.6 159.2 %all-reduce.6.cloned.1.call-start = ((), (), s32[]{:S(2)}) async-start(), calls=%async_computation.28 | async-start | bytes 491520 | tf_op jit(solution)/shard_map/psum | solution.py:353
  1920.0 197.5 %reduce-scatter.18.cloned.1.call-start = ((), (), s32[]{:S(2)}) async-start(), calls=%async_computation.23 | async-start | bytes 3932160 | tf_op jit(solution)/shard_map/reduce_scatter | solution.py:334
  1949.9 10.4 copy-start.35
  1960.3 57.1 %copy-start.22 = (bf16[2,64,1024]{2,1,0:T(8,128)(2,1)}, bf16[2,64,1024]{2,1,0:T(8,128)(2,1)S(1)}, u32[]{:S(2)}) copy-start(bf16[2,64,1024]{2,1,0:T(8,128)(2,1)S(1)} %fusion.80) | copy-start | bytes 786436
  1976.4 21.8 copy-start.24
  1976.4 21.8 copy-start.26
  1998.2 8.6 copy-start.38
  2020.2 140.3 %reduce-scatter.14.cloned.1.call-start = ((), (), s32[]{:S(2)}) async-start(), calls=%async_computation.20 | async-start | bytes 3932160 | tf_op jit(solution)/shard_map/reduce_scatter | solution.py:238
  2025.3 200.2 %reduce-scatter.24.cloned.1.call-start = ((), (), s32[]{:S(2)}) async-start(), calls=%async_computation.26 | async-start | bytes 884736 | tf_op jit(solution)/shard_map/reduce_scatter | solution.py:347
  2028.2 263.3 %reduce-scatter.22.cloned.1.call-start = ((), (), s32[]{:S(2)}) async-start(), calls=%async_computation.25 | async-start | bytes 884736 | tf_op jit(solution)/shard_map/reduce_scatter | solution.py:346
  2030.2 334.0 %reduce-scatter.26.cloned.1.call-start = ((), (), s32[]{:S(2)}) async-start(), calls=%async_computation.27 | async-start | bytes 2654208 | tf_op jit(solution)/shard_map/reduce_scatter | solution.py:348
  2036.0 401.0 %reduce-scatter.20.cloned.1.call-start = ((), (), s32[]{:S(2)}) async-start(), calls=%async_computation.24 | async-start | bytes 2654208 | tf_op jit(solution)/shard_map/reduce_scatter | solution.py:345
  2040.5 893.9 %reduce-scatter.32.cloned.1.call-start = ((), (), s32[]{:S(2)}) async-start(), calls=%async_computation.31 | async-start | bytes 35389440 | tf_op jit(solution)/shard_map/reduce_scatter | solution.py:351
  2041.2 1390.1 %reduce-scatter.28.cloned.1.call-start = ((), (), s32[]{:S(2)}) async-start(), calls=%async_computation.29 | async-start | bytes 35389440 | tf_op jit(solution)/shard_map/reduce_scatter | solution.py:349
  2041.8 1886.7 %reduce-scatter.30.cloned.1.call-start = ((), (), s32[]{:S(2)}) async-start(), calls=%async_computation.30 | async-start | bytes 35389440 | tf_op jit(solution)/shard_map/reduce_scatter | solution.py:350
  2041.9 75.7 %copy-start.11 = (bf16[256,1536]{1,0:T(8,128)(2,1)S(1)}, bf16[256,1536]{1,0:T(8,128)(2,1)}, u32[]{:S(2)}) copy-start(bf16[256,1536]{1,0:T(8,128)(2,1)} %param.18) | copy-start | bytes 2359300
  2041.9 75.7 %copy-start.47 = (f32[1536]{0:T(1024)S(1)}, f32[1536]{0:T(1024)}, u32[]{:S(2)}) copy-start(f32[1536]{0:T(1024)} %copy-done.46) | copy-start | bytes 18436
  2041.9 75.7 %copy-start.61 = (f32[256]{0:T(256)S(1)}, f32[256]{0:T(256)}, u32[]{:S(2)}) copy-start(f32[256]{0:T(256)} %copy-done.60) | copy-start | bytes 3076
  2041.9 118.5 %copy-start.9 = (f32[256,1536]{1,0:T(8,128)S(1)}, f32[256,1536]{1,0:T(8,128)}, u32[]{:S(2)}) copy-start(f32[256,1536]{1,0:T(8,128)} %copy-done.8) | copy-start | bytes 4718596
  2041.9 118.5 %copy-start.12 = (bf16[256,1536]{1,0:T(8,128)(2,1)S(1)}, bf16[256,1536]{1,0:T(8,128)(2,1)}, u32[]{:S(2)}) copy-start(bf16[256,1536]{1,0:T(8,128)(2,1)} %param.19) | copy-start | bytes 2359300
  (49 other events, 218.1 us)
Sparse Core Ops, SparseCore 0:
  38.0 25.7 all-gather.10
  66.0 42.0 all-gather.12
  110.3 40.5 all-gather.14
  156.9 57.5 reduce-scatter.11
  217.4 28.4 all-gather.16
  248.0 214.5 all-gather.22
  464.1 26.6 all-gather.24
  493.0 214.4 all-gather.18
  709.7 212.6 all-gather.20
  1876.0 36.0 reduce-scatter.15
  1917.7 28.4 all-gather.26
  1951.6 125.1 all-reduce.5
  2079.4 38.1 reduce-scatter.17
  2120.0 38.0 reduce-scatter.13
  2161.8 63.6 reduce-scatter.23
  2229.2 62.2 reduce-scatter.21
  2295.4 68.7 reduce-scatter.25
  2368.1 68.8 reduce-scatter.19
  2441.4 492.8 reduce-scatter.31
  2938.6 492.6 reduce-scatter.27
  3435.8 492.6 reduce-scatter.29
where the time goes:
time: 3950 us; the launch traced here: 3940 us
  waiting for transfers between devices  2540 us (64%)
  matrix products  417 us (11%)
  local copies, waits for them, and re-layouts  414 us (10%)
  other arithmetic  391 us (10%)
  blocking collectives  157 us (4%)
    reduce_scatter x1, waiting for transfers between devices, on_device(): lax.psum_scatter(grad_down_w, 'dp', scatter_dimension=2, tiled=True)  497 us
    reduce_scatter x1, waiting for transfers between devices, on_device(): lax.psum_scatter(grad_up_w, 'dp', scatter_dimension=1, tiled=True)  497 us
    reduce_scatter x1, waiting for transfers between devices, on_device(): lax.psum_scatter(grad_gate_w, 'dp', scatter_dimension=1, tiled=True)  497 us
    all_gather x1, waiting for transfers between devices, on_device(): lax.all_gather(w_gate, 'dp', axis=1, tiled=True)  217 us
    all_gather x1, waiting for transfers between devices, on_device(): lax.all_gather(w_up, 'dp', axis=1, tiled=True)  215 us
    scatter-add x5, other arithmetic, expert_forward(): running = running.at[owner_ids].add(block_gates[:, None] * expert_out)  134 us
    scatter-add x5, other arithmetic, expert_backward(): running = running.at[owner_ids].add(grad_stacked.reshape(-1, width))  134 us
    all_gather x1, waiting for transfers between devices, on_device(): lax.all_gather(w_down, 'dp', axis=2, tiled=True)  129 us
  transfers between devices with their start and end apart: 21, of which 17 were waited for; matrix products, arithmetic and copies ran while one was open for 6% of the time, Pallas kernels for 0%

commit v1 on v0

v1 whole, which is shorter than its diff:
```python
import jax
import jax.numpy as jnp
from jax import lax
from jax.sharding import Mesh, PartitionSpec as P

HEAD_DIM = 64
EPSILON = 1e-05
LANES = 128
HIGHEST = lax.Precision.HIGHEST
f32 = jnp.float32
bf16 = jnp.bfloat16


def rms_scale(values):
    return lax.rsqrt(jnp.mean(values * values, axis=-1, keepdims=True) + EPSILON)


def norm_backward(values, scale, gain, grad_normed):
    normal_x = values * scale
    grad_hat = grad_normed * gain
    grad_values = scale * (
        grad_hat - normal_x * jnp.mean(grad_hat * normal_x, axis=-1, keepdims=True)
    )
    return grad_values, normal_x


def rotary_tables(row_count, half):
    position = jnp.arange(row_count, dtype=jnp.int32).astype(f32)
    inverse = jnp.power(10000.0, -jnp.arange(half, dtype=jnp.int32).astype(f32) / half)
    angle = position[:, None] * inverse[None, :]
    return jnp.cos(angle)[:, None, :], jnp.sin(angle)[:, None, :]


def rotate(tensor, cosine, sine):
    half = tensor.shape[-1] // 2
    first = tensor[..., :half]
    second = tensor[..., half:]
    return jnp.concatenate(
        [first * cosine - second * sine, second * cosine + first * sine], axis=-1
    )


def masked_scores(query, keys, prefix_len):
    seq_len, heads_kv, head_size = keys.shape
    grouped = query.reshape(seq_len, heads_kv, -1, head_size)
    scores = jnp.einsum(
        "qhgd,khd->hgqk", grouped, keys, preferred_element_type=f32
    ) * head_size ** (-0.5)
    row_ids = jnp.arange(seq_len, dtype=jnp.int32)
    allowed = (row_ids[None, :] <= row_ids[:, None]) | (row_ids[None, :] < prefix_len)
    return jnp.where(allowed, scores, -1e30), grouped


def attend_forward(query, keys, values, prefix_len):
    scores, _ = masked_scores(query, keys, prefix_len)
    highest = jnp.max(scores, axis=-1, keepdims=True)
    shifted = jnp.exp(scores - highest)
    summed = jnp.sum(shifted, axis=-1, keepdims=True)
    weights = (shifted / summed).astype(bf16)
    output = jnp.einsum("hgqk,khd->qhgd", weights, values, preferred_element_type=f32)
    return output.reshape(query.shape[0], -1).astype(bf16), highest + jnp.log(summed)


def attend_backward(query, keys, values, grad_mixed, log_total, prefix_len):
    scores, grouped = masked_scores(query, keys, prefix_len)
    weights = jnp.exp(scores - log_total)
    seq_len, heads_kv, head_size = keys.shape
    grad_grouped = grad_mixed.reshape(seq_len, heads_kv, -1, head_size)
    grad_weights = jnp.einsum(
        "qhgd,khd->hgqk", grad_grouped, values, preferred_element_type=f32
    )
    grad_scores = (
        weights * (grad_weights - jnp.sum(weights * grad_weights, axis=-1, keepdims=True))
    ).astype(bf16)
    scaling = head_size ** (-0.5)
    grad_query = (
        jnp.einsum("hgqk,khd->qhgd", grad_scores, keys, preferred_element_type=f32) * scaling
    )
    grad_keys = (
        jnp.einsum("hgqk,qhgd->khd", grad_scores, grouped, preferred_element_type=f32) * scaling
    )
    grad_values = jnp.einsum(
        "hgqk,qhgd->khd", weights.astype(bf16), grad_grouped, preferred_element_type=f32
    )
    return grad_query.reshape(seq_len, -1, head_size), grad_keys, grad_values


def exchange(pieces, axis, size):
    me = lax.axis_index(axis)
    result = jnp.zeros_like(pieces)
    own = lax.dynamic_index_in_dim(pieces, me, 0)
    result = lax.dynamic_update_slice_in_dim(result, own, me, 0)
    for shift in range(1, size):
        piece = lax.dynamic_index_in_dim(pieces, (me + shift) % size, 0)
        got = lax.ppermute(piece, axis, [(m, (m + shift) % size) for m in range(size)])
        result = lax.dynamic_update_slice_in_dim(result, got, (me - shift) % size, 0)
    return result


def solution(mesh):
    n_dp, n_tensor = mesh.shape["dp"], mesh.shape["tensor"]
    inner = 4
    outer = n_dp // inner
    grid = Mesh(mesh.devices.reshape(inner, outer, n_tensor), ("i", "o", "t"))
    dp = ("i", "o")
    shared = ("i", "t")

    def to_owner_order(values):
        rows = values.shape[0]
        if outer == 1:
            return values
        split = jnp.swapaxes(values.reshape(rows, inner, outer, -1), 1, 2)
        if outer == 2:
            split = jnp.where(lax.axis_index("o") == 0, split, split[:, ::-1])
        return split.reshape(rows, -1)

    def from_owner_order(values):
        rows = values.shape[0]
        if outer == 1:
            return values
        split = values.reshape(rows, outer, inner, -1)
        if outer == 2:
            split = jnp.where(lax.axis_index("o") == 0, split, split[:, ::-1])
        return jnp.swapaxes(split, 1, 2).reshape(rows, -1)

    def gather_outer(values):
        if outer == 1:
            return values
        if outer == 2:
            other = lax.ppermute(values, "o", [(0, 1), (1, 0)])
            return jnp.concatenate([values, other], axis=0)
        return lax.all_gather(values, "o", axis=0, tiled=True)

    def reduce_outer(values):
        if outer == 1:
            return values.astype(bf16)
        if outer == 2:
            rows = values.shape[0] // 2
            got = lax.ppermute(values[rows:].astype(bf16), "o", [(0, 1), (1, 0)])
            return (values[:rows] + got.astype(f32)).astype(bf16)
        return lax.psum_scatter(values.astype(bf16), "o", scatter_dimension=0, tiled=True)

    def on_device(
        tokens,
        cotangent,
        prefix,
        routes,
        norm1,
        w_query,
        w_key,
        w_value,
        w_out,
        norm2,
        w_router,
        w_gate,
        w_up,
        w_down,
    ):
        rows, width = tokens.shape
        group = routes.shape[0]
        n_experts, depth, hidden = w_gate.shape
        own_experts = n_experts // inner
        own_hidden = own_experts * hidden
        q_cols, k_cols = w_query.shape[1], w_key.shape[1]
        qkv_cols = q_cols + 2 * k_cols
        attn_cols = qkv_cols + q_cols
        side_cols = -(-(n_experts + 2) // LANES) * LANES
        gate_cols = -(-2 * n_experts // LANES) * LANES
        me_i, me_t = lax.axis_index("i"), lax.axis_index("t")

        weights3 = jnp.stack([w_gate, w_up, jnp.swapaxes(w_down, 1, 2)])
        pieces = weights3.reshape(3, inner, own_experts, depth, hidden)
        pieces = pieces.transpose(1, 3, 0, 2, 4).reshape(inner, depth, 3 * own_hidden)
        owned = gather_outer(exchange(pieces, "i", inner).reshape(inner * depth, -1))
        w_gate_up = owned[:, : 2 * own_hidden]
        w_down_t = owned[:, 2 * own_hidden :]

        side = jnp.concatenate(
            [
                w_router,
                norm1[:, None],
                norm2[:, None],
                jnp.zeros((depth, side_cols - n_experts - 2), bf16),
            ],
            axis=1,
        )
        pack = jnp.concatenate([w_query, w_key, w_value, w_out.T, side], axis=1)
        packed = lax.all_gather(pack, dp, axis=0, tiled=True)
        tokens_all = lax.all_gather(tokens, "t", axis=0, tiled=True).astype(f32)
        w_qkv = packed[:, :qkv_cols]
        w_out_t = packed[:, qkv_cols:attn_cols]
        router = packed[:, attn_cols : attn_cols + n_experts]
        gains = packed[:, attn_cols + n_experts : attn_cols + n_experts + 2].astype(f32).T
        gain_one, gain_two = gains[0], gains[1]

        cot_order, _ = lax.optimization_barrier((to_owner_order(cotangent), tokens_all))
        cot_all = lax.all_gather(cot_order, shared, axis=0, tiled=True)

        normal_all = tokens_all * rms_scale(tokens_all)
        normed_one = (normal_all * gain_one).astype(bf16)
        cosine, sine = rotary_tables(group, HEAD_DIM // 2)
        qkv = jnp.dot(normed_one, w_qkv, preferred_element_type=f32)
        query = rotate(qkv[:, :q_cols].reshape(group, -1, HEAD_DIM), cosine, sine).astype(bf16)
        keys = rotate(
            qkv[:, q_cols : q_cols + k_cols].reshape(group, -1, HEAD_DIM), cosine, sine
        ).astype(bf16)
        values = qkv[:, q_cols + k_cols :].astype(bf16).reshape(group, -1, HEAD_DIM)
        attended, log_total = attend_forward(query, keys, values, prefix[0])
        branch = lax.dot_general(
            attended, w_out_t, (((1,), (1,)), ((), ())), preferred_element_type=f32
        ).astype(bf16)
        tokens_f = tokens.astype(f32)
        middle = tokens_f + lax.psum_scatter(
            branch, "t", scatter_dimension=0, tiled=True
        ).astype(f32)
        scale_two = rms_scale(middle)
        normed_two = (middle * scale_two * gain_two).astype(bf16)

        logits = jnp.dot(normed_two, router, preferred_element_type=f32)
        own_routes = lax.dynamic_slice_in_dim(routes, me_t * rows, rows, 0)
        expert_ids = jnp.arange(n_experts, dtype=jnp.int32)
        routed = jnp.any(own_routes[:, :, None] == expert_ids[None, None, :], axis=1)
        gates = jnp.where(routed, jax.nn.softmax(jnp.where(routed, logits, -1e30), axis=-1), 0.0)
        gates_high = gates.astype(bf16)
        gates_low = (gates - gates_high.astype(f32)).astype(bf16)
        shipped = jnp.concatenate(
            [
                to_owner_order(normed_two),
                gates_high,
                gates_low,
                jnp.zeros((rows, gate_cols - 2 * n_experts), bf16),
            ],
            axis=1,
        )
        shared_all = lax.all_gather(shipped, shared, axis=0, tiled=True)
        count = shared_all.shape[0]
        normed_all = shared_all[:, :width]

        slot = jnp.arange(gate_cols, dtype=jnp.int32)[:, None]
        owner = me_i * own_experts + jnp.arange(own_hidden, dtype=jnp.int32)[None, :] // hidden
        spread = ((slot == owner) | (slot == owner + n_experts)).astype(bf16)
        gate_wide = jnp.dot(shared_all[:, width:], spread, preferred_element_type=f32)
        gate_up = jnp.dot(normed_all, w_gate_up, preferred_element_type=f32)
        gate_part, up_part = gate_up[:, :own_hidden], gate_up[:, own_hidden:]
        cot_part = jnp.dot(cot_all, w_down_t, preferred_element_type=f32)
        sigmoid_g = jax.nn.sigmoid(gate_part)
        silu_g = gate_part * sigmoid_g
        act = silu_g * up_part
        gated = (act * gate_wide).astype(bf16)
        grad_act = cot_part * gate_wide
        grad_gate_up = jnp.concatenate(
            [
                (grad_act * up_part * sigmoid_g * (1.0 + gate_part * (1.0 - sigmoid_g))).astype(
                    bf16
                ),
                (grad_act * silu_g).astype(bf16),
            ],
            axis=1,
        )
        grad_gates = jnp.sum((act * cot_part).reshape(count, own_experts, hidden), axis=-1)
        gate_block = lax.dynamic_update_slice(
            jnp.zeros((count, side_cols), f32), grad_gates, (0, me_i * own_experts)
        )
        grad_normed_part = lax.dot_general(
            grad_gate_up, w_gate_up, (((1,), (1,)), ((), ())), preferred_element_type=f32
        )
        grad_shipped = jnp.concatenate([grad_normed_part, gate_block], axis=1).astype(bf16)
        grad_back = lax.psum_scatter(grad_shipped, shared, scatter_dimension=0, tiled=True)

        expert_part = lax.dot_general(
            gated, w_down_t, (((1,), (1,)), ((), ())), preferred_element_type=f32
        ).astype(bf16)
        contract_rows = (((0,), (0,)), ((), ()))
        grad_w = jnp.concatenate(
            [
                lax.dot_general(
                    normed_all, grad_gate_up, contract_rows, preferred_element_type=f32
                ),
                lax.dot_general(cot_all, gated, contract_rows, preferred_element_type=f32),
            ],
            axis=1,
        )

        grad_back = grad_back.astype(f32)
        grad_chosen = grad_back[:, width : width + n_experts]
        grad_logits = gates * (
            grad_chosen - jnp.sum(gates * grad_chosen, axis=-1, keepdims=True)
        )
        grad_normed_two = from_owner_order(grad_back[:, :width]) + jnp.dot(
            grad_logits, router.astype(f32).T, precision=HIGHEST
        )
        grad_middle_part, normal_two = norm_backward(
            middle, scale_two, gain_two, grad_normed_two
        )
        grad_middle = cotangent.astype(f32) + grad_middle_part
        grad_gain_two = jnp.sum(grad_normed_two * normal_two, axis=0)
        grad_router_part = lax.dot_general(
            normed_two.astype(f32), grad_logits, contract_rows, precision=HIGHEST
        )
        grad_branch = lax.all_gather(grad_middle.astype(bf16), "t", axis=0, tiled=True)

        grad_branch_tie, expert_part = lax.optimization_barrier((grad_branch, expert_part))
        expert_share = from_owner_order(
            lax.psum_scatter(expert_part, shared, scatter_dimension=0, tiled=True)
        ).astype(f32)
        mixed = (middle + expert_share).astype(bf16)

        grad_attended = jnp.dot(
            grad_branch_tie, w_out_t, preferred_element_type=f32
        ).astype(bf16)
        grad_query, grad_keys, grad_values = attend_backward(
            query, keys, values, grad_attended, log_total, prefix[0]
        )
        grad_qkv = jnp.concatenate(
            [
                rotate(grad_query, cosine, -sine).astype(bf16).reshape(group, -1),
                rotate(grad_keys, cosine, -sine).astype(bf16).reshape(group, -1),
                grad_values.astype(bf16).reshape(group, -1),
            ],
            axis=1,
        )
        grad_normed_one = lax.dot_general(
            grad_qkv, w_qkv, (((1,), (1,)), ((), ())), preferred_element_type=f32
        )
        grad_gain_one = jnp.sum(grad_normed_one * normal_all, axis=0)
        own_grad_one = lax.psum_scatter(
            grad_normed_one.astype(bf16), "t", scatter_dimension=0, tiled=True
        ).astype(f32)
        grad_input_part, _ = norm_backward(tokens_f, rms_scale(tokens_f), gain_one, own_grad_one)
        grad_tokens = grad_middle + grad_input_part

        grad_attn = jnp.concatenate(
            [
                lax.dot_general(normed_one, grad_qkv, contract_rows, preferred_element_type=f32),
                lax.dot_general(grad_branch_tie, attended, contract_rows, preferred_element_type=f32),
            ],
            axis=1,
        ).astype(bf16)
        shard_attn = lax.psum_scatter(grad_attn, dp, scatter_dimension=0, tiled=True).astype(f32)
        sums = jnp.concatenate(
            [grad_router_part, grad_gain_one[:, None], grad_gain_two[:, None]], axis=1
        )
        sums = lax.psum(sums, ("i", "o", "t"))
        first = (me_i * outer + lax.axis_index("o")) * depth
        own_sums = lax.dynamic_slice_in_dim(sums, first, depth, 0)

        reduced = reduce_outer(grad_w).reshape(inner, depth, 3 * own_hidden)
        returned = exchange(reduced, "i", inner).reshape(inner, depth, 3, own_experts, hidden)
        grad3 = returned.transpose(2, 0, 3, 1, 4).reshape(3, n_experts, depth, hidden).astype(f32)
        return (
            mixed,
            grad_tokens,
            own_sums[:, n_experts],
            shard_attn[:, :q_cols],
            shard_attn[:, q_cols : q_cols + k_cols],
            shard_attn[:, q_cols + k_cols : qkv_cols],
            shard_attn[:, qkv_cols:].T,
            own_sums[:, n_experts + 1],
            own_sums[:, :n_experts],
            grad3[0],
            grad3[1],
            jnp.swapaxes(grad3[2], 1, 2),
        )

    in_specs = (
        P(("i", "o", "t"), None),
        P(("i", "o", "t"), None),
        P(dp),
        P(dp, None),
        P(dp),
        P(dp, "t"),
        P(dp, "t"),
        P(dp, "t"),
        P("t", dp),
        P(dp),
        P(dp, None),
        P(None, dp, "t"),
        P(None, dp, "t"),
        P(None, "t", dp),
    )
    out_specs = (
        P(("i", "o", "t"), None),
        P(("i", "o", "t"), None),
        P(dp),
        P(dp, "t"),
        P(dp, "t"),
        P(dp, "t"),
        P("t", dp),
        P(dp),
        P(dp, None),
        P(None, dp, "t"),
        P(None, dp, "t"),
        P(None, "t", dp),
    )
    return jax.shard_map(
        on_device, mesh=grid, in_specs=in_specs, out_specs=out_specs, check_vma=False
    )
```

time: 3950 us -> 1480 us (0.37)
  waiting for transfers between devices: 2540 us -> 883 us
  other arithmetic: 391 us -> 93.6 us
  local copies, waits for them, and re-layouts: 414 us -> 132 us
  blocking collectives: 157 us -> 0 us
  matrix products: 417 us -> 318 us
    reduce_scatter x11 -> x4, waiting for transfers between devices: 1900 us -> 268 us  [the longest x1 207 us: on_device(): lax.psum_scatter(grad_shipped, shared, scatter_dimension=0, tiled=True)]
    ppermute x0 -> x8, waiting for transfers between devices: none -> 520 us  [the longest x6 243 us: exchange(): lax.ppermute(piece, axis, [(m, (m + shift) % size) for m in range(size)])]
    all_gather x9 -> x5, waiting for transfers between devices: 599 us -> 92.3 us  [the longest x1 64.6 us: on_device(): packed = lax.all_gather(pack, dp, axis=0, tiled=True)]
    gather x21 -> x0, local copies, waits for them, and re-layouts: 303 us -> none  [the longest x5 78 us: expert_backward(): cot_group[owner_ids].astype(f32)]
    scatter-add x10 -> x0, other arithmetic: 268 us -> none  [the longest x5 134 us: expert_forward(): running = running.at[owner_ids].add(block_gates[:, None] * expert_out)]
    dot_general x64 -> x20, matrix products: 393 us -> 296 us  [the longest x1 50.8 us: on_device(): cot_part = jnp.dot(cot_all, w_down_t, preferred_element_type=f32)]
    all_gather x3 -> x0, blocking collectives: 93.9 us -> none  [the longest x1 31.8 us: on_device(): lax.all_gather(w_value, 'dp', axis=0, tiled=True)]
    scatter x2 -> x0, local copies, waits for them, and re-layouts: 60.9 us -> none  [the longest x1 30.5 us: on_device(): owners = jnp.zeros((n_experts * capacity,), jnp.int32).at[flat_slots].set...]
  transfers between devices with their start and end apart: 21 -> 19, of which waited for: 17 -> 12; matrix products, arithmetic and copies ran while one was open for 6% -> 20% of each run, Pallas kernels for 0% -> 0%
where the time goes in v1:
time: 1480 us; the launch traced here: 1460 us
  waiting for transfers between devices  883 us (60%)
  matrix products  318 us (21%)
  local copies, waits for them, and re-layouts  132 us (9%)
  other arithmetic  93.6 us (6%)
  between operations  16.1 us (1%)
  starting transfers between devices  14.8 us (1%)
    ppermute x6, waiting for transfers between devices, exchange(): lax.ppermute(piece, axis, [(m, (m + shift) % size) for m in range(size)])  243 us
    reduce_scatter x1, waiting for transfers between devices, on_device(): lax.psum_scatter(grad_shipped, shared, scatter_dimension=0, tiled=True)  207 us
    ppermute x1, waiting for transfers between devices, reduce_outer(): got = lax.ppermute(values[rows:].astype(bf16), 'o', [(0, 1), (1, 0)])  150 us
    ppermute x1, waiting for transfers between devices, gather_outer(): other = lax.ppermute(values, 'o', [(0, 1), (1, 0)])  128 us
    all_gather x1, waiting for transfers between devices, on_device(): packed = lax.all_gather(pack, dp, axis=0, tiled=True)  64.6 us
    dot_general x1, matrix products, on_device(): cot_part = jnp.dot(cot_all, w_down_t, preferred_element_type=f32)  50.8 us
    dot_general x1, matrix products, on_device(): gate_up = jnp.dot(normed_all, w_gate_up, preferred_element_type=f32)  42.5 us
    dot_general x1, matrix products, on_device(): lax.dot_general(normed_all, grad_gate_up, contract_rows, preferred_elemen...  42.1 us
  transfers between devices with their start and end apart: 19, of which 12 were waited for; matrix products, arithmetic and copies ran while one was open for 20% of the time, Pallas kernels for 0%

profile of v1, /device:TPU:0, one launch (start us, length us, event | category | flops | bytes accessed | tf_op | source)
XLA Modules:
  0.0 1456.7 jit_solution(1669380362670273995)
XLA Ops:
  15.5 25.3 %all-gather.6.cloned.1.call-done = bf16[1024,1536]{1,0:T(8,128)(2,1)} async-done(((bf16[256,1536]{1,0:T(8,128)(2,1)}), bf16[1024,1536]{1,0:T(8,128)(2,1)}) %all-gather.6.cloned.1.call-update) | async-done | bytes 3145744 | tf_op jit(solution)/shard_map/all_gather | solution.py:189
  40.8 2.7 multiply_reduce_fusion.1
  43.6 64.6 %all-gather.8.cloned.1.call-done = bf16[1536,1152]{1,0:T(8,128)(2,1)} async-done(((bf16[192,1152]{1,0:T(8,128)(2,1)}), bf16[1536,1152]{1,0:T(8,128)(2,1)}) %all-gather.8.cloned.1.call-update) | async-done | bytes 3538960 | tf_op jit(solution)/shard_map/all_gather | solution.py:188
  110.1 3.9 fusion.25
  116.8 5.6 fusion.76
  122.5 4.0 fusion.3
  126.5 4.4 copy-done.2
  131.4 10.5 fusion.32
  142.0 5.1 convolution_convert_fusion.2
  147.6 36.3 %reduce-scatter.8.cloned.1.call-done = bf16[256,1536]{1,0:T(8,128)(2,1)} async-done(((bf16[1024,1536]{1,0:T(8,128)(2,1)}), bf16[256,1536]{1,0:T(8,128)(2,1)}) %reduce-scatter.8.cloned.1.call-update) | async-done | bytes 786448 | tf_op jit(solution)/shard_map/reduce_scatter | solution.py:213
  192.4 2.9 copy.153
  195.2 4.3 copy.154
  199.5 4.3 copy.155
  203.8 4.0 pad_maximum_fusion.5
  207.9 2.7 constant_dynamic-slice_fusion.5
  210.6 3.8 copy.157
  215.8 3.8 copy.158
  222.0 3.8 copy.159
  228.4 3.0 broadcast.210.clone
  232.6 33.4 %collective-permute-done = bf16[1,192,3840]{2,1,0:T(8,128)(2,1)} collective-permute-done((bf16[1,192,3840]{2,1,0:T(8,128)(2,1)}, bf16[1,192,3840]{2,1,0:T(8,128)(2,1)}, u32[]{:S(2)}, u32[]{:S(2)}) %collective-permute-start) | collective-permute-done | bytes 1474592 | tf_op jit(solution)/shard_map/ppermute | solution.py:95
  266.1 2.6 constant_dynamic-update-slice_fusion.5
  268.6 78.2 %collective-permute-done.1 = bf16[1,192,3840]{2,1,0:T(8,128)(2,1)} collective-permute-done((bf16[1,192,3840]{2,1,0:T(8,128)(2,1)}, bf16[1,192,3840]{2,1,0:T(8,128)(2,1)}, u32[]{:S(2)}, u32[]{:S(2)}) %collective-permute-start.1) | collective-permute-done | bytes 1474592 | tf_op jit(solution)/shard_map/ppermute | solution.py:95
  346.9 2.7 constant_dynamic-update-slice_fusion.4
  349.5 2.6 constant_dynamic-update-slice_fusion.3
  353.6 127.6 %collective-permute-done.3 = bf16[768,3840]{1,0:T(8,128)(2,1)} collective-permute-done((bf16[768,3840]{1,0:T(8,128)(2,1)}, bf16[768,3840]{1,0:T(8,128)(2,1)}, u32[]{:S(2)}, u32[]{:S(2)}) %collective-permute-start.3) | collective-permute-done | bytes 5898272 | tf_op jit(solution)/shard_map/ppermute | solution.py:130
  481.2 6.9 fusion.99
  488.0 10.1 fusion.42
  498.2 42.5 %fusion.16 = f32[4096,2560]{0,1:T(8,128)} fusion(bf16[4096,1664]{0,1:T(8,128)(2,1)} %all-gather.12.cloned.1.call-done, bf16[768,3840]{1,0:T(8,128)(2,1)} %bitcast.26, bf16[768,3840]{1,0:T(8,128)(2,1)} %collective-permute-done.3), kind=kOutput, calls=%fused_computation.35 | convolution fusion | flops 32227983360 | bytes 66322432 | tf_op jit(solution)/shard_map/dot_general | solution.py:243
  540.7 50.8 %multiply_convert_fusion.2 = (bf16[4096,1280]{0,1:T(8,128)(2,1)}, bf16[4096,1280]{0,1:T(8,128)(2,1)}, bf16[4096,1280]{0,1:T(8,128)(2,1)}, f32[4096,1280]{0,1:T(8,128)}) fusion(f32[4096,2560]{0,1:T(8,128)} %fusion.16, f32[4096,1280]{0,1:T(8,128)} %fusion.42, bf16[4096,1536]{0,1:T(8,128)(2,1)} %all-gather.10.cloned.1.call-done, ...), kind=kOutput, calls=%fused_computation.15 | convolution fusion | flops 16208363520 | bytes 139722752 | tf_op jit(solution)/shard_map/dot_general | solution.py:245
  591.5 7.8 reduce_sum.112
  599.4 40.0 %convolution_convert_fusion = bf16[4096,1536]{0,1:T(8,128)(2,1)} fusion(bf16[4096,1280]{0,1:T(8,128)(2,1)} %get-tuple-element.84, bf16[4096,1280]{0,1:T(8,128)(2,1)} %get-tuple-element.83, bf16[1536,2560]{1,0:T(8,128)(2,1)} %fusion.99), kind=kOutput, calls=%fused_computation.20 | convolution fusion | flops 32260489216 | bytes 41418752 | tf_op jit(solution)/shard_map/dot_general | solution.py:264
  640.6 14.5 pad_maximum_fusion.1
  655.6 206.9 %reduce-scatter.10.cloned.1.call-done = bf16[256,1664]{0,1:T(8,128)(2,1)} async-done(((bf16[4096,1664]{0,1:T(8,128)(2,1)}), bf16[256,1664]{0,1:T(8,128)(2,1)}) %reduce-scatter.10.cloned.1.call-update) | async-done | bytes 851984 | tf_op jit(solution)/shard_map/reduce_scatter | solution.py:268
  867.8 3.0 copy.164
  870.9 3.7 multiply_reduce_fusion.2
  877.3 23.3 %convolution_convert_fusion.1 = bf16[4096,1536]{1,0:T(8,128)(2,1)} fusion(bf16[4096,1280]{0,1:T(8,128)(2,1)} %get-tuple-element.85, bf16[768,3840]{1,0:T(8,128)(2,1)} %collective-permute-done.3, bf16[768,3840]{1,0:T(8,128)(2,1)} %bitcast.26), kind=kOutput, calls=%fused_computation.21 | convolution fusion | flops 16120283136 | bytes 34865152 | tf_op jit(solution)/shard_map/dot_general | solution.py:270
  905.1 3.6 convolution_convert_fusion.5
  908.7 16.0 %fusion = (f32[2,3,1024]{2,1,0:T(4,128)S(1)}, f32[2,1024,1024,3]{2,1,3,0:T(8,128)}) fusion(f32[2,3,1024,1024]{2,3,1,0:T(8,128)} %copy-done.2, f32[2,3,1024]{2,1,0:T(4,128)S(1)} %log_add_fusion, bf16[1024,2,64,1]{0,2,3,1:T(8,128)(2,1)S(1)} %bitcast.145, bf16[1024,2,3,64]{0,3,2,1:T(8,128)(2,1)S(1)} %bitcast.129), kind=kOutput, calls=%fused_computation.2 | convolution fusion | flops 824174592 | bytes 51429376 | tf_op jit(solution)/shard_map/qhgd,khd->hgqk/dot_general | solution.py:69
  924.8 17.1 %fusion.2 = bf16[2,3,1024,1024]{2,3,1,0:T(8,128)(2,1)S(1)} fusion(f32[2,1024,1024,3]{2,1,3,0:T(8,128)} %get-tuple-element.125, f32[2,3,1024,1024]{2,3,1,0:T(8,128)} %copy-done.2, f32[2,3,1024]{2,1,0:T(4,128)S(1)} %get-tuple-element.124, f32[2,3,1024]{2,1,0:T(4,128)S(1)} %log_add_fusion), kind=kLoop, calls=%fused_computation.4 | loop fusion | flops 25165824 | bytes 62963712 | tf_op jit(solution)/shard_map/convert_element_type | solution.py:74
  944.2 5.7 fusion.38
  949.9 12.4 fusion.39
  962.4 4.4 convolution_convert_fusion.4
  967.4 4.6 multiply_reduce_fusion
  972.8 3.6 convolution_convert_fusion.3
  976.7 2.9 copy.190
  980.9 23.7 %fusion.78 = f32[1536,1280]{1,0:T(8,128)} fusion(bf16[4096,1536]{0,1:T(8,128)(2,1)} %all-gather.10.cloned.1.call-done, bf16[4096,1280]{0,1:T(8,128)(2,1)} %get-tuple-element.85), kind=kOutput, calls=%fused_computation.180 | convolution fusion | flops 16106127360 | bytes 30932992 | tf_op jit(solution)/shard_map/dot_general | solution.py:279
  1004.6 42.1 %fusion.6 = f32[1536,2560]{1,0:T(8,128)} fusion(bf16[4096,1280]{0,1:T(8,128)(2,1)} %get-tuple-element.84, bf16[4096,1280]{0,1:T(8,128)(2,1)} %get-tuple-element.83, bf16[4096,1664]{0,1:T(8,128)(2,1)} %all-gather.12.cloned.1.call-done), kind=kOutput, calls=%fused_computation.23 | convolution fusion | flops 32254197760 | bytes 49283072 | tf_op jit(solution)/shard_map/dot_general | solution.py:276
  1046.7 7.6 fusion.14
  1055.7 149.9 %collective-permute-done.4 = bf16[768,3840]{1,0:T(8,128)(2,1)S(1)} collective-permute-done((bf16[768,3840]{1,0:T(8,128)(2,1)}, bf16[768,3840]{1,0:T(8,128)(2,1)S(1)}, u32[]{:S(2)}, u32[]{:S(2)}) %collective-permute-start.4) | collective-permute-done | bytes 5898272 | tf_op jit(solution)/shard_map/ppermute | solution.py:139
  1205.6 6.2 fusion.13
  1213.8 2.5 copy-done.6
  1221.8 31.9 %collective-permute-done.5 = bf16[1,192,3840]{2,1,0:T(8,128)(2,1)} collective-permute-done((bf16[1,192,3840]{2,1,0:T(8,128)(2,1)}, bf16[1,192,3840]{2,1,0:T(8,128)(2,1)}, u32[]{:S(2)}, u32[]{:S(2)}) %collective-permute-start.5) | collective-permute-done | bytes 1474592 | tf_op jit(solution)/shard_map/ppermute | solution.py:95
  1253.7 2.8 constant_dynamic-update-slice_fusion.2
  1256.6 99.1 %collective-permute-done.6 = bf16[1,192,3840]{2,1,0:T(8,128)(2,1)} collective-permute-done((bf16[1,192,3840]{2,1,0:T(8,128)(2,1)S(1)}, bf16[1,192,3840]{2,1,0:T(8,128)(2,1)}, u32[]{:S(2)}, u32[]{:S(2)}) %collective-permute-start.6) | collective-permute-done | bytes 1474592 | tf_op jit(solution)/shard_map/ppermute | solution.py:95
  1355.7 2.6 constant_dynamic-update-slice_fusion.1
  1358.3 2.6 constant_dynamic-update-slice_fusion
  1360.9 10.9 copy.173
  1371.8 11.9 fusion.73
  1383.7 5.6 copy.174
  1389.3 5.5 copy.179
  1394.8 5.6 copy.180
  1412.5 25.1 %reduce-scatter.12.cloned.1.call-done = bf16[256,1536]{1,0:T(8,128)(2,1)} async-done(((bf16[4096,1536]{1,0:T(8,128)(2,1)}), bf16[256,1536]{1,0:T(8,128)(2,1)}) %reduce-scatter.12.cloned.1.call-update) | async-done | bytes 786448 | tf_op jit(solution)/shard_map/reduce_scatter | solution.py:304
  1442.3 3.1 copy.168
  1445.4 4.4 fusion.30
  (238 shorter events, 75.6 us)
Async XLA Ops:
  7.2 140.4 %copy-start = (s32[1024,8]{0,1:T(8,128)S(1)}, s32[1024,8]{0,1:T(8,128)}, u32[]{:S(2)}) copy-start(s32[1024,8]{0,1:T(8,128)} %param.17) | copy-start | bytes 98308
  7.2 33.6 %all-gather.6.cloned.1.call-start = ((), (), s32[]{:S(2)}) async-start(), calls=%async_computation.5 | async-start | bytes 3932160 | tf_op jit(solution)/shard_map/all_gather | solution.py:189
  7.9 100.3 %all-gather.8.cloned.1.call-start = ((), (), s32[]{:S(2)}) async-start(), calls=%async_computation.6 | async-start | bytes 3981312 | tf_op jit(solution)/shard_map/all_gather | solution.py:188
  12.3 171.6 %reduce-scatter.8.cloned.1.call-start = ((), (), s32[]{:S(2)}) async-start(), calls=%async_computation.7 | async-start | bytes 3932160 | tf_op jit(solution)/shard_map/reduce_scatter | solution.py:213
  14.2 101.8 %copy-start.17 = (f32[1024,32]{0,1:T(8,128)}, f32[1024,32]{0,1:T(8,128)S(1)}, u32[]{:S(2)}) copy-start(f32[1024,32]{0,1:T(8,128)S(1)} %get-tuple-element.118) | copy-start | bytes 393220
  40.8 69.3 %copy-start.20 = (bf16[1024,1536]{1,0:T(8,128)(2,1)S(1)}, bf16[1024,1536]{1,0:T(8,128)(2,1)}, u32[]{:S(2)}) copy-start(bf16[1024,1536]{1,0:T(8,128)(2,1)} %all-gather.6.cloned.1.call-done) | copy-start | bytes 9437188
  43.6 70.5 %copy-start.59 = (f32[1024]{0:T(1024)}, f32[1024]{0:T(1024)S(1)}, u32[]{:S(2)}) copy-start(f32[1024]{0:T(1024)S(1)} %add_rsqrt_fusion) | copy-start | bytes 12292
  110.1 75.3 %copy-start.40 = (f32[1536]{0:T(1024)}, f32[1536]{0:T(1024)S(1)}, u32[]{:S(2)}) copy-start(f32[1536]{0:T(1024)S(1)} %get-tuple-element.81) | copy-start | bytes 18436
  116.0 6.5 copy-start.24
  122.5 8.4 copy-start.2
  122.5 8.9 copy-start.43
  122.5 8.9 copy-start.30
  130.9 11.0 copy-start.45
  141.9 5.2 copy-start.61
  141.9 5.2 copy-start.13
  142.0 41.9 %copy-start.3 = (bf16[256,1536]{1,0:T(8,128)(2,1)S(1)}, bf16[256,1536]{1,0:T(8,128)(2,1)}, u32[]{:S(2)}) copy-start(bf16[256,1536]{1,0:T(8,128)(2,1)} %param.14) | copy-start | bytes 2359300
  147.1 340.9 %all-gather.12.cloned.1.call-start = ((), (), s32[]{:S(2)}) async-start(), calls=%async_computation.9 | async-start | bytes 14483456 | tf_op jit(solution)/shard_map/all_gather | solution.py:235
  147.6 43.6 %copy-start.37 = (pred[256,40]{0,1:T(8,128)(4,1)}, pred[256,40]{0,1:T(8,128)(4,1)S(1)}, u32[]{:S(2)}) copy-start(pred[256,40]{0,1:T(8,128)(4,1)S(1)} %fusion.53) | copy-start | bytes 30724
  186.8 5.5 copy-start.11
  191.3 349.5 %all-gather.10.cloned.1.call-start = ((), (), s32[]{:S(2)}) async-start(), calls=%async_computation.8 | async-start | bytes 13369344 | tf_op jit(solution)/shard_map/all_gather | solution.py:197
  192.3 670.2 %reduce-scatter.10.cloned.1.call-start = ((), (), s32[]{:S(2)}) async-start(), calls=%async_computation.10 | async-start | bytes 14483456 | tf_op jit(solution)/shard_map/reduce_scatter | solution.py:268
  214.3 51.7 %collective-permute-start = (bf16[1,192,3840]{2,1,0:T(8,128)(2,1)}, bf16[1,192,3840]{2,1,0:T(8,128)(2,1)}, u32[]{:S(2)}, u32[]{:S(2)}) collective-permute-start(bf16[1,192,3840]{2,1,0:T(8,128)(2,1)} %copy.157), channel_id=1, source_target_pairs={{0,8},{8,16},{16,24},{24,0},{1,9},{9,17},{17,25},{25,1},{2,10},{10... | collective-permute-start | bytes 4423688 | tf_op jit(solution)/shard_map/ppermute | solution.py:95
  219.6 127.3 %collective-permute-start.1 = (bf16[1,192,3840]{2,1,0:T(8,128)(2,1)}, bf16[1,192,3840]{2,1,0:T(8,128)(2,1)}, u32[]{:S(2)}, u32[]{:S(2)}) collective-permute-start(bf16[1,192,3840]{2,1,0:T(8,128)(2,1)} %copy.158), channel_id=1, source_target_pairs={{0,16},{8,24},{16,0},{24,8},{1,17},{9,25},{17,1},{25,9},{2,18},{10... | collective-permute-start | bytes 4423688 | tf_op jit(solution)/shard_map/ppermute | solution.py:95
  225.7 123.8 %collective-permute-start.2 = (bf16[1,192,3840]{2,1,0:T(8,128)(2,1)}, bf16[1,192,3840]{2,1,0:T(8,128)(2,1)}, u32[]{:S(2)}, u32[]{:S(2)}) collective-permute-start(bf16[1,192,3840]{2,1,0:T(8,128)(2,1)} %copy.159), channel_id=1, source_target_pairs={{0,24},{8,0},{16,8},{24,16},{1,25},{9,1},{17,9},{25,17},{2,26},{10... | collective-permute-start | bytes 4423688 | tf_op jit(solution)/shard_map/ppermute | solution.py:95
  352.1 129.1 %collective-permute-start.3 = (bf16[768,3840]{1,0:T(8,128)(2,1)}, bf16[768,3840]{1,0:T(8,128)(2,1)}, u32[]{:S(2)}, u32[]{:S(2)}) collective-permute-start(bf16[768,3840]{1,0:T(8,128)(2,1)} %bitcast.26), channel_id=1, source_target_pairs={{0,4},{4,0},{1,5},{5,1},{2,6},{6,2},{3,7},{7,3},{8,12},{12,8},{9,1... | collective-permute-start | bytes 17694728 | tf_op jit(solution)/shard_map/ppermute | solution.py:130
  655.1 209.9 %copy-start.27 = (f32[256,40]{0,1:T(8,128)S(1)}, f32[256,40]{0,1:T(8,128)}, u32[]{:S(2)}) copy-start(f32[256,40]{0,1:T(8,128)} %copy-done.26) | copy-start | bytes 122884
  655.1 209.9 %copy-start.38 = (pred[256,40]{0,1:T(8,128)(4,1)S(1)}, pred[256,40]{0,1:T(8,128)(4,1)}, u32[]{:S(2)}) copy-start(pred[256,40]{0,1:T(8,128)(4,1)} %copy-done.37) | copy-start | bytes 30724
  655.1 209.9 %copy-start.50 = (f32[256]{0:T(256)S(1)}, f32[256]{0:T(256)}, u32[]{:S(2)}) copy-start(f32[256]{0:T(256)} %copy-done.49) | copy-start | bytes 3076
  655.1 209.9 %copy-start.52 = (f32[256]{0:T(256)S(1)}, f32[256]{0:T(256)}, u32[]{:S(2)}) copy-start(f32[256]{0:T(256)} %copy-done.51) | copy-start | bytes 3076
  655.1 250.0 %all-gather.14.cloned.1.call-start = ((), (), s32[]{:S(2)}) async-start(), calls=%async_computation.11 | async-start | bytes 3932160 | tf_op jit(solution)/shard_map/all_gather | solution.py:300
  865.0 5.8 copy-start.4
  865.0 5.8 copy-start.7
  865.0 5.8 copy-start.41
  865.0 5.8 copy-start.54
  866.5 9.2 copy-start.14
  870.8 6.5 copy-start.44
  870.8 6.5 copy-start.46
  877.2 523.2 %all-reduce.2.cloned.1.call-start = ((), (), s32[]{:S(2)}) async-start(), calls=%async_computation.14 | async-start | bytes 589824 | tf_op jit(solution)/shard_map/psum | solution.py:343
  877.3 23.4 %copy-start.12 = (bf16[256,1536]{1,0:T(8,128)(2,1)S(1)}, bf16[256,1536]{1,0:T(8,128)(2,1)}, u32[]{:S(2)}) copy-start(bf16[256,1536]{1,0:T(8,128)(2,1)} %copy-done.11) | copy-start | bytes 2359300
  902.7 6.1 copy-start.31
  908.7 16.0 %copy-start.19 = (bf16[1024,384]{0,1:T(8,128)(2,1)}, bf16[1024,384]{0,1:T(8,128)(2,1)S(1)}, u32[]{:S(2)}) copy-start(bf16[1024,384]{0,1:T(8,128)(2,1)S(1)} %convolution_convert_fusion.5) | copy-start | bytes 2359300
  924.8 17.1 %copy-start.34 = (bf16[1024,2,32]{0,2,1:T(8,128)(2,1)S(1)}, bf16[1024,2,32]{0,2,1:T(8,128)(2,1)}, u32[]{:S(2)}) copy-start(bf16[1024,2,32]{0,2,1:T(8,128)(2,1)} %get-tuple-element.108) | copy-start | bytes 393220
  924.8 17.1 %copy-start.35 = (bf16[1024,2,32]{0,2,1:T(8,128)(2,1)S(1)}, bf16[1024,2,32]{0,2,1:T(8,128)(2,1)}, u32[]{:S(2)}) copy-start(bf16[1024,2,32]{0,2,1:T(8,128)(2,1)} %get-tuple-element.109) | copy-start | bytes 393220
  949.9 12.4 copy-start.62
  962.4 4.9 copy-start.21
  962.4 4.9 copy-start.36
  962.4 4.9 copy-start.60
  967.3 5.5 copy-start.22
  967.4 5.5 copy-start.48
  972.7 430.7 %reduce-scatter.16.cloned.1.call-start = ((), (), s32[]{:S(2)}) async-start(), calls=%async_computation.15 | async-start | bytes 3538944
  979.6 431.3 %reduce-scatter.14.cloned.1.call-start = ((), (), s32[]{:S(2)}) async-start(), calls=%async_computation.13 | async-start | bytes 3932160 | tf_op jit(solution)/shard_map/reduce_scatter | solution.py:326
  980.2 457.3 %reduce-scatter.12.cloned.1.call-start = ((), (), s32[]{:S(2)}) async-start(), calls=%async_computation.12 | async-start | bytes 13369344 | tf_op jit(solution)/shard_map/reduce_scatter | solution.py:304
  1054.3 151.4 %collective-permute-start.4 = (bf16[768,3840]{1,0:T(8,128)(2,1)}, bf16[768,3840]{1,0:T(8,128)(2,1)S(1)}, u32[]{:S(2)}, u32[]{:S(2)}) collective-permute-start(bf16[768,3840]{1,0:T(8,128)(2,1)} %fusion.14), channel_id=1, source_target_pairs={{0,4},{4,0},{1,5},{5,1},{2,6},{6,2},{3,7},{7,3},{8,12},{12,8},{9,1... | collective-permute-start | bytes 17694728 | tf_op jit(solution)/shard_map/ppermute | solution.py:139
  1216.3 37.4 %collective-permute-start.5 = (bf16[1,192,3840]{2,1,0:T(8,128)(2,1)}, bf16[1,192,3840]{2,1,0:T(8,128)(2,1)}, u32[]{:S(2)}, u32[]{:S(2)}) collective-permute-start(bf16[1,192,3840]{2,1,0:T(8,128)(2,1)} %get-tuple-element.98), channel_id=1, source_target_pairs={{0,8},{8,16},{16,24},{24,0},{1,9},{9,17},{17,25},{25,1},{2,10},{10... | collective-permute-start | bytes 4423688 | tf_op jit(solution)/shard_map/ppermute | solution.py:95
  1217.9 137.7 %collective-permute-start.6 = (bf16[1,192,3840]{2,1,0:T(8,128)(2,1)S(1)}, bf16[1,192,3840]{2,1,0:T(8,128)(2,1)}, u32[]{:S(2)}, u32[]{:S(2)}) collective-permute-start(bf16[1,192,3840]{2,1,0:T(8,128)(2,1)S(1)} %get-tuple-element.97), channel_id=1, source_target_pairs={{0,16},{8,24},{16,0},{24,8},{1,17},{9,25},{17,1},{25,9},{2,18},{10... | collective-permute-start | bytes 4423688 | tf_op jit(solution)/shard_map/ppermute | solution.py:95
  1220.4 137.9 %collective-permute-start.7 = (bf16[1,192,3840]{2,1,0:T(8,128)(2,1)S(1)}, bf16[1,192,3840]{2,1,0:T(8,128)(2,1)}, u32[]{:S(2)}, u32[]{:S(2)}) collective-permute-start(bf16[1,192,3840]{2,1,0:T(8,128)(2,1)S(1)} %get-tuple-element.96), channel_id=1, source_target_pairs={{0,24},{8,0},{16,8},{24,16},{1,25},{9,1},{17,9},{25,17},{2,26},{10... | collective-permute-start | bytes 4423688 | tf_op jit(solution)/shard_map/ppermute | solution.py:95
  1394.8 5.6 copy-start.58
  1394.8 16.1 %copy-start.5 = (bf16[256,1536]{1,0:T(8,128)(2,1)S(1)}, bf16[256,1536]{1,0:T(8,128)(2,1)}, u32[]{:S(2)}) copy-start(bf16[256,1536]{1,0:T(8,128)(2,1)} %param.14) | copy-start | bytes 2359300
  1406.5 38.9 %copy-start.8 = (bf16[256,1536]{1,0:T(8,128)(2,1)S(1)}, bf16[256,1536]{1,0:T(8,128)(2,1)}, u32[]{:S(2)}) copy-start(bf16[256,1536]{1,0:T(8,128)(2,1)} %reduce-scatter.8.cloned.1.call-done) | copy-start | bytes 2359300
  1406.5 38.9 %copy-start.10 = (f32[256,1536]{1,0:T(8,128)S(1)}, f32[256,1536]{1,0:T(8,128)}, u32[]{:S(2)}) copy-start(f32[256,1536]{1,0:T(8,128)} %copy-done.9) | copy-start | bytes 4718596
  1406.5 38.9 %copy-start.42 = (f32[1536]{0:T(1024)S(1)}, f32[1536]{0:T(1024)}, u32[]{:S(2)}) copy-start(f32[1536]{0:T(1024)} %copy-done.40) | copy-start | bytes 18436
  1406.5 38.9 %copy-start.55 = (f32[256]{0:T(256)S(1)}, f32[256]{0:T(256)}, u32[]{:S(2)}) copy-start(f32[256]{0:T(256)} %copy-done.53) | copy-start | bytes 3076
  1406.5 38.9 %copy-start.57 = (f32[256]{0:T(256)S(1)}, f32[256]{0:T(256)}, u32[]{:S(2)}) copy-start(f32[256]{0:T(256)} %copy-done.56) | copy-start | bytes 3076
  1442.3 7.5 copy-start.1
  (18 other events, 51.5 us)
Sparse Core Ops, SparseCore 0:
  9.6 31.2 all-gather.5
  43.6 64.5 all-gather.7
  147.2 36.6 reduce-scatter.7
  191.4 216.8 all-gather.11
  410.8 107.9 all-gather.9
  655.2 207.1 reduce-scatter.9
  877.3 27.6 all-gather.13
  972.9 127.0 all-reduce.1
  1103.6 94.1 reduce-scatter.15
  1200.2 36.2 reduce-scatter.13
  1240.5 196.9 reduce-scatter.11

commit v2 on v1

--- a/solution.py
+++ b/solution.py
@@ -1,6 +1,7 @@
 import jax
 import jax.numpy as jnp
 from jax import lax
+from jax.experimental.layout import Layout, with_layout_constraint
 from jax.sharding import Mesh, PartitionSpec as P
 
 HEAD_DIM = 64
@@ -85,16 +86,34 @@
     return grad_query.reshape(seq_len, -1, head_size), grad_keys, grad_values
 
 
-def exchange(pieces, axis, size):
+def swap(values, axis, size, bit):
+    return lax.ppermute(values, axis, [(m, m ^ bit) for m in range(size)])
+
+
+def gather_line(block, axis, size):
     me = lax.axis_index(axis)
-    result = jnp.zeros_like(pieces)
-    own = lax.dynamic_index_in_dim(pieces, me, 0)
-    result = lax.dynamic_update_slice_in_dim(result, own, me, 0)
-    for shift in range(1, size):
-        piece = lax.dynamic_index_in_dim(pieces, (me + shift) % size, 0)
-        got = lax.ppermute(piece, axis, [(m, (m + shift) % size) for m in range(size)])
-        result = lax.dynamic_update_slice_in_dim(result, got, (me - shift) % size, 0)
-    return result
+    up, down = [block], [block]
+    for _ in range(1, size):
+        up.append(lax.ppermute(up[-1], axis, [(m, m + 1) for m in range(size - 1)]))
+        down.append(lax.ppermute(down[-1], axis, [(m + 1, m) for m in range(size - 1)]))
+    return [block] + [jnp.where(me >= s, up[s], down[size - s]) for s in range(1, size)]
+
+
+def tie(*values):
+    return lax.optimization_barrier(values)
+
+
+def by_rows(values):
+    return with_layout_constraint(values, Layout(major_to_minor=(0, 1)))
+
+
+def split(values):
+    high = values.astype(bf16)
+    return high, (values - high.astype(f32)).astype(bf16)
+
+
+def put(result, piece, *starts):
+    return lax.dynamic_update_slice(result, piece, starts)
 
 
 def solution(mesh):
@@ -123,22 +142,62 @@
             split = jnp.where(lax.axis_index("o") == 0, split, split[:, ::-1])
         return jnp.swapaxes(split, 1, 2).reshape(rows, -1)
 
-    def gather_outer(values):
+    def pass_on(piece):
         if outer == 1:
-            return values
+            return piece[None]
         if outer == 2:
-            other = lax.ppermute(values, "o", [(0, 1), (1, 0)])
-            return jnp.concatenate([values, other], axis=0)
-        return lax.all_gather(values, "o", axis=0, tiled=True)
-
-    def reduce_outer(values):
+            return jnp.stack([piece, swap(piece, "o", 2, 1)])
+        return lax.all_gather(piece, "o", axis=0)
+
+    def sum_outer(parts):
         if outer == 1:
-            return values.astype(bf16)
+            return parts[0]
         if outer == 2:
-            rows = values.shape[0] // 2
-            got = lax.ppermute(values[rows:].astype(bf16), "o", [(0, 1), (1, 0)])
-            return (values[:rows] + got.astype(f32)).astype(bf16)
-        return lax.psum_scatter(values.astype(bf16), "o", scatter_dimension=0, tiled=True)
+            return (parts[0].astype(f32) + swap(parts[1], "o", 2, 1).astype(f32)).astype(bf16)
+        return lax.psum_scatter(parts, "o", scatter_dimension=0, tiled=False)
+
+    def share(block):
+        rows, width = block.shape
+        if n_tensor != 4:
+            return lax.all_gather(block, shared, axis=0, tiled=True)
+        me_i, me_t = lax.axis_index("i"), lax.axis_index("t")
+        result = jnp.zeros((inner * n_tensor * rows, width), block.dtype)
+        for shift, near in enumerate(gather_line(block, "i", inner)):
+            pair = jnp.concatenate([near, swap(near, "t", n_tensor, 2)], axis=0)
+            for bit, part in ((0, pair), (1, swap(pair, "t", n_tensor, 1))):
+                place = (me_i - shift) % inner * n_tensor + (me_t ^ bit)
+                result = put(result, part[:rows], place * rows, 0)
+                result = put(result, part[rows:], (place ^ 2) * rows, 0)
+        return result
+
+    def sum_across(values):
+        rows, width = values.shape[0] // (inner * n_tensor), values.shape[1]
+        me_i, me_t = lax.axis_index("i"), lax.axis_index("t")
+        blocks = values.reshape(inner, 2, 2, rows, width)
+        result = []
+        for shift in range(inner):
+            block = lax.dynamic_index_in_dim(blocks, (me_i + shift) % inner, 0, keepdims=False)
+            for axis, bit, own in ((1, 1, me_t % 2), (0, 2, me_t // 2)):
+                keep = lax.dynamic_index_in_dim(block, own, axis, keepdims=False)
+                send = lax.dynamic_index_in_dim(block, 1 - own, axis, keepdims=False)
+                got = swap(send, "t", n_tensor, bit)
+                block = (keep.astype(f32) + got.astype(f32)).astype(bf16)
+            result.append(block)
+        return result
+
+    def sum_line(parts):
+        total = parts[0].astype(f32)
+        for shift in range(1, inner):
+            pairs = [(m, (m + shift) % inner) for m in range(inner)]
+            total = total + lax.ppermute(parts[shift], "i", pairs).astype(f32)
+        return total
+
+    def sum_tensor(values):
+        if n_tensor != 4:
+            return lax.psum(values, "t")
+        for bit in (1, 2):
+            values = values + swap(values, "t", n_tensor, bit)
+        return values
 
     def on_device(
         tokens,
@@ -164,16 +223,9 @@
         q_cols, k_cols = w_query.shape[1], w_key.shape[1]
         qkv_cols = q_cols + 2 * k_cols
         attn_cols = qkv_cols + q_cols
-        side_cols = -(-(n_experts + 2) // LANES) * LANES
+        side_cols = -(-(2 * n_experts + 2) // LANES) * LANES
         gate_cols = -(-2 * n_experts // LANES) * LANES
         me_i, me_t = lax.axis_index("i"), lax.axis_index("t")
-
-        weights3 = jnp.stack([w_gate, w_up, jnp.swapaxes(w_down, 1, 2)])
-        pieces = weights3.reshape(3, inner, own_experts, depth, hidden)
-        pieces = pieces.transpose(1, 3, 0, 2, 4).reshape(inner, depth, 3 * own_hidden)
-        owned = gather_outer(exchange(pieces, "i", inner).reshape(inner * depth, -1))
-        w_gate_up = owned[:, : 2 * own_hidden]
-        w_down_t = owned[:, 2 * own_hidden :]
 
         side = jnp.concatenate(
             [
@@ -185,16 +237,36 @@
             axis=1,
         )
         pack = jnp.concatenate([w_query, w_key, w_value, w_out.T, side], axis=1)
+        tokens_all = lax.all_gather(tokens, "t", axis=0, tiled=True).astype(f32)
         packed = lax.all_gather(pack, dp, axis=0, tiled=True)
-        tokens_all = lax.all_gather(tokens, "t", axis=0, tiled=True).astype(f32)
+
+        def expert_piece(target):
+            first = target * own_experts
+            parts = [
+                jnp.swapaxes(lax.dynamic_slice_in_dim(w, first, own_experts, 0), 0, 1)
+                for w in (w_gate, w_up)
+            ]
+            down = lax.dynamic_slice_in_dim(w_down, first, own_experts, 0)
+            parts.append(down.transpose(2, 0, 1))
+            return jnp.concatenate([p.reshape(depth, own_hidden) for p in parts], axis=1)
+
+        def to_owner(piece, shift):
+            return lax.ppermute(piece, "i", [(m, (m + shift) % inner) for m in range(inner)])
+
+        pieces = [expert_piece((me_i + shift) % inner) for shift in range(inner)]
+        pieces[0], pieces[1], tokens_all = tie(pieces[0], pieces[1], tokens_all)
+        owned = [pass_on(pieces[0])]
+        near = to_owner(pieces[1], 1)
+        pieces[2], pieces[3], owned[0], near, packed = tie(
+            pieces[2], pieces[3], owned[0], near, packed
+        )
+        owned.append(pass_on(near))
+
         w_qkv = packed[:, :qkv_cols]
         w_out_t = packed[:, qkv_cols:attn_cols]
         router = packed[:, attn_cols : attn_cols + n_experts]
         gains = packed[:, attn_cols + n_experts : attn_cols + n_experts + 2].astype(f32).T
         gain_one, gain_two = gains[0], gains[1]
-
-        cot_order, _ = lax.optimization_barrier((to_owner_order(cotangent), tokens_all))
-        cot_all = lax.all_gather(cot_order, shared, axis=0, tiled=True)
 
         normal_all = tokens_all * rms_scale(tokens_all)
         normed_one = (normal_all * gain_one).astype(bf16)
@@ -206,13 +278,17 @@
         ).astype(bf16)
         values = qkv[:, q_cols + k_cols :].astype(bf16).reshape(group, -1, HEAD_DIM)
         attended, log_total = attend_forward(query, keys, values, prefix[0])
+        near = to_owner(pieces[2], 2)
+        pieces[3], attended = tie(pieces[3], attended)
         branch = lax.dot_general(
             attended, w_out_t, (((1,), (1,)), ((), ())), preferred_element_type=f32
         ).astype(bf16)
         tokens_f = tokens.astype(f32)
-        middle = tokens_f + lax.psum_scatter(
-            branch, "t", scatter_dimension=0, tiled=True
-        ).astype(f32)
+        branch = lax.psum_scatter(branch, "t", scatter_dimension=0, tiled=True)
+        last = to_owner(pieces[3], 3)
+        near, owned[1], branch = tie(near, owned[1], branch)
+        owned += [pass_on(near), pass_on(last)]
+        middle = tokens_f + branch.astype(f32)
         scale_two = rms_scale(middle)
         normed_two = (middle * scale_two * gain_two).astype(bf16)
 
@@ -232,7 +308,14 @@
             ],
             axis=1,
         )
-        shared_all = lax.all_gather(shipped, shared, axis=0, tiled=True)
+        shared_all = by_rows(lax.all_gather(by_rows(shipped), shared, axis=0, tiled=True))
+        w_owned = jnp.zeros((outer, inner, depth, 3 * own_hidden), bf16)
+        for shift in range(inner):
+            w_owned = put(w_owned, owned[shift][:, None], 0, (me_i - shift) % inner, 0, 0)
+        w_owned = w_owned.reshape(outer * inner * depth, 3 * own_hidden)
+        cot_order, shared_all, w_owned = tie(by_rows(to_owner_order(cotangent)), shared_all, w_owned)
+        w_gate_up, w_down_t = w_owned[:, : 2 * own_hidden], w_owned[:, 2 * own_hidden :]
+        cot_all = by_rows(share(cot_order))
         count = shared_all.shape[0]
         normed_all = shared_all[:, :width]
 
@@ -242,11 +325,30 @@
         gate_wide = jnp.dot(shared_all[:, width:], spread, preferred_element_type=f32)
         gate_up = jnp.dot(normed_all, w_gate_up, preferred_element_type=f32)
         gate_part, up_part = gate_up[:, :own_hidden], gate_up[:, own_hidden:]
-        cot_part = jnp.dot(cot_all, w_down_t, preferred_element_type=f32)
         sigmoid_g = jax.nn.sigmoid(gate_part)
         silu_g = gate_part * sigmoid_g
         act = silu_g * up_part
         gated = (act * gate_wide).astype(bf16)
+        expert_part = lax.dot_general(
+            gated, w_down_t, (((1,), (1,)), ((), ())), preferred_element_type=f32
+        ).astype(bf16)
+        expert_part, cot_all = tie(by_rows(expert_part), cot_all)
+        if n_tensor == 4:
+            share_parts = sum_across(expert_part)
+        else:
+            share_parts = [lax.psum_scatter(expert_part, shared, scatter_dimension=0, tiled=True)]
+        contract_rows = (((0,), (0,)), ((), ()))
+
+        def to_sum(grad):
+            by_owner = grad.reshape(outer, inner, depth, -1)
+            return [
+                sum_outer(
+                    lax.dynamic_index_in_dim(by_owner, (me_i + shift) % inner, 1, keepdims=False)
+                )
+                for shift in range(inner)
+            ]
+
+        cot_part = jnp.dot(cot_all, w_down_t, preferred_element_type=f32)
         grad_act = cot_part * gate_wide
         grad_gate_up = jnp.concatenate(
             [
@@ -264,29 +366,41 @@
         grad_normed_part = lax.dot_general(
             grad_gate_up, w_gate_up, (((1,), (1,)), ((), ())), preferred_element_type=f32
         )
-        grad_shipped = jnp.concatenate([grad_normed_part, gate_block], axis=1).astype(bf16)
-        grad_back = lax.psum_scatter(grad_shipped, shared, scatter_dimension=0, tiled=True)
-
-        expert_part = lax.dot_general(
-            gated, w_down_t, (((1,), (1,)), ((), ())), preferred_element_type=f32
-        ).astype(bf16)
-        contract_rows = (((0,), (0,)), ((), ()))
-        grad_w = jnp.concatenate(
-            [
-                lax.dot_general(
-                    normed_all, grad_gate_up, contract_rows, preferred_element_type=f32
-                ),
-                lax.dot_general(cot_all, gated, contract_rows, preferred_element_type=f32),
-            ],
-            axis=1,
-        )
+        gates_back = lax.psum_scatter(
+            gate_block.astype(bf16), shared, scatter_dimension=0, tiled=True
+        )
+        grad_normed_part, share_parts, gates_back = tie(
+            by_rows(grad_normed_part.astype(bf16)), share_parts, gates_back
+        )
+        grad_back = lax.psum_scatter(grad_normed_part, shared, scatter_dimension=0, tiled=True)
+        cot_rows, normed_rows, _ = tie(cot_all, normed_all, grad_normed_part)
+        grad_w_down = lax.dot_general(
+            cot_rows, gated, contract_rows, preferred_element_type=f32
+        ).astype(bf16)
+        grad_w_down, normed_rows = tie(grad_w_down, normed_rows)
+        down_sums = to_sum(grad_w_down)
+        grad_w_gate_up = lax.dot_general(
+            normed_rows, grad_gate_up, contract_rows, preferred_element_type=f32
+        ).astype(bf16)
+        gate_up_sums = to_sum(grad_w_gate_up)
+        sent_down = down_sums[:1] + [to_owner(down_sums[s], s) for s in range(1, inner)]
+        sent_gate_up = gate_up_sums[:1] + [to_owner(gate_up_sums[s], s) for s in range(1, inner)]
+        if n_tensor == 4:
+            expert_share = sum_line(share_parts)
+        else:
+            expert_share = share_parts[0].astype(f32)
+        sent_down, gate_up_sums, expert_share, grad_back = tie(
+            sent_down, gate_up_sums, expert_share, grad_back
+        )
+        sent_gate_up[0] = gate_up_sums[0]
+        mixed = (middle + from_owner_order(expert_share)).astype(bf16)
 
         grad_back = grad_back.astype(f32)
-        grad_chosen = grad_back[:, width : width + n_experts]
+        grad_chosen = gates_back[:, :n_experts].astype(f32)
         grad_logits = gates * (
             grad_chosen - jnp.sum(gates * grad_chosen, axis=-1, keepdims=True)
         )
-        grad_normed_two = from_owner_order(grad_back[:, :width]) + jnp.dot(
+        grad_normed_two = from_owner_order(grad_back) + jnp.dot(
             grad_logits, router.astype(f32).T, precision=HIGHEST
         )
         grad_middle_part, normal_two = norm_backward(
@@ -298,15 +412,24 @@
             normed_two.astype(f32), grad_logits, contract_rows, precision=HIGHEST
         )
         grad_branch = lax.all_gather(grad_middle.astype(bf16), "t", axis=0, tiled=True)
-
-        grad_branch_tie, expert_part = lax.optimization_barrier((grad_branch, expert_part))
-        expert_share = from_owner_order(
-            lax.psum_scatter(expert_part, shared, scatter_dimension=0, tiled=True)
-        ).astype(f32)
-        mixed = (middle + expert_share).astype(bf16)
-
+        grad_out_part = lax.dot_general(
+            grad_branch, attended, contract_rows, preferred_element_type=f32
+        ).astype(bf16)
+        grad_out_part, sent_gate_up[1], grad_branch = tie(
+            jnp.concatenate(
+                [
+                    grad_out_part,
+                    *split(jnp.concatenate([grad_router_part, grad_gain_two[:, None]], axis=1)),
+                    jnp.zeros((width, side_cols - 2 * n_experts - 2), bf16),
+                ],
+                axis=1,
+            ),
+            sent_gate_up[1],
+            grad_branch,
+        )
+        shard_out = lax.psum_scatter(grad_out_part, dp, scatter_dimension=0, tiled=True)
         grad_attended = jnp.dot(
-            grad_branch_tie, w_out_t, preferred_element_type=f32
+            grad_branch, w_out_t, preferred_element_type=f32
         ).astype(bf16)
         grad_query, grad_keys, grad_values = attend_backward(
             query, keys, values, grad_attended, log_total, prefix[0]
@@ -331,35 +454,47 @@
 
         grad_attn = jnp.concatenate(
             [
-                lax.dot_general(normed_one, grad_qkv, contract_rows, preferred_element_type=f32),
-                lax.dot_general(grad_branch_tie, attended, contract_rows, preferred_element_type=f32),
+                lax.dot_general(
+                    normed_one, grad_qkv, contract_rows, preferred_element_type=f32
+                ).astype(bf16),
+                *split(grad_gain_one[:, None]),
+                jnp.zeros((width, LANES - 2), bf16),
             ],
             axis=1,
-        ).astype(bf16)
+        )
+        grad_attn, own_grad_one, shard_out, sent_gate_up[2] = tie(
+            grad_attn, own_grad_one, shard_out, sent_gate_up[2]
+        )
         shard_attn = lax.psum_scatter(grad_attn, dp, scatter_dimension=0, tiled=True).astype(f32)
-        sums = jnp.concatenate(
-            [grad_router_part, grad_gain_one[:, None], grad_gain_two[:, None]], axis=1
-        )
-        sums = lax.psum(sums, ("i", "o", "t"))
-        first = (me_i * outer + lax.axis_index("o")) * depth
-        own_sums = lax.dynamic_slice_in_dim(sums, first, depth, 0)
-
-        reduced = reduce_outer(grad_w).reshape(inner, depth, 3 * own_hidden)
-        returned = exchange(reduced, "i", inner).reshape(inner, depth, 3, own_experts, hidden)
-        grad3 = returned.transpose(2, 0, 3, 1, 4).reshape(3, n_experts, depth, hidden).astype(f32)
+        gain_sum = sum_tensor(shard_attn[:, qkv_cols] + shard_attn[:, qkv_cols + 1])
+        shard_out = shard_out.astype(f32)
+        side_sum = shard_out[:, q_cols : q_cols + 2 * (n_experts + 1)].reshape(depth, 2, -1)
+        side_sum = sum_tensor(jnp.sum(side_sum, axis=1))
+
+        grad_gate = jnp.zeros((n_experts, depth, hidden), f32)
+        grad_up, grad_down = grad_gate, jnp.zeros((n_experts, hidden, depth), f32)
+        for shift in range(inner):
+            start = (me_i - shift) % inner * own_experts
+            part = sent_down[shift]
+            part = part.reshape(depth, own_experts, hidden).transpose(1, 2, 0)
+            grad_down = put(grad_down, part.astype(f32), start, 0, 0)
+            part = sent_gate_up[shift]
+            part = part.reshape(depth, 2, own_experts, hidden).transpose(1, 2, 0, 3).astype(f32)
+            grad_gate = put(grad_gate, part[0], start, 0, 0)
+            grad_up = put(grad_up, part[1], start, 0, 0)
         return (
             mixed,
             grad_tokens,
-            own_sums[:, n_experts],
+            gain_sum,
             shard_attn[:, :q_cols],
             shard_attn[:, q_cols : q_cols + k_cols],
             shard_attn[:, q_cols + k_cols : qkv_cols],
-            shard_attn[:, qkv_cols:].T,
-            own_sums[:, n_experts + 1],
-            own_sums[:, :n_experts],
-            grad3[0],
-            grad3[1],
-            jnp.swapaxes(grad3[2], 1, 2),
+            shard_out[:, :q_cols].T,
+            side_sum[:, n_experts],
+            side_sum[:, :n_experts],
+            grad_gate,
+            grad_up,
+            grad_down,
         )
 
     in_specs = (

time: 1480 us -> 1370 us (0.926); the launches traced: 1460 us -> 1370 us
  waiting for transfers between devices: 883 us -> 585 us
  local copies, waits for them, and re-layouts: 132 us -> 237 us
  starting transfers between devices: 14.8 us -> 82.2 us
  other arithmetic: 93.6 us -> 111 us
  matrix products: 318 us -> 333 us
    reduce_scatter x3, waiting for transfers between devices: 268 us -> 8.1 us  [the longest x1 8.08 us: on_device(): lax.psum_scatter(grad_normed_part, shared, scatter_dimension=0, tiled=True)]
    ppermute x8 -> x50, waiting for transfers between devices: 520 us -> 421 us  [the longest x32 272 us: swap(): return lax.ppermute(values, axis, [(m, m ^ bit) for m in range(size)])]
    unnamed x12, waiting for transfers between devices: 1.82 us -> 85.7 us
    ppermute x8 -> x50, starting transfers between devices: 13.7 us -> 81.6 us  [the longest x9 35 us: to_owner(): lax.ppermute(piece, 'i', [(m, (m + shift) % inner) for m in range(inner)])]
    all_gather x1, waiting for transfers between devices: 64.6 us -> 12.4 us  [on_device(): packed = lax.all_gather(pack, dp, axis=0, tiled=True)]
    all_gather x2 -> x1, waiting for transfers between devices: 0.01 us -> 29.9 us  [on_device(): lax.all_gather(by_rows(shipped), shared, axis=0, tiled=True)]
    all_gather x1, waiting for transfers between devices: 2.39 us -> 28.1 us  [on_device(): lax.all_gather(grad_middle.astype(bf16), 't', axis=0, tiled=True)]
    all_gather x1, waiting for transfers between devices: 25.3 us -> 0.01 us  [on_device(): tokens_all = lax.all_gather(tokens, 't', axis=0, tiled=True).astype(f32)]
  transfers between devices with their start and end apart: 19 -> 60, of which waited for: 12 -> 31; matrix products, arithmetic and copies ran while one was open for 20% -> 40% of each run, Pallas kernels for 0% -> 0%
where the time goes in v2:
time: 1370 us
  waiting for transfers between devices  585 us (43%)
  matrix products  333 us (24%)
  local copies, waits for them, and re-layouts  237 us (17%)
  other arithmetic  111 us (8%)
  starting transfers between devices  82.2 us (6%)
  between operations  16.9 us (1%)
    ppermute x32, waiting for transfers between devices, swap(): return lax.ppermute(values, axis, [(m, m ^ bit) for m in range(size)])  272 us
    ppermute x9, waiting for transfers between devices, to_owner(): lax.ppermute(piece, 'i', [(m, (m + shift) % inner) for m in range(inner)])  93.7 us
    unnamed x12, waiting for transfers between devices  85.7 us
    dot_general x1, matrix products, on_device(): cot_part = jnp.dot(cot_all, w_down_t, preferred_element_type=f32)  47.6 us
    dot_general x1, matrix products, on_device(): gate_up = jnp.dot(normed_all, w_gate_up, preferred_element_type=f32)  41.7 us
    dot_general x1, matrix products, on_device(): lax.dot_general(normed_rows, grad_gate_up, contract_rows, preferred_eleme...  40.9 us
    dot_general x1, matrix products, on_device(): lax.dot_general(grad_gate_up, w_gate_up, (((1,), (1,)), ((), ())), prefer...  40 us
    ppermute x9, starting transfers between devices, to_owner(): lax.ppermute(piece, 'i', [(m, (m + shift) % inner) for m in range(inner)])  35 us
  transfers between devices with their start and end apart: 60, of which 31 were waited for; matrix products, arithmetic and copies ran while one was open for 40% of the time, Pallas kernels for 0%

profile of v2, /device:TPU:0, one launch (start us, length us, event | category | flops | bytes accessed | tf_op | source)
XLA Modules:
  0.0 1365.2 jit_solution(11349772813445451425)
XLA Ops:
  12.4 4.0 dynamic-slice_bitcast_fusion.21
  42.0 5.3 convert_element_type.524
  65.2 30.0 %collective-permute-done = bf16[192,3840]{1,0:T(8,128)(2,1)} collective-permute-done((bf16[192,3840]{1,0:T(8,128)(2,1)}, bf16[192,3840]{1,0:T(8,128)(2,1)}, u32[]{:S(2)}, u32[]{:S(2)}) %collective-permute-start) | collective-permute-done | bytes 1474592 | tf_op jit(solution)/shard_map/ppermute | solution.py:90
  95.2 4.2 copy.274
  99.4 4.2 pad_maximum_fusion.5
  103.6 15.6 %collective-permute-done.1 = bf16[192,3840]{1,0:T(8,128)(2,1)} collective-permute-done((bf16[192,3840]{1,0:T(8,128)(2,1)}, bf16[192,3840]{1,0:T(8,128)(2,1)}, u32[]{:S(2)}, u32[]{:S(2)}) %collective-permute-start.1) | collective-permute-done | bytes 1474592 | tf_op jit(solution)/shard_map/ppermute | solution.py:254
  119.2 12.4 all-gather.7.cloned.1.call-done
  134.1 5.8 fusion.34
  142.6 5.6 fusion.96
  152.1 4.6 copy-done.2
  157.2 10.7 fusion.45
  168.8 4.8 convolution_convert_fusion.3
  178.0 30.3 %collective-permute-done.3 = bf16[192,3840]{1,0:T(8,128)(2,1)} collective-permute-done((bf16[192,3840]{1,0:T(8,128)(2,1)}, bf16[192,3840]{1,0:T(8,128)(2,1)}, u32[]{:S(2)}, u32[]{:S(2)}) %collective-permute-start.3) | collective-permute-done | bytes 1474592 | tf_op jit(solution)/shard_map/ppermute | solution.py:90
  212.0 31.0 %collective-permute-done.2 = bf16[192,3840]{1,0:T(8,128)(2,1)S(1)} collective-permute-done((bf16[192,3840]{1,0:T(8,128)(2,1)}, bf16[192,3840]{1,0:T(8,128)(2,1)S(1)}, u32[]{:S(2)}, u32[]{:S(2)}) %collective-permute-start.2) | collective-permute-done | bytes 1474592 | tf_op jit(solution)/shard_map/ppermute | solution.py:254
  257.6 4.4 copy.290
  262.7 5.1 broadcast_in_dim.99
  269.7 47.1 %collective-permute-done.5 = bf16[192,3840]{1,0:T(8,128)(2,1)} collective-permute-done((bf16[192,3840]{1,0:T(8,128)(2,1)}, bf16[192,3840]{1,0:T(8,128)(2,1)}, u32[]{:S(2)}, u32[]{:S(2)}) %collective-permute-start.5) | collective-permute-done | bytes 1474592 | tf_op jit(solution)/shard_map/ppermute | solution.py:254
  321.1 29.2 %collective-permute-done.6 = bf16[192,3840]{1,0:T(8,128)(2,1)S(1)} collective-permute-done((bf16[192,3840]{1,0:T(8,128)(2,1)}, bf16[192,3840]{1,0:T(8,128)(2,1)S(1)}, u32[]{:S(2)}, u32[]{:S(2)}) %collective-permute-start.6) | collective-permute-done | bytes 1474592 | tf_op jit(solution)/shard_map/ppermute | solution.py:90
  353.5 29.9 %all-gather.9.cloned.1.call-done = bf16[4096,1664]{1,0:T(8,128)(2,1)} async-done(((bf16[256,1664]{1,0:T(8,128)(2,1)}), bf16[4096,1664]{1,0:T(8,128)(2,1)}) %all-gather.9.cloned.1.call-update) | async-done | bytes 13631504 | tf_op jit(solution)/shard_map/all_gather | solution.py:311
  385.2 17.9 %collective-permute-done.7 = bf16[256,1536]{1,0:T(8,128)(2,1)S(1)} collective-permute-done((bf16[256,1536]{1,0:T(8,128)(2,1)S(1)}, bf16[256,1536]{1,0:T(8,128)(2,1)S(1)}, u32[]{:S(2)}, u32[]{:S(2)}) %collective-permute-start.7) | collective-permute-done | bytes 786464 | tf_op jit(solution)/shard_map/ppermute | solution.py:90
  406.7 4.6 collective-permute-start.9
  411.3 5.3 broadcast_in_dim.104
  418.5 8.1 collective-permute-done.11
  429.8 16.9 %collective-permute-done.12 = bf16[256,1536]{1,0:T(8,128)(2,1)S(1)} collective-permute-done((bf16[256,1536]{1,0:T(8,128)(2,1)}, bf16[256,1536]{1,0:T(8,128)(2,1)S(1)}, u32[]{:S(2)}, u32[]{:S(2)}) %collective-permute-start.12) | collective-permute-done | bytes 786464 | tf_op jit(solution)/shard_map/ppermute | solution.py:98
  448.5 16.5 %collective-permute-done.13 = bf16[256,1536]{1,0:T(8,128)(2,1)S(1)} collective-permute-done((bf16[256,1536]{1,0:T(8,128)(2,1)S(1)}, bf16[256,1536]{1,0:T(8,128)(2,1)S(1)}, u32[]{:S(2)}, u32[]{:S(2)}) %collective-permute-start.13) | collective-permute-done | bytes 786464 | tf_op jit(solution)/shard_map/ppermute | solution.py:90
  471.8 14.6 %collective-permute-done.15 = bf16[256,1536]{1,0:T(8,128)(2,1)S(1)} collective-permute-done((bf16[256,1536]{1,0:T(8,128)(2,1)}, bf16[256,1536]{1,0:T(8,128)(2,1)S(1)}, u32[]{:S(2)}, u32[]{:S(2)}) %collective-permute-start.15) | collective-permute-done | bytes 786464 | tf_op jit(solution)/shard_map/ppermute | solution.py:97
  489.1 18.6 %collective-permute-done.16 = bf16[256,1536]{1,0:T(8,128)(2,1)S(1)} collective-permute-done((bf16[256,1536]{1,0:T(8,128)(2,1)S(1)}, bf16[256,1536]{1,0:T(8,128)(2,1)S(1)}, u32[]{:S(2)}, u32[]{:S(2)}) %collective-permute-start.16) | collective-permute-done | bytes 786464 | tf_op jit(solution)/shard_map/ppermute | solution.py:90
  508.9 41.7 %fusion.14 = f32[4096,2560]{0,1:T(8,128)} fusion(bf16[1536,3840]{1,0:T(8,128)(2,1)} %bitcast.297, bf16[4096,1664]{1,0:T(8,128)(2,1)} %all-gather.9.cloned.1.call-done), kind=kOutput, calls=%fused_computation.28 | convolution fusion | flops 32212254720 | bytes 62390272 | tf_op jit(solution)/shard_map/dot_general | solution.py:326
  550.6 4.3 collective-permute-start.18
  557.8 14.5 %collective-permute-done.18 = bf16[256,1536]{1,0:T(8,128)(2,1)S(1)} collective-permute-done((bf16[256,1536]{1,0:T(8,128)(2,1)S(1)}, bf16[256,1536]{1,0:T(8,128)(2,1)S(1)}, u32[]{:S(2)}, u32[]{:S(2)}) %collective-permute-start.18) | collective-permute-done | bytes 786464 | tf_op jit(solution)/shard_map/ppermute | solution.py:97
  575.1 26.7 %multiply_convert_fusion.2 = (bf16[4096,1280]{0,1:T(8,128)(2,1)}, f32[4096,1280]{0,1:T(8,128)}) fusion(f32[4096,2560]{0,1:T(8,128)} %fusion.14, s32[1280]{0:T(1024)S(1)} %get-tuple-element.243, s32[1280]{0:T(1024)S(1)} %get-tuple-element.242, bf16[4096,1664]{1,0:T(8,128)(2,1)} %all-gather.9.cloned.1.call-done), kind=kOutput, calls=%fused_computation.13 | convolution fusion | flops 1379368960 | bytes 74459136 | tf_op jit(solution)/shard_map/dot_general | solution.py:325
  602.0 20.1 %convolution_convert_fusion = bf16[4096,1536]{1,0:T(8,128)(2,1)S(1)} fusion(bf16[4096,1280]{0,1:T(8,128)(2,1)} %get-tuple-element.236, bf16[1536,3840]{1,0:T(8,128)(2,1)} %bitcast.298), kind=kOutput, calls=%fused_computation.18 | convolution fusion | flops 16112418816 | bytes 27000832 | tf_op jit(solution)/shard_map/dot_general | solution.py:332
  640.1 47.6 %multiply_convert_fusion.1 = (bf16[4096,1280]{0,1:T(8,128)(2,1)}, bf16[4096,1280]{0,1:T(8,128)(2,1)}, f32[4096,1280]{0,1:T(8,128)}) fusion(f32[4096,2560]{0,1:T(8,128)} %fusion.14, f32[4096,1280]{0,1:T(8,128)} %get-tuple-element.237, bf16[4096,1536]{1,0:T(8,128)(2,1)} %slice_dynamic-update-slice_fusion, bf16[1536,3840]{1,0:T(8,128)(2,1)} %bitcast.299), kind=kOutput, calls=%fused_computation.12 | convolution fusion | flops 16190013440 | bytes 121372672 | tf_op jit(solution)/shard_map/dot_general | solution.py:351
  687.7 7.8 reduce_sum.123
  697.9 10.1 dynamic_update_slice.119
  708.1 40.0 %convolution_convert_fusion.1 = bf16[4096,1536]{1,0:T(8,128)(2,1)} fusion(bf16[4096,1280]{0,1:T(8,128)(2,1)} %get-tuple-element.169, bf16[4096,1280]{0,1:T(8,128)(2,1)} %get-tuple-element.168, bf16[1536,3840]{1,0:T(8,128)(2,1)} %bitcast.300), kind=kOutput, calls=%fused_computation.19 | convolution fusion | flops 32260489216 | bytes 41418752 | tf_op jit(solution)/shard_map/dot_general | solution.py:366
  768.1 10.5 collective-permute-done.28
  779.7 15.7 %collective-permute-done.26 = bf16[256,1536]{0,1:T(8,128)(2,1)S(1)} collective-permute-done((bf16[256,1536]{0,1:T(8,128)(2,1)S(1)}, bf16[256,1536]{0,1:T(8,128)(2,1)S(1)}, u32[]{:S(2)}, u32[]{:S(2)}) %collective-permute-start.26) | collective-permute-done | bytes 786464 | tf_op jit(solution)/shard_map/ppermute | solution.py:90
  796.6 15.7 %collective-permute-done.24 = bf16[256,1536]{0,1:T(8,128)(2,1)S(1)} collective-permute-done((bf16[256,1536]{0,1:T(8,128)(2,1)S(1)}, bf16[256,1536]{0,1:T(8,128)(2,1)S(1)}, u32[]{:S(2)}, u32[]{:S(2)}) %collective-permute-start.24) | collective-permute-done | bytes 786464 | tf_op jit(solution)/shard_map/ppermute | solution.py:90
  813.4 15.2 %collective-permute-done.22 = bf16[256,1536]{0,1:T(8,128)(2,1)S(1)} collective-permute-done((bf16[256,1536]{0,1:T(8,128)(2,1)S(1)}, bf16[256,1536]{0,1:T(8,128)(2,1)S(1)}, u32[]{:S(2)}, u32[]{:S(2)}) %collective-permute-start.22) | collective-permute-done | bytes 786464 | tf_op jit(solution)/shard_map/ppermute | solution.py:90
  829.0 10.7 slice.225
  839.7 4.4 collective-permute-start.40
  846.8 24.2 %convolution_convert_fusion.2 = bf16[1536,1280]{1,0:T(8,128)(2,1)S(1)} fusion(bf16[4096,1536]{1,0:T(8,128)(2,1)} %slice_dynamic-update-slice_fusion, bf16[4096,1280]{0,1:T(8,128)(2,1)} %get-tuple-element.236), kind=kOutput, calls=%fused_computation.26 | convolution fusion | flops 16108093440 | bytes 27000832 | tf_op jit(solution)/shard_map/dot_general | solution.py:377
  875.0 40.9 %fusion.11 = bf16[1536,2560]{1,0:T(8,128)(2,1)S(1)} fusion(bf16[4096,1536]{1,0:T(8,128)(2,1)} %slice.225, bf16[4096,1280]{0,1:T(8,128)(2,1)} %get-tuple-element.169, bf16[4096,1280]{0,1:T(8,128)(2,1)} %get-tuple-element.168), kind=kOutput, calls=%fused_computation.24 | convolution fusion | flops 32258129920 | bytes 41418752 | tf_op jit(solution)/shard_map/dot_general | solution.py:382
  919.0 11.2 collective-permute-done.32
  931.2 9.6 collective-permute-done.34
  945.1 21.7 %collective-permute-start.31 = (bf16[192,1280]{1,0:T(8,128)(2,1)S(1)}, bf16[192,1280]{1,0:T(8,128)(2,1)S(1)}, u32[]{:S(2)}, u32[]{:S(2)}) collective-permute-start(bf16[192,1280]{1,0:T(8,128)(2,1)S(1)} %get-tuple-element.191), channel_id=1, source_target_pairs={{0,8},{8,16},{16,24},{24,0},{1,9},{9,17},{17,25},{25,1},{2,10},{10... | collective-permute-start | bytes 1474568 | tf_op jit(solution)/shard_map/ppermute | solution.py:254
  970.0 12.9 collective-permute-done.37
  984.7 19.3 %collective-permute-done.38 = bf16[192,2560]{1,0:T(8,128)(2,1)S(1)} collective-permute-done((bf16[192,2560]{1,0:T(8,128)(2,1)S(1)}, bf16[192,2560]{1,0:T(8,128)(2,1)S(1)}, u32[]{:S(2)}, u32[]{:S(2)}) %collective-permute-start.38) | collective-permute-done | bytes 983072 | tf_op jit(solution)/shard_map/ppermute | solution.py:90
  1004.0 18.6 %collective-permute-done.39 = bf16[192,2560]{1,0:T(8,128)(2,1)S(1)} collective-permute-done((bf16[192,2560]{1,0:T(8,128)(2,1)S(1)}, bf16[192,2560]{1,0:T(8,128)(2,1)S(1)}, u32[]{:S(2)}, u32[]{:S(2)}) %collective-permute-start.39) | collective-permute-done | bytes 983072 | tf_op jit(solution)/shard_map/ppermute | solution.py:90
  1025.3 8.1 reduce-scatter.15.cloned.1.call-done
  1049.9 28.1 %all-gather.11.cloned.1.call-done = bf16[1024,1536]{1,0:T(8,128)(2,1)} async-done(((bf16[256,1536]{1,0:T(8,128)(2,1)}), bf16[1024,1536]{1,0:T(8,128)(2,1)}) %all-gather.11.cloned.1.call-update) | async-done | bytes 3145744 | tf_op jit(solution)/shard_map/all_gather | solution.py:414
  1086.0 16.0 %fusion = (f32[2,3,1024]{2,1,0:T(4,128)S(1)}, f32[2,1024,1024,3]{2,1,3,0:T(8,128)}) fusion(f32[2,3,1024,1024]{2,3,1,0:T(8,128)} %copy-done.2, f32[2,3,1024]{2,1,0:T(4,128)S(1)} %log_add_fusion, bf16[1024,2,64,1]{0,2,3,1:T(8,128)(2,1)S(1)} %bitcast.351, bf16[1024,2,3,64]{0,3,2,1:T(8,128)(2,1)S(1)} %bitcast.320), kind=kOutput, calls=%fused_computation.2 | convolution fusion | flops 824174592 | bytes 51429376 | tf_op jit(solution)/shard_map/qhgd,khd->hgqk/dot_general | solution.py:70
  1102.1 16.9 %fusion.2 = bf16[2,3,1024,1024]{2,3,1,0:T(8,128)(2,1)S(1)} fusion(f32[2,1024,1024,3]{2,1,3,0:T(8,128)} %get-tuple-element.240, f32[2,3,1024,1024]{2,3,1,0:T(8,128)} %copy-done.2, f32[2,3,1024]{2,1,0:T(4,128)S(1)} %get-tuple-element.239, f32[2,3,1024]{2,1,0:T(4,128)S(1)} %log_add_fusion), kind=kLoop, calls=%fused_computation.4 | loop fusion | flops 25165824 | bytes 62963712 | tf_op jit(solution)/shard_map/convert_element_type | solution.py:75
  1119.0 4.6 copy-done.3
  1123.5 5.7 fusion.51
  1132.4 7.0 convolution_multiply_fusion
  1140.6 10.3 fusion.52
  1150.9 8.4 multiply_reduce_fusion
  1163.9 5.4 convolution_convert_fusion.4
  1171.1 47.5 %reduce-scatter.19.cloned.1.call-done = bf16[192,512]{1,0:T(8,128)(2,1)} async-done(((bf16[1536,512]{1,0:T(8,128)(2,1)}), bf16[192,512]{1,0:T(8,128)(2,1)}) %reduce-scatter.19.cloned.1.call-update) | async-done | bytes 196624
  1219.7 4.5 copy.346
  1310.2 37.3 %reduce-scatter.21.cloned.1.call-done = bf16[192,768]{1,0:T(8,128)(2,1)} async-done(((bf16[1536,768]{1,0:T(8,128)(2,1)}), bf16[192,768]{1,0:T(8,128)(2,1)}) %reduce-scatter.21.cloned.1.call-update) | async-done | bytes 294928
  1348.8 4.6 fusion.39
  (462 shorter events, 313.7 us)
Async XLA Ops:
  7.2 170.6 %copy-start = (s32[1024,8]{0,1:T(8,128)S(1)}, s32[1024,8]{0,1:T(8,128)}, u32[]{:S(2)}) copy-start(s32[1024,8]{0,1:T(8,128)} %param.17) | copy-start | bytes 98308
  7.2 34.8 %all-gather.5.cloned.1.call-start = ((), (), s32[]{:S(2)}) async-start(), calls=%async_computation.6 | async-start | bytes 3932160 | tf_op jit(solution)/shard_map/all_gather | solution.py:240
  7.9 123.7 %all-gather.7.cloned.1.call-start = ((), (), s32[]{:S(2)}) async-start(), calls=%async_computation.7 | async-start | bytes 3981312 | tf_op jit(solution)/shard_map/all_gather | solution.py:241
  12.3 230.7 %reduce-scatter.11.cloned.1.call-start = ((), (), s32[]{:S(2)}) async-start(), calls=%async_computation.8 | async-start | bytes 3932160 | tf_op jit(solution)/shard_map/reduce_scatter | solution.py:287
  38.1 103.7 %copy-start.31 = (f32[1024,32]{0,1:T(8,128)}, f32[1024,32]{0,1:T(8,128)S(1)}, u32[]{:S(2)}) copy-start(f32[1024,32]{0,1:T(8,128)S(1)} %get-tuple-element.231) | copy-start | bytes 393220
  49.4 45.8 %collective-permute-start = (bf16[192,3840]{1,0:T(8,128)(2,1)}, bf16[192,3840]{1,0:T(8,128)(2,1)}, u32[]{:S(2)}, u32[]{:S(2)}) collective-permute-start(bf16[192,3840]{1,0:T(8,128)(2,1)} %copy.273), channel_id=1, source_target_pairs={{0,4},{4,0},{1,5},{5,1},{2,6},{6,2},{3,7},{7,3},{8,12},{12,8},{9,1... | collective-permute-start | bytes 4423688 | tf_op jit(solution)/shard_map/ppermute | solution.py:90
  58.9 60.3 %collective-permute-start.1 = (bf16[192,3840]{1,0:T(8,128)(2,1)}, bf16[192,3840]{1,0:T(8,128)(2,1)}, u32[]{:S(2)}, u32[]{:S(2)}) collective-permute-start(bf16[192,3840]{1,0:T(8,128)(2,1)} %copy.275), channel_id=1, source_target_pairs={{0,8},{8,16},{16,24},{24,0},{1,9},{9,17},{17,25},{25,1},{2,10},{10... | collective-permute-start | bytes 4423688 | tf_op jit(solution)/shard_map/ppermute | solution.py:254
  65.2 68.3 %copy-start.75 = (f32[1024]{0:T(1024)}, f32[1024]{0:T(1024)S(1)}, u32[]{:S(2)}) copy-start(f32[1024]{0:T(1024)S(1)} %add_rsqrt_fusion) | copy-start | bytes 12292
  133.5 111.6 %copy-start.65 = (f32[1536]{0:T(1024)}, f32[1536]{0:T(1024)S(1)}, u32[]{:S(2)}) copy-start(f32[1536]{0:T(1024)S(1)} %get-tuple-element.157) | copy-start | bytes 18436
  173.6 209.8 %all-gather.9.cloned.1.call-start = ((), (), s32[]{:S(2)}) async-start(), calls=%async_computation.9 | async-start | bytes 14483456 | tf_op jit(solution)/shard_map/all_gather | solution.py:311
  173.6 34.6 %collective-permute-start.3 = (bf16[192,3840]{1,0:T(8,128)(2,1)}, bf16[192,3840]{1,0:T(8,128)(2,1)}, u32[]{:S(2)}, u32[]{:S(2)}) collective-permute-start(bf16[192,3840]{1,0:T(8,128)(2,1)} %collective-permute-done.1), channel_id=1, source_target_pairs={{0,4},{4,0},{1,5},{5,1},{2,6},{6,2},{3,7},{7,3},{8,12},{12,8},{9,1... | collective-permute-start | bytes 4423688 | tf_op jit(solution)/shard_map/ppermute | solution.py:90
  177.2 65.8 %collective-permute-start.2 = (bf16[192,3840]{1,0:T(8,128)(2,1)}, bf16[192,3840]{1,0:T(8,128)(2,1)S(1)}, u32[]{:S(2)}, u32[]{:S(2)}) collective-permute-start(bf16[192,3840]{1,0:T(8,128)(2,1)} %copy.279), channel_id=1, source_target_pairs={{0,16},{8,24},{16,0},{24,8},{1,17},{9,25},{17,1},{25,9},{2,18},{10... | collective-permute-start | bytes 4423688 | tf_op jit(solution)/shard_map/ppermute | solution.py:254
  252.7 576.3 %reduce-scatter.13.cloned.1.call-start = ((), (), s32[]{:S(2)}) async-start(), calls=%async_computation.10 | async-start | bytes 1114112 | tf_op jit(solution)/shard_map/reduce_scatter | solution.py:369
  254.9 61.9 %collective-permute-start.5 = (bf16[192,3840]{1,0:T(8,128)(2,1)}, bf16[192,3840]{1,0:T(8,128)(2,1)}, u32[]{:S(2)}, u32[]{:S(2)}) collective-permute-start(bf16[192,3840]{1,0:T(8,128)(2,1)} %copy.291), channel_id=1, source_target_pairs={{0,24},{8,0},{16,8},{24,16},{1,25},{9,1},{17,9},{25,17},{2,26},{10... | collective-permute-start | bytes 4423688 | tf_op jit(solution)/shard_map/ppermute | solution.py:254
  261.9 57.3 %collective-permute-start.4 = (bf16[192,3840]{1,0:T(8,128)(2,1)}, bf16[192,3840]{1,0:T(8,128)(2,1)S(1)}, u32[]{:S(2)}, u32[]{:S(2)}) collective-permute-start(bf16[192,3840]{1,0:T(8,128)(2,1)} %copy-done.47), channel_id=1, source_target_pairs={{0,4},{4,0},{1,5},{5,1},{2,6},{6,2},{3,7},{7,3},{8,12},{12,8},{9,1... | collective-permute-start | bytes 4423688 | tf_op jit(solution)/shard_map/ppermute | solution.py:90
  316.8 33.6 %collective-permute-start.6 = (bf16[192,3840]{1,0:T(8,128)(2,1)}, bf16[192,3840]{1,0:T(8,128)(2,1)S(1)}, u32[]{:S(2)}, u32[]{:S(2)}) collective-permute-start(bf16[192,3840]{1,0:T(8,128)(2,1)} %collective-permute-done.5), channel_id=1, source_target_pairs={{0,4},{4,0},{1,5},{5,1},{2,6},{6,2},{3,7},{7,3},{8,12},{12,8},{9,1... | collective-permute-start | bytes 4423688 | tf_op jit(solution)/shard_map/ppermute | solution.py:90
  383.4 19.7 %collective-permute-start.7 = (bf16[256,1536]{1,0:T(8,128)(2,1)S(1)}, bf16[256,1536]{1,0:T(8,128)(2,1)S(1)}, u32[]{:S(2)}, u32[]{:S(2)}) collective-permute-start(bf16[256,1536]{1,0:T(8,128)(2,1)S(1)} %copy-done.11), channel_id=1, source_target_pairs={{0,2},{1,3},{2,0},{3,1},{4,6},{5,7},{6,4},{7,5},{8,10},{9,11},{10,... | collective-permute-start | bytes 2359304 | tf_op jit(solution)/shard_map/ppermute | solution.py:90
  384.0 21.4 %collective-permute-start.10 = (bf16[256,1536]{1,0:T(8,128)(2,1)S(1)}, bf16[256,1536]{1,0:T(8,128)(2,1)}, u32[]{:S(2)}, u32[]{:S(2)}) collective-permute-start(bf16[256,1536]{1,0:T(8,128)(2,1)S(1)} %copy-done.11), channel_id=1, source_target_pairs={{8,0},{16,8},{24,16},{9,1},{17,9},{25,17},{10,2},{18,10},{26,18},{... | collective-permute-start | bytes 2359304 | tf_op jit(solution)/shard_map/ppermute | solution.py:98
  404.3 23.5 %collective-permute-start.8 = (bf16[512,1536]{1,0:T(8,128)(2,1)}, bf16[512,1536]{1,0:T(8,128)(2,1)S(1)}, u32[]{:S(2)}, u32[]{:S(2)}) collective-permute-start(bf16[512,1536]{1,0:T(8,128)(2,1)} %pad_maximum_fusion.11), channel_id=1, source_target_pairs={{0,1},{1,0},{2,3},{3,2},{4,5},{5,4},{6,7},{7,6},{8,9},{9,8},{10,11... | collective-permute-start | bytes 4718600 | tf_op jit(solution)/shard_map/ppermute | solution.py:90
  405.4 21.1 %collective-permute-start.11 = (bf16[256,1536]{1,0:T(8,128)(2,1)}, bf16[256,1536]{1,0:T(8,128)(2,1)}, u32[]{:S(2)}, u32[]{:S(2)}) collective-permute-start(bf16[256,1536]{1,0:T(8,128)(2,1)} %collective-permute-done.10), channel_id=1, source_target_pairs={{8,0},{16,8},{24,16},{9,1},{17,9},{25,17},{10,2},{18,10},{26,18},{... | collective-permute-start | bytes 2359304 | tf_op jit(solution)/shard_map/ppermute | solution.py:98
  406.7 23.1 %collective-permute-start.9 = (bf16[256,1536]{1,0:T(8,128)(2,1)S(1)}, bf16[256,1536]{1,0:T(8,128)(2,1)S(1)}, u32[]{:S(2)}, u32[]{:S(2)}) collective-permute-start(bf16[256,1536]{1,0:T(8,128)(2,1)S(1)} %copy-done.11), channel_id=1, source_target_pairs={{0,8},{8,16},{16,24},{1,9},{9,17},{17,25},{2,10},{10,18},{18,26},{... | collective-permute-start | bytes 2359304 | tf_op jit(solution)/shard_map/ppermute | solution.py:97
  426.5 20.2 %collective-permute-start.12 = (bf16[256,1536]{1,0:T(8,128)(2,1)}, bf16[256,1536]{1,0:T(8,128)(2,1)S(1)}, u32[]{:S(2)}, u32[]{:S(2)}) collective-permute-start(bf16[256,1536]{1,0:T(8,128)(2,1)} %collective-permute-done.11), channel_id=1, source_target_pairs={{8,0},{16,8},{24,16},{9,1},{17,9},{25,17},{10,2},{18,10},{26,18},{... | collective-permute-start | bytes 2359304 | tf_op jit(solution)/shard_map/ppermute | solution.py:98
  447.8 17.2 %collective-permute-start.13 = (bf16[256,1536]{1,0:T(8,128)(2,1)S(1)}, bf16[256,1536]{1,0:T(8,128)(2,1)S(1)}, u32[]{:S(2)}, u32[]{:S(2)}) collective-permute-start(bf16[256,1536]{1,0:T(8,128)(2,1)S(1)} %get-tuple-element.164), channel_id=1, source_target_pairs={{0,2},{1,3},{2,0},{3,1},{4,6},{5,7},{6,4},{7,5},{8,10},{9,11},{10,... | collective-permute-start | bytes 2359304 | tf_op jit(solution)/shard_map/ppermute | solution.py:90
  466.3 3.6 collective-permute-start.14
  466.3 20.1 %collective-permute-start.15 = (bf16[256,1536]{1,0:T(8,128)(2,1)}, bf16[256,1536]{1,0:T(8,128)(2,1)S(1)}, u32[]{:S(2)}, u32[]{:S(2)}) collective-permute-start(bf16[256,1536]{1,0:T(8,128)(2,1)} %copy-done.54), channel_id=1, source_target_pairs={{0,8},{8,16},{16,24},{1,9},{9,17},{17,25},{2,10},{10,18},{18,26},{... | collective-permute-start | bytes 2359304 | tf_op jit(solution)/shard_map/ppermute | solution.py:97
  488.6 19.1 %collective-permute-start.16 = (bf16[256,1536]{1,0:T(8,128)(2,1)S(1)}, bf16[256,1536]{1,0:T(8,128)(2,1)S(1)}, u32[]{:S(2)}, u32[]{:S(2)}) collective-permute-start(bf16[256,1536]{1,0:T(8,128)(2,1)S(1)} %get-tuple-element.162), channel_id=1, source_target_pairs={{0,2},{1,3},{2,0},{3,1},{4,6},{5,7},{6,4},{7,5},{8,10},{9,11},{10,... | collective-permute-start | bytes 2359304 | tf_op jit(solution)/shard_map/ppermute | solution.py:90
  508.9 46.9 %collective-permute-start.17 = (bf16[512,1536]{1,0:T(8,128)(2,1)}, bf16[512,1536]{1,0:T(8,128)(2,1)S(1)}, u32[]{:S(2)}, u32[]{:S(2)}) collective-permute-start(bf16[512,1536]{1,0:T(8,128)(2,1)} %pad_maximum_fusion.13), channel_id=1, source_target_pairs={{0,1},{1,0},{2,3},{3,2},{4,5},{5,4},{6,7},{7,6},{8,9},{9,8},{10,11... | collective-permute-start | bytes 4718600 | tf_op jit(solution)/shard_map/ppermute | solution.py:90
  550.6 21.7 %collective-permute-start.18 = (bf16[256,1536]{1,0:T(8,128)(2,1)S(1)}, bf16[256,1536]{1,0:T(8,128)(2,1)S(1)}, u32[]{:S(2)}, u32[]{:S(2)}) collective-permute-start(bf16[256,1536]{1,0:T(8,128)(2,1)S(1)} %collective-permute-done.15), channel_id=1, source_target_pairs={{0,8},{8,16},{16,24},{1,9},{9,17},{17,25},{2,10},{10,18},{18,26},{... | collective-permute-start | bytes 2359304 | tf_op jit(solution)/shard_map/ppermute | solution.py:97
  574.5 27.3 %collective-permute-start.19 = (bf16[256,1536]{1,0:T(8,128)(2,1)S(1)}, bf16[256,1536]{1,0:T(8,128)(2,1)S(1)}, u32[]{:S(2)}, u32[]{:S(2)}) collective-permute-start(bf16[256,1536]{1,0:T(8,128)(2,1)S(1)} %get-tuple-element.160), channel_id=1, source_target_pairs={{0,2},{1,3},{2,0},{3,1},{4,6},{5,7},{6,4},{7,5},{8,10},{9,11},{10,... | collective-permute-start | bytes 2359304 | tf_op jit(solution)/shard_map/ppermute | solution.py:90
  601.9 21.2 %collective-permute-start.20 = (bf16[512,1536]{1,0:T(8,128)(2,1)S(1)}, bf16[512,1536]{1,0:T(8,128)(2,1)S(1)}, u32[]{:S(2)}, u32[]{:S(2)}) collective-permute-start(bf16[512,1536]{1,0:T(8,128)(2,1)S(1)} %pad_maximum_fusion.14), channel_id=1, source_target_pairs={{0,1},{1,0},{2,3},{3,2},{4,5},{5,4},{6,7},{7,6},{8,9},{9,8},{10,11... | collective-permute-start | bytes 4718600 | tf_op jit(solution)/shard_map/ppermute | solution.py:90
  631.2 124.4 %collective-permute-start.27 = (bf16[2,256,1536]{1,2,0:T(8,128)(2,1)}, bf16[2,256,1536]{1,2,0:T(8,128)(2,1)}, u32[]{:S(2)}, u32[]{:S(2)}) collective-permute-start(bf16[2,256,1536]{1,2,0:T(8,128)(2,1)} %bitcast.346), channel_id=1, source_target_pairs={{0,1},{1,0},{2,3},{3,2},{4,5},{5,4},{6,7},{7,6},{8,9},{9,8},{10,11... | collective-permute-start | bytes 4718600 | tf_op jit(solution)/shard_map/ppermute | solution.py:90
  634.4 125.3 %collective-permute-start.25 = (bf16[2,256,1536]{1,2,0:T(8,128)(2,1)}, bf16[2,256,1536]{1,2,0:T(8,128)(2,1)}, u32[]{:S(2)}, u32[]{:S(2)}) collective-permute-start(bf16[2,256,1536]{1,2,0:T(8,128)(2,1)} %bitcast.345), channel_id=1, source_target_pairs={{0,1},{1,0},{2,3},{3,2},{4,5},{5,4},{6,7},{7,6},{8,9},{9,8},{10,11... | collective-permute-start | bytes 4718600 | tf_op jit(solution)/shard_map/ppermute | solution.py:90
  637.0 125.2 %collective-permute-start.23 = (bf16[2,256,1536]{1,2,0:T(8,128)(2,1)}, bf16[2,256,1536]{1,2,0:T(8,128)(2,1)}, u32[]{:S(2)}, u32[]{:S(2)}) collective-permute-start(bf16[2,256,1536]{1,2,0:T(8,128)(2,1)} %bitcast.344), channel_id=1, source_target_pairs={{0,1},{1,0},{2,3},{3,2},{4,5},{5,4},{6,7},{7,6},{8,9},{9,8},{10,11... | collective-permute-start | bytes 4718600 | tf_op jit(solution)/shard_map/ppermute | solution.py:90
  640.0 125.6 %collective-permute-start.21 = (bf16[2,256,1536]{1,2,0:T(8,128)(2,1)}, bf16[2,256,1536]{1,2,0:T(8,128)(2,1)}, u32[]{:S(2)}, u32[]{:S(2)}) collective-permute-start(bf16[2,256,1536]{1,2,0:T(8,128)(2,1)} %bitcast.343), channel_id=1, source_target_pairs={{0,1},{1,0},{2,3},{3,2},{4,5},{5,4},{6,7},{7,6},{8,9},{9,8},{10,11... | collective-permute-start | bytes 4718600 | tf_op jit(solution)/shard_map/ppermute | solution.py:90
  708.0 325.3 %reduce-scatter.15.cloned.1.call-start = ((), (), s32[]{:S(2)}) async-start(), calls=%async_computation.11 | async-start | bytes 13369344 | tf_op jit(solution)/shard_map/reduce_scatter | solution.py:375
  758.1 20.5 %collective-permute-start.28 = (bf16[256,1536]{0,1:T(8,128)(2,1)S(1)}, bf16[256,1536]{0,1:T(8,128)(2,1)S(1)}, u32[]{:S(2)}, u32[]{:S(2)}) collective-permute-start(bf16[256,1536]{0,1:T(8,128)(2,1)S(1)} %dynamic-slice_bitcast_fusion.8), channel_id=1, source_target_pairs={{0,2},{1,3},{2,0},{3,1},{4,6},{5,7},{6,4},{7,5},{8,10},{9,11},{10,... | collective-permute-start | bytes 2359304 | tf_op jit(solution)/shard_map/ppermute | solution.py:90
  761.6 33.9 %collective-permute-start.26 = (bf16[256,1536]{0,1:T(8,128)(2,1)S(1)}, bf16[256,1536]{0,1:T(8,128)(2,1)S(1)}, u32[]{:S(2)}, u32[]{:S(2)}) collective-permute-start(bf16[256,1536]{0,1:T(8,128)(2,1)S(1)} %dynamic-slice_bitcast_fusion.9), channel_id=1, source_target_pairs={{0,2},{1,3},{2,0},{3,1},{4,6},{5,7},{6,4},{7,5},{8,10},{9,11},{10,... | collective-permute-start | bytes 2359304 | tf_op jit(solution)/shard_map/ppermute | solution.py:90
  764.1 48.2 %collective-permute-start.24 = (bf16[256,1536]{0,1:T(8,128)(2,1)S(1)}, bf16[256,1536]{0,1:T(8,128)(2,1)S(1)}, u32[]{:S(2)}, u32[]{:S(2)}) collective-permute-start(bf16[256,1536]{0,1:T(8,128)(2,1)S(1)} %dynamic-slice_bitcast_fusion.10), channel_id=1, source_target_pairs={{0,2},{1,3},{2,0},{3,1},{4,6},{5,7},{6,4},{7,5},{8,10},{9,11},{10,... | collective-permute-start | bytes 2359304 | tf_op jit(solution)/shard_map/ppermute | solution.py:90
  767.5 61.2 %collective-permute-start.22 = (bf16[256,1536]{0,1:T(8,128)(2,1)S(1)}, bf16[256,1536]{0,1:T(8,128)(2,1)S(1)}, u32[]{:S(2)}, u32[]{:S(2)}) collective-permute-start(bf16[256,1536]{0,1:T(8,128)(2,1)S(1)} %dynamic-slice_bitcast_fusion.11), channel_id=1, source_target_pairs={{0,2},{1,3},{2,0},{3,1},{4,6},{5,7},{6,4},{7,5},{8,10},{9,11},{10,... | collective-permute-start | bytes 2359304 | tf_op jit(solution)/shard_map/ppermute | solution.py:90
  829.0 249.1 %all-gather.11.cloned.1.call-start = ((), (), s32[]{:S(2)}) async-start(), calls=%async_computation.12 | async-start | bytes 3932160 | tf_op jit(solution)/shard_map/all_gather | solution.py:414
  839.7 102.0 %collective-permute-start.40 = (bf16[256,1536]{0,1:T(8,128)(2,1)}, bf16[256,1536]{0,1:T(8,128)(2,1)}, u32[]{:S(2)}, u32[]{:S(2)}) collective-permute-start(bf16[256,1536]{0,1:T(8,128)(2,1)} %fusion.43), channel_id=1, source_target_pairs={{0,8},{8,16},{16,24},{24,0},{1,9},{9,17},{17,25},{25,1},{2,10},{10... | collective-permute-start | bytes 2359304 | tf_op jit(solution)/shard_map/ppermute | solution.py:192
  844.1 98.8 %collective-permute-start.41 = (bf16[256,1536]{0,1:T(8,128)(2,1)}, bf16[256,1536]{0,1:T(8,128)(2,1)}, u32[]{:S(2)}, u32[]{:S(2)}) collective-permute-start(bf16[256,1536]{0,1:T(8,128)(2,1)} %fusion.42), channel_id=1, source_target_pairs={{0,16},{8,24},{16,0},{24,8},{1,17},{9,25},{17,1},{25,9},{2,18},{10... | collective-permute-start | bytes 2359304 | tf_op jit(solution)/shard_map/ppermute | solution.py:192
  844.1 101.0 %collective-permute-start.42 = (bf16[256,1536]{0,1:T(8,128)(2,1)}, bf16[256,1536]{0,1:T(8,128)(2,1)}, u32[]{:S(2)}, u32[]{:S(2)}) collective-permute-start(bf16[256,1536]{0,1:T(8,128)(2,1)} %fusion.41), channel_id=1, source_target_pairs={{0,24},{8,0},{16,8},{24,16},{1,25},{9,1},{17,9},{25,17},{2,26},{10... | collective-permute-start | bytes 2359304 | tf_op jit(solution)/shard_map/ppermute | solution.py:192
  872.4 43.5 %collective-permute-start.29 = (bf16[192,1280]{1,0:T(8,128)(2,1)}, bf16[192,1280]{1,0:T(8,128)(2,1)S(1)}, u32[]{:S(2)}, u32[]{:S(2)}) collective-permute-start(bf16[192,1280]{1,0:T(8,128)(2,1)} %get-tuple-element.196), channel_id=1, source_target_pairs={{0,4},{4,0},{1,5},{5,1},{2,6},{6,2},{3,7},{7,3},{8,12},{12,8},{9,1... | collective-permute-start | bytes 1474568 | tf_op jit(solution)/shard_map/ppermute | solution.py:90
  873.9 43.0 %collective-permute-start.30 = (bf16[192,1280]{1,0:T(8,128)(2,1)}, bf16[192,1280]{1,0:T(8,128)(2,1)S(1)}, u32[]{:S(2)}, u32[]{:S(2)}) collective-permute-start(bf16[192,1280]{1,0:T(8,128)(2,1)} %get-tuple-element.195), channel_id=1, source_target_pairs={{0,4},{4,0},{1,5},{5,1},{2,6},{6,2},{3,7},{7,3},{8,12},{12,8},{9,1... | collective-permute-start | bytes 1474568 | tf_op jit(solution)/shard_map/ppermute | solution.py:90
  915.9 14.4 %collective-permute-start.32 = (bf16[192,1280]{1,0:T(8,128)(2,1)}, bf16[192,1280]{1,0:T(8,128)(2,1)S(1)}, u32[]{:S(2)}, u32[]{:S(2)}) collective-permute-start(bf16[192,1280]{1,0:T(8,128)(2,1)} %get-tuple-element.194), channel_id=1, source_target_pairs={{0,4},{4,0},{1,5},{5,1},{2,6},{6,2},{3,7},{7,3},{8,12},{12,8},{9,1... | collective-permute-start | bytes 1474568 | tf_op jit(solution)/shard_map/ppermute | solution.py:90
  916.9 23.9 %collective-permute-start.34 = (bf16[192,1280]{1,0:T(8,128)(2,1)}, bf16[192,1280]{1,0:T(8,128)(2,1)S(1)}, u32[]{:S(2)}, u32[]{:S(2)}) collective-permute-start(bf16[192,1280]{1,0:T(8,128)(2,1)} %get-tuple-element.193), channel_id=1, source_target_pairs={{0,4},{4,0},{1,5},{5,1},{2,6},{6,2},{3,7},{7,3},{8,12},{12,8},{9,1... | collective-permute-start | bytes 1474568 | tf_op jit(solution)/shard_map/ppermute | solution.py:90
  930.3 39.7 %collective-permute-start.36 = (bf16[192,2560]{1,0:T(8,128)(2,1)S(1)}, bf16[192,2560]{1,0:T(8,128)(2,1)S(1)}, u32[]{:S(2)}, u32[]{:S(2)}) collective-permute-start(bf16[192,2560]{1,0:T(8,128)(2,1)S(1)} %get-tuple-element.186), channel_id=1, source_target_pairs={{0,4},{4,0},{1,5},{5,1},{2,6},{6,2},{3,7},{7,3},{8,12},{12,8},{9,1... | collective-permute-start | bytes 2949128 | tf_op jit(solution)/shard_map/ppermute | solution.py:90
  940.8 42.1 %collective-permute-start.37 = (bf16[192,2560]{1,0:T(8,128)(2,1)S(1)}, bf16[192,2560]{1,0:T(8,128)(2,1)S(1)}, u32[]{:S(2)}, u32[]{:S(2)}) collective-permute-start(bf16[192,2560]{1,0:T(8,128)(2,1)S(1)} %get-tuple-element.185), channel_id=1, source_target_pairs={{0,4},{4,0},{1,5},{5,1},{2,6},{6,2},{3,7},{7,3},{8,12},{12,8},{9,1... | collective-permute-start | bytes 2949128 | tf_op jit(solution)/shard_map/ppermute | solution.py:90
  941.8 62.3 %collective-permute-start.38 = (bf16[192,2560]{1,0:T(8,128)(2,1)S(1)}, bf16[192,2560]{1,0:T(8,128)(2,1)S(1)}, u32[]{:S(2)}, u32[]{:S(2)}) collective-permute-start(bf16[192,2560]{1,0:T(8,128)(2,1)S(1)} %get-tuple-element.184), channel_id=1, source_target_pairs={{0,4},{4,0},{1,5},{5,1},{2,6},{6,2},{3,7},{7,3},{8,12},{12,8},{9,1... | collective-permute-start | bytes 2949128 | tf_op jit(solution)/shard_map/ppermute | solution.py:90
  942.9 79.7 %collective-permute-start.39 = (bf16[192,2560]{1,0:T(8,128)(2,1)S(1)}, bf16[192,2560]{1,0:T(8,128)(2,1)S(1)}, u32[]{:S(2)}, u32[]{:S(2)}) collective-permute-start(bf16[192,2560]{1,0:T(8,128)(2,1)S(1)} %get-tuple-element.183), channel_id=1, source_target_pairs={{0,4},{4,0},{1,5},{5,1},{2,6},{6,2},{3,7},{7,3},{8,12},{12,8},{9,1... | collective-permute-start | bytes 2949128 | tf_op jit(solution)/shard_map/ppermute | solution.py:90
  945.1 80.2 %collective-permute-start.31 = (bf16[192,1280]{1,0:T(8,128)(2,1)S(1)}, bf16[192,1280]{1,0:T(8,128)(2,1)S(1)}, u32[]{:S(2)}, u32[]{:S(2)}) collective-permute-start(bf16[192,1280]{1,0:T(8,128)(2,1)S(1)} %get-tuple-element.191), channel_id=1, source_target_pairs={{0,8},{8,16},{16,24},{24,0},{1,9},{9,17},{17,25},{25,1},{2,10},{10... | collective-permute-start | bytes 1474568 | tf_op jit(solution)/shard_map/ppermute | solution.py:254
  970.0 55.2 %collective-permute-start.33 = (bf16[192,1280]{1,0:T(8,128)(2,1)S(1)}, bf16[192,1280]{1,0:T(8,128)(2,1)S(1)}, u32[]{:S(2)}, u32[]{:S(2)}) collective-permute-start(bf16[192,1280]{1,0:T(8,128)(2,1)S(1)} %get-tuple-element.190), channel_id=1, source_target_pairs={{0,16},{8,24},{16,0},{24,8},{1,17},{9,25},{17,1},{25,9},{2,18},{10... | collective-permute-start | bytes 1474568 | tf_op jit(solution)/shard_map/ppermute | solution.py:254
  983.0 42.3 %collective-permute-start.35 = (bf16[192,1280]{1,0:T(8,128)(2,1)S(1)}, bf16[192,1280]{1,0:T(8,128)(2,1)}, u32[]{:S(2)}, u32[]{:S(2)}) collective-permute-start(bf16[192,1280]{1,0:T(8,128)(2,1)S(1)} %get-tuple-element.189), channel_id=1, source_target_pairs={{0,24},{8,0},{16,8},{24,16},{1,25},{9,1},{17,9},{25,17},{2,26},{10... | collective-permute-start | bytes 1474568 | tf_op jit(solution)/shard_map/ppermute | solution.py:254
  1045.1 173.5 %reduce-scatter.19.cloned.1.call-start = ((), (), s32[]{:S(2)}) async-start(), calls=%async_computation.14 | async-start | bytes 1769472
  1045.9 37.4 %collective-permute-start.43 = (bf16[192,2560]{1,0:T(8,128)(2,1)}, bf16[192,2560]{1,0:T(8,128)(2,1)}, u32[]{:S(2)}, u32[]{:S(2)}) collective-permute-start(bf16[192,2560]{1,0:T(8,128)(2,1)} %get-tuple-element.181), channel_id=1, source_target_pairs={{0,8},{8,16},{16,24},{24,0},{1,9},{9,17},{17,25},{25,1},{2,10},{10... | collective-permute-start | bytes 2949128 | tf_op jit(solution)/shard_map/ppermute | solution.py:254
  1132.0 176.6 %reduce-scatter.17.cloned.1.call-start = ((), (), s32[]{:S(2)}) async-start(), calls=%async_computation.13 | async-start | bytes 3932160 | tf_op jit(solution)/shard_map/reduce_scatter | solution.py:449
  1159.4 188.2 %reduce-scatter.21.cloned.1.call-start = ((), (), s32[]{:S(2)}) async-start(), calls=%async_computation.15 | async-start | bytes 2654208
  1159.5 60.2 %collective-permute-start.44 = (bf16[192,2560]{1,0:T(8,128)(2,1)}, bf16[192,2560]{1,0:T(8,128)(2,1)}, u32[]{:S(2)}, u32[]{:S(2)}) collective-permute-start(bf16[192,2560]{1,0:T(8,128)(2,1)} %get-tuple-element.180), channel_id=1, source_target_pairs={{0,16},{8,24},{16,0},{24,8},{1,17},{9,25},{17,1},{25,9},{2,18},{10... | collective-permute-start | bytes 2949128 | tf_op jit(solution)/shard_map/ppermute | solution.py:254
  1161.9 62.4 %collective-permute-start.49 = (bf16[192,2560]{1,0:T(8,128)(2,1)S(1)}, bf16[192,2560]{1,0:T(8,128)(2,1)}, u32[]{:S(2)}, u32[]{:S(2)}) collective-permute-start(bf16[192,2560]{1,0:T(8,128)(2,1)S(1)} %copy-done.53), channel_id=1, source_target_pairs={{0,24},{8,0},{16,8},{24,16},{1,25},{9,1},{17,9},{25,17},{2,26},{10... | collective-permute-start | bytes 2949128 | tf_op jit(solution)/shard_map/ppermute | solution.py:254
  1296.5 6.8 collective-permute-start.47
  1303.2 4.2 collective-permute-start.48
  1348.7 4.7 collective-permute-start.45
  1353.4 4.0 collective-permute-start.46
  (75 other events, 692.2 us)
Sparse Core Ops, SparseCore 0:
  9.6 31.2 all-gather.4
  43.0 88.5 all-gather.6
  173.7 35.2 reduce-scatter.10
  252.8 130.5 all-gather.8
  708.1 59.4 reduce-scatter.12
  829.1 204.2 reduce-scatter.14
  1045.2 32.8 all-gather.10
  1132.1 86.4 reduce-scatter.18
  1221.1 53.2 reduce-scatter.16
  1277.8 69.6 reduce-scatter.20

commit v3 on v2

--- a/solution.py
+++ b/solution.py
@@ -39,6 +39,10 @@
     return jnp.concatenate(
         [first * cosine - second * sine, second * cosine + first * sine], axis=-1
     )
+
+
+def tie(*values):
+    return lax.optimization_barrier(values)
 
 
 def masked_scores(query, keys, prefix_len):
@@ -62,7 +66,7 @@
     return output.reshape(query.shape[0], -1).astype(bf16), highest + jnp.log(summed)
 
 
-def attend_backward(query, keys, values, grad_mixed, log_total, prefix_len):
+def attend_backward(query, keys, values, grad_mixed, log_total, prefix_len, hold):
     scores, grouped = masked_scores(query, keys, prefix_len)
     weights = jnp.exp(scores - log_total)
     seq_len, heads_kv, head_size = keys.shape
@@ -73,6 +77,7 @@
     grad_scores = (
         weights * (grad_weights - jnp.sum(weights * grad_weights, axis=-1, keepdims=True))
     ).astype(bf16)
+    grad_scores, hold = tie(grad_scores, hold)
     scaling = head_size ** (-0.5)
     grad_query = (
         jnp.einsum("hgqk,khd->qhgd", grad_scores, keys, preferred_element_type=f32) * scaling
@@ -83,24 +88,11 @@
     grad_values = jnp.einsum(
         "hgqk,qhgd->khd", weights.astype(bf16), grad_grouped, preferred_element_type=f32
     )
-    return grad_query.reshape(seq_len, -1, head_size), grad_keys, grad_values
+    return grad_query.reshape(seq_len, -1, head_size), grad_keys, grad_values, hold
 
 
 def swap(values, axis, size, bit):
     return lax.ppermute(values, axis, [(m, m ^ bit) for m in range(size)])
-
-
-def gather_line(block, axis, size):
-    me = lax.axis_index(axis)
-    up, down = [block], [block]
-    for _ in range(1, size):
-        up.append(lax.ppermute(up[-1], axis, [(m, m + 1) for m in range(size - 1)]))
-        down.append(lax.ppermute(down[-1], axis, [(m + 1, m) for m in range(size - 1)]))
-    return [block] + [jnp.where(me >= s, up[s], down[size - s]) for s in range(1, size)]
-
-
-def tie(*values):
-    return lax.optimization_barrier(values)
 
 
 def by_rows(values):
@@ -142,12 +134,10 @@
             split = jnp.where(lax.axis_index("o") == 0, split, split[:, ::-1])
         return jnp.swapaxes(split, 1, 2).reshape(rows, -1)
 
-    def pass_on(piece):
-        if outer == 1:
-            return piece[None]
+    def pass_on(pair):
         if outer == 2:
-            return jnp.stack([piece, swap(piece, "o", 2, 1)])
-        return lax.all_gather(piece, "o", axis=0)
+            return tuple(jnp.stack([piece, swap(piece, "o", 2, 1)]) for piece in pair)
+        return tuple(lax.all_gather(piece, "o", axis=0) for piece in pair)
 
     def sum_outer(parts):
         if outer == 1:
@@ -156,41 +146,28 @@
             return (parts[0].astype(f32) + swap(parts[1], "o", 2, 1).astype(f32)).astype(bf16)
         return lax.psum_scatter(parts, "o", scatter_dimension=0, tiled=False)
 
-    def share(block):
+    def gather_t(block):
+        if n_tensor != 4:
+            return lax.all_gather(block, "t", axis=0, tiled=True)
         rows, width = block.shape
+        me_t = lax.axis_index("t")
+        result = jnp.zeros((n_tensor * rows, width), block.dtype)
+        pair = jnp.concatenate([block, swap(block, "t", n_tensor, 2)], axis=0)
+        for bit, part in ((0, pair), (1, swap(pair, "t", n_tensor, 1))):
+            result = put(result, part[:rows], (me_t ^ bit) * rows, 0)
+            result = put(result, part[rows:], (me_t ^ bit ^ 2) * rows, 0)
+        return result
+
+    def scatter_t(values):
         if n_tensor != 4:
-            return lax.all_gather(block, shared, axis=0, tiled=True)
-        me_i, me_t = lax.axis_index("i"), lax.axis_index("t")
-        result = jnp.zeros((inner * n_tensor * rows, width), block.dtype)
-        for shift, near in enumerate(gather_line(block, "i", inner)):
-            pair = jnp.concatenate([near, swap(near, "t", n_tensor, 2)], axis=0)
-            for bit, part in ((0, pair), (1, swap(pair, "t", n_tensor, 1))):
-                place = (me_i - shift) % inner * n_tensor + (me_t ^ bit)
-                result = put(result, part[:rows], place * rows, 0)
-                result = put(result, part[rows:], (place ^ 2) * rows, 0)
-        return result
-
-    def sum_across(values):
-        rows, width = values.shape[0] // (inner * n_tensor), values.shape[1]
-        me_i, me_t = lax.axis_index("i"), lax.axis_index("t")
-        blocks = values.reshape(inner, 2, 2, rows, width)
-        result = []
-        for shift in range(inner):
-            block = lax.dynamic_index_in_dim(blocks, (me_i + shift) % inner, 0, keepdims=False)
-            for axis, bit, own in ((1, 1, me_t % 2), (0, 2, me_t // 2)):
-                keep = lax.dynamic_index_in_dim(block, own, axis, keepdims=False)
-                send = lax.dynamic_index_in_dim(block, 1 - own, axis, keepdims=False)
-                got = swap(send, "t", n_tensor, bit)
-                block = (keep.astype(f32) + got.astype(f32)).astype(bf16)
-            result.append(block)
-        return result
-
-    def sum_line(parts):
-        total = parts[0].astype(f32)
-        for shift in range(1, inner):
-            pairs = [(m, (m + shift) % inner) for m in range(inner)]
-            total = total + lax.ppermute(parts[shift], "i", pairs).astype(f32)
-        return total
+            return lax.psum_scatter(values, "t", scatter_dimension=0, tiled=True).astype(f32)
+        me_t = lax.axis_index("t")
+        block = values.reshape(2, 2, -1, values.shape[1])
+        for axis, bit, own in ((1, 1, me_t % 2), (0, 2, me_t // 2)):
+            keep = lax.dynamic_index_in_dim(block, own, axis, keepdims=False)
+            send = lax.dynamic_index_in_dim(block, 1 - own, axis, keepdims=False)
+            block = keep.astype(f32) + swap(send.astype(bf16), "t", n_tensor, bit).astype(f32)
+        return block
 
     def sum_tensor(values):
         if n_tensor != 4:
@@ -242,25 +219,28 @@
 
         def expert_piece(target):
             first = target * own_experts
-            parts = [
+            gate, up = (
                 jnp.swapaxes(lax.dynamic_slice_in_dim(w, first, own_experts, 0), 0, 1)
                 for w in (w_gate, w_up)
-            ]
-            down = lax.dynamic_slice_in_dim(w_down, first, own_experts, 0)
-            parts.append(down.transpose(2, 0, 1))
-            return jnp.concatenate([p.reshape(depth, own_hidden) for p in parts], axis=1)
+            )
+            down = lax.dynamic_slice_in_dim(w_down, first, own_experts, 0).transpose(2, 0, 1)
+            gate_up = jnp.concatenate(
+                [gate.reshape(depth, own_hidden), up.reshape(depth, own_hidden)], axis=1
+            )
+            return gate_up, down.reshape(depth, own_hidden)
 
         def to_owner(piece, shift):
-            return lax.ppermute(piece, "i", [(m, (m + shift) % inner) for m in range(inner)])
+            pairs = [(m, (m + shift) % inner) for m in range(inner)]
+            return jax.tree.map(lambda part: lax.ppermute(part, "i", pairs), piece)
 
         pieces = [expert_piece((me_i + shift) % inner) for shift in range(inner)]
-        pieces[0], pieces[1], tokens_all = tie(pieces[0], pieces[1], tokens_all)
+        far_gate_up, far_down = to_owner(pieces[2], 2)
+        far_down, tokens_all = tie(far_down, tokens_all)
+        pieces[0], pieces[1], pieces[3], far_gate_up, packed = tie(
+            pieces[0], pieces[1], pieces[3], far_gate_up, packed
+        )
+        near = to_owner(pieces[1], 1)
         owned = [pass_on(pieces[0])]
-        near = to_owner(pieces[1], 1)
-        pieces[2], pieces[3], owned[0], near, packed = tie(
-            pieces[2], pieces[3], owned[0], near, packed
-        )
-        owned.append(pass_on(near))
 
         w_qkv = packed[:, :qkv_cols]
         w_out_t = packed[:, qkv_cols:attn_cols]
@@ -278,16 +258,15 @@
         ).astype(bf16)
         values = qkv[:, q_cols + k_cols :].astype(bf16).reshape(group, -1, HEAD_DIM)
         attended, log_total = attend_forward(query, keys, values, prefix[0])
-        near = to_owner(pieces[2], 2)
-        pieces[3], attended = tie(pieces[3], attended)
+        pieces[3], near, owned[0], attended = tie(pieces[3], near, owned[0], attended)
+        last = to_owner(pieces[3], 3)
         branch = lax.dot_general(
             attended, w_out_t, (((1,), (1,)), ((), ())), preferred_element_type=f32
         ).astype(bf16)
         tokens_f = tokens.astype(f32)
         branch = lax.psum_scatter(branch, "t", scatter_dimension=0, tiled=True)
-        last = to_owner(pieces[3], 3)
-        near, owned[1], branch = tie(near, owned[1], branch)
-        owned += [pass_on(near), pass_on(last)]
+        far_gate_up, near, last, branch = tie(far_gate_up, near, last, branch)
+        owned += [pass_on(near), pass_on((far_gate_up, far_down)), pass_on(last)]
         middle = tokens_f + branch.astype(f32)
         scale_two = rms_scale(middle)
         normed_two = (middle * scale_two * gain_two).astype(bf16)
@@ -309,13 +288,19 @@
             axis=1,
         )
         shared_all = by_rows(lax.all_gather(by_rows(shipped), shared, axis=0, tiled=True))
-        w_owned = jnp.zeros((outer, inner, depth, 3 * own_hidden), bf16)
+        w_gate_up = jnp.zeros((outer, inner, depth, 2 * own_hidden), bf16)
+        w_down_t = jnp.zeros((outer, inner, depth, own_hidden), bf16)
         for shift in range(inner):
-            w_owned = put(w_owned, owned[shift][:, None], 0, (me_i - shift) % inner, 0, 0)
-        w_owned = w_owned.reshape(outer * inner * depth, 3 * own_hidden)
-        cot_order, shared_all, w_owned = tie(by_rows(to_owner_order(cotangent)), shared_all, w_owned)
-        w_gate_up, w_down_t = w_owned[:, : 2 * own_hidden], w_owned[:, 2 * own_hidden :]
-        cot_all = by_rows(share(cot_order))
+            source = (me_i - shift) % inner
+            w_gate_up = put(w_gate_up, owned[shift][0][:, None], 0, source, 0, 0)
+            w_down_t = put(w_down_t, owned[shift][1][:, None], 0, source, 0, 0)
+        cot_order, shared_all, w_gate_up, w_down_t = tie(
+            by_rows(to_owner_order(cotangent)),
+            shared_all,
+            w_gate_up.reshape(outer * inner * depth, 2 * own_hidden),
+            w_down_t.reshape(outer * inner * depth, own_hidden),
+        )
+        cot_all = by_rows(lax.all_gather(cot_order, shared, axis=0, tiled=True))
         count = shared_all.shape[0]
         normed_all = shared_all[:, :width]
 
@@ -333,11 +318,12 @@
             gated, w_down_t, (((1,), (1,)), ((), ())), preferred_element_type=f32
         ).astype(bf16)
         expert_part, cot_all = tie(by_rows(expert_part), cot_all)
-        if n_tensor == 4:
-            share_parts = sum_across(expert_part)
-        else:
-            share_parts = [lax.psum_scatter(expert_part, shared, scatter_dimension=0, tiled=True)]
+        expert_share = lax.psum_scatter(expert_part, shared, scatter_dimension=0, tiled=True)
         contract_rows = (((0,), (0,)), ((), ()))
+        grad_w_down = lax.dot_general(
+            cot_all, gated, contract_rows, preferred_element_type=f32
+        ).astype(bf16)
+        grad_w_down, cot_all = tie(grad_w_down, cot_all)
 
         def to_sum(grad):
             by_owner = grad.reshape(outer, inner, depth, -1)
@@ -348,6 +334,7 @@
                 for shift in range(inner)
             ]
 
+        down_sums = to_sum(grad_w_down)
         cot_part = jnp.dot(cot_all, w_down_t, preferred_element_type=f32)
         grad_act = cot_part * gate_wide
         grad_gate_up = jnp.concatenate(
@@ -366,41 +353,25 @@
         grad_normed_part = lax.dot_general(
             grad_gate_up, w_gate_up, (((1,), (1,)), ((), ())), preferred_element_type=f32
         )
-        gates_back = lax.psum_scatter(
-            gate_block.astype(bf16), shared, scatter_dimension=0, tiled=True
-        )
-        grad_normed_part, share_parts, gates_back = tie(
-            by_rows(grad_normed_part.astype(bf16)), share_parts, gates_back
-        )
-        grad_back = lax.psum_scatter(grad_normed_part, shared, scatter_dimension=0, tiled=True)
-        cot_rows, normed_rows, _ = tie(cot_all, normed_all, grad_normed_part)
-        grad_w_down = lax.dot_general(
-            cot_rows, gated, contract_rows, preferred_element_type=f32
-        ).astype(bf16)
-        grad_w_down, normed_rows = tie(grad_w_down, normed_rows)
-        down_sums = to_sum(grad_w_down)
+        grad_shipped = jnp.concatenate([grad_normed_part, gate_block], axis=1).astype(bf16)
+        grad_shipped, down_sums, expert_share = tie(by_rows(grad_shipped), down_sums, expert_share)
+        grad_back = lax.psum_scatter(grad_shipped, shared, scatter_dimension=0, tiled=True)
+        normed_rows, _ = tie(normed_all, grad_shipped)
         grad_w_gate_up = lax.dot_general(
             normed_rows, grad_gate_up, contract_rows, preferred_element_type=f32
         ).astype(bf16)
         gate_up_sums = to_sum(grad_w_gate_up)
+        gate_up_sums, down_sums, grad_back = tie(gate_up_sums, down_sums, grad_back)
         sent_down = down_sums[:1] + [to_owner(down_sums[s], s) for s in range(1, inner)]
         sent_gate_up = gate_up_sums[:1] + [to_owner(gate_up_sums[s], s) for s in range(1, inner)]
-        if n_tensor == 4:
-            expert_share = sum_line(share_parts)
-        else:
-            expert_share = share_parts[0].astype(f32)
-        sent_down, gate_up_sums, expert_share, grad_back = tie(
-            sent_down, gate_up_sums, expert_share, grad_back
-        )
-        sent_gate_up[0] = gate_up_sums[0]
-        mixed = (middle + from_owner_order(expert_share)).astype(bf16)
+        mixed = (middle + from_owner_order(expert_share).astype(f32)).astype(bf16)
 
         grad_back = grad_back.astype(f32)
-        grad_chosen = gates_back[:, :n_experts].astype(f32)
+        grad_chosen = grad_back[:, width : width + n_experts]
         grad_logits = gates * (
             grad_chosen - jnp.sum(gates * grad_chosen, axis=-1, keepdims=True)
         )
-        grad_normed_two = from_owner_order(grad_back) + jnp.dot(
+        grad_normed_two = from_owner_order(grad_back[:, :width]) + jnp.dot(
             grad_logits, router.astype(f32).T, precision=HIGHEST
         )
         grad_middle_part, normal_two = norm_backward(
@@ -411,11 +382,11 @@
         grad_router_part = lax.dot_general(
             normed_two.astype(f32), grad_logits, contract_rows, precision=HIGHEST
         )
-        grad_branch = lax.all_gather(grad_middle.astype(bf16), "t", axis=0, tiled=True)
+        grad_branch = gather_t(grad_middle.astype(bf16))
         grad_out_part = lax.dot_general(
             grad_branch, attended, contract_rows, preferred_element_type=f32
         ).astype(bf16)
-        grad_out_part, sent_gate_up[1], grad_branch = tie(
+        grad_out_part, sent_down[2], grad_branch = tie(
             jnp.concatenate(
                 [
                     grad_out_part,
@@ -424,15 +395,24 @@
                 ],
                 axis=1,
             ),
-            sent_gate_up[1],
+            sent_down[2],
             grad_branch,
         )
         shard_out = lax.psum_scatter(grad_out_part, dp, scatter_dimension=0, tiled=True)
         grad_attended = jnp.dot(
             grad_branch, w_out_t, preferred_element_type=f32
         ).astype(bf16)
-        grad_query, grad_keys, grad_values = attend_backward(
-            query, keys, values, grad_attended, log_total, prefix[0]
+        grad_query, grad_keys, grad_values, (sent_down[1], sent_down[3]) = attend_backward(
+            query,
+            keys,
+            values,
+            grad_attended,
+            log_total,
+            prefix[0],
+            (sent_down[1], sent_down[3]),
+        )
+        grad_query, grad_keys, grad_values, shard_out, sent_gate_up[2] = tie(
+            grad_query, grad_keys, grad_values, shard_out, sent_gate_up[2]
         )
         grad_qkv = jnp.concatenate(
             [
@@ -446,9 +426,7 @@
             grad_qkv, w_qkv, (((1,), (1,)), ((), ())), preferred_element_type=f32
         )
         grad_gain_one = jnp.sum(grad_normed_one * normal_all, axis=0)
-        own_grad_one = lax.psum_scatter(
-            grad_normed_one.astype(bf16), "t", scatter_dimension=0, tiled=True
-        ).astype(f32)
+        own_grad_one = scatter_t(grad_normed_one.astype(bf16))
         grad_input_part, _ = norm_backward(tokens_f, rms_scale(tokens_f), gain_one, own_grad_one)
         grad_tokens = grad_middle + grad_input_part
 
@@ -461,9 +439,6 @@
                 jnp.zeros((width, LANES - 2), bf16),
             ],
             axis=1,
-        )
-        grad_attn, own_grad_one, shard_out, sent_gate_up[2] = tie(
-            grad_attn, own_grad_one, shard_out, sent_gate_up[2]
         )
         shard_attn = lax.psum_scatter(grad_attn, dp, scatter_dimension=0, tiled=True).astype(f32)
         gain_sum = sum_tensor(shard_attn[:, qkv_cols] + shard_attn[:, qkv_cols + 1])

time: 1370 us -> 1070 us (0.78)
  waiting for transfers between devices: 585 us -> 379 us
  local copies, waits for them, and re-layouts: 237 us -> 187 us
  starting transfers between devices: 82.2 us -> 54.7 us
  other arithmetic: 111 us -> 84.3 us
    ppermute x32 -> x24, waiting for transfers between devices: 272 us -> 186 us  [swap(): return lax.ppermute(values, axis, [(m, m ^ bit) for m in range(size)])]
    unnamed x12 -> x11, waiting for transfers between devices: 85.7 us -> 42.9 us
    convert_element_type x10 -> x2, other arithmetic: 29.9 us -> 3.82 us  [the longest x1 2.53 us: on_device(): grad_back = grad_back.astype(f32)]
    ppermute x18 -> x12, starting transfers between devices: 57.1 us -> 31.8 us  [to_owner(): return jax.tree.map(lambda part: lax.ppermute(part, 'i', pairs), piece)]
    sub x0 -> x1, matrix products: none -> 24.4 us  [attend_backward(): grad_weights - jnp.sum(weights * grad_weights, axis=-1, keepdims=True)]
    all_gather x1, waiting for transfers between devices: 29.9 us -> 6.86 us  [on_device(): lax.all_gather(by_rows(shipped), shared, axis=0, tiled=True)]
    dot_general x2 -> x1, matrix products: 40.2 us -> 22.2 us  [on_device(): lax.dot_general(cot_all, gated, contract_rows, preferred_element_type=f32)]
    all_gather x1, waiting for transfers between devices: 28.1 us -> 10.3 us  [on_device(): cot_all = by_rows(lax.all_gather(cot_order, shared, axis=0, tiled=True))]
  transfers between devices with their start and end apart: 60 -> 45, of which waited for: 31 -> 21; matrix products, arithmetic and copies ran while one was open for 40% -> 53% of each run, Pallas kernels for 0% -> 0%
where the time goes in v3:
time: 1070 us; the launch traced here: 1060 us
  waiting for transfers between devices  379 us (35%)
  matrix products  340 us (32%)
  local copies, waits for them, and re-layouts  187 us (17%)
  other arithmetic  84.3 us (8%)
  starting transfers between devices  54.7 us (5%)
  between operations  16.6 us (2%)
    ppermute x24, waiting for transfers between devices, swap(): return lax.ppermute(values, axis, [(m, m ^ bit) for m in range(size)])  186 us
    ppermute x12, waiting for transfers between devices, to_owner(): return jax.tree.map(lambda part: lax.ppermute(part, 'i', pairs), piece)  131 us
    dot_general x1, matrix products, on_device(): cot_part = jnp.dot(cot_all, w_down_t, preferred_element_type=f32)  46.1 us
    dot_general x1, matrix products, on_device(): lax.dot_general(normed_rows, grad_gate_up, contract_rows, preferred_eleme...  43.5 us
    unnamed x11, waiting for transfers between devices  42.9 us
    dot_general x1, matrix products, on_device(): gate_up = jnp.dot(normed_all, w_gate_up, preferred_element_type=f32)  41.4 us
    dot_general x1, matrix products, on_device(): lax.dot_general(grad_gate_up, w_gate_up, (((1,), (1,)), ((), ())), prefer...  40.3 us
    ppermute x12, starting transfers between devices, to_owner(): return jax.tree.map(lambda part: lax.ppermute(part, 'i', pairs), piece)  31.8 us
  transfers between devices with their start and end apart: 45, of which 21 were waited for; matrix products, arithmetic and copies ran while one was open for 53% of the time, Pallas kernels for 0%

profile of v3, /device:TPU:0, one launch (start us, length us, event | category | flops | bytes accessed | tf_op | source)
XLA Modules:
  0.0 1062.6 jit_solution(15353631479113132533)
XLA Ops:
  12.4 3.1 dynamic-slice_bitcast_fusion.18
  18.7 4.1 collective-permute-start
  22.8 2.8 dynamic-slice_bitcast_fusion.17
  46.6 83.2 %collective-permute-done.5 = bf16[192,1280]{1,0:T(8,128)(2,1)} collective-permute-done((bf16[192,1280]{1,0:T(8,128)(2,1)}, bf16[192,1280]{1,0:T(8,128)(2,1)}, u32[]{:S(2)}, u32[]{:S(2)}) %collective-permute-start.5) | collective-permute-done | bytes 491552 | tf_op jit(solution)/shard_map/ppermute | solution.py:234
  132.2 5.8 fusion.28
  148.7 5.7 fusion.83
  154.5 3.8 fusion.3
  158.2 4.6 copy-done.2
  163.3 11.4 %fusion.36 = bf16[2,64,3,1024]{3,1,2,0:T(8,128)(2,1)} fusion(bf16[1024,2,64,1]{0,2,3,1:T(8,128)(2,1)S(1)} %bitcast.368, f32[2,3,1024,1024]{2,3,1,0:T(8,128)} %copy-done.2, f32[2,3,1024]{2,1,0:T(4,128)S(1)} %fusion.3, f32[2,3,1024]{2,1,0:T(4,128)S(1)} %get-tuple-element.254), kind=kOutput, calls=%fused_computation.84 | convolution fusion | flops 824573952 | bytes 26263552 | tf_op jit(solution)/shard_map/hgqk,khd->qhgd/dot_general | solution.py:65
  182.5 4.8 convolution_convert_fusion.3
  189.9 4.1 collective-permute-start.6
  194.2 11.2 %collective-permute-start.7 = (bf16[192,1280]{1,0:T(8,128)(2,1)S(1)}, bf16[192,1280]{1,0:T(8,128)(2,1)S(1)}, u32[]{:S(2)}, u32[]{:S(2)}) collective-permute-start(bf16[192,1280]{1,0:T(8,128)(2,1)S(1)} %copy.285), channel_id=1, source_target_pairs={{0,24},{8,0},{16,8},{24,16},{1,25},{9,1},{17,9},{25,17},{2,26},{10... | collective-permute-start | bytes 1474568 | tf_op jit(solution)/shard_map/ppermute | solution.py:234
  205.7 19.4 %collective-permute-done.7 = bf16[192,1280]{1,0:T(8,128)(2,1)S(1)} collective-permute-done((bf16[192,1280]{1,0:T(8,128)(2,1)S(1)}, bf16[192,1280]{1,0:T(8,128)(2,1)S(1)}, u32[]{:S(2)}, u32[]{:S(2)}) %collective-permute-start.7) | collective-permute-done | bytes 491552 | tf_op jit(solution)/shard_map/ppermute | solution.py:234
  242.9 3.9 broadcast_in_dim.114
  252.2 8.9 collective-permute-done.11
  264.8 27.9 %collective-permute-done.13 = bf16[192,1280]{1,0:T(8,128)(2,1)S(1)} collective-permute-done((bf16[192,1280]{1,0:T(8,128)(2,1)S(1)}, bf16[192,1280]{1,0:T(8,128)(2,1)S(1)}, u32[]{:S(2)}, u32[]{:S(2)}) %collective-permute-start.13) | collective-permute-done | bytes 491552 | tf_op jit(solution)/shard_map/ppermute | solution.py:95
  292.8 3.4 fusion.17
  296.2 17.5 %collective-permute-done.9 = bf16[192,2560]{1,0:T(8,128)(2,1)S(1)} collective-permute-done((bf16[192,2560]{1,0:T(8,128)(2,1)}, bf16[192,2560]{1,0:T(8,128)(2,1)S(1)}, u32[]{:S(2)}, u32[]{:S(2)}) %collective-permute-start.9) | collective-permute-done | bytes 983072 | tf_op jit(solution)/shard_map/ppermute | solution.py:95
  316.4 17.1 %collective-permute-done.10 = bf16[192,2560]{1,0:T(8,128)(2,1)S(1)} collective-permute-done((bf16[192,2560]{1,0:T(8,128)(2,1)S(1)}, bf16[192,2560]{1,0:T(8,128)(2,1)S(1)}, u32[]{:S(2)}, u32[]{:S(2)}) %collective-permute-start.10) | collective-permute-done | bytes 983072 | tf_op jit(solution)/shard_map/ppermute | solution.py:95
  335.0 6.9 all-gather.9.cloned.1.call-done
  342.0 41.4 %fusion.79 = f32[4096,2560]{0,1:T(8,128)} fusion(bf16[1536,2560]{1,0:T(8,128)(2,1)} %bitcast.61, bf16[4096,1664]{1,0:T(8,128)(2,1)} %all-gather.9.cloned.1.call-done), kind=kOutput, calls=%fused_computation.244 | convolution fusion | flops 32212254720 | bytes 62390272 | tf_op jit(solution)/shard_map/dot_general | solution.py:311
  383.4 24.8 %multiply_convert_fusion.2 = (bf16[4096,1280]{0,1:T(8,128)(2,1)S(1)}, f32[4096,1280]{0,1:T(8,128)}) fusion(f32[4096,2560]{0,1:T(8,128)} %fusion.79, s32[1280]{0:T(1024)S(1)} %get-tuple-element.263, s32[1280]{0:T(1024)S(1)} %get-tuple-element.262, bf16[4096,1664]{1,0:T(8,128)(2,1)} %all-gather.9.cloned.1.call-done), kind=kOutput, calls=%fused_computation.13 | convolution fusion | flops 1379368960 | bytes 74459136 | tf_op jit(solution)/shard_map/dot_general | solution.py:310
  408.2 3.9 copy-done.81
  412.2 20.2 %convolution_convert_fusion = bf16[4096,1536]{1,0:T(8,128)(2,1)} fusion(bf16[4096,1280]{0,1:T(8,128)(2,1)S(1)} %get-tuple-element.258, bf16[1536,1280]{1,0:T(8,128)(2,1)S(1)} %bitcast.326), kind=kOutput, calls=%fused_computation.18 | convolution fusion | flops 16112418816 | bytes 27000832 | tf_op jit(solution)/shard_map/dot_general | solution.py:317
  432.4 10.3 all-gather.11.cloned.1.call-done
  442.7 22.2 %convolution_convert_fusion.2 = bf16[1536,1280]{1,0:T(8,128)(2,1)S(1)} fusion(bf16[4096,1536]{1,0:T(8,128)(2,1)} %all-gather.11.cloned.1.call-done, bf16[4096,1280]{0,1:T(8,128)(2,1)} %copy-done.81), kind=kOutput, calls=%fused_computation.29 | convolution fusion | flops 16108093440 | bytes 27000832 | tf_op jit(solution)/shard_map/dot_general | solution.py:323
  470.3 46.1 %multiply_convert_fusion.1 = (bf16[4096,1280]{0,1:T(8,128)(2,1)}, bf16[4096,1280]{0,1:T(8,128)(2,1)}, f32[4096,1280]{0,1:T(8,128)}) fusion(f32[4096,2560]{0,1:T(8,128)} %fusion.79, f32[4096,1280]{0,1:T(8,128)} %get-tuple-element.259, bf16[4096,1536]{1,0:T(8,128)(2,1)} %all-gather.11.cloned.1.call-done, bf16[1536,1280]{1,0:T(8,128)(2,1)S(1)} %bitcast.327), kind=kOutput, calls=%fused_computation.12 | convolution fusion | flops 16190013440 | bytes 121372672 | tf_op jit(solution)/shard_map/dot_general | solution.py:338
  516.4 8.1 reduce_sum.123
  525.1 3.9 dynamic_update_slice.83
  529.0 40.3 %convolution_convert_fusion.1 = bf16[4096,1536]{1,0:T(8,128)(2,1)} fusion(bf16[1536,2560]{1,0:T(8,128)(2,1)} %bitcast.61, bf16[4096,1280]{0,1:T(8,128)(2,1)} %get-tuple-element.199, bf16[4096,1280]{0,1:T(8,128)(2,1)} %get-tuple-element.198), kind=kOutput, calls=%fused_computation.19 | convolution fusion | flops 32260489216 | bytes 41418752 | tf_op jit(solution)/shard_map/dot_general | solution.py:353
  569.3 12.1 %pad_maximum_fusion.1 = bf16[4096,1664]{1,0:T(8,128)(2,1)} fusion(bf16[4096,128]{1,0:T(8,128)(2,1)S(1)} %dynamic_update_slice.83, bf16[4096,1536]{1,0:T(8,128)(2,1)} %convolution_convert_fusion.1), kind=kLoop, calls=%fused_computation.20 | loop fusion | flops 27262976 | bytes 27262976 | tf_op jit(solution)/shard_map/concatenate | solution.py:356
  581.5 3.4 fusion.50
  585.0 11.0 %slice.204 = bf16[4096,1536]{1,0:T(8,128)(2,1)} slice(bf16[4096,1664]{1,0:T(8,128)(2,1)} %all-gather.9.cloned.1.call-done), slice={[0:4096], [0:1536]} | slice | bytes 25165824 | tf_op jit(solution)/shard_map/slice | solution.py:305
  596.0 43.5 %fusion.11 = bf16[1536,2560]{1,0:T(8,128)(2,1)S(1)} fusion(bf16[4096,1536]{1,0:T(8,128)(2,1)} %slice.204, bf16[4096,1280]{0,1:T(8,128)(2,1)} %get-tuple-element.199, bf16[4096,1280]{0,1:T(8,128)(2,1)} %get-tuple-element.198), kind=kOutput, calls=%fused_computation.25 | convolution fusion | flops 32258129920 | bytes 41418752 | tf_op jit(solution)/shard_map/dot_general | solution.py:360
  643.9 20.6 %collective-permute-done.18 = bf16[192,2560]{1,0:T(8,128)(2,1)S(1)} collective-permute-done((bf16[192,2560]{1,0:T(8,128)(2,1)S(1)}, bf16[192,2560]{1,0:T(8,128)(2,1)S(1)}, u32[]{:S(2)}, u32[]{:S(2)}) %collective-permute-start.18) | collective-permute-done | bytes 983072 | tf_op jit(solution)/shard_map/ppermute | solution.py:95
  664.4 21.1 %collective-permute-done.19 = bf16[192,2560]{1,0:T(8,128)(2,1)S(1)} collective-permute-done((bf16[192,2560]{1,0:T(8,128)(2,1)S(1)}, bf16[192,2560]{1,0:T(8,128)(2,1)S(1)}, u32[]{:S(2)}, u32[]{:S(2)}) %collective-permute-start.19) | collective-permute-done | bytes 983072 | tf_op jit(solution)/shard_map/ppermute | solution.py:95
  685.5 21.1 %collective-permute-done.20 = bf16[192,2560]{1,0:T(8,128)(2,1)S(1)} collective-permute-done((bf16[192,2560]{1,0:T(8,128)(2,1)S(1)}, bf16[192,2560]{1,0:T(8,128)(2,1)S(1)}, u32[]{:S(2)}, u32[]{:S(2)}) %collective-permute-start.20) | collective-permute-done | bytes 983072 | tf_op jit(solution)/shard_map/ppermute | solution.py:95
  706.6 19.9 %collective-permute-done.21 = bf16[192,2560]{1,0:T(8,128)(2,1)S(1)} collective-permute-done((bf16[192,2560]{1,0:T(8,128)(2,1)S(1)}, bf16[192,2560]{1,0:T(8,128)(2,1)S(1)}, u32[]{:S(2)}, u32[]{:S(2)}) %collective-permute-start.21) | collective-permute-done | bytes 983072 | tf_op jit(solution)/shard_map/ppermute | solution.py:95
  734.0 3.0 copy.306
  738.1 3.2 multiply_reduce_fusion.3
  745.5 17.0 %collective-permute-done.22 = bf16[256,1536]{1,0:T(8,128)(2,1)S(1)} collective-permute-done((bf16[256,1536]{1,0:T(8,128)(2,1)S(1)}, bf16[256,1536]{1,0:T(8,128)(2,1)S(1)}, u32[]{:S(2)}, u32[]{:S(2)}) %collective-permute-start.22) | collective-permute-done | bytes 786464 | tf_op jit(solution)/shard_map/ppermute | solution.py:95
  767.6 3.1 copy.302
  770.7 4.6 collective-permute-start.24
  775.6 3.6 collective-permute-start.26
  790.2 3.4 convolution_convert_fusion.5
  795.2 13.6 %collective-permute-done.24 = bf16[192,1280]{1,0:T(8,128)(2,1)} collective-permute-done((bf16[192,1280]{1,0:T(8,128)(2,1)}, bf16[192,1280]{1,0:T(8,128)(2,1)}, u32[]{:S(2)}, u32[]{:S(2)}) %collective-permute-start.24) | collective-permute-done | bytes 491552 | tf_op jit(solution)/shard_map/ppermute | solution.py:234
  811.6 2.9 copy.345
  814.6 24.4 %fusion.2 = bf16[2,3,1024,1024]{2,3,1,0:T(8,128)(2,1)} fusion(f32[2,3,1024,1024]{2,3,1,0:T(8,128)} %copy-done.2, f32[2,3,1024]{2,1,0:T(4,128)S(1)} %log_add_fusion, bf16[1024,2,64,1]{0,2,3,1:T(8,128)(2,1)S(1)} %bitcast.369, bf16[1024,2,3,64]{0,3,2,1:T(8,128)(2,1)S(1)} %bitcast.358), kind=kOutput, calls=%fused_computation.4 | convolution fusion | flops 1648368640 | bytes 38821888 | tf_op jit(solution)/shard_map/sub | solution.py:78
  839.0 9.6 fusion.42
  848.6 4.4 convolution_multiply_fusion
  853.0 13.1 %fusion.38 = bf16[1024,2,64]{0,2,1:T(8,128)(2,1)} fusion(bf16[1024,2,3,64]{0,3,2,1:T(8,128)(2,1)} %bitcast.359, f32[2,3,1024,1024]{2,3,1,0:T(8,128)} %copy-done.2, f32[2,3,1024]{2,1,0:T(4,128)S(1)} %log_add_fusion), kind=kOutput, calls=%fused_computation.101 | convolution fusion | flops 817889280 | bytes 26238976 | tf_op jit(solution)/shard_map/hgqk,qhgd->khd/dot_general | solution.py:88
  866.1 42.1 %reduce-scatter.16.cloned.1.call-done = bf16[192,512]{1,0:T(8,128)(2,1)} async-done(((bf16[1536,512]{1,0:T(8,128)(2,1)}), bf16[192,512]{1,0:T(8,128)(2,1)}) %reduce-scatter.16.cloned.1.call-update) | async-done | bytes 196624
  911.3 5.3 convolution_convert_fusion.4
  916.6 4.7 multiply_reduce_fusion
  923.2 4.3 copy.347
  927.5 3.0 slice_bitcast_fusion.3
  952.0 2.8 copy.313
  954.8 2.8 dynamic-slice_bitcast_fusion
  961.6 14.3 %collective-permute-done.35 = bf16[192,2560]{1,0:T(8,128)(2,1)} collective-permute-done((bf16[192,2560]{1,0:T(8,128)(2,1)}, bf16[192,2560]{1,0:T(8,128)(2,1)}, u32[]{:S(2)}, u32[]{:S(2)}) %collective-permute-start.35) | collective-permute-done | bytes 983072 | tf_op jit(solution)/shard_map/ppermute | solution.py:234
  978.7 3.6 slice_bitcast_fusion
  986.4 2.8 copy.318
  1009.5 3.1 slice_bitcast_fusion.1
  1027.3 14.0 %collective-permute-done.33 = f32[192,41]{0,1:T(8,128)S(1)} collective-permute-done((f32[192,41]{0,1:T(8,128)S(1)}, f32[192,41]{0,1:T(8,128)S(1)}, u32[]{:S(2)}, u32[]{:S(2)}) %collective-permute-start.33) | collective-permute-done | bytes 31520 | tf_op jit(solution)/shard_map/ppermute | solution.py:95
  1046.0 5.1 fusion.33
  (421 shorter events, 208.7 us)
Async XLA Ops:
  7.2 198.3 %copy-start = (s32[1024,8]{0,1:T(8,128)S(1)}, s32[1024,8]{0,1:T(8,128)}, u32[]{:S(2)}) copy-start(s32[1024,8]{0,1:T(8,128)} %param.17) | copy-start | bytes 98308
  7.2 36.6 %all-gather.7.cloned.1.call-start = ((), (), s32[]{:S(2)}) async-start(), calls=%async_computation.6 | async-start | bytes 3932160 | tf_op jit(solution)/shard_map/all_gather | solution.py:217
  7.9 122.4 %all-gather.5.cloned.1.call-start = ((), (), s32[]{:S(2)}) async-start(), calls=%async_computation.5 | async-start | bytes 3981312 | tf_op jit(solution)/shard_map/all_gather | solution.py:218
  12.3 214.8 %reduce-scatter.10.cloned.1.call-start = ((), (), s32[]{:S(2)}) async-start(), calls=%async_computation.7 | async-start | bytes 3932160 | tf_op jit(solution)/shard_map/reduce_scatter | solution.py:267
  18.7 111.6 %collective-permute-start = (bf16[192,2560]{1,0:T(8,128)(2,1)}, bf16[192,2560]{1,0:T(8,128)(2,1)}, u32[]{:S(2)}, u32[]{:S(2)}) collective-permute-start(bf16[192,2560]{1,0:T(8,128)(2,1)} %copy.271), channel_id=1, source_target_pairs={{0,16},{8,24},{16,0},{24,8},{1,17},{9,25},{17,1},{25,9},{2,18},{10... | collective-permute-start | bytes 2949128 | tf_op jit(solution)/shard_map/ppermute | solution.py:234
  27.9 101.8 %collective-permute-start.5 = (bf16[192,1280]{1,0:T(8,128)(2,1)}, bf16[192,1280]{1,0:T(8,128)(2,1)}, u32[]{:S(2)}, u32[]{:S(2)}) collective-permute-start(bf16[192,1280]{1,0:T(8,128)(2,1)} %copy.282), channel_id=1, source_target_pairs={{0,16},{8,24},{16,0},{24,8},{1,17},{9,25},{17,1},{25,9},{2,18},{10... | collective-permute-start | bytes 1474568 | tf_op jit(solution)/shard_map/ppermute | solution.py:234
  34.0 106.9 %copy-start.10 = (bf16[192,2560]{0,1:T(8,128)(2,1)}, bf16[192,2560]{0,1:T(8,128)(2,1)S(1)}, u32[]{:S(2)}) copy-start(bf16[192,2560]{0,1:T(8,128)(2,1)S(1)} %pad_maximum_fusion.8) | copy-start | bytes 2949124
  35.3 104.9 %copy-start.39 = (f32[1024,32]{0,1:T(8,128)}, f32[1024,32]{0,1:T(8,128)S(1)}, u32[]{:S(2)}) copy-start(f32[1024,32]{0,1:T(8,128)S(1)} %get-tuple-element.253) | copy-start | bytes 393220
  42.0 101.8 %copy-start.21 = (bf16[192,10,128]{0,2,1:T(8,128)(2,1)}, bf16[192,10,128]{0,2,1:T(8,128)(2,1)S(1)}, u32[]{:S(2)}) copy-start(bf16[192,10,128]{0,2,1:T(8,128)(2,1)S(1)} %copy.262) | copy-start | bytes 1474564
  46.6 83.2 %copy-start.6 = (f32[1024,1536]{1,0:T(8,128)}, f32[1024,1536]{1,0:T(8,128)S(1)}, u32[]{:S(2)}) copy-start(f32[1024,1536]{1,0:T(8,128)S(1)} %convert_element_type.431) | copy-start | bytes 18874372
  132.2 96.4 %copy-start.66 = (f32[1536]{0:T(1024)}, f32[1536]{0:T(1024)S(1)}, u32[]{:S(2)}) copy-start(f32[1536]{0:T(1024)S(1)} %get-tuple-element.191) | copy-start | bytes 18436
  142.3 36.3 %collective-permute-start.3 = (bf16[192,2560]{1,0:T(8,128)(2,1)}, bf16[192,2560]{1,0:T(8,128)(2,1)}, u32[]{:S(2)}, u32[]{:S(2)}) collective-permute-start(bf16[192,2560]{1,0:T(8,128)(2,1)} %copy.277), channel_id=1, source_target_pairs={{0,4},{4,0},{1,5},{5,1},{2,6},{6,2},{3,7},{7,3},{8,12},{12,8},{9,1... | collective-permute-start | bytes 2949128 | tf_op jit(solution)/shard_map/ppermute | solution.py:95
  144.8 31.1 %collective-permute-start.4 = (bf16[192,1280]{1,0:T(8,128)(2,1)}, bf16[192,1280]{1,0:T(8,128)(2,1)}, u32[]{:S(2)}, u32[]{:S(2)}) collective-permute-start(bf16[192,1280]{1,0:T(8,128)(2,1)} %copy.279), channel_id=1, source_target_pairs={{0,4},{4,0},{1,5},{5,1},{2,6},{6,2},{3,7},{7,3},{8,12},{12,8},{9,1... | collective-permute-start | bytes 1474568 | tf_op jit(solution)/shard_map/ppermute | solution.py:95
  146.7 35.8 %collective-permute-start.1 = (bf16[192,2560]{1,0:T(8,128)(2,1)}, bf16[192,2560]{1,0:T(8,128)(2,1)}, u32[]{:S(2)}, u32[]{:S(2)}) collective-permute-start(bf16[192,2560]{1,0:T(8,128)(2,1)} %copy.275), channel_id=1, source_target_pairs={{0,8},{8,16},{16,24},{24,0},{1,9},{9,17},{17,25},{25,1},{2,10},{10... | collective-permute-start | bytes 2949128 | tf_op jit(solution)/shard_map/ppermute | solution.py:234
  148.4 34.0 %collective-permute-start.2 = (bf16[192,1280]{1,0:T(8,128)(2,1)}, bf16[192,1280]{1,0:T(8,128)(2,1)}, u32[]{:S(2)}, u32[]{:S(2)}) collective-permute-start(bf16[192,1280]{1,0:T(8,128)(2,1)} %copy.276), channel_id=1, source_target_pairs={{0,8},{8,16},{16,24},{24,0},{1,9},{9,17},{17,25},{25,1},{2,10},{10... | collective-permute-start | bytes 1474568 | tf_op jit(solution)/shard_map/ppermute | solution.py:234
  187.3 39.8 %copy-start.4 = (bf16[256,1536]{1,0:T(8,128)(2,1)S(1)}, bf16[256,1536]{1,0:T(8,128)(2,1)}, u32[]{:S(2)}) copy-start(bf16[256,1536]{1,0:T(8,128)(2,1)} %param.14) | copy-start | bytes 2359300
  187.3 154.6 %all-gather.9.cloned.1.call-start = ((), (), s32[]{:S(2)}) async-start(), calls=%async_computation.8 | async-start | bytes 14483456 | tf_op jit(solution)/shard_map/all_gather | solution.py:290
  189.9 35.2 %collective-permute-start.6 = (bf16[192,2560]{1,0:T(8,128)(2,1)}, bf16[192,2560]{1,0:T(8,128)(2,1)S(1)}, u32[]{:S(2)}, u32[]{:S(2)}) collective-permute-start(bf16[192,2560]{1,0:T(8,128)(2,1)} %copy.284), channel_id=1, source_target_pairs={{0,24},{8,0},{16,8},{24,16},{1,25},{9,1},{17,9},{25,17},{2,26},{10... | collective-permute-start | bytes 2949128 | tf_op jit(solution)/shard_map/ppermute | solution.py:234
  194.2 30.9 %collective-permute-start.7 = (bf16[192,1280]{1,0:T(8,128)(2,1)S(1)}, bf16[192,1280]{1,0:T(8,128)(2,1)S(1)}, u32[]{:S(2)}, u32[]{:S(2)}) collective-permute-start(bf16[192,1280]{1,0:T(8,128)(2,1)S(1)} %copy.285), channel_id=1, source_target_pairs={{0,24},{8,0},{16,8},{24,16},{1,25},{9,1},{17,9},{25,17},{2,26},{10... | collective-permute-start | bytes 1474568 | tf_op jit(solution)/shard_map/ppermute | solution.py:234
  234.4 208.2 %all-gather.11.cloned.1.call-start = ((), (), s32[]{:S(2)}) async-start(), calls=%async_computation.9 | async-start | bytes 13369344 | tf_op jit(solution)/shard_map/all_gather | solution.py:303
  236.2 27.4 %collective-permute-start.12 = (bf16[192,1280]{1,0:T(8,128)(2,1)}, bf16[192,1280]{1,0:T(8,128)(2,1)S(1)}, u32[]{:S(2)}, u32[]{:S(2)}) collective-permute-start(bf16[192,1280]{1,0:T(8,128)(2,1)} %collective-permute-done.5), channel_id=1, source_target_pairs={{0,4},{4,0},{1,5},{5,1},{2,6},{6,2},{3,7},{7,3},{8,12},{12,8},{9,1... | collective-permute-start | bytes 1474568 | tf_op jit(solution)/shard_map/ppermute | solution.py:95
  242.4 18.6 %collective-permute-start.11 = (bf16[192,1280]{1,0:T(8,128)(2,1)}, bf16[192,1280]{1,0:T(8,128)(2,1)S(1)}, u32[]{:S(2)}, u32[]{:S(2)}) collective-permute-start(bf16[192,1280]{1,0:T(8,128)(2,1)} %collective-permute-done.2), channel_id=1, source_target_pairs={{0,4},{4,0},{1,5},{5,1},{2,6},{6,2},{3,7},{7,3},{8,12},{12,8},{9,1... | collective-permute-start | bytes 1474568 | tf_op jit(solution)/shard_map/ppermute | solution.py:95
  248.2 44.6 %collective-permute-start.8 = (bf16[192,2560]{1,0:T(8,128)(2,1)}, bf16[192,2560]{1,0:T(8,128)(2,1)S(1)}, u32[]{:S(2)}, u32[]{:S(2)}) collective-permute-start(bf16[192,2560]{1,0:T(8,128)(2,1)} %collective-permute-done.1), channel_id=1, source_target_pairs={{0,4},{4,0},{1,5},{5,1},{2,6},{6,2},{3,7},{7,3},{8,12},{12,8},{9,1... | collective-permute-start | bytes 2949128 | tf_op jit(solution)/shard_map/ppermute | solution.py:95
  250.1 42.6 %collective-permute-start.13 = (bf16[192,1280]{1,0:T(8,128)(2,1)S(1)}, bf16[192,1280]{1,0:T(8,128)(2,1)S(1)}, u32[]{:S(2)}, u32[]{:S(2)}) collective-permute-start(bf16[192,1280]{1,0:T(8,128)(2,1)S(1)} %copy-done.62), channel_id=1, source_target_pairs={{0,4},{4,0},{1,5},{5,1},{2,6},{6,2},{3,7},{7,3},{8,12},{12,8},{9,1... | collective-permute-start | bytes 1474568 | tf_op jit(solution)/shard_map/ppermute | solution.py:95
  250.8 62.9 %collective-permute-start.9 = (bf16[192,2560]{1,0:T(8,128)(2,1)}, bf16[192,2560]{1,0:T(8,128)(2,1)S(1)}, u32[]{:S(2)}, u32[]{:S(2)}) collective-permute-start(bf16[192,2560]{1,0:T(8,128)(2,1)} %collective-permute-done), channel_id=1, source_target_pairs={{0,4},{4,0},{1,5},{5,1},{2,6},{6,2},{3,7},{7,3},{8,12},{12,8},{9,1... | collective-permute-start | bytes 2949128 | tf_op jit(solution)/shard_map/ppermute | solution.py:95
  261.0 72.5 %collective-permute-start.10 = (bf16[192,2560]{1,0:T(8,128)(2,1)S(1)}, bf16[192,2560]{1,0:T(8,128)(2,1)S(1)}, u32[]{:S(2)}, u32[]{:S(2)}) collective-permute-start(bf16[192,2560]{1,0:T(8,128)(2,1)S(1)} %copy-done.58), channel_id=1, source_target_pairs={{0,4},{4,0},{1,5},{5,1},{2,6},{6,2},{3,7},{7,3},{8,12},{12,8},{9,1... | collective-permute-start | bytes 2949128 | tf_op jit(solution)/shard_map/ppermute | solution.py:95
  292.8 23.6 %copy-start.25 = (bf16[2,4,192,1280]{3,2,1,0:T(8,128)(2,1)}, bf16[2,4,192,1280]{3,2,1,0:T(8,128)(2,1)S(1)}, u32[]{:S(2)}) copy-start(bf16[2,4,192,1280]{3,2,1,0:T(8,128)(2,1)S(1)} %fusion.49) | copy-start | bytes 11796484
  341.9 243.0 %reduce-scatter.12.cloned.1.call-start = ((), (), s32[]{:S(2)}) async-start(), calls=%async_computation.10 | async-start | bytes 13369344 | tf_op jit(solution)/shard_map/reduce_scatter | solution.py:321
  383.4 28.8 %copy-start.26 = (bf16[2,4,192,1280]{3,2,1,0:T(8,128)(2,1)S(1)}, bf16[2,4,192,1280]{3,2,1,0:T(8,128)(2,1)}, u32[]{:S(2)}) copy-start(bf16[2,4,192,1280]{3,2,1,0:T(8,128)(2,1)} %copy-done.25) | copy-start | bytes 11796484
  442.6 286.7 %reduce-scatter.14.cloned.1.call-start = ((), (), s32[]{:S(2)}) async-start(), calls=%async_computation.11 | async-start | bytes 14483456 | tf_op jit(solution)/shard_map/reduce_scatter | solution.py:358
  464.9 51.5 %copy-start.38 = (bf16[1536,1280]{1,0:T(8,128)(2,1)}, bf16[1536,1280]{1,0:T(8,128)(2,1)S(1)}, u32[]{:S(2)}) copy-start(bf16[1536,1280]{1,0:T(8,128)(2,1)S(1)} %convolution_convert_fusion.2) | copy-start | bytes 11796484
  466.2 115.2 %collective-permute-start.14 = (bf16[192,1280]{1,0:T(8,128)(2,1)}, bf16[192,1280]{1,0:T(8,128)(2,1)S(1)}, u32[]{:S(2)}, u32[]{:S(2)}) collective-permute-start(bf16[192,1280]{1,0:T(8,128)(2,1)} %get-tuple-element.218), channel_id=1, source_target_pairs={{0,4},{4,0},{1,5},{5,1},{2,6},{6,2},{3,7},{7,3},{8,12},{12,8},{9,1... | collective-permute-start | bytes 1474568 | tf_op jit(solution)/shard_map/ppermute | solution.py:95
  467.7 113.8 %collective-permute-start.15 = (bf16[192,1280]{1,0:T(8,128)(2,1)}, bf16[192,1280]{1,0:T(8,128)(2,1)S(1)}, u32[]{:S(2)}, u32[]{:S(2)}) collective-permute-start(bf16[192,1280]{1,0:T(8,128)(2,1)} %get-tuple-element.217), channel_id=1, source_target_pairs={{0,4},{4,0},{1,5},{5,1},{2,6},{6,2},{3,7},{7,3},{8,12},{12,8},{9,1... | collective-permute-start | bytes 1474568 | tf_op jit(solution)/shard_map/ppermute | solution.py:95
  468.3 113.2 %collective-permute-start.16 = (bf16[192,1280]{1,0:T(8,128)(2,1)}, bf16[192,1280]{1,0:T(8,128)(2,1)}, u32[]{:S(2)}, u32[]{:S(2)}) collective-permute-start(bf16[192,1280]{1,0:T(8,128)(2,1)} %get-tuple-element.216), channel_id=1, source_target_pairs={{0,4},{4,0},{1,5},{5,1},{2,6},{6,2},{3,7},{7,3},{8,12},{12,8},{9,1... | collective-permute-start | bytes 1474568 | tf_op jit(solution)/shard_map/ppermute | solution.py:95
  469.7 111.7 %collective-permute-start.17 = (bf16[192,1280]{1,0:T(8,128)(2,1)}, bf16[192,1280]{1,0:T(8,128)(2,1)}, u32[]{:S(2)}, u32[]{:S(2)}) collective-permute-start(bf16[192,1280]{1,0:T(8,128)(2,1)} %get-tuple-element.215), channel_id=1, source_target_pairs={{0,4},{4,0},{1,5},{5,1},{2,6},{6,2},{3,7},{7,3},{8,12},{12,8},{9,1... | collective-permute-start | bytes 1474568 | tf_op jit(solution)/shard_map/ppermute | solution.py:95
  584.9 323.3 %reduce-scatter.16.cloned.1.call-start = ((), (), s32[]{:S(2)}) async-start(), calls=%async_computation.12 | async-start | bytes 1769472
  639.7 24.7 %collective-permute-start.18 = (bf16[192,2560]{1,0:T(8,128)(2,1)S(1)}, bf16[192,2560]{1,0:T(8,128)(2,1)S(1)}, u32[]{:S(2)}, u32[]{:S(2)}) collective-permute-start(bf16[192,2560]{1,0:T(8,128)(2,1)S(1)} %get-tuple-element.208), channel_id=1, source_target_pairs={{0,4},{4,0},{1,5},{5,1},{2,6},{6,2},{3,7},{7,3},{8,12},{12,8},{9,1... | collective-permute-start | bytes 2949128 | tf_op jit(solution)/shard_map/ppermute | solution.py:95
  641.3 44.2 %collective-permute-start.19 = (bf16[192,2560]{1,0:T(8,128)(2,1)S(1)}, bf16[192,2560]{1,0:T(8,128)(2,1)S(1)}, u32[]{:S(2)}, u32[]{:S(2)}) collective-permute-start(bf16[192,2560]{1,0:T(8,128)(2,1)S(1)} %get-tuple-element.207), channel_id=1, source_target_pairs={{0,4},{4,0},{1,5},{5,1},{2,6},{6,2},{3,7},{7,3},{8,12},{12,8},{9,1... | collective-permute-start | bytes 2949128 | tf_op jit(solution)/shard_map/ppermute | solution.py:95
  641.8 64.7 %collective-permute-start.20 = (bf16[192,2560]{1,0:T(8,128)(2,1)S(1)}, bf16[192,2560]{1,0:T(8,128)(2,1)S(1)}, u32[]{:S(2)}, u32[]{:S(2)}) collective-permute-start(bf16[192,2560]{1,0:T(8,128)(2,1)S(1)} %get-tuple-element.206), channel_id=1, source_target_pairs={{0,4},{4,0},{1,5},{5,1},{2,6},{6,2},{3,7},{7,3},{8,12},{12,8},{9,1... | collective-permute-start | bytes 2949128 | tf_op jit(solution)/shard_map/ppermute | solution.py:95
  643.3 83.2 %collective-permute-start.21 = (bf16[192,2560]{1,0:T(8,128)(2,1)S(1)}, bf16[192,2560]{1,0:T(8,128)(2,1)S(1)}, u32[]{:S(2)}, u32[]{:S(2)}) collective-permute-start(bf16[192,2560]{1,0:T(8,128)(2,1)S(1)} %get-tuple-element.205), channel_id=1, source_target_pairs={{0,4},{4,0},{1,5},{5,1},{2,6},{6,2},{3,7},{7,3},{8,12},{12,8},{9,1... | collective-permute-start | bytes 2949128 | tf_op jit(solution)/shard_map/ppermute | solution.py:95
  741.5 23.3 %copy-start.70 = (f32[2,3,1024]{2,1,0:T(4,128)S(1)}, f32[2,3,1024]{2,1,0:T(4,128)}, u32[]{:S(2)}) copy-start(f32[2,3,1024]{2,1,0:T(4,128)} %copy-done.69) | copy-start | bytes 73732
  741.5 23.3 %copy-start.72 = (f32[2,3,1024]{2,1,0:T(4,128)S(1)}, f32[2,3,1024]{2,1,0:T(4,128)}, u32[]{:S(2)}) copy-start(f32[2,3,1024]{2,1,0:T(4,128)} %copy-done.71) | copy-start | bytes 73732
  744.1 18.4 %collective-permute-start.22 = (bf16[256,1536]{1,0:T(8,128)(2,1)S(1)}, bf16[256,1536]{1,0:T(8,128)(2,1)S(1)}, u32[]{:S(2)}, u32[]{:S(2)}) collective-permute-start(bf16[256,1536]{1,0:T(8,128)(2,1)S(1)} %get-tuple-element.194), channel_id=1, source_target_pairs={{0,2},{1,3},{2,0},{3,1},{4,6},{5,7},{6,4},{7,5},{8,10},{9,11},{10,... | collective-permute-start | bytes 2359304 | tf_op jit(solution)/shard_map/ppermute | solution.py:95
  764.6 21.0 %collective-permute-start.23 = (bf16[512,1536]{1,0:T(8,128)(2,1)}, bf16[512,1536]{1,0:T(8,128)(2,1)}, u32[]{:S(2)}, u32[]{:S(2)}) collective-permute-start(bf16[512,1536]{1,0:T(8,128)(2,1)} %pad_maximum_fusion.7), channel_id=1, source_target_pairs={{0,1},{1,0},{2,3},{3,2},{4,5},{5,4},{6,7},{7,6},{8,9},{9,8},{10,11... | collective-permute-start | bytes 4718600 | tf_op jit(solution)/shard_map/ppermute | solution.py:95
  770.7 38.1 %collective-permute-start.24 = (bf16[192,1280]{1,0:T(8,128)(2,1)}, bf16[192,1280]{1,0:T(8,128)(2,1)}, u32[]{:S(2)}, u32[]{:S(2)}) collective-permute-start(bf16[192,1280]{1,0:T(8,128)(2,1)} %get-tuple-element.109), channel_id=1, source_target_pairs={{0,16},{8,24},{16,0},{24,8},{1,17},{9,25},{17,1},{25,9},{2,18},{10... | collective-permute-start | bytes 1474568 | tf_op jit(solution)/shard_map/ppermute | solution.py:234
  775.3 63.7 %collective-permute-start.25 = (bf16[192,1280]{1,0:T(8,128)(2,1)}, bf16[192,1280]{1,0:T(8,128)(2,1)}, u32[]{:S(2)}, u32[]{:S(2)}) collective-permute-start(bf16[192,1280]{1,0:T(8,128)(2,1)} %get-tuple-element.111), channel_id=1, source_target_pairs={{0,8},{8,16},{16,24},{24,0},{1,9},{9,17},{17,25},{25,1},{2,10},{10... | collective-permute-start | bytes 1474568 | tf_op jit(solution)/shard_map/ppermute | solution.py:234
  775.6 63.5 %collective-permute-start.26 = (bf16[192,1280]{1,0:T(8,128)(2,1)}, bf16[192,1280]{1,0:T(8,128)(2,1)}, u32[]{:S(2)}, u32[]{:S(2)}) collective-permute-start(bf16[192,1280]{1,0:T(8,128)(2,1)} %get-tuple-element.112), channel_id=1, source_target_pairs={{0,24},{8,0},{16,8},{24,16},{1,25},{9,1},{17,9},{25,17},{2,26},{10... | collective-permute-start | bytes 1474568 | tf_op jit(solution)/shard_map/ppermute | solution.py:234
  781.9 170.1 %collective-permute-start.34 = (bf16[192,2560]{1,0:T(8,128)(2,1)}, bf16[192,2560]{1,0:T(8,128)(2,1)}, u32[]{:S(2)}, u32[]{:S(2)}) collective-permute-start(bf16[192,2560]{1,0:T(8,128)(2,1)} %get-tuple-element.121), channel_id=1, source_target_pairs={{0,8},{8,16},{16,24},{24,0},{1,9},{9,17},{17,25},{25,1},{2,10},{10... | collective-permute-start | bytes 2949128 | tf_op jit(solution)/shard_map/ppermute | solution.py:234
  785.6 123.7 %collective-permute-start.27 = (bf16[192,2560]{1,0:T(8,128)(2,1)}, bf16[192,2560]{1,0:T(8,128)(2,1)}, u32[]{:S(2)}, u32[]{:S(2)}) collective-permute-start(bf16[192,2560]{1,0:T(8,128)(2,1)} %get-tuple-element.115), channel_id=1, source_target_pairs={{0,16},{8,24},{16,0},{24,8},{1,17},{9,25},{17,1},{25,9},{2,18},{10... | collective-permute-start | bytes 2949128 | tf_op jit(solution)/shard_map/ppermute | solution.py:234
  814.5 230.2 %reduce-scatter.18.cloned.1.call-start = ((), (), s32[]{:S(2)}) async-start(), calls=%async_computation.13 | async-start | bytes 2654208
  814.5 24.5 %copy-start.54 = (bf16[1024,6,32]{0,2,1:T(8,128)(2,1)S(1)}, bf16[1024,6,32]{0,2,1:T(8,128)(2,1)}, u32[]{:S(2)}) copy-start(bf16[1024,6,32]{0,2,1:T(8,128)(2,1)} %get-tuple-element.241) | copy-start | bytes 1179652
  853.0 56.3 %copy-start.40 = (f32[1024,32]{0,1:T(8,128)S(1)}, f32[1024,32]{0,1:T(8,128)}, u32[]{:S(2)}) copy-start(f32[1024,32]{0,1:T(8,128)} %copy-done.39) | copy-start | bytes 393220
  853.0 56.3 %copy-start.55 = (f32[1024,32]{0,1:T(8,128)S(1)}, f32[1024,32]{0,1:T(8,128)}, u32[]{:S(2)}) copy-start(f32[1024,32]{0,1:T(8,128)} %get-tuple-element.251) | copy-start | bytes 393220
  866.1 45.0 %copy-start.24 = (f32[1024,2,64]{0,2,1:T(8,128)S(1)}, f32[1024,2,64]{0,2,1:T(8,128)}, u32[]{:S(2)}) copy-start(f32[1024,2,64]{0,2,1:T(8,128)} %fusion.42) | copy-start | bytes 1572868
  866.1 45.1 %copy-start.74 = (f32[1536]{0:T(1024)S(1)}, f32[1536]{0:T(1024)}, u32[]{:S(2)}) copy-start(f32[1536]{0:T(1024)} %copy-done.73) | copy-start | bytes 18436
  866.1 45.1 %copy-start.78 = (f32[1024]{0:T(1024)S(1)}, f32[1024]{0:T(1024)}, u32[]{:S(2)}) copy-start(f32[1024]{0:T(1024)} %copy-done.77) | copy-start | bytes 12292
  938.4 37.6 %collective-permute-start.35 = (bf16[192,2560]{1,0:T(8,128)(2,1)}, bf16[192,2560]{1,0:T(8,128)(2,1)}, u32[]{:S(2)}, u32[]{:S(2)}) collective-permute-start(bf16[192,2560]{1,0:T(8,128)(2,1)} %get-tuple-element.123), channel_id=1, source_target_pairs={{0,24},{8,0},{16,8},{24,16},{1,25},{9,1},{17,9},{25,17},{2,26},{10... | collective-permute-start | bytes 2949128 | tf_op jit(solution)/shard_map/ppermute | solution.py:234
  957.6 59.2 %collective-permute-start.28 = (bf16[2,256,1536]{2,1,0:T(8,128)(2,1)}, bf16[2,256,1536]{2,1,0:T(8,128)(2,1)}, u32[]{:S(2)}, u32[]{:S(2)}) collective-permute-start(bf16[2,256,1536]{2,1,0:T(8,128)(2,1)} %dynamic-slice_bitcast_fusion), channel_id=1, source_target_pairs={{0,1},{1,0},{2,3},{3,2},{4,5},{5,4},{6,7},{7,6},{8,9},{9,8},{10,11... | collective-permute-start | bytes 4718600 | tf_op jit(solution)/shard_map/ppermute | solution.py:95
  1016.7 8.2 collective-permute-start.32
  1020.2 22.3 %collective-permute-start.29 = (bf16[256,1536]{1,0:T(8,128)(2,1)}, bf16[256,1536]{1,0:T(8,128)(2,1)}, u32[]{:S(2)}, u32[]{:S(2)}) collective-permute-start(bf16[256,1536]{1,0:T(8,128)(2,1)} %fusion.55), channel_id=1, source_target_pairs={{0,2},{1,3},{2,0},{3,1},{4,6},{5,7},{6,4},{7,5},{8,10},{9,11},{10,... | collective-permute-start | bytes 2359304 | tf_op jit(solution)/shard_map/ppermute | solution.py:95
  1024.9 16.5 %collective-permute-start.33 = (f32[192,41]{0,1:T(8,128)S(1)}, f32[192,41]{0,1:T(8,128)S(1)}, u32[]{:S(2)}, u32[]{:S(2)}) collective-permute-start(f32[192,41]{0,1:T(8,128)S(1)} %add.384), channel_id=1, source_target_pairs={{0,2},{1,3},{2,0},{3,1},{4,6},{5,7},{6,4},{7,5},{8,10},{9,11},{10,... | collective-permute-start | bytes 94472 | tf_op jit(solution)/shard_map/ppermute | solution.py:95
  1026.5 19.5 %copy-start.19 = (bf16[256,1536]{1,0:T(8,128)(2,1)S(1)}, bf16[256,1536]{1,0:T(8,128)(2,1)}, u32[]{:S(2)}) copy-start(bf16[256,1536]{1,0:T(8,128)(2,1)} %param.15) | copy-start | bytes 2359300
  1045.9 5.2 collective-permute-start.30
  1051.1 4.0 collective-permute-start.31
  (65 other events, 365.9 us)
Sparse Core Ops, SparseCore 0:
  9.6 31.2 all-gather.6
  43.0 86.5 all-gather.4
  187.4 39.5 reduce-scatter.9
  234.5 107.3 all-gather.8
  344.0 98.5 all-gather.10
  446.5 133.1 reduce-scatter.11
  585.0 144.2 reduce-scatter.13
  814.6 93.5 reduce-scatter.15
  927.7 84.1 reduce-scatter.17

commit v4 on v3

--- a/solution.py
+++ b/solution.py
@@ -170,11 +170,12 @@
         return block
 
     def sum_tensor(values):
-        if n_tensor != 4:
-            return lax.psum(values, "t")
-        for bit in (1, 2):
-            values = values + swap(values, "t", n_tensor, bit)
-        return values
+        me_t = lax.axis_index("t")
+        slots = put(jnp.zeros((n_tensor, *values.shape), f32), values[None], me_t, 0, 0)
+        for shift in range(1, n_tensor):
+            got = lax.ppermute(values, "t", [(m, (m + shift) % n_tensor) for m in range(n_tensor)])
+            slots = put(slots, got[None], (me_t - shift) % n_tensor, 0, 0)
+        return jnp.sum(slots, axis=0)
 
     def on_device(
         tokens,
@@ -200,7 +201,7 @@
         q_cols, k_cols = w_query.shape[1], w_key.shape[1]
         qkv_cols = q_cols + 2 * k_cols
         attn_cols = qkv_cols + q_cols
-        side_cols = -(-(2 * n_experts + 2) // LANES) * LANES
+        side_cols = -(-(2 * n_experts + 4) // LANES) * LANES
         gate_cols = -(-2 * n_experts // LANES) * LANES
         me_i, me_t = lax.axis_index("i"), lax.axis_index("t")
 
@@ -214,8 +215,8 @@
             axis=1,
         )
         pack = jnp.concatenate([w_query, w_key, w_value, w_out.T, side], axis=1)
-        tokens_all = lax.all_gather(tokens, "t", axis=0, tiled=True).astype(f32)
         packed = lax.all_gather(pack, dp, axis=0, tiled=True)
+        tokens_all = gather_t(tokens)
 
         def expert_piece(target):
             first = target * own_experts
@@ -234,11 +235,9 @@
             return jax.tree.map(lambda part: lax.ppermute(part, "i", pairs), piece)
 
         pieces = [expert_piece((me_i + shift) % inner) for shift in range(inner)]
-        far_gate_up, far_down = to_owner(pieces[2], 2)
-        far_down, tokens_all = tie(far_down, tokens_all)
-        pieces[0], pieces[1], pieces[3], far_gate_up, packed = tie(
-            pieces[0], pieces[1], pieces[3], far_gate_up, packed
-        )
+        pieces, packed = tie(pieces, packed)
+        tokens_all = tokens_all.astype(f32)
+        far_down = to_owner(pieces[2][1], 2)
         near = to_owner(pieces[1], 1)
         owned = [pass_on(pieces[0])]
 
@@ -257,17 +256,16 @@
             qkv[:, q_cols : q_cols + k_cols].reshape(group, -1, HEAD_DIM), cosine, sine
         ).astype(bf16)
         values = qkv[:, q_cols + k_cols :].astype(bf16).reshape(group, -1, HEAD_DIM)
+        query, keys, values, far_down = tie(query, keys, values, far_down)
         attended, log_total = attend_forward(query, keys, values, prefix[0])
-        pieces[3], near, owned[0], attended = tie(pieces[3], near, owned[0], attended)
-        last = to_owner(pieces[3], 3)
+        far_piece, near, owned[0], attended = tie(pieces[2][0], near, owned[0], attended)
+        far_gate_up = to_owner(far_piece, 2)
         branch = lax.dot_general(
             attended, w_out_t, (((1,), (1,)), ((), ())), preferred_element_type=f32
         ).astype(bf16)
         tokens_f = tokens.astype(f32)
-        branch = lax.psum_scatter(branch, "t", scatter_dimension=0, tiled=True)
-        far_gate_up, near, last, branch = tie(far_gate_up, near, last, branch)
-        owned += [pass_on(near), pass_on((far_gate_up, far_down)), pass_on(last)]
-        middle = tokens_f + branch.astype(f32)
+        branch = scatter_t(branch)
+        middle = tokens_f + branch
         scale_two = rms_scale(middle)
         normed_two = (middle * scale_two * gain_two).astype(bf16)
 
@@ -287,6 +285,9 @@
             ],
             axis=1,
         )
+        last, near, far_gate_up, shipped = tie(pieces[3], near, far_gate_up, shipped)
+        last = to_owner(last, 3)
+        owned += [pass_on(near), pass_on((far_gate_up, far_down)), pass_on(last)]
         shared_all = by_rows(lax.all_gather(by_rows(shipped), shared, axis=0, tiled=True))
         w_gate_up = jnp.zeros((outer, inner, depth, 2 * own_hidden), bf16)
         w_down_t = jnp.zeros((outer, inner, depth, own_hidden), bf16)
@@ -308,16 +309,23 @@
         owner = me_i * own_experts + jnp.arange(own_hidden, dtype=jnp.int32)[None, :] // hidden
         spread = ((slot == owner) | (slot == owner + n_experts)).astype(bf16)
         gate_wide = jnp.dot(shared_all[:, width:], spread, preferred_element_type=f32)
-        gate_up = jnp.dot(normed_all, w_gate_up, preferred_element_type=f32)
-        gate_part, up_part = gate_up[:, :own_hidden], gate_up[:, own_hidden:]
-        sigmoid_g = jax.nn.sigmoid(gate_part)
-        silu_g = gate_part * sigmoid_g
-        act = silu_g * up_part
-        gated = (act * gate_wide).astype(bf16)
+        gate_up = jnp.dot(normed_all, w_gate_up, preferred_element_type=f32).astype(bf16)
+        gate_up, gate_wide = tie(gate_up, gate_wide.astype(bf16))
+
+        def activate(gate_up):
+            gate_part = gate_up[:, :own_hidden].astype(f32)
+            up_part = gate_up[:, own_hidden:].astype(f32)
+            sigmoid_g = jax.nn.sigmoid(gate_part)
+            return gate_part, up_part, sigmoid_g, gate_part * sigmoid_g
+
+        _, up_part, _, silu_g = activate(gate_up)
+        gated = (silu_g * up_part * gate_wide.astype(f32)).astype(bf16)
         expert_part = lax.dot_general(
             gated, w_down_t, (((1,), (1,)), ((), ())), preferred_element_type=f32
         ).astype(bf16)
-        expert_part, cot_all = tie(by_rows(expert_part), cot_all)
+        expert_part, cot_all, gate_up, gate_wide = tie(
+            by_rows(expert_part), cot_all, gate_up, gate_wide
+        )
         expert_share = lax.psum_scatter(expert_part, shared, scatter_dimension=0, tiled=True)
         contract_rows = (((0,), (0,)), ((), ()))
         grad_w_down = lax.dot_general(
@@ -336,7 +344,8 @@
 
         down_sums = to_sum(grad_w_down)
         cot_part = jnp.dot(cot_all, w_down_t, preferred_element_type=f32)
-        grad_act = cot_part * gate_wide
+        gate_part, up_part, sigmoid_g, silu_g = activate(gate_up)
+        grad_act = cot_part * gate_wide.astype(f32)
         grad_gate_up = jnp.concatenate(
             [
                 (grad_act * up_part * sigmoid_g * (1.0 + gate_part * (1.0 - sigmoid_g))).astype(
@@ -346,9 +355,9 @@
             ],
             axis=1,
         )
-        grad_gates = jnp.sum((act * cot_part).reshape(count, own_experts, hidden), axis=-1)
-        gate_block = lax.dynamic_update_slice(
-            jnp.zeros((count, side_cols), f32), grad_gates, (0, me_i * own_experts)
+        chosen = (jnp.arange(side_cols, dtype=jnp.int32)[None, :] == owner.T).astype(bf16)
+        gate_block = jnp.dot(
+            (silu_g * up_part * cot_part).astype(bf16), chosen, preferred_element_type=f32
         )
         grad_normed_part = lax.dot_general(
             grad_gate_up, w_gate_up, (((1,), (1,)), ((), ())), preferred_element_type=f32
@@ -356,13 +365,13 @@
         grad_shipped = jnp.concatenate([grad_normed_part, gate_block], axis=1).astype(bf16)
         grad_shipped, down_sums, expert_share = tie(by_rows(grad_shipped), down_sums, expert_share)
         grad_back = lax.psum_scatter(grad_shipped, shared, scatter_dimension=0, tiled=True)
-        normed_rows, _ = tie(normed_all, grad_shipped)
+        shared_rows, _ = tie(shared_all, grad_shipped)
         grad_w_gate_up = lax.dot_general(
-            normed_rows, grad_gate_up, contract_rows, preferred_element_type=f32
+            shared_rows[:, :width], grad_gate_up, contract_rows, preferred_element_type=f32
         ).astype(bf16)
         gate_up_sums = to_sum(grad_w_gate_up)
-        gate_up_sums, down_sums, grad_back = tie(gate_up_sums, down_sums, grad_back)
         sent_down = down_sums[:1] + [to_owner(down_sums[s], s) for s in range(1, inner)]
+        gate_up_sums, sent_down, grad_back = tie(gate_up_sums, sent_down, grad_back)
         sent_gate_up = gate_up_sums[:1] + [to_owner(gate_up_sums[s], s) for s in range(1, inner)]
         mixed = (middle + from_owner_order(expert_share).astype(f32)).astype(bf16)
 
@@ -386,34 +395,17 @@
         grad_out_part = lax.dot_general(
             grad_branch, attended, contract_rows, preferred_element_type=f32
         ).astype(bf16)
-        grad_out_part, sent_down[2], grad_branch = tie(
-            jnp.concatenate(
-                [
-                    grad_out_part,
-                    *split(jnp.concatenate([grad_router_part, grad_gain_two[:, None]], axis=1)),
-                    jnp.zeros((width, side_cols - 2 * n_experts - 2), bf16),
-                ],
-                axis=1,
-            ),
-            sent_down[2],
-            grad_branch,
-        )
-        shard_out = lax.psum_scatter(grad_out_part, dp, scatter_dimension=0, tiled=True)
+        grad_out_part, sent_gate_up[2], grad_branch = tie(
+            grad_out_part, sent_gate_up[2], grad_branch
+        )
         grad_attended = jnp.dot(
             grad_branch, w_out_t, preferred_element_type=f32
         ).astype(bf16)
-        grad_query, grad_keys, grad_values, (sent_down[1], sent_down[3]) = attend_backward(
-            query,
-            keys,
-            values,
-            grad_attended,
-            log_total,
-            prefix[0],
-            (sent_down[1], sent_down[3]),
-        )
-        grad_query, grad_keys, grad_values, shard_out, sent_gate_up[2] = tie(
-            grad_query, grad_keys, grad_values, shard_out, sent_gate_up[2]
-        )
+        sent_near = (sent_gate_up[1], sent_gate_up[3])
+        grad_query, grad_keys, grad_values, sent_near = attend_backward(
+            query, keys, values, grad_attended, log_total, prefix[0], sent_near
+        )
+        sent_gate_up[1], sent_gate_up[3] = sent_near
         grad_qkv = jnp.concatenate(
             [
                 rotate(grad_query, cosine, -sine).astype(bf16).reshape(group, -1),
@@ -427,24 +419,31 @@
         )
         grad_gain_one = jnp.sum(grad_normed_one * normal_all, axis=0)
         own_grad_one = scatter_t(grad_normed_one.astype(bf16))
-        grad_input_part, _ = norm_backward(tokens_f, rms_scale(tokens_f), gain_one, own_grad_one)
-        grad_tokens = grad_middle + grad_input_part
-
+        sums = jnp.concatenate(
+            [grad_router_part, grad_gain_one[:, None], grad_gain_two[:, None]], axis=1
+        )
+        (sums,) = tie(
+            jnp.concatenate(
+                [*split(sums), jnp.zeros((width, side_cols - 2 * n_experts - 4), bf16)], axis=1
+            )
+        )
         grad_attn = jnp.concatenate(
             [
                 lax.dot_general(
                     normed_one, grad_qkv, contract_rows, preferred_element_type=f32
                 ).astype(bf16),
-                *split(grad_gain_one[:, None]),
-                jnp.zeros((width, LANES - 2), bf16),
+                grad_out_part,
+                sums,
             ],
             axis=1,
         )
-        shard_attn = lax.psum_scatter(grad_attn, dp, scatter_dimension=0, tiled=True).astype(f32)
-        gain_sum = sum_tensor(shard_attn[:, qkv_cols] + shard_attn[:, qkv_cols + 1])
-        shard_out = shard_out.astype(f32)
-        side_sum = shard_out[:, q_cols : q_cols + 2 * (n_experts + 1)].reshape(depth, 2, -1)
-        side_sum = sum_tensor(jnp.sum(side_sum, axis=1))
+        shard_attn = lax.psum_scatter(by_rows(grad_attn), dp, scatter_dimension=0, tiled=True)
+        shard_attn, own_grad_one = tie(shard_attn, own_grad_one)
+        shard_attn = shard_attn.astype(f32)
+        grad_input_part, _ = norm_backward(tokens_f, rms_scale(tokens_f), gain_one, own_grad_one)
+        grad_tokens = grad_middle + grad_input_part
+        side_sum = shard_attn[:, attn_cols : attn_cols + 2 * n_experts + 4]
+        side_sum = sum_tensor(jnp.sum(side_sum.reshape(depth, 2, -1), axis=1).T)
 
         grad_gate = jnp.zeros((n_experts, depth, hidden), f32)
         grad_up, grad_down = grad_gate, jnp.zeros((n_experts, hidden, depth), f32)
@@ -460,13 +459,13 @@
         return (
             mixed,
             grad_tokens,
-            gain_sum,
+            side_sum[n_experts],
             shard_attn[:, :q_cols],
             shard_attn[:, q_cols : q_cols + k_cols],
             shard_attn[:, q_cols + k_cols : qkv_cols],
-            shard_out[:, :q_cols].T,
-            side_sum[:, n_experts],
-            side_sum[:, :n_experts],
+            shard_attn[:, qkv_cols:attn_cols].T,
+            side_sum[n_experts + 1],
+            side_sum[:n_experts].T,
             grad_gate,
             grad_up,
             grad_down,

time: 1070 us -> 1120 us (1.047)
  waiting for transfers between devices: 379 us -> 414 us
  other arithmetic: 84.3 us -> 97.9 us
    reduce_scatter x1, waiting for transfers between devices: 0.21 us -> 53.2 us  [on_device(): lax.psum_scatter(grad_shipped, shared, scatter_dimension=0, tiled=True)]
    unnamed x11 -> x6, waiting for transfers between devices: 42.9 us -> 0.1 us
    all_gather x1, waiting for transfers between devices: 0.02 us -> 30.1 us  [on_device(): packed = lax.all_gather(pack, dp, axis=0, tiled=True)]
    dot_general x1, matrix products: 24.8 us -> 4.11 us  [on_device(): jnp.dot(shared_all[:, width:], spread, preferred_element_type=f32)]
    ppermute x12, starting transfers between devices: 31.8 us -> 11.9 us  [to_owner(): return jax.tree.map(lambda part: lax.ppermute(part, 'i', pairs), piece)]
    dot_general x2 -> x3, matrix products: 84.9 us -> 102 us  [the longest x1 43.4 us: on_device(): jnp.dot(normed_all, w_gate_up, preferred_element_type=f32).astype(bf16)]
    all_gather x1, waiting for transfers between devices: 6.86 us -> 21.9 us  [on_device(): lax.all_gather(by_rows(shipped), shared, axis=0, tiled=True)]
    ppermute x12, waiting for transfers between devices: 131 us -> 118 us  [to_owner(): return jax.tree.map(lambda part: lax.ppermute(part, 'i', pairs), piece)]
  transfers between devices with their start and end apart: 45 -> 45, of which waited for: 21 -> 19; matrix products, arithmetic and copies ran while one was open for 53% -> 48% of each run, Pallas kernels for 0% -> 0%
where the time goes in v4:
time: 1120 us; the launch traced here: 1100 us
  waiting for transfers between devices  414 us (37%)
  matrix products  334 us (30%)
  local copies, waits for them, and re-layouts  192 us (17%)
  other arithmetic  97.9 us (9%)
  starting transfers between devices  50 us (4%)
  between operations  16.6 us (1%)
    ppermute x24, waiting for transfers between devices, swap(): return lax.ppermute(values, axis, [(m, m ^ bit) for m in range(size)])  174 us
    ppermute x12, waiting for transfers between devices, to_owner(): return jax.tree.map(lambda part: lax.ppermute(part, 'i', pairs), piece)  118 us
    reduce_scatter x1, waiting for transfers between devices, on_device(): lax.psum_scatter(grad_shipped, shared, scatter_dimension=0, tiled=True)  53.2 us
    dot_general x1, matrix products, on_device(): jnp.dot(normed_all, w_gate_up, preferred_element_type=f32).astype(bf16)  43.4 us
    dot_general x1, matrix products, on_device(): lax.dot_general(shared_rows[:, :width], grad_gate_up, contract_rows, pref...  41.9 us
    dot_general x1, matrix products, on_device(): lax.dot_general(grad_gate_up, w_gate_up, (((1,), (1,)), ((), ())), prefer...  39.8 us
    dot_general x1, matrix products, on_device(): cot_part = jnp.dot(cot_all, w_down_t, preferred_element_type=f32)  38.3 us
    all_gather x1, waiting for transfers between devices, on_device(): packed = lax.all_gather(pack, dp, axis=0, tiled=True)  30.1 us
  transfers between devices with their start and end apart: 45, of which 19 were waited for; matrix products, arithmetic and copies ran while one was open for 48% of the time, Pallas kernels for 0%

profile of v4, /device:TPU:0, one launch (start us, length us, event | category | flops | bytes accessed | tf_op | source)
XLA Modules:
  0.0 1104.9 jit_solution(6064338003425868215)
XLA Ops:
  11.6 3.1 collective-permute-start.4
  14.7 3.5 dynamic-slice_bitcast_fusion.19
  48.9 30.1 %all-gather.4.cloned.1.call-done = bf16[1536,1152]{1,0:T(8,128)(2,1)} async-done(((bf16[192,1152]{1,0:T(8,128)(2,1)}), bf16[1536,1152]{1,0:T(8,128)(2,1)}) %all-gather.4.cloned.1.call-update) | async-done | bytes 3538960 | tf_op jit(solution)/shard_map/all_gather | solution.py:218
  80.9 4.9 fusion.56
  107.4 38.1 %collective-permute-done.6 = bf16[192,1280]{1,0:T(8,128)(2,1)} collective-permute-done((bf16[192,1280]{1,0:T(8,128)(2,1)}, bf16[192,1280]{1,0:T(8,128)(2,1)}, u32[]{:S(2)}, u32[]{:S(2)}) %collective-permute-start.6) | collective-permute-done | bytes 491552 | tf_op jit(solution)/shard_map/ppermute | solution.py:235
  145.6 10.6 fusion.123
  156.2 10.3 fusion.3
  166.5 11.5 %fusion.63 = bf16[2,64,3,1024]{3,1,2,0:T(8,128)(2,1)} fusion(f32[2,3,1024,1024]{2,3,1,0:T(8,128)} %get-tuple-element.204, f32[2,3,1024]{2,1,0:T(4,128)S(1)} %fusion.3, f32[2,3,1024]{2,1,0:T(4,128)S(1)} %get-tuple-element.203, bf16[1024,2,64]{0,2,1:T(8,128)(2,1)S(1)} %bitcast.384), kind=kOutput, calls=%fused_computation.115 | convolution fusion | flops 824573952 | bytes 26263552 | tf_op jit(solution)/shard_map/hgqk,khd->qhgd/dot_general | solution.py:65
  184.1 3.1 convolution_convert_fusion.5
  190.2 3.7 collective-permute-done.7
  202.0 16.7 %collective-permute-done.8 = bf16[256,1536]{1,0:T(8,128)(2,1)S(1)} collective-permute-done((bf16[256,1536]{1,0:T(8,128)(2,1)}, bf16[256,1536]{1,0:T(8,128)(2,1)S(1)}, u32[]{:S(2)}, u32[]{:S(2)}) %collective-permute-start.8) | collective-permute-done | bytes 786464 | tf_op jit(solution)/shard_map/ppermute | solution.py:95
  227.0 10.2 all-gather.8.cloned.1.call-start
  249.8 3.8 broadcast_in_dim.123
  257.1 9.2 collective-permute-done.14
  266.8 7.4 collective-permute-done.16
  278.2 16.7 %collective-permute-done.12 = bf16[192,2560]{1,0:T(8,128)(2,1)} collective-permute-done((bf16[192,2560]{1,0:T(8,128)(2,1)S(1)}, bf16[192,2560]{1,0:T(8,128)(2,1)}, u32[]{:S(2)}, u32[]{:S(2)}) %collective-permute-start.12) | collective-permute-done | bytes 983072 | tf_op jit(solution)/shard_map/ppermute | solution.py:235
  296.3 22.5 %collective-permute-done.17 = bf16[192,1280]{1,0:T(8,128)(2,1)S(1)} collective-permute-done((bf16[192,1280]{1,0:T(8,128)(2,1)}, bf16[192,1280]{1,0:T(8,128)(2,1)S(1)}, u32[]{:S(2)}, u32[]{:S(2)}) %collective-permute-start.17) | collective-permute-done | bytes 491552 | tf_op jit(solution)/shard_map/ppermute | solution.py:95
  320.0 3.4 fusion.45
  326.0 12.3 %collective-permute-done.13 = bf16[192,2560]{1,0:T(8,128)(2,1)S(1)} collective-permute-done((bf16[192,2560]{1,0:T(8,128)(2,1)}, bf16[192,2560]{1,0:T(8,128)(2,1)S(1)}, u32[]{:S(2)}, u32[]{:S(2)}) %collective-permute-start.13) | collective-permute-done | bytes 983072 | tf_op jit(solution)/shard_map/ppermute | solution.py:95
  340.9 21.9 %all-gather.6.cloned.1.call-done = bf16[4096,1664]{1,0:T(8,128)(2,1)} async-done(((bf16[256,1664]{1,0:T(8,128)(2,1)}), bf16[4096,1664]{1,0:T(8,128)(2,1)}) %all-gather.6.cloned.1.call-update) | async-done | bytes 13631504 | tf_op jit(solution)/shard_map/all_gather | solution.py:291
  363.0 4.1 convolution_convert_fusion.2
  367.1 43.4 %convolution_convert_fusion = bf16[4096,2560]{1,0:T(8,128)(2,1)} fusion(bf16[1536,2560]{1,0:T(8,128)(2,1)} %bitcast.65, bf16[4096,1664]{1,0:T(8,128)(2,1)} %all-gather.6.cloned.1.call-done), kind=kOutput, calls=%fused_computation.16 | convolution fusion | flops 32222740480 | bytes 41418752 | tf_op jit(solution)/shard_map/dot_general | solution.py:312
  410.6 11.6 %fusion.18 = bf16[4096,1280]{1,0:T(8,128)(2,1)S(1)} fusion(bf16[4096,1280]{1,0:T(8,128)(2,1)S(1)} %convolution_convert_fusion.2, bf16[4096,2560]{1,0:T(8,128)(2,1)} %convolution_convert_fusion), kind=kLoop, calls=%fused_computation.35 | loop fusion | flops 52428800 | bytes 41943040 | tf_op jit(solution)/shard_map/convert_element_type | solution.py:322
  422.2 3.8 copy-done.15
  426.0 20.9 %convolution_convert_fusion.1 = bf16[4096,1536]{1,0:T(8,128)(2,1)} fusion(bf16[4096,1280]{1,0:T(8,128)(2,1)S(1)} %fusion.18, bf16[1536,1280]{1,0:T(8,128)(2,1)} %bitcast.347), kind=kOutput, calls=%fused_computation.37 | convolution fusion | flops 16112418816 | bytes 27000832 | tf_op jit(solution)/shard_map/dot_general | solution.py:323
  446.9 16.9 %all-gather.8.cloned.1.call-done = bf16[4096,1536]{1,0:T(8,128)(2,1)} async-done(((bf16[256,1536]{1,0:T(8,128)(2,1)}), bf16[4096,1536]{1,0:T(8,128)(2,1)}) %all-gather.8.cloned.1.call-update) | async-done | bytes 12582928 | tf_op jit(solution)/shard_map/all_gather | solution.py:304
  464.3 22.3 %convolution_convert_fusion.4 = bf16[1536,1280]{1,0:T(8,128)(2,1)S(1)} fusion(bf16[4096,1536]{1,0:T(8,128)(2,1)} %all-gather.8.cloned.1.call-done, bf16[4096,1280]{1,0:T(8,128)(2,1)} %copy-done.15), kind=kOutput, calls=%fused_computation.54 | convolution fusion | flops 16108093440 | bytes 27000832 | tf_op jit(solution)/shard_map/dot_general | solution.py:331
  494.2 38.3 %fusion.11 = (bf16[4096,1280]{1,0:T(8,128)(2,1)}, bf16[4096,1280]{1,0:T(8,128)(2,1)}, f32[4096,1280]{1,0:T(8,128)}) fusion(bf16[4096,1280]{1,0:T(8,128)(2,1)} %copy-done.2, bf16[4096,2560]{1,0:T(8,128)(2,1)} %convolution_convert_fusion, bf16[4096,1536]{1,0:T(8,128)(2,1)} %all-gather.8.cloned.1.call-done, bf16[1536,1280]{1,0:T(8,128)(2,1)S(1)} %bitcast.348), kind=kOutput, calls=%fused_computation.25 | convolution fusion | flops 16195256320 | bytes 89915392 | tf_op jit(solution)/shard_map/dot_general | solution.py:346
  532.5 16.3 %fusion.41 = bf16[4096,128]{1,0:T(8,128)(2,1)S(1)} fusion(f32[4096,1280]{1,0:T(8,128)} %get-tuple-element.207, bf16[4096,2560]{1,0:T(8,128)(2,1)} %convolution_convert_fusion, s32[1280]{0:T(1024)S(1)} %copy-done.77), kind=kOutput, calls=%fused_computation.60 | convolution fusion | flops 1390051328 | bytes 42996736 | tf_op jit(solution)/shard_map/dot_general | solution.py:359
  548.8 39.8 %convolution_convert_fusion.3 = bf16[4096,1536]{1,0:T(8,128)(2,1)} fusion(bf16[1536,2560]{1,0:T(8,128)(2,1)} %bitcast.65, bf16[4096,1280]{1,0:T(8,128)(2,1)} %get-tuple-element.146, bf16[4096,1280]{1,0:T(8,128)(2,1)} %get-tuple-element.145), kind=kOutput, calls=%fused_computation.39 | convolution fusion | flops 32260489216 | bytes 41418752 | tf_op jit(solution)/shard_map/dot_general | solution.py:362
  588.6 12.2 %pad_maximum_fusion.1 = bf16[4096,1664]{1,0:T(8,128)(2,1)} fusion(bf16[4096,128]{1,0:T(8,128)(2,1)S(1)} %fusion.41, bf16[4096,1536]{1,0:T(8,128)(2,1)} %convolution_convert_fusion.3), kind=kLoop, calls=%fused_computation.40 | loop fusion | flops 27262976 | bytes 27262976 | tf_op jit(solution)/shard_map/concatenate | solution.py:365
  600.8 3.3 fusion.78
  604.2 41.9 %fusion.27 = bf16[1536,2560]{1,0:T(8,128)(2,1)} fusion(bf16[4096,1280]{1,0:T(8,128)(2,1)} %get-tuple-element.146, bf16[4096,1280]{1,0:T(8,128)(2,1)} %get-tuple-element.145, bf16[4096,1664]{1,0:T(8,128)(2,1)} %all-gather.6.cloned.1.call-done), kind=kOutput, calls=%fused_computation.47 | convolution fusion | flops 32258129920 | bytes 41418752 | tf_op jit(solution)/shard_map/dot_general | solution.py:369
  652.7 20.6 %collective-permute-done.22 = bf16[192,2560]{1,0:T(8,128)(2,1)S(1)} collective-permute-done((bf16[192,2560]{1,0:T(8,128)(2,1)S(1)}, bf16[192,2560]{1,0:T(8,128)(2,1)S(1)}, u32[]{:S(2)}, u32[]{:S(2)}) %collective-permute-start.22) | collective-permute-done | bytes 983072 | tf_op jit(solution)/shard_map/ppermute | solution.py:95
  673.3 21.0 %collective-permute-done.23 = bf16[192,2560]{1,0:T(8,128)(2,1)S(1)} collective-permute-done((bf16[192,2560]{1,0:T(8,128)(2,1)S(1)}, bf16[192,2560]{1,0:T(8,128)(2,1)S(1)}, u32[]{:S(2)}, u32[]{:S(2)}) %collective-permute-start.23) | collective-permute-done | bytes 983072 | tf_op jit(solution)/shard_map/ppermute | solution.py:95
  694.6 20.7 %collective-permute-done.24 = bf16[192,2560]{1,0:T(8,128)(2,1)S(1)} collective-permute-done((bf16[192,2560]{1,0:T(8,128)(2,1)S(1)}, bf16[192,2560]{1,0:T(8,128)(2,1)S(1)}, u32[]{:S(2)}, u32[]{:S(2)}) %collective-permute-start.24) | collective-permute-done | bytes 983072 | tf_op jit(solution)/shard_map/ppermute | solution.py:95
  715.4 17.8 %collective-permute-done.25 = bf16[192,2560]{1,0:T(8,128)(2,1)S(1)} collective-permute-done((bf16[192,2560]{1,0:T(8,128)(2,1)S(1)}, bf16[192,2560]{1,0:T(8,128)(2,1)S(1)}, u32[]{:S(2)}, u32[]{:S(2)}) %collective-permute-start.25) | collective-permute-done | bytes 983072 | tf_op jit(solution)/shard_map/ppermute | solution.py:95
  735.7 53.2 %reduce-scatter.6.cloned.1.call-done = bf16[256,1664]{1,0:T(8,128)(2,1)} async-done(((bf16[4096,1664]{1,0:T(8,128)(2,1)}), bf16[256,1664]{1,0:T(8,128)(2,1)}) %reduce-scatter.6.cloned.1.call-update) | async-done | bytes 851984 | tf_op jit(solution)/shard_map/reduce_scatter | solution.py:367
  795.2 2.9 multiply_reduce_fusion.1
  800.7 16.9 %collective-permute-done.29 = bf16[256,1536]{1,0:T(8,128)(2,1)S(1)} collective-permute-done((bf16[256,1536]{1,0:T(8,128)(2,1)S(1)}, bf16[256,1536]{1,0:T(8,128)(2,1)S(1)}, u32[]{:S(2)}, u32[]{:S(2)}) %collective-permute-start.29) | collective-permute-done | bytes 786464 | tf_op jit(solution)/shard_map/ppermute | solution.py:95
  821.1 3.2 collective-permute-start.33
  826.7 2.9 convolution_convert_fusion.7
  829.6 56.3 %collective-permute-done.31 = bf16[192,2560]{1,0:T(8,128)(2,1)} collective-permute-done((bf16[192,2560]{1,0:T(8,128)(2,1)S(1)}, bf16[192,2560]{1,0:T(8,128)(2,1)}, u32[]{:S(2)}, u32[]{:S(2)}) %collective-permute-start.31) | collective-permute-done | bytes 983072 | tf_op jit(solution)/shard_map/ppermute | solution.py:235
  889.5 28.5 %fusion.2 = bf16[2,3,1024,1024]{2,3,1,0:T(8,128)(2,1)} fusion(f32[2,3,1024,1024]{2,3,1,0:T(8,128)} %get-tuple-element.204, f32[2,3,1024]{2,1,0:T(4,128)S(1)} %log_add_fusion, bf16[1024,2,3,64]{0,3,2,1:T(8,128)(2,1)S(1)} %bitcast.376, bf16[1024,2,64]{0,2,1:T(8,128)(2,1)} %bitcast.383), kind=kOutput, calls=%fused_computation.11 | convolution fusion | flops 1648368640 | bytes 38821888 | tf_op jit(solution)/shard_map/sub | solution.py:78
  918.0 8.2 convolution_multiply_fusion
  926.9 4.7 fusion.68
  931.6 12.4 %fusion.69 = bf16[2,64,1024]{2,1,0:T(8,128)(2,1)S(1)} fusion(bf16[1024,2,3,64]{0,3,2,1:T(8,128)(2,1)} %bitcast.377, f32[2,3,1024,1024]{2,3,1,0:T(8,128)} %get-tuple-element.204, f32[2,3,1024]{2,1,0:T(4,128)S(1)} %log_add_fusion), kind=kOutput, calls=%fused_computation.135 | convolution fusion | flops 818020352 | bytes 26238976 | tf_op jit(solution)/shard_map/hgqk,qhgd->khd/dot_general | solution.py:88
  946.4 6.3 fusion.120
  952.7 4.3 convolution_convert_fusion.6
  960.3 3.0 pad_maximum_fusion.6
  968.1 3.2 copy.321
  975.3 2.8 copy.338
  978.1 3.5 slice_bitcast_fusion.3
  981.6 2.8 copy.346
  1009.0 2.8 copy.339
  1018.3 2.8 copy.340
  1021.1 3.5 slice_bitcast_fusion.2
  1027.3 3.0 copy.342
  1030.3 3.5 slice_bitcast_fusion.1
  1036.5 2.8 copy.344
  1039.3 3.5 slice_bitcast_fusion
  1042.8 2.8 copy.349
  1064.0 12.2 %collective-permute-done.35 = bf16[256,1536]{1,0:T(8,128)(2,1)S(1)} collective-permute-done((bf16[256,1536]{1,0:T(8,128)(2,1)S(1)}, bf16[256,1536]{1,0:T(8,128)(2,1)S(1)}, u32[]{:S(2)}, u32[]{:S(2)}) %collective-permute-start.35) | collective-permute-done | bytes 786464 | tf_op jit(solution)/shard_map/ppermute | solution.py:95
  1085.2 3.8 fusion.61
  (424 shorter events, 234.7 us)
Async XLA Ops:
  7.2 193.2 %copy-start = (s32[1024,8]{0,1:T(8,128)S(1)}, s32[1024,8]{0,1:T(8,128)}, u32[]{:S(2)}) copy-start(s32[1024,8]{0,1:T(8,128)} %param.17) | copy-start | bytes 98308
  7.2 71.8 %all-gather.4.cloned.1.call-start = ((), (), s32[]{:S(2)}) async-start(), calls=%async_computation.3 | async-start | bytes 3981312 | tf_op jit(solution)/shard_map/all_gather | solution.py:218
  11.6 351.3 %all-gather.6.cloned.1.call-start = ((), (), s32[]{:S(2)}) async-start(), calls=%async_computation.4 | async-start | bytes 14483456 | tf_op jit(solution)/shard_map/all_gather | solution.py:291
  11.6 29.4 %collective-permute-start.4 = (bf16[256,1536]{1,0:T(8,128)(2,1)}, bf16[256,1536]{1,0:T(8,128)(2,1)S(1)}, u32[]{:S(2)}, u32[]{:S(2)}) collective-permute-start(bf16[256,1536]{1,0:T(8,128)(2,1)} %param.14), channel_id=1, source_target_pairs={{0,2},{1,3},{2,0},{3,1},{4,6},{5,7},{6,4},{7,5},{8,10},{9,11},{10,... | collective-permute-start | bytes 2359304 | tf_op jit(solution)/shard_map/ppermute | solution.py:95
  41.2 5.2 collective-permute-start.5
  42.5 63.2 %copy-start.43 = (f32[1024,32]{0,1:T(8,128)}, f32[1024,32]{0,1:T(8,128)S(1)}, u32[]{:S(2)}) copy-start(f32[1024,32]{0,1:T(8,128)S(1)} %get-tuple-element.202) | copy-start | bytes 393220
  48.9 36.9 %copy-start.81 = (f32[1024]{0:T(1024)}, f32[1024]{0:T(1024)S(1)}, u32[]{:S(2)}) copy-start(f32[1024]{0:T(1024)S(1)} %add_rsqrt_fusion) | copy-start | bytes 12292
  80.9 140.3 %copy-start.70 = (f32[1536]{0:T(1024)}, f32[1536]{0:T(1024)S(1)}, u32[]{:S(2)}) copy-start(f32[1536]{0:T(1024)S(1)} %get-tuple-element.136) | copy-start | bytes 18436
  90.8 54.7 %collective-permute-start.6 = (bf16[192,1280]{1,0:T(8,128)(2,1)}, bf16[192,1280]{1,0:T(8,128)(2,1)}, u32[]{:S(2)}, u32[]{:S(2)}) collective-permute-start(bf16[192,1280]{1,0:T(8,128)(2,1)} %copy.297), channel_id=1, source_target_pairs={{0,16},{8,24},{16,0},{24,8},{1,17},{9,25},{17,1},{25,9},{2,18},{10... | collective-permute-start | bytes 1474568 | tf_op jit(solution)/shard_map/ppermute | solution.py:235
  95.0 83.0 %collective-permute-start.3 = (bf16[192,1280]{1,0:T(8,128)(2,1)}, bf16[192,1280]{1,0:T(8,128)(2,1)}, u32[]{:S(2)}, u32[]{:S(2)}) collective-permute-start(bf16[192,1280]{1,0:T(8,128)(2,1)} %copy.295), channel_id=1, source_target_pairs={{0,4},{4,0},{1,5},{5,1},{2,6},{6,2},{3,7},{7,3},{8,12},{12,8},{9,1... | collective-permute-start | bytes 1474568 | tf_op jit(solution)/shard_map/ppermute | solution.py:95
  96.9 83.7 %collective-permute-start.2 = (bf16[192,2560]{1,0:T(8,128)(2,1)}, bf16[192,2560]{1,0:T(8,128)(2,1)}, u32[]{:S(2)}, u32[]{:S(2)}) collective-permute-start(bf16[192,2560]{1,0:T(8,128)(2,1)} %copy.293), channel_id=1, source_target_pairs={{0,4},{4,0},{1,5},{5,1},{2,6},{6,2},{3,7},{7,3},{8,12},{12,8},{9,1... | collective-permute-start | bytes 2949128 | tf_op jit(solution)/shard_map/ppermute | solution.py:95
  100.7 83.4 %collective-permute-start = (bf16[192,2560]{1,0:T(8,128)(2,1)}, bf16[192,2560]{1,0:T(8,128)(2,1)}, u32[]{:S(2)}, u32[]{:S(2)}) collective-permute-start(bf16[192,2560]{1,0:T(8,128)(2,1)} %copy.291), channel_id=1, source_target_pairs={{0,8},{8,16},{16,24},{24,0},{1,9},{9,17},{17,25},{25,1},{2,10},{10... | collective-permute-start | bytes 2949128 | tf_op jit(solution)/shard_map/ppermute | solution.py:235
  103.4 80.7 %collective-permute-start.1 = (bf16[192,1280]{1,0:T(8,128)(2,1)}, bf16[192,1280]{1,0:T(8,128)(2,1)}, u32[]{:S(2)}, u32[]{:S(2)}) collective-permute-start(bf16[192,1280]{1,0:T(8,128)(2,1)} %copy.292), channel_id=1, source_target_pairs={{0,8},{8,16},{16,24},{24,0},{1,9},{9,17},{17,25},{25,1},{2,10},{10... | collective-permute-start | bytes 1474568 | tf_op jit(solution)/shard_map/ppermute | solution.py:235
  105.6 50.5 %copy-start.57 = (bf16[1024,2,64]{0,2,1:T(8,128)(2,1)}, bf16[1024,2,64]{0,2,1:T(8,128)(2,1)S(1)}, u32[]{:S(2)}) copy-start(bf16[1024,2,64]{0,2,1:T(8,128)(2,1)S(1)} %pad_maximum_fusion.21) | copy-start | bytes 786436
  107.4 48.7 %copy-start.11 = (bf16[1024,6,64]{0,2,1:T(8,128)(2,1)}, bf16[1024,6,64]{0,2,1:T(8,128)(2,1)S(1)}, u32[]{:S(2)}) copy-start(bf16[1024,6,64]{0,2,1:T(8,128)(2,1)S(1)} %pad_maximum_fusion.16) | copy-start | bytes 2359300
  166.5 12.8 %copy-start.25 = (bf16[192,10,128]{0,2,1:T(8,128)(2,1)S(1)}, bf16[192,10,128]{0,2,1:T(8,128)(2,1)}, u32[]{:S(2)}) copy-start(bf16[192,10,128]{0,2,1:T(8,128)(2,1)} %copy.278) | copy-start | bytes 1474564
  190.2 3.8 collective-permute-start.7
  198.9 19.8 %collective-permute-start.8 = (bf16[256,1536]{1,0:T(8,128)(2,1)}, bf16[256,1536]{1,0:T(8,128)(2,1)S(1)}, u32[]{:S(2)}, u32[]{:S(2)}) collective-permute-start(bf16[256,1536]{1,0:T(8,128)(2,1)} %fusion.85), channel_id=1, source_target_pairs={{0,2},{1,3},{2,0},{3,1},{4,6},{5,7},{6,4},{7,5},{8,10},{9,11},{10,... | collective-permute-start | bytes 2359304 | tf_op jit(solution)/shard_map/ppermute | solution.py:95
  202.0 25.0 %collective-permute-start.9 = (bf16[192,2560]{1,0:T(8,128)(2,1)}, bf16[192,2560]{1,0:T(8,128)(2,1)}, u32[]{:S(2)}, u32[]{:S(2)}) collective-permute-start(bf16[192,2560]{1,0:T(8,128)(2,1)} %copy.303), channel_id=1, source_target_pairs={{0,16},{8,24},{16,0},{24,8},{1,17},{9,25},{17,1},{25,9},{2,18},{10... | collective-permute-start | bytes 2949128 | tf_op jit(solution)/shard_map/ppermute | solution.py:235
  223.0 14.3 %copy-start.22 = (bf16[256,1536]{1,0:T(8,128)(2,1)S(1)}, bf16[256,1536]{1,0:T(8,128)(2,1)}, u32[]{:S(2)}) copy-start(bf16[256,1536]{1,0:T(8,128)(2,1)} %param.15) | copy-start | bytes 2359300
  227.0 236.8 %all-gather.8.cloned.1.call-start = ((), (), s32[]{:S(2)}) async-start(), calls=%async_computation.5 | async-start | bytes 13369344 | tf_op jit(solution)/shard_map/all_gather | solution.py:304
  241.3 35.6 %collective-permute-start.15 = (bf16[192,1280]{1,0:T(8,128)(2,1)}, bf16[192,1280]{1,0:T(8,128)(2,1)}, u32[]{:S(2)}, u32[]{:S(2)}) collective-permute-start(bf16[192,1280]{1,0:T(8,128)(2,1)} %collective-permute-done.6), channel_id=1, source_target_pairs={{0,4},{4,0},{1,5},{5,1},{2,6},{6,2},{3,7},{7,3},{8,12},{12,8},{9,1... | collective-permute-start | bytes 1474568 | tf_op jit(solution)/shard_map/ppermute | solution.py:95
  244.3 22.0 %collective-permute-start.14 = (bf16[192,1280]{1,0:T(8,128)(2,1)}, bf16[192,1280]{1,0:T(8,128)(2,1)}, u32[]{:S(2)}, u32[]{:S(2)}) collective-permute-start(bf16[192,1280]{1,0:T(8,128)(2,1)} %collective-permute-done.1), channel_id=1, source_target_pairs={{0,4},{4,0},{1,5},{5,1},{2,6},{6,2},{3,7},{7,3},{8,12},{12,8},{9,1... | collective-permute-start | bytes 1474568 | tf_op jit(solution)/shard_map/ppermute | solution.py:95
  246.8 27.4 %collective-permute-start.16 = (bf16[192,1280]{1,0:T(8,128)(2,1)}, bf16[192,1280]{1,0:T(8,128)(2,1)}, u32[]{:S(2)}, u32[]{:S(2)}) collective-permute-start(bf16[192,1280]{1,0:T(8,128)(2,1)} %copy.313), channel_id=1, source_target_pairs={{0,24},{8,0},{16,8},{24,16},{1,25},{9,1},{17,9},{25,17},{2,26},{10... | collective-permute-start | bytes 1474568 | tf_op jit(solution)/shard_map/ppermute | solution.py:235
  248.3 46.5 %collective-permute-start.12 = (bf16[192,2560]{1,0:T(8,128)(2,1)S(1)}, bf16[192,2560]{1,0:T(8,128)(2,1)}, u32[]{:S(2)}, u32[]{:S(2)}) collective-permute-start(bf16[192,2560]{1,0:T(8,128)(2,1)S(1)} %copy.311), channel_id=1, source_target_pairs={{0,24},{8,0},{16,8},{24,16},{1,25},{9,1},{17,9},{25,17},{2,26},{10... | collective-permute-start | bytes 2949128 | tf_op jit(solution)/shard_map/ppermute | solution.py:235
  256.2 63.8 %collective-permute-start.10 = (bf16[192,2560]{1,0:T(8,128)(2,1)}, bf16[192,2560]{1,0:T(8,128)(2,1)S(1)}, u32[]{:S(2)}, u32[]{:S(2)}) collective-permute-start(bf16[192,2560]{1,0:T(8,128)(2,1)} %collective-permute-done), channel_id=1, source_target_pairs={{0,4},{4,0},{1,5},{5,1},{2,6},{6,2},{3,7},{7,3},{8,12},{12,8},{9,1... | collective-permute-start | bytes 2949128 | tf_op jit(solution)/shard_map/ppermute | solution.py:95
  266.3 57.1 %collective-permute-start.11 = (bf16[192,2560]{1,0:T(8,128)(2,1)}, bf16[192,2560]{1,0:T(8,128)(2,1)S(1)}, u32[]{:S(2)}, u32[]{:S(2)}) collective-permute-start(bf16[192,2560]{1,0:T(8,128)(2,1)} %collective-permute-done.9), channel_id=1, source_target_pairs={{0,4},{4,0},{1,5},{5,1},{2,6},{6,2},{3,7},{7,3},{8,12},{12,8},{9,1... | collective-permute-start | bytes 2949128 | tf_op jit(solution)/shard_map/ppermute | solution.py:95
  274.2 44.7 %collective-permute-start.17 = (bf16[192,1280]{1,0:T(8,128)(2,1)}, bf16[192,1280]{1,0:T(8,128)(2,1)S(1)}, u32[]{:S(2)}, u32[]{:S(2)}) collective-permute-start(bf16[192,1280]{1,0:T(8,128)(2,1)} %collective-permute-done.16), channel_id=1, source_target_pairs={{0,4},{4,0},{1,5},{5,1},{2,6},{6,2},{3,7},{7,3},{8,12},{12,8},{9,1... | collective-permute-start | bytes 1474568 | tf_op jit(solution)/shard_map/ppermute | solution.py:95
  294.9 43.5 %collective-permute-start.13 = (bf16[192,2560]{1,0:T(8,128)(2,1)}, bf16[192,2560]{1,0:T(8,128)(2,1)S(1)}, u32[]{:S(2)}, u32[]{:S(2)}) collective-permute-start(bf16[192,2560]{1,0:T(8,128)(2,1)} %collective-permute-done.12), channel_id=1, source_target_pairs={{0,4},{4,0},{1,5},{5,1},{2,6},{6,2},{3,7},{7,3},{8,12},{12,8},{9,1... | collective-permute-start | bytes 2949128 | tf_op jit(solution)/shard_map/ppermute | solution.py:95
  362.9 241.2 %reduce-scatter.4.cloned.1.call-start = ((), (), s32[]{:S(2)}) async-start(), calls=%async_computation.6 | async-start | bytes 13369344 | tf_op jit(solution)/shard_map/reduce_scatter | solution.py:329
  367.1 43.5 %copy-start.2 = (bf16[4096,1280]{1,0:T(8,128)(2,1)}, bf16[4096,1280]{1,0:T(8,128)(2,1)S(1)}, u32[]{:S(2)}) copy-start(bf16[4096,1280]{1,0:T(8,128)(2,1)S(1)} %convolution_convert_fusion.2) | copy-start | bytes 31457284
  463.8 325.1 %reduce-scatter.6.cloned.1.call-start = ((), (), s32[]{:S(2)}) async-start(), calls=%async_computation.7 | async-start | bytes 14483456 | tf_op jit(solution)/shard_map/reduce_scatter | solution.py:367
  490.2 110.6 %collective-permute-start.18 = (bf16[192,1280]{1,0:T(8,128)(2,1)}, bf16[192,1280]{1,0:T(8,128)(2,1)}, u32[]{:S(2)}, u32[]{:S(2)}) collective-permute-start(bf16[192,1280]{1,0:T(8,128)(2,1)} %get-tuple-element.164), channel_id=1, source_target_pairs={{0,4},{4,0},{1,5},{5,1},{2,6},{6,2},{3,7},{7,3},{8,12},{12,8},{9,1... | collective-permute-start | bytes 1474568 | tf_op jit(solution)/shard_map/ppermute | solution.py:95
  491.6 109.1 %collective-permute-start.19 = (bf16[192,1280]{1,0:T(8,128)(2,1)}, bf16[192,1280]{1,0:T(8,128)(2,1)}, u32[]{:S(2)}, u32[]{:S(2)}) collective-permute-start(bf16[192,1280]{1,0:T(8,128)(2,1)} %get-tuple-element.163), channel_id=1, source_target_pairs={{0,4},{4,0},{1,5},{5,1},{2,6},{6,2},{3,7},{7,3},{8,12},{12,8},{9,1... | collective-permute-start | bytes 1474568 | tf_op jit(solution)/shard_map/ppermute | solution.py:95
  492.2 108.6 %collective-permute-start.20 = (bf16[192,1280]{1,0:T(8,128)(2,1)}, bf16[192,1280]{1,0:T(8,128)(2,1)}, u32[]{:S(2)}, u32[]{:S(2)}) collective-permute-start(bf16[192,1280]{1,0:T(8,128)(2,1)} %get-tuple-element.162), channel_id=1, source_target_pairs={{0,4},{4,0},{1,5},{5,1},{2,6},{6,2},{3,7},{7,3},{8,12},{12,8},{9,1... | collective-permute-start | bytes 1474568 | tf_op jit(solution)/shard_map/ppermute | solution.py:95
  493.6 38.9 %copy-start.77 = (s32[1280]{0:T(1024)S(1)}, s32[1280]{0:T(1024)}, u32[]{:S(2)}) copy-start(s32[1280]{0:T(1024)} %copy-done.76) | copy-start | bytes 15364
  493.6 107.1 %collective-permute-start.21 = (bf16[192,1280]{1,0:T(8,128)(2,1)}, bf16[192,1280]{1,0:T(8,128)(2,1)}, u32[]{:S(2)}, u32[]{:S(2)}) collective-permute-start(bf16[192,1280]{1,0:T(8,128)(2,1)} %get-tuple-element.161), channel_id=1, source_target_pairs={{0,4},{4,0},{1,5},{5,1},{2,6},{6,2},{3,7},{7,3},{8,12},{12,8},{9,1... | collective-permute-start | bytes 1474568 | tf_op jit(solution)/shard_map/ppermute | solution.py:95
  604.1 473.4 %reduce-scatter.8.cloned.1.call-start = ((), (), s32[]{:S(2)}) async-start(), calls=%async_computation.8 | async-start | bytes 3981312 | tf_op jit(solution)/shard_map/reduce_scatter | solution.py:440
  646.0 87.1 %copy-start.18 = (bf16[1536,2560]{1,0:T(8,128)(2,1)S(1)}, bf16[1536,2560]{1,0:T(8,128)(2,1)}, u32[]{:S(2)}) copy-start(bf16[1536,2560]{1,0:T(8,128)(2,1)} %fusion.27) | copy-start | bytes 23592964
  648.5 24.7 %collective-permute-start.22 = (bf16[192,2560]{1,0:T(8,128)(2,1)S(1)}, bf16[192,2560]{1,0:T(8,128)(2,1)S(1)}, u32[]{:S(2)}, u32[]{:S(2)}) collective-permute-start(bf16[192,2560]{1,0:T(8,128)(2,1)S(1)} %get-tuple-element.154), channel_id=1, source_target_pairs={{0,4},{4,0},{1,5},{5,1},{2,6},{6,2},{3,7},{7,3},{8,12},{12,8},{9,1... | collective-permute-start | bytes 2949128 | tf_op jit(solution)/shard_map/ppermute | solution.py:95
  649.1 45.2 %collective-permute-start.23 = (bf16[192,2560]{1,0:T(8,128)(2,1)S(1)}, bf16[192,2560]{1,0:T(8,128)(2,1)S(1)}, u32[]{:S(2)}, u32[]{:S(2)}) collective-permute-start(bf16[192,2560]{1,0:T(8,128)(2,1)S(1)} %get-tuple-element.153), channel_id=1, source_target_pairs={{0,4},{4,0},{1,5},{5,1},{2,6},{6,2},{3,7},{7,3},{8,12},{12,8},{9,1... | collective-permute-start | bytes 2949128 | tf_op jit(solution)/shard_map/ppermute | solution.py:95
  650.6 64.7 %collective-permute-start.24 = (bf16[192,2560]{1,0:T(8,128)(2,1)S(1)}, bf16[192,2560]{1,0:T(8,128)(2,1)S(1)}, u32[]{:S(2)}, u32[]{:S(2)}) collective-permute-start(bf16[192,2560]{1,0:T(8,128)(2,1)S(1)} %get-tuple-element.152), channel_id=1, source_target_pairs={{0,4},{4,0},{1,5},{5,1},{2,6},{6,2},{3,7},{7,3},{8,12},{12,8},{9,1... | collective-permute-start | bytes 2949128 | tf_op jit(solution)/shard_map/ppermute | solution.py:95
  651.2 82.0 %collective-permute-start.25 = (bf16[192,2560]{1,0:T(8,128)(2,1)S(1)}, bf16[192,2560]{1,0:T(8,128)(2,1)S(1)}, u32[]{:S(2)}, u32[]{:S(2)}) collective-permute-start(bf16[192,2560]{1,0:T(8,128)(2,1)S(1)} %get-tuple-element.151), channel_id=1, source_target_pairs={{0,4},{4,0},{1,5},{5,1},{2,6},{6,2},{3,7},{7,3},{8,12},{12,8},{9,1... | collective-permute-start | bytes 2949128 | tf_op jit(solution)/shard_map/ppermute | solution.py:95
  652.7 83.1 %collective-permute-start.26 = (bf16[192,1280]{1,0:T(8,128)(2,1)S(1)}, bf16[192,1280]{1,0:T(8,128)(2,1)}, u32[]{:S(2)}, u32[]{:S(2)}) collective-permute-start(bf16[192,1280]{1,0:T(8,128)(2,1)S(1)} %get-tuple-element.114), channel_id=1, source_target_pairs={{0,8},{8,16},{16,24},{24,0},{1,9},{9,17},{17,25},{25,1},{2,10},{10... | collective-permute-start | bytes 1474568 | tf_op jit(solution)/shard_map/ppermute | solution.py:235
  673.2 62.5 %collective-permute-start.27 = (bf16[192,1280]{1,0:T(8,128)(2,1)S(1)}, bf16[192,1280]{1,0:T(8,128)(2,1)}, u32[]{:S(2)}, u32[]{:S(2)}) collective-permute-start(bf16[192,1280]{1,0:T(8,128)(2,1)S(1)} %get-tuple-element.115), channel_id=1, source_target_pairs={{0,16},{8,24},{16,0},{24,8},{1,17},{9,25},{17,1},{25,9},{2,18},{10... | collective-permute-start | bytes 1474568 | tf_op jit(solution)/shard_map/ppermute | solution.py:235
  694.3 41.4 %collective-permute-start.28 = (bf16[192,1280]{1,0:T(8,128)(2,1)S(1)}, bf16[192,1280]{1,0:T(8,128)(2,1)}, u32[]{:S(2)}, u32[]{:S(2)}) collective-permute-start(bf16[192,1280]{1,0:T(8,128)(2,1)S(1)} %get-tuple-element.116), channel_id=1, source_target_pairs={{0,24},{8,0},{16,8},{24,16},{1,25},{9,1},{17,9},{25,17},{2,26},{10... | collective-permute-start | bytes 1474568 | tf_op jit(solution)/shard_map/ppermute | solution.py:235
  798.3 19.6 %copy-start.68 = (f32[2,3,1024]{2,1,0:T(4,128)S(1)}, f32[2,3,1024]{2,1,0:T(4,128)}, u32[]{:S(2)}) copy-start(f32[2,3,1024]{2,1,0:T(4,128)} %copy-done.67) | copy-start | bytes 73732
  798.4 19.6 %copy-start.73 = (f32[2,3,1024]{2,1,0:T(4,128)S(1)}, f32[2,3,1024]{2,1,0:T(4,128)}, u32[]{:S(2)}) copy-start(f32[2,3,1024]{2,1,0:T(4,128)} %copy-done.72) | copy-start | bytes 73732
  798.4 19.6 %copy-start.64 = (bf16[192,2560]{1,0:T(8,128)(2,1)S(1)}, bf16[192,2560]{1,0:T(8,128)(2,1)}, u32[]{:S(2)}) copy-start(bf16[192,2560]{1,0:T(8,128)(2,1)} %get-tuple-element.118) | copy-start | bytes 2949124
  798.4 25.9 %copy-start.21 = (bf16[256,1536]{1,0:T(8,128)(2,1)S(1)}, bf16[256,1536]{1,0:T(8,128)(2,1)}, u32[]{:S(2)}) copy-start(bf16[256,1536]{1,0:T(8,128)(2,1)} %copy-done.20) | copy-start | bytes 2359300
  799.3 18.4 %collective-permute-start.29 = (bf16[256,1536]{1,0:T(8,128)(2,1)S(1)}, bf16[256,1536]{1,0:T(8,128)(2,1)S(1)}, u32[]{:S(2)}, u32[]{:S(2)}) collective-permute-start(bf16[256,1536]{1,0:T(8,128)(2,1)S(1)} %get-tuple-element.139), channel_id=1, source_target_pairs={{0,2},{1,3},{2,0},{3,1},{4,6},{5,7},{6,4},{7,5},{8,10},{9,11},{10,... | collective-permute-start | bytes 2359304 | tf_op jit(solution)/shard_map/ppermute | solution.py:95
  817.8 8.8 collective-permute-start.30
  818.0 67.9 %collective-permute-start.31 = (bf16[192,2560]{1,0:T(8,128)(2,1)S(1)}, bf16[192,2560]{1,0:T(8,128)(2,1)}, u32[]{:S(2)}, u32[]{:S(2)}) collective-permute-start(bf16[192,2560]{1,0:T(8,128)(2,1)S(1)} %copy-done.64), channel_id=1, source_target_pairs={{0,16},{8,24},{16,0},{24,8},{1,17},{9,25},{17,1},{25,9},{2,18},{10... | collective-permute-start | bytes 2949128 | tf_op jit(solution)/shard_map/ppermute | solution.py:235
  820.5 97.6 %collective-permute-start.32 = (bf16[192,2560]{1,0:T(8,128)(2,1)}, bf16[192,2560]{1,0:T(8,128)(2,1)}, u32[]{:S(2)}, u32[]{:S(2)}) collective-permute-start(bf16[192,2560]{1,0:T(8,128)(2,1)} %get-tuple-element.120), channel_id=1, source_target_pairs={{0,8},{8,16},{16,24},{24,0},{1,9},{9,17},{17,25},{25,1},{2,10},{10... | collective-permute-start | bytes 2949128 | tf_op jit(solution)/shard_map/ppermute | solution.py:235
  821.1 96.9 %collective-permute-start.33 = (bf16[192,2560]{1,0:T(8,128)(2,1)}, bf16[192,2560]{1,0:T(8,128)(2,1)}, u32[]{:S(2)}, u32[]{:S(2)}) collective-permute-start(bf16[192,2560]{1,0:T(8,128)(2,1)} %get-tuple-element.121), channel_id=1, source_target_pairs={{0,24},{8,0},{16,8},{24,16},{1,25},{9,1},{17,9},{25,17},{2,26},{10... | collective-permute-start | bytes 2949128 | tf_op jit(solution)/shard_map/ppermute | solution.py:235
  889.5 28.5 %copy-start.58 = (bf16[1024,2,64]{0,2,1:T(8,128)(2,1)S(1)}, bf16[1024,2,64]{0,2,1:T(8,128)(2,1)}, u32[]{:S(2)}) copy-start(bf16[1024,2,64]{0,2,1:T(8,128)(2,1)} %copy-done.57) | copy-start | bytes 786436
  931.6 14.2 %copy-start.28 = (f32[1024,2,64]{0,2,1:T(8,128)S(1)}, f32[1024,2,64]{0,2,1:T(8,128)}, u32[]{:S(2)}) copy-start(f32[1024,2,64]{0,2,1:T(8,128)} %fusion.68) | copy-start | bytes 1572868
  990.3 63.3 %collective-permute-start.34 = (bf16[2,256,1536]{2,1,0:T(8,128)(2,1)}, bf16[2,256,1536]{2,1,0:T(8,128)(2,1)}, u32[]{:S(2)}, u32[]{:S(2)}) collective-permute-start(bf16[2,256,1536]{2,1,0:T(8,128)(2,1)} %dynamic-slice_bitcast_fusion), channel_id=1, source_target_pairs={{0,1},{1,0},{2,3},{3,2},{4,5},{5,4},{6,7},{7,6},{8,9},{9,8},{10,11... | collective-permute-start | bytes 4718600 | tf_op jit(solution)/shard_map/ppermute | solution.py:95
  1056.2 20.0 %collective-permute-start.35 = (bf16[256,1536]{1,0:T(8,128)(2,1)S(1)}, bf16[256,1536]{1,0:T(8,128)(2,1)S(1)}, u32[]{:S(2)}, u32[]{:S(2)}) collective-permute-start(bf16[256,1536]{1,0:T(8,128)(2,1)S(1)} %fusion.86), channel_id=1, source_target_pairs={{0,2},{1,3},{2,0},{3,1},{4,6},{5,7},{6,4},{7,5},{8,10},{9,11},{10,... | collective-permute-start | bytes 2359304 | tf_op jit(solution)/shard_map/ppermute | solution.py:95
  1064.0 18.7 %copy-start.7 = (bf16[256,1536]{1,0:T(8,128)(2,1)S(1)}, bf16[256,1536]{1,0:T(8,128)(2,1)}, u32[]{:S(2)}) copy-start(bf16[256,1536]{1,0:T(8,128)(2,1)} %param.14) | copy-start | bytes 2359300
  1078.5 13.5 %collective-permute-start.36 = (f32[42,192]{1,0:T(8,128)S(1)}, f32[42,192]{1,0:T(8,128)S(1)}, u32[]{:S(2)}, u32[]{:S(2)}) collective-permute-start(f32[42,192]{1,0:T(8,128)S(1)} %bitcast.387), channel_id=1, source_target_pairs={{0,1},{1,2},{2,3},{3,0},{4,5},{5,6},{6,7},{7,4},{8,9},{9,10},{10,1... | collective-permute-start | bytes 96776 | tf_op jit(solution)/shard_map/ppermute | solution.py:176
  1078.5 13.5 %collective-permute-start.37 = (f32[42,192]{1,0:T(8,128)S(1)}, f32[42,192]{1,0:T(8,128)S(1)}, u32[]{:S(2)}, u32[]{:S(2)}) collective-permute-start(f32[42,192]{1,0:T(8,128)S(1)} %bitcast.388), channel_id=1, source_target_pairs={{0,2},{1,3},{2,0},{3,1},{4,6},{5,7},{6,4},{7,5},{8,10},{9,11},{10,... | collective-permute-start | bytes 96776 | tf_op jit(solution)/shard_map/ppermute | solution.py:176
  1080.2 14.8 %collective-permute-start.38 = (f32[42,192]{1,0:T(8,128)S(1)}, f32[42,192]{1,0:T(8,128)S(1)}, u32[]{:S(2)}, u32[]{:S(2)}) collective-permute-start(f32[42,192]{1,0:T(8,128)S(1)} %bitcast.389), channel_id=1, source_target_pairs={{0,3},{1,0},{2,1},{3,2},{4,7},{5,4},{6,5},{7,6},{8,11},{9,8},{10,9... | collective-permute-start | bytes 96776 | tf_op jit(solution)/shard_map/ppermute | solution.py:176
  1085.2 12.6 %copy-start.1 = (s32[1024,8]{0,1:T(8,128)S(1)}, s32[1024,8]{0,1:T(8,128)}, u32[]{:S(2)}) copy-start(s32[1024,8]{0,1:T(8,128)} %param.17) | copy-start | bytes 98308
  (66 other events, 280.8 us)
Sparse Core Ops, SparseCore 0:
  11.7 67.3 all-gather.3
  227.1 135.7 all-gather.5
  365.2 98.5 all-gather.7
  467.7 133.1 reduce-scatter.3
  604.9 184.0 reduce-scatter.5
  963.5 77.5 reduce-scatter.7

commit v5 on v4

--- a/solution.py
+++ b/solution.py
@@ -146,17 +146,18 @@
             return (parts[0].astype(f32) + swap(parts[1], "o", 2, 1).astype(f32)).astype(bf16)
         return lax.psum_scatter(parts, "o", scatter_dimension=0, tiled=False)
 
-    def gather_t(block):
+    def gather_t(block, hold=()):
         if n_tensor != 4:
-            return lax.all_gather(block, "t", axis=0, tiled=True)
+            return tie(lax.all_gather(block, "t", axis=0, tiled=True), hold)
         rows, width = block.shape
         me_t = lax.axis_index("t")
         result = jnp.zeros((n_tensor * rows, width), block.dtype)
         pair = jnp.concatenate([block, swap(block, "t", n_tensor, 2)], axis=0)
+        pair, hold = tie(pair, hold)
         for bit, part in ((0, pair), (1, swap(pair, "t", n_tensor, 1))):
             result = put(result, part[:rows], (me_t ^ bit) * rows, 0)
             result = put(result, part[rows:], (me_t ^ bit ^ 2) * rows, 0)
-        return result
+        return result, hold
 
     def scatter_t(values):
         if n_tensor != 4:
@@ -216,7 +217,7 @@
         )
         pack = jnp.concatenate([w_query, w_key, w_value, w_out.T, side], axis=1)
         packed = lax.all_gather(pack, dp, axis=0, tiled=True)
-        tokens_all = gather_t(tokens)
+        tokens_all, _ = gather_t(tokens)
 
         def expert_piece(target):
             first = target * own_experts
@@ -237,8 +238,7 @@
         pieces = [expert_piece((me_i + shift) % inner) for shift in range(inner)]
         pieces, packed = tie(pieces, packed)
         tokens_all = tokens_all.astype(f32)
-        far_down = to_owner(pieces[2][1], 2)
-        near = to_owner(pieces[1], 1)
+        far_gate_up = to_owner(pieces[2][0], 2)
         owned = [pass_on(pieces[0])]
 
         w_qkv = packed[:, :qkv_cols]
@@ -256,15 +256,16 @@
             qkv[:, q_cols : q_cols + k_cols].reshape(group, -1, HEAD_DIM), cosine, sine
         ).astype(bf16)
         values = qkv[:, q_cols + k_cols :].astype(bf16).reshape(group, -1, HEAD_DIM)
-        query, keys, values, far_down = tie(query, keys, values, far_down)
         attended, log_total = attend_forward(query, keys, values, prefix[0])
-        far_piece, near, owned[0], attended = tie(pieces[2][0], near, owned[0], attended)
-        far_gate_up = to_owner(far_piece, 2)
+        far_down, near, far_gate_up, owned[0], attended = tie(
+            pieces[2][1], pieces[1], far_gate_up, owned[0], attended
+        )
+        far_down, near = to_owner(far_down, 2), to_owner(near, 1)
         branch = lax.dot_general(
             attended, w_out_t, (((1,), (1,)), ((), ())), preferred_element_type=f32
         ).astype(bf16)
         tokens_f = tokens.astype(f32)
-        branch = scatter_t(branch)
+        branch, far_down = tie(scatter_t(branch), far_down)
         middle = tokens_f + branch
         scale_two = rms_scale(middle)
         normed_two = (middle * scale_two * gain_two).astype(bf16)
@@ -285,7 +286,7 @@
             ],
             axis=1,
         )
-        last, near, far_gate_up, shipped = tie(pieces[3], near, far_gate_up, shipped)
+        last, near, shipped = tie(pieces[3], near, shipped)
         last = to_owner(last, 3)
         owned += [pass_on(near), pass_on((far_gate_up, far_down)), pass_on(last)]
         shared_all = by_rows(lax.all_gather(by_rows(shipped), shared, axis=0, tiled=True))
@@ -355,24 +356,32 @@
             ],
             axis=1,
         )
+        products, grad_gate_up, down_sums = tie(
+            (silu_g * up_part * cot_part).astype(bf16), grad_gate_up, down_sums
+        )
+        sent_down = down_sums[:1] + [to_owner(down_sums[s], s) for s in range(1, inner)]
         chosen = (jnp.arange(side_cols, dtype=jnp.int32)[None, :] == owner.T).astype(bf16)
-        gate_block = jnp.dot(
-            (silu_g * up_part * cot_part).astype(bf16), chosen, preferred_element_type=f32
-        )
+        gate_block = jnp.dot(products, chosen, preferred_element_type=f32)
         grad_normed_part = lax.dot_general(
             grad_gate_up, w_gate_up, (((1,), (1,)), ((), ())), preferred_element_type=f32
         )
         grad_shipped = jnp.concatenate([grad_normed_part, gate_block], axis=1).astype(bf16)
-        grad_shipped, down_sums, expert_share = tie(by_rows(grad_shipped), down_sums, expert_share)
+        grad_shipped, sent_down, expert_share = tie(by_rows(grad_shipped), sent_down, expert_share)
         grad_back = lax.psum_scatter(grad_shipped, shared, scatter_dimension=0, tiled=True)
         shared_rows, _ = tie(shared_all, grad_shipped)
         grad_w_gate_up = lax.dot_general(
             shared_rows[:, :width], grad_gate_up, contract_rows, preferred_element_type=f32
         ).astype(bf16)
         gate_up_sums = to_sum(grad_w_gate_up)
-        sent_down = down_sums[:1] + [to_owner(down_sums[s], s) for s in range(1, inner)]
-        gate_up_sums, sent_down, grad_back = tie(gate_up_sums, sent_down, grad_back)
-        sent_gate_up = gate_up_sums[:1] + [to_owner(gate_up_sums[s], s) for s in range(1, inner)]
+        grad_down = jnp.zeros((n_experts, hidden, depth), f32)
+        for shift in range(inner):
+            part = sent_down[shift].reshape(depth, own_experts, hidden).transpose(1, 2, 0)
+            grad_down = put(
+                grad_down, part.astype(f32), (me_i - shift) % inner * own_experts, 0, 0
+            )
+        gate_up_sums, grad_down, grad_back = tie(gate_up_sums, grad_down, grad_back)
+        far_sum_gate, far_sum_up = jnp.split(gate_up_sums[2], 2, axis=1)
+        sent_gate_up = {0: jnp.split(gate_up_sums[0], 2, axis=1)}
         mixed = (middle + from_owner_order(expert_share).astype(f32)).astype(bf16)
 
         grad_back = grad_back.astype(f32)
@@ -391,21 +400,37 @@
         grad_router_part = lax.dot_general(
             normed_two.astype(f32), grad_logits, contract_rows, precision=HIGHEST
         )
-        grad_branch = gather_t(grad_middle.astype(bf16))
+        sent_gate = to_owner(far_sum_gate, 2)
+        grad_branch, (sent_gate, far_sum_up) = gather_t(
+            grad_middle.astype(bf16), (sent_gate, far_sum_up)
+        )
+        sent_up = to_owner(far_sum_up, 2)
         grad_out_part = lax.dot_general(
             grad_branch, attended, contract_rows, preferred_element_type=f32
         ).astype(bf16)
-        grad_out_part, sent_gate_up[2], grad_branch = tie(
-            grad_out_part, sent_gate_up[2], grad_branch
-        )
+        grad_out_part, grad_branch, near_sum, sent_up = tie(
+            grad_out_part, grad_branch, gate_up_sums[1], sent_up
+        )
+        sent_gate_up[2] = (sent_gate, sent_up)
+        sent_gate_up[1] = to_owner(near_sum, 1)
         grad_attended = jnp.dot(
             grad_branch, w_out_t, preferred_element_type=f32
         ).astype(bf16)
-        sent_near = (sent_gate_up[1], sent_gate_up[3])
-        grad_query, grad_keys, grad_values, sent_near = attend_backward(
-            query, keys, values, grad_attended, log_total, prefix[0], sent_near
-        )
-        sent_gate_up[1], sent_gate_up[3] = sent_near
+        grad_query, grad_keys, grad_values, (sent_gate_up[1], last_sum) = attend_backward(
+            query,
+            keys,
+            values,
+            grad_attended,
+            log_total,
+            prefix[0],
+            (sent_gate_up[1], gate_up_sums[3]),
+        )
+        sent_gate_up[3] = to_owner(last_sum, 3)
+        grad_query, grad_keys, grad_values, sent_gate_up[3] = tie(
+            grad_query, grad_keys, grad_values, sent_gate_up[3]
+        )
+        for shift in (1, 3):
+            sent_gate_up[shift] = jnp.split(sent_gate_up[shift], 2, axis=1)
         grad_qkv = jnp.concatenate(
             [
                 rotate(grad_query, cosine, -sine).astype(bf16).reshape(group, -1),
@@ -438,24 +463,25 @@
             axis=1,
         )
         shard_attn = lax.psum_scatter(by_rows(grad_attn), dp, scatter_dimension=0, tiled=True)
-        shard_attn, own_grad_one = tie(shard_attn, own_grad_one)
         shard_attn = shard_attn.astype(f32)
         grad_input_part, _ = norm_backward(tokens_f, rms_scale(tokens_f), gain_one, own_grad_one)
         grad_tokens = grad_middle + grad_input_part
         side_sum = shard_attn[:, attn_cols : attn_cols + 2 * n_experts + 4]
         side_sum = sum_tensor(jnp.sum(side_sum.reshape(depth, 2, -1), axis=1).T)
 
+        sent_gate_up[1], sent_gate_up[3], own_grad_one = tie(
+            sent_gate_up[1], sent_gate_up[3], own_grad_one
+        )
         grad_gate = jnp.zeros((n_experts, depth, hidden), f32)
-        grad_up, grad_down = grad_gate, jnp.zeros((n_experts, hidden, depth), f32)
+        grad_up = grad_gate
         for shift in range(inner):
             start = (me_i - shift) % inner * own_experts
-            part = sent_down[shift]
-            part = part.reshape(depth, own_experts, hidden).transpose(1, 2, 0)
-            grad_down = put(grad_down, part.astype(f32), start, 0, 0)
-            part = sent_gate_up[shift]
-            part = part.reshape(depth, 2, own_experts, hidden).transpose(1, 2, 0, 3).astype(f32)
-            grad_gate = put(grad_gate, part[0], start, 0, 0)
-            grad_up = put(grad_up, part[1], start, 0, 0)
+            gate, up = (
+                jnp.swapaxes(part.reshape(depth, own_experts, hidden), 0, 1).astype(f32)
+                for part in sent_gate_up[shift]
+            )
+            grad_gate = put(grad_gate, gate, start, 0, 0)
+            grad_up = put(grad_up, up, start, 0, 0)
         return (
             mixed,
             grad_tokens,

time: 1120 us -> 1030 us (0.920)
  waiting for transfers between devices: 414 us -> 355 us
  matrix products: 334 us -> 315 us
  local copies, waits for them, and re-layouts: 192 us -> 178 us
    ppermute x24, waiting for transfers between devices: 174 us -> 132 us  [swap(): return lax.ppermute(values, axis, [(m, m ^ bit) for m in range(size)])]
    reduce_scatter x1, waiting for transfers between devices: 53.2 us -> 12 us  [on_device(): lax.psum_scatter(grad_shipped, shared, scatter_dimension=0, tiled=True)]
    squeeze x12 -> x0, local copies, waits for them, and re-layouts: 35.6 us -> none  [the longest x8 24.8 us: on_device(): grad_up = put(grad_up, part[1], start, 0, 0)]
    concatenate x0 -> x1, other arithmetic: none -> 19.3 us  [on_device(): jnp.concatenate([(grad_act * up_part * sigmoid_g * (1.0 + gate_part * (1....]
    dot_general x1, matrix products: 16.3 us -> 3.98 us  [on_device(): gate_block = jnp.dot(products, chosen, preferred_element_type=f32)]
    reduce_scatter x1, waiting for transfers between devices: 0.01 us -> 12.2 us  [on_device(): lax.psum_scatter(expert_part, shared, scatter_dimension=0, tiled=True)]
    convert_element_type x12 -> x24, local copies, waits for them, and re-layouts: 30.7 us -> 38.1 us  [the longest x16 30.6 us: on_device(): jnp.swapaxes(part.reshape(depth, own_experts, hidden), 0, 1).astype(f32)]
    ppermute x12 -> x13, waiting for transfers between devices: 118 us -> 123 us  [to_owner(): return jax.tree.map(lambda part: lax.ppermute(part, 'i', pairs), piece)]
  transfers between devices with their start and end apart: 45 -> 46, of which waited for: 19 -> 24; matrix products, arithmetic and copies ran while one was open for 48% -> 52% of each run, Pallas kernels for 0% -> 0%
where the time goes in v5:
time: 1030 us; the launch traced here: 1020 us
  waiting for transfers between devices  355 us (34%)
  matrix products  315 us (31%)
  local copies, waits for them, and re-layouts  178 us (17%)
  other arithmetic  107 us (10%)
  starting transfers between devices  44.9 us (4%)
  between operations  16.9 us (2%)
    ppermute x24, waiting for transfers between devices, swap(): return lax.ppermute(values, axis, [(m, m ^ bit) for m in range(size)])  132 us
    ppermute x13, waiting for transfers between devices, to_owner(): return jax.tree.map(lambda part: lax.ppermute(part, 'i', pairs), piece)  123 us
    dot_general x1, matrix products, on_device(): jnp.dot(normed_all, w_gate_up, preferred_element_type=f32).astype(bf16)  43.5 us
    dot_general x1, matrix products, on_device(): lax.dot_general(shared_rows[:, :width], grad_gate_up, contract_rows, pref...  40 us
    dot_general x1, matrix products, on_device(): lax.dot_general(grad_gate_up, w_gate_up, (((1,), (1,)), ((), ())), prefer...  38.3 us
    dot_general x1, matrix products, on_device(): cot_part = jnp.dot(cot_all, w_down_t, preferred_element_type=f32)  37.9 us
    sub x1, matrix products, attend_backward(): grad_weights - jnp.sum(weights * grad_weights, axis=-1, keepdims=True)  35 us
    convert_element_type x16, local copies, waits for them, and re-layouts, on_device(): jnp.swapaxes(part.reshape(depth, own_experts, hidden), 0, 1).astype(f32)  30.6 us
  transfers between devices with their start and end apart: 46, of which 24 were waited for; matrix products, arithmetic and copies ran while one was open for 52% of the time, Pallas kernels for 0%

profile of v5, /device:TPU:0, one launch (start us, length us, event | category | flops | bytes accessed | tf_op | source)
XLA Modules:
  0.0 1017.4 jit_solution(166203472767394972)
XLA Ops:
  11.6 3.1 collective-permute-start.3
  14.7 4.0 dynamic-slice_bitcast_fusion.19
  49.1 29.9 %all-gather.4.cloned.1.call-done = bf16[1536,1152]{1,0:T(8,128)(2,1)} async-done(((bf16[192,1152]{1,0:T(8,128)(2,1)}), bf16[1536,1152]{1,0:T(8,128)(2,1)}) %all-gather.4.cloned.1.call-update) | async-done | bytes 3538960 | tf_op jit(solution)/shard_map/all_gather | solution.py:219
  80.9 3.9 fusion.50
  95.8 5.7 fusion.105
  101.6 3.8 fusion.3
  105.4 4.6 copy-done.2
  110.5 11.4 %fusion.57 = bf16[2,64,3,1024]{3,1,2,0:T(8,128)(2,1)} fusion(bf16[1024,2,64,1]{0,2,3,1:T(8,128)(2,1)S(1)} %bitcast.378, f32[2,3,1024,1024]{2,3,1,0:T(8,128)} %copy-done.2, f32[2,3,1024]{2,1,0:T(4,128)S(1)} %fusion.3, f32[2,3,1024]{2,1,0:T(4,128)S(1)} %get-tuple-element.226), kind=kOutput, calls=%fused_computation.113 | convolution fusion | flops 824573952 | bytes 26263552 | tf_op jit(solution)/shard_map/hgqk,khd->qhgd/dot_general | solution.py:65
  128.2 9.2 collective-permute-done
  137.4 3.1 convolution_convert_fusion.6
  143.4 3.7 collective-permute-done.5
  154.9 13.5 %copy.310 = bf16[192,2560]{1,0:T(8,128)(2,1)} copy(bf16[192,2560]{0,1:T(8,128)(2,1)S(1)} %copy-done.32) | data formatting | bytes 1966080 | tf_op jit(solution)/shard_map/optimization_barrier | solution.py:45
  168.4 3.7 collective-permute-start.8
  175.0 36.2 %collective-permute-done.7 = bf16[192,1280]{1,0:T(8,128)(2,1)S(1)} collective-permute-done((bf16[192,1280]{1,0:T(8,128)(2,1)}, bf16[192,1280]{1,0:T(8,128)(2,1)S(1)}, u32[]{:S(2)}, u32[]{:S(2)}) %collective-permute-start.7) | collective-permute-done | bytes 491552 | tf_op jit(solution)/shard_map/ppermute | solution.py:236
  228.8 3.7 broadcast_in_dim.123
  239.1 21.0 %collective-permute-done.16 = bf16[192,1280]{1,0:T(8,128)(2,1)} collective-permute-done((bf16[192,1280]{1,0:T(8,128)(2,1)}, bf16[192,1280]{1,0:T(8,128)(2,1)}, u32[]{:S(2)}, u32[]{:S(2)}) %collective-permute-start.16) | collective-permute-done | bytes 491552 | tf_op jit(solution)/shard_map/ppermute | solution.py:236
  263.0 21.9 %collective-permute-done.12 = bf16[192,2560]{1,0:T(8,128)(2,1)} collective-permute-done((bf16[192,2560]{1,0:T(8,128)(2,1)S(1)}, bf16[192,2560]{1,0:T(8,128)(2,1)}, u32[]{:S(2)}, u32[]{:S(2)}) %collective-permute-start.12) | collective-permute-done | bytes 983072 | tf_op jit(solution)/shard_map/ppermute | solution.py:236
  286.3 15.8 %collective-permute-done.17 = bf16[192,1280]{1,0:T(8,128)(2,1)S(1)} collective-permute-done((bf16[192,1280]{1,0:T(8,128)(2,1)}, bf16[192,1280]{1,0:T(8,128)(2,1)S(1)}, u32[]{:S(2)}, u32[]{:S(2)}) %collective-permute-start.17) | collective-permute-done | bytes 491552 | tf_op jit(solution)/shard_map/ppermute | solution.py:95
  303.3 3.4 fusion.39
  309.2 12.1 %collective-permute-done.13 = bf16[192,2560]{1,0:T(8,128)(2,1)S(1)} collective-permute-done((bf16[192,2560]{1,0:T(8,128)(2,1)}, bf16[192,2560]{1,0:T(8,128)(2,1)S(1)}, u32[]{:S(2)}, u32[]{:S(2)}) %collective-permute-start.13) | collective-permute-done | bytes 983072 | tf_op jit(solution)/shard_map/ppermute | solution.py:95
  323.9 28.9 %all-gather.6.cloned.1.call-done = bf16[4096,1664]{1,0:T(8,128)(2,1)} async-done(((bf16[256,1664]{1,0:T(8,128)(2,1)}), bf16[4096,1664]{1,0:T(8,128)(2,1)}) %all-gather.6.cloned.1.call-update) | async-done | bytes 13631504 | tf_op jit(solution)/shard_map/all_gather | solution.py:292
  353.0 4.1 convolution_convert_fusion.2
  357.1 43.5 %convolution_convert_fusion = bf16[4096,2560]{1,0:T(8,128)(2,1)} fusion(bf16[1536,2560]{1,0:T(8,128)(2,1)} %bitcast.66, bf16[4096,1664]{1,0:T(8,128)(2,1)} %all-gather.6.cloned.1.call-done), kind=kOutput, calls=%fused_computation.16 | convolution fusion | flops 32222740480 | bytes 41418752 | tf_op jit(solution)/shard_map/dot_general | solution.py:313
  400.6 11.6 %fusion.18 = bf16[4096,1280]{1,0:T(8,128)(2,1)S(1)} fusion(bf16[4096,1280]{1,0:T(8,128)(2,1)S(1)} %convolution_convert_fusion.2, bf16[4096,2560]{1,0:T(8,128)(2,1)} %convolution_convert_fusion), kind=kLoop, calls=%fused_computation.35 | loop fusion | flops 52428800 | bytes 41943040 | tf_op jit(solution)/shard_map/convert_element_type | solution.py:323
  412.2 4.0 copy-done.16
  416.2 20.8 %convolution_convert_fusion.1 = bf16[4096,1536]{1,0:T(8,128)(2,1)} fusion(bf16[4096,1280]{1,0:T(8,128)(2,1)S(1)} %fusion.18, bf16[1536,1280]{1,0:T(8,128)(2,1)} %bitcast.336), kind=kOutput, calls=%fused_computation.37 | convolution fusion | flops 16112418816 | bytes 27000832 | tf_op jit(solution)/shard_map/dot_general | solution.py:324
  437.0 16.8 %all-gather.8.cloned.1.call-done = bf16[4096,1536]{1,0:T(8,128)(2,1)} async-done(((bf16[256,1536]{1,0:T(8,128)(2,1)}), bf16[4096,1536]{1,0:T(8,128)(2,1)}) %all-gather.8.cloned.1.call-update) | async-done | bytes 12582928 | tf_op jit(solution)/shard_map/all_gather | solution.py:305
  453.8 22.7 %convolution_convert_fusion.4 = bf16[1536,1280]{1,0:T(8,128)(2,1)S(1)} fusion(bf16[4096,1536]{1,0:T(8,128)(2,1)} %all-gather.8.cloned.1.call-done, bf16[4096,1280]{1,0:T(8,128)(2,1)} %copy-done.16), kind=kOutput, calls=%fused_computation.52 | convolution fusion | flops 16108093440 | bytes 27000832 | tf_op jit(solution)/shard_map/dot_general | solution.py:332
  482.0 37.9 %fusion.13 = (bf16[4096,1280]{1,0:T(8,128)(2,1)}, bf16[4096,1280]{1,0:T(8,128)(2,1)}, bf16[4096,1280]{1,0:T(8,128)(2,1)}) fusion(bf16[4096,1280]{1,0:T(8,128)(2,1)} %copy-done.3, bf16[4096,2560]{1,0:T(8,128)(2,1)} %convolution_convert_fusion, bf16[4096,1536]{1,0:T(8,128)(2,1)} %all-gather.8.cloned.1.call-done, bf16[1536,1280]{1,0:T(8,128)(2,1)S(1)} %bitcast.337), kind=kOutput, calls=%fused_computation.27 | convolution fusion | flops 16210984960 | bytes 79429632 | tf_op jit(solution)/shard_map/dot_general | solution.py:347
  519.9 19.3 %pad_maximum_fusion = bf16[4096,2560]{1,0:T(8,128)(2,1)} fusion(bf16[4096,1280]{1,0:T(8,128)(2,1)} %get-tuple-element.168, bf16[4096,1280]{1,0:T(8,128)(2,1)} %get-tuple-element.167), kind=kLoop, calls=%fused_computation.32 | loop fusion | flops 41943040 | bytes 41943040 | tf_op jit(solution)/shard_map/concatenate | solution.py:350
  539.2 3.1 fusion.69
  547.0 4.0 convolution_convert_fusion.5
  550.9 38.3 %convolution_convert_fusion.3 = bf16[4096,1536]{1,0:T(8,128)(2,1)S(1)} fusion(bf16[4096,2560]{1,0:T(8,128)(2,1)} %pad_maximum_fusion, bf16[1536,2560]{1,0:T(8,128)(2,1)} %bitcast.66), kind=kOutput, calls=%fused_computation.39 | convolution fusion | flops 32218546176 | bytes 41418752 | tf_op jit(solution)/shard_map/dot_general | solution.py:365
  589.3 7.3 pad_maximum_fusion.1
  596.6 12.2 %reduce-scatter.4.cloned.1.call-done = bf16[256,1536]{1,0:T(8,128)(2,1)} async-done(((bf16[4096,1536]{1,0:T(8,128)(2,1)}), bf16[256,1536]{1,0:T(8,128)(2,1)}) %reduce-scatter.4.cloned.1.call-update) | async-done | bytes 786448 | tf_op jit(solution)/shard_map/reduce_scatter | solution.py:330
  609.1 40.0 %fusion.27 = bf16[1536,2560]{1,0:T(8,128)(2,1)S(1)} fusion(bf16[4096,2560]{1,0:T(8,128)(2,1)} %pad_maximum_fusion, bf16[4096,1664]{1,0:T(8,128)(2,1)} %all-gather.6.cloned.1.call-done), kind=kOutput, calls=%fused_computation.47 | convolution fusion | flops 32216186880 | bytes 41418752 | tf_op jit(solution)/shard_map/dot_general | solution.py:372
  651.0 3.2 copy-done.19
  672.3 6.8 collective-permute-done.25
  679.1 21.1 %collective-permute-done.26 = bf16[192,2560]{1,0:T(8,128)(2,1)} collective-permute-done((bf16[192,2560]{1,0:T(8,128)(2,1)}, bf16[192,2560]{1,0:T(8,128)(2,1)}, u32[]{:S(2)}, u32[]{:S(2)}) %collective-permute-start.26) | collective-permute-done | bytes 983072 | tf_op jit(solution)/shard_map/ppermute | solution.py:95
  700.2 21.1 %collective-permute-done.27 = bf16[192,2560]{1,0:T(8,128)(2,1)} collective-permute-done((bf16[192,2560]{1,0:T(8,128)(2,1)}, bf16[192,2560]{1,0:T(8,128)(2,1)}, u32[]{:S(2)}, u32[]{:S(2)}) %collective-permute-start.27) | collective-permute-done | bytes 983072 | tf_op jit(solution)/shard_map/ppermute | solution.py:95
  721.3 19.8 %collective-permute-done.28 = bf16[192,2560]{1,0:T(8,128)(2,1)} collective-permute-done((bf16[192,2560]{1,0:T(8,128)(2,1)}, bf16[192,2560]{1,0:T(8,128)(2,1)}, u32[]{:S(2)}, u32[]{:S(2)}) %collective-permute-start.28) | collective-permute-done | bytes 983072 | tf_op jit(solution)/shard_map/ppermute | solution.py:95
  741.1 6.0 fusion.42
  747.1 12.0 %reduce-scatter.6.cloned.1.call-done = bf16[256,1664]{1,0:T(8,128)(2,1)} async-done(((bf16[4096,1664]{1,0:T(8,128)(2,1)}), bf16[256,1664]{1,0:T(8,128)(2,1)}) %reduce-scatter.6.cloned.1.call-update) | async-done | bytes 851984 | tf_op jit(solution)/shard_map/reduce_scatter | solution.py:370
  763.8 3.0 copy.341
  767.9 2.9 multiply_reduce_fusion
  774.6 15.2 %collective-permute-done.29 = bf16[256,1536]{1,0:T(8,128)(2,1)S(1)} collective-permute-done((bf16[256,1536]{1,0:T(8,128)(2,1)S(1)}, bf16[256,1536]{1,0:T(8,128)(2,1)S(1)}, u32[]{:S(2)}, u32[]{:S(2)}) %collective-permute-start.29) | collective-permute-done | bytes 786464 | tf_op jit(solution)/shard_map/ppermute | solution.py:95
  790.0 6.3 collective-permute-done.30
  799.8 2.9 convolution_convert_fusion.8
  802.7 20.4 %collective-permute-done.32 = bf16[192,1280]{1,0:T(8,128)(2,1)S(1)} collective-permute-done((bf16[192,1280]{1,0:T(8,128)(2,1)S(1)}, bf16[192,1280]{1,0:T(8,128)(2,1)S(1)}, u32[]{:S(2)}, u32[]{:S(2)}) %collective-permute-start.32) | collective-permute-done | bytes 491552 | tf_op jit(solution)/shard_map/ppermute | solution.py:236
  823.1 2.9 convolution_convert_fusion.9
  826.1 35.0 %fusion.2 = bf16[2,3,1024,1024]{2,3,1,0:T(8,128)(2,1)} fusion(f32[2,3,1024,1024]{2,3,1,0:T(8,128)} %copy-done.2, f32[2,3,1024]{2,1,0:T(4,128)S(1)} %log_add_fusion, bf16[1024,2,64,1]{0,2,3,1:T(8,128)(2,1)S(1)} %bitcast.379, bf16[1024,2,3,64]{0,3,2,1:T(8,128)(2,1)S(1)} %bitcast.369), kind=kOutput, calls=%fused_computation.11 | convolution fusion | flops 1648368640 | bytes 38821888 | tf_op jit(solution)/shard_map/sub | solution.py:78
  861.1 10.9 %fusion.58 = bf16[1024,2,64]{0,2,1:T(8,128)(2,1)} fusion(bf16[1024,2,3,64]{0,3,2,1:T(8,128)(2,1)S(1)} %bitcast.370, f32[2,3,1024,1024]{2,3,1,0:T(8,128)} %copy-done.2, f32[2,3,1024]{2,1,0:T(4,128)S(1)} %log_add_fusion), kind=kOutput, calls=%fused_computation.121 | convolution fusion | flops 817889280 | bytes 26238976 | tf_op jit(solution)/shard_map/hgqk,qhgd->khd/dot_general | solution.py:88
  872.0 3.6 collective-permute-start.34
  875.6 9.6 fusion.62
  885.2 3.4 convolution_multiply_fusion
  888.6 8.2 collective-permute-done.34
  897.3 4.6 fusion.36
  901.9 4.3 convolution_convert_fusion.7
  908.4 3.2 pad_maximum_fusion.2
  917.1 3.1 copy.329
  946.8 14.2 %collective-permute-done.36 = bf16[256,1536]{1,0:T(8,128)(2,1)S(1)} collective-permute-done((bf16[256,1536]{1,0:T(8,128)(2,1)S(1)}, bf16[256,1536]{1,0:T(8,128)(2,1)S(1)}, u32[]{:S(2)}, u32[]{:S(2)}) %collective-permute-start.36) | collective-permute-done | bytes 786464 | tf_op jit(solution)/shard_map/ppermute | solution.py:95
  970.0 2.7 copy.369
  974.0 2.8 copy.357
  979.2 2.7 copy.361
  (447 shorter events, 220.6 us)
Async XLA Ops:
  7.2 146.6 %copy-start = (s32[1024,8]{0,1:T(8,128)S(1)}, s32[1024,8]{0,1:T(8,128)}, u32[]{:S(2)}) copy-start(s32[1024,8]{0,1:T(8,128)} %param.17) | copy-start | bytes 98308
  7.2 71.8 %all-gather.4.cloned.1.call-start = ((), (), s32[]{:S(2)}) async-start(), calls=%async_computation.3 | async-start | bytes 3981312 | tf_op jit(solution)/shard_map/all_gather | solution.py:219
  11.6 341.3 %all-gather.6.cloned.1.call-start = ((), (), s32[]{:S(2)}) async-start(), calls=%async_computation.4 | async-start | bytes 14483456 | tf_op jit(solution)/shard_map/all_gather | solution.py:292
  11.6 31.9 %collective-permute-start.3 = (bf16[256,1536]{1,0:T(8,128)(2,1)}, bf16[256,1536]{1,0:T(8,128)(2,1)}, u32[]{:S(2)}, u32[]{:S(2)}) collective-permute-start(bf16[256,1536]{1,0:T(8,128)(2,1)} %param.14), channel_id=1, source_target_pairs={{0,2},{1,3},{2,0},{3,1},{4,6},{5,7},{6,4},{7,5},{8,10},{9,11},{10,... | collective-permute-start | bytes 2359304 | tf_op jit(solution)/shard_map/ppermute | solution.py:95
  44.8 3.5 collective-permute-start.4
  46.1 40.9 %copy-start.47 = (f32[1024,32]{0,1:T(8,128)}, f32[1024,32]{0,1:T(8,128)S(1)}, u32[]{:S(2)}) copy-start(f32[1024,32]{0,1:T(8,128)S(1)} %get-tuple-element.225) | copy-start | bytes 393220
  48.4 36.5 %copy-start.12 = (bf16[1024,1536]{1,0:T(8,128)(2,1)}, bf16[1024,1536]{1,0:T(8,128)(2,1)S(1)}, u32[]{:S(2)}) copy-start(bf16[1024,1536]{1,0:T(8,128)(2,1)S(1)} %slice_dynamic-update-slice_fusion.2) | copy-start | bytes 9437188
  49.1 35.8 %copy-start.86 = (f32[1024]{0:T(1024)}, f32[1024]{0:T(1024)S(1)}, u32[]{:S(2)}) copy-start(f32[1024]{0:T(1024)S(1)} %add_rsqrt_fusion) | copy-start | bytes 12292
  80.9 131.2 %copy-start.72 = (f32[1536]{0:T(1024)}, f32[1536]{0:T(1024)S(1)}, u32[]{:S(2)}) copy-start(f32[1536]{0:T(1024)S(1)} %get-tuple-element.158) | copy-start | bytes 18436
  88.8 33.2 %collective-permute-start.2 = (bf16[192,1280]{1,0:T(8,128)(2,1)}, bf16[192,1280]{1,0:T(8,128)(2,1)}, u32[]{:S(2)}, u32[]{:S(2)}) collective-permute-start(bf16[192,1280]{1,0:T(8,128)(2,1)} %copy.302), channel_id=1, source_target_pairs={{0,4},{4,0},{1,5},{5,1},{2,6},{6,2},{3,7},{7,3},{8,12},{12,8},{9,1... | collective-permute-start | bytes 1474568 | tf_op jit(solution)/shard_map/ppermute | solution.py:95
  91.0 33.7 %collective-permute-start.1 = (bf16[192,2560]{1,0:T(8,128)(2,1)}, bf16[192,2560]{1,0:T(8,128)(2,1)}, u32[]{:S(2)}, u32[]{:S(2)}) collective-permute-start(bf16[192,2560]{1,0:T(8,128)(2,1)} %copy.300), channel_id=1, source_target_pairs={{0,4},{4,0},{1,5},{5,1},{2,6},{6,2},{3,7},{7,3},{8,12},{12,8},{9,1... | collective-permute-start | bytes 2949128 | tf_op jit(solution)/shard_map/ppermute | solution.py:95
  93.8 43.6 %collective-permute-start = (bf16[192,2560]{1,0:T(8,128)(2,1)}, bf16[192,2560]{1,0:T(8,128)(2,1)}, u32[]{:S(2)}, u32[]{:S(2)}) collective-permute-start(bf16[192,2560]{1,0:T(8,128)(2,1)} %copy.299), channel_id=1, source_target_pairs={{0,16},{8,24},{16,0},{24,8},{1,17},{9,25},{17,1},{25,9},{2,18},{10... | collective-permute-start | bytes 2949128 | tf_op jit(solution)/shard_map/ppermute | solution.py:236
  143.4 3.8 collective-permute-start.5
  151.2 20.9 %copy-start.51 = (bf16[192,10,128]{0,2,1:T(8,128)(2,1)S(1)}, bf16[192,10,128]{0,2,1:T(8,128)(2,1)}, u32[]{:S(2)}) copy-start(bf16[192,10,128]{0,2,1:T(8,128)(2,1)} %copy.289) | copy-start | bytes 1474564
  152.2 21.0 %collective-permute-start.6 = (bf16[256,1536]{1,0:T(8,128)(2,1)}, bf16[256,1536]{1,0:T(8,128)(2,1)}, u32[]{:S(2)}, u32[]{:S(2)}) collective-permute-start(bf16[256,1536]{1,0:T(8,128)(2,1)} %fusion.76), channel_id=1, source_target_pairs={{0,2},{1,3},{2,0},{3,1},{4,6},{5,7},{6,4},{7,5},{8,10},{9,11},{10,... | collective-permute-start | bytes 2359304 | tf_op jit(solution)/shard_map/ppermute | solution.py:95
  154.9 56.2 %copy-start.10 = (bf16[256,1536]{1,0:T(8,128)(2,1)S(1)}, bf16[256,1536]{1,0:T(8,128)(2,1)}, u32[]{:S(2)}) copy-start(bf16[256,1536]{1,0:T(8,128)(2,1)} %param.14) | copy-start | bytes 2359300
  154.9 56.2 %collective-permute-start.7 = (bf16[192,1280]{1,0:T(8,128)(2,1)}, bf16[192,1280]{1,0:T(8,128)(2,1)S(1)}, u32[]{:S(2)}, u32[]{:S(2)}) collective-permute-start(bf16[192,1280]{1,0:T(8,128)(2,1)} %copy.306), channel_id=1, source_target_pairs={{0,16},{8,24},{16,0},{24,8},{1,17},{9,25},{17,1},{25,9},{2,18},{10... | collective-permute-start | bytes 1474568 | tf_op jit(solution)/shard_map/ppermute | solution.py:236
  168.4 49.5 %collective-permute-start.8 = (bf16[192,2560]{1,0:T(8,128)(2,1)}, bf16[192,2560]{1,0:T(8,128)(2,1)}, u32[]{:S(2)}, u32[]{:S(2)}) collective-permute-start(bf16[192,2560]{1,0:T(8,128)(2,1)} %copy.310), channel_id=1, source_target_pairs={{0,8},{8,16},{16,24},{24,0},{1,9},{9,17},{17,25},{25,1},{2,10},{10... | collective-permute-start | bytes 2949128 | tf_op jit(solution)/shard_map/ppermute | solution.py:236
  173.1 44.8 %collective-permute-start.9 = (bf16[192,1280]{1,0:T(8,128)(2,1)}, bf16[192,1280]{1,0:T(8,128)(2,1)}, u32[]{:S(2)}, u32[]{:S(2)}) collective-permute-start(bf16[192,1280]{1,0:T(8,128)(2,1)} %copy.311), channel_id=1, source_target_pairs={{0,8},{8,16},{16,24},{24,0},{1,9},{9,17},{17,25},{25,1},{2,10},{10... | collective-permute-start | bytes 1474568 | tf_op jit(solution)/shard_map/ppermute | solution.py:236
  217.9 235.8 %all-gather.8.cloned.1.call-start = ((), (), s32[]{:S(2)}) async-start(), calls=%async_computation.5 | async-start | bytes 13369344 | tf_op jit(solution)/shard_map/all_gather | solution.py:305
  224.4 13.4 %collective-permute-start.14 = (bf16[192,1280]{1,0:T(8,128)(2,1)}, bf16[192,1280]{1,0:T(8,128)(2,1)}, u32[]{:S(2)}, u32[]{:S(2)}) collective-permute-start(bf16[192,1280]{1,0:T(8,128)(2,1)} %collective-permute-done.9), channel_id=1, source_target_pairs={{0,4},{4,0},{1,5},{5,1},{2,6},{6,2},{3,7},{7,3},{8,12},{12,8},{9,1... | collective-permute-start | bytes 1474568 | tf_op jit(solution)/shard_map/ppermute | solution.py:95
  225.9 34.2 %collective-permute-start.16 = (bf16[192,1280]{1,0:T(8,128)(2,1)}, bf16[192,1280]{1,0:T(8,128)(2,1)}, u32[]{:S(2)}, u32[]{:S(2)}) collective-permute-start(bf16[192,1280]{1,0:T(8,128)(2,1)} %copy.321), channel_id=1, source_target_pairs={{0,24},{8,0},{16,8},{24,16},{1,25},{9,1},{17,9},{25,17},{2,26},{10... | collective-permute-start | bytes 1474568 | tf_op jit(solution)/shard_map/ppermute | solution.py:236
  227.5 57.3 %collective-permute-start.12 = (bf16[192,2560]{1,0:T(8,128)(2,1)S(1)}, bf16[192,2560]{1,0:T(8,128)(2,1)}, u32[]{:S(2)}, u32[]{:S(2)}) collective-permute-start(bf16[192,2560]{1,0:T(8,128)(2,1)S(1)} %copy.319), channel_id=1, source_target_pairs={{0,24},{8,0},{16,8},{24,16},{1,25},{9,1},{17,9},{25,17},{2,26},{10... | collective-permute-start | bytes 2949128 | tf_op jit(solution)/shard_map/ppermute | solution.py:236
  235.1 27.8 %copy-start.68 = (bf16[192,1280]{1,0:T(8,128)(2,1)S(1)}, bf16[192,1280]{1,0:T(8,128)(2,1)}, u32[]{:S(2)}) copy-start(bf16[192,1280]{1,0:T(8,128)(2,1)} %copy-done.67) | copy-start | bytes 1474564
  235.1 27.8 %collective-permute-start.15 = (bf16[192,1280]{1,0:T(8,128)(2,1)}, bf16[192,1280]{1,0:T(8,128)(2,1)S(1)}, u32[]{:S(2)}, u32[]{:S(2)}) collective-permute-start(bf16[192,1280]{1,0:T(8,128)(2,1)} %copy-done.67), channel_id=1, source_target_pairs={{0,4},{4,0},{1,5},{5,1},{2,6},{6,2},{3,7},{7,3},{8,12},{12,8},{9,1... | collective-permute-start | bytes 1474568 | tf_op jit(solution)/shard_map/ppermute | solution.py:95
  236.6 66.6 %collective-permute-start.10 = (bf16[192,2560]{1,0:T(8,128)(2,1)}, bf16[192,2560]{1,0:T(8,128)(2,1)S(1)}, u32[]{:S(2)}, u32[]{:S(2)}) collective-permute-start(bf16[192,2560]{1,0:T(8,128)(2,1)} %collective-permute-done.8), channel_id=1, source_target_pairs={{0,4},{4,0},{1,5},{5,1},{2,6},{6,2},{3,7},{7,3},{8,12},{12,8},{9,1... | collective-permute-start | bytes 2949128 | tf_op jit(solution)/shard_map/ppermute | solution.py:95
  237.8 68.8 %collective-permute-start.11 = (bf16[192,2560]{1,0:T(8,128)(2,1)}, bf16[192,2560]{1,0:T(8,128)(2,1)S(1)}, u32[]{:S(2)}, u32[]{:S(2)}) collective-permute-start(bf16[192,2560]{1,0:T(8,128)(2,1)} %collective-permute-done), channel_id=1, source_target_pairs={{0,4},{4,0},{1,5},{5,1},{2,6},{6,2},{3,7},{7,3},{8,12},{12,8},{9,1... | collective-permute-start | bytes 2949128 | tf_op jit(solution)/shard_map/ppermute | solution.py:95
  260.1 42.0 %collective-permute-start.17 = (bf16[192,1280]{1,0:T(8,128)(2,1)}, bf16[192,1280]{1,0:T(8,128)(2,1)S(1)}, u32[]{:S(2)}, u32[]{:S(2)}) collective-permute-start(bf16[192,1280]{1,0:T(8,128)(2,1)} %collective-permute-done.16), channel_id=1, source_target_pairs={{0,4},{4,0},{1,5},{5,1},{2,6},{6,2},{3,7},{7,3},{8,12},{12,8},{9,1... | collective-permute-start | bytes 1474568 | tf_op jit(solution)/shard_map/ppermute | solution.py:95
  284.8 36.5 %collective-permute-start.13 = (bf16[192,2560]{1,0:T(8,128)(2,1)}, bf16[192,2560]{1,0:T(8,128)(2,1)S(1)}, u32[]{:S(2)}, u32[]{:S(2)}) collective-permute-start(bf16[192,2560]{1,0:T(8,128)(2,1)} %collective-permute-done.12), channel_id=1, source_target_pairs={{0,4},{4,0},{1,5},{5,1},{2,6},{6,2},{3,7},{7,3},{8,12},{12,8},{9,1... | collective-permute-start | bytes 2949128 | tf_op jit(solution)/shard_map/ppermute | solution.py:95
  352.9 255.9 %reduce-scatter.4.cloned.1.call-start = ((), (), s32[]{:S(2)}) async-start(), calls=%async_computation.6 | async-start | bytes 13369344 | tf_op jit(solution)/shard_map/reduce_scatter | solution.py:330
  357.1 43.5 %copy-start.3 = (bf16[4096,1280]{1,0:T(8,128)(2,1)}, bf16[4096,1280]{1,0:T(8,128)(2,1)S(1)}, u32[]{:S(2)}) copy-start(bf16[4096,1280]{1,0:T(8,128)(2,1)S(1)} %convolution_convert_fusion.2) | copy-start | bytes 31457284
  453.8 305.2 %reduce-scatter.6.cloned.1.call-start = ((), (), s32[]{:S(2)}) async-start(), calls=%async_computation.7 | async-start | bytes 14483456 | tf_op jit(solution)/shard_map/reduce_scatter | solution.py:370
  477.9 61.3 %collective-permute-start.18 = (bf16[192,1280]{1,0:T(8,128)(2,1)}, bf16[192,1280]{1,0:T(8,128)(2,1)}, u32[]{:S(2)}, u32[]{:S(2)}) collective-permute-start(bf16[192,1280]{1,0:T(8,128)(2,1)} %get-tuple-element.187), channel_id=1, source_target_pairs={{0,4},{4,0},{1,5},{5,1},{2,6},{6,2},{3,7},{7,3},{8,12},{12,8},{9,1... | collective-permute-start | bytes 1474568 | tf_op jit(solution)/shard_map/ppermute | solution.py:95
  479.4 59.8 %collective-permute-start.19 = (bf16[192,1280]{1,0:T(8,128)(2,1)}, bf16[192,1280]{1,0:T(8,128)(2,1)}, u32[]{:S(2)}, u32[]{:S(2)}) collective-permute-start(bf16[192,1280]{1,0:T(8,128)(2,1)} %get-tuple-element.186), channel_id=1, source_target_pairs={{0,4},{4,0},{1,5},{5,1},{2,6},{6,2},{3,7},{7,3},{8,12},{12,8},{9,1... | collective-permute-start | bytes 1474568 | tf_op jit(solution)/shard_map/ppermute | solution.py:95
  480.0 59.3 %collective-permute-start.20 = (bf16[192,1280]{1,0:T(8,128)(2,1)}, bf16[192,1280]{1,0:T(8,128)(2,1)}, u32[]{:S(2)}, u32[]{:S(2)}) collective-permute-start(bf16[192,1280]{1,0:T(8,128)(2,1)} %get-tuple-element.185), channel_id=1, source_target_pairs={{0,4},{4,0},{1,5},{5,1},{2,6},{6,2},{3,7},{7,3},{8,12},{12,8},{9,1... | collective-permute-start | bytes 1474568 | tf_op jit(solution)/shard_map/ppermute | solution.py:95
  481.4 57.8 %collective-permute-start.21 = (bf16[192,1280]{1,0:T(8,128)(2,1)}, bf16[192,1280]{1,0:T(8,128)(2,1)}, u32[]{:S(2)}, u32[]{:S(2)}) collective-permute-start(bf16[192,1280]{1,0:T(8,128)(2,1)} %get-tuple-element.184), channel_id=1, source_target_pairs={{0,4},{4,0},{1,5},{5,1},{2,6},{6,2},{3,7},{7,3},{8,12},{12,8},{9,1... | collective-permute-start | bytes 1474568 | tf_op jit(solution)/shard_map/ppermute | solution.py:95
  519.9 27.0 %slice-start = ((s8[10485760]{0:T(1024)(128)(4,1)}), s8[4194304]{0:T(1024)(128)(4,1)S(1)}, s32[]{:S(2)}) async-start(s8[10485760]{0:T(1024)(128)(4,1)} %bitcast.393), calls=%async_computation.9 | async-start | bytes 8388608
  519.9 27.0 %slice-start.1 = ((s8[10485760]{0:T(1024)(128)(4,1)}), s8[4194304]{0:T(1024)(128)(4,1)S(1)}, s32[]{:S(2)}) async-start(s8[10485760]{0:T(1024)(128)(4,1)} %bitcast.393), calls=%async_computation.10 | async-start | bytes 8388608
  519.9 27.0 %slice-start.2 = ((s8[10485760]{0:T(1024)(128)(4,1)}), s8[2097152]{0:T(1024)(128)(4,1)S(1)}, s32[]{:S(2)}) async-start(s8[10485760]{0:T(1024)(128)(4,1)} %bitcast.393), calls=%async_computation.11 | async-start | bytes 4194304
  542.3 54.2 %collective-permute-start.22 = (bf16[192,1280]{1,0:T(8,128)(2,1)}, bf16[192,1280]{1,0:T(8,128)(2,1)}, u32[]{:S(2)}, u32[]{:S(2)}) collective-permute-start(bf16[192,1280]{1,0:T(8,128)(2,1)} %get-tuple-element.121), channel_id=1, source_target_pairs={{0,8},{8,16},{16,24},{24,0},{1,9},{9,17},{17,25},{25,1},{2,10},{10... | collective-permute-start | bytes 1474568 | tf_op jit(solution)/shard_map/ppermute | solution.py:236
  542.8 53.8 %collective-permute-start.23 = (bf16[192,1280]{1,0:T(8,128)(2,1)}, bf16[192,1280]{1,0:T(8,128)(2,1)}, u32[]{:S(2)}, u32[]{:S(2)}) collective-permute-start(bf16[192,1280]{1,0:T(8,128)(2,1)} %get-tuple-element.122), channel_id=1, source_target_pairs={{0,16},{8,24},{16,0},{24,8},{1,17},{9,25},{17,1},{25,9},{2,18},{10... | collective-permute-start | bytes 1474568 | tf_op jit(solution)/shard_map/ppermute | solution.py:236
  544.6 52.0 %collective-permute-start.24 = (bf16[192,1280]{1,0:T(8,128)(2,1)}, bf16[192,1280]{1,0:T(8,128)(2,1)}, u32[]{:S(2)}, u32[]{:S(2)}) collective-permute-start(bf16[192,1280]{1,0:T(8,128)(2,1)} %get-tuple-element.123), channel_id=1, source_target_pairs={{0,24},{8,0},{16,8},{24,16},{1,25},{9,1},{17,9},{25,17},{2,26},{10... | collective-permute-start | bytes 1474568 | tf_op jit(solution)/shard_map/ppermute | solution.py:236
  608.8 386.0 %reduce-scatter.8.cloned.1.call-start = ((), (), s32[]{:S(2)}) async-start(), calls=%async_computation.8 | async-start | bytes 3981312 | tf_op jit(solution)/shard_map/reduce_scatter | solution.py:465
  654.2 24.9 %collective-permute-start.25 = (bf16[192,2560]{1,0:T(8,128)(2,1)}, bf16[192,2560]{1,0:T(8,128)(2,1)}, u32[]{:S(2)}, u32[]{:S(2)}) collective-permute-start(bf16[192,2560]{1,0:T(8,128)(2,1)} %get-tuple-element.177), channel_id=1, source_target_pairs={{0,4},{4,0},{1,5},{5,1},{2,6},{6,2},{3,7},{7,3},{8,12},{12,8},{9,1... | collective-permute-start | bytes 2949128 | tf_op jit(solution)/shard_map/ppermute | solution.py:95
  655.6 44.6 %collective-permute-start.26 = (bf16[192,2560]{1,0:T(8,128)(2,1)}, bf16[192,2560]{1,0:T(8,128)(2,1)}, u32[]{:S(2)}, u32[]{:S(2)}) collective-permute-start(bf16[192,2560]{1,0:T(8,128)(2,1)} %get-tuple-element.176), channel_id=1, source_target_pairs={{0,4},{4,0},{1,5},{5,1},{2,6},{6,2},{3,7},{7,3},{8,12},{12,8},{9,1... | collective-permute-start | bytes 2949128 | tf_op jit(solution)/shard_map/ppermute | solution.py:95
  656.2 65.0 %collective-permute-start.27 = (bf16[192,2560]{1,0:T(8,128)(2,1)}, bf16[192,2560]{1,0:T(8,128)(2,1)}, u32[]{:S(2)}, u32[]{:S(2)}) collective-permute-start(bf16[192,2560]{1,0:T(8,128)(2,1)} %get-tuple-element.175), channel_id=1, source_target_pairs={{0,4},{4,0},{1,5},{5,1},{2,6},{6,2},{3,7},{7,3},{8,12},{12,8},{9,1... | collective-permute-start | bytes 2949128 | tf_op jit(solution)/shard_map/ppermute | solution.py:95
  657.7 83.4 %collective-permute-start.28 = (bf16[192,2560]{1,0:T(8,128)(2,1)}, bf16[192,2560]{1,0:T(8,128)(2,1)}, u32[]{:S(2)}, u32[]{:S(2)}) collective-permute-start(bf16[192,2560]{1,0:T(8,128)(2,1)} %get-tuple-element.174), channel_id=1, source_target_pairs={{0,4},{4,0},{1,5},{5,1},{2,6},{6,2},{3,7},{7,3},{8,12},{12,8},{9,1... | collective-permute-start | bytes 2949128 | tf_op jit(solution)/shard_map/ppermute | solution.py:95
  771.3 25.0 %copy-start.76 = (f32[2,3,1024]{2,1,0:T(4,128)S(1)}, f32[2,3,1024]{2,1,0:T(4,128)}, u32[]{:S(2)}) copy-start(f32[2,3,1024]{2,1,0:T(4,128)} %copy-done.75) | copy-start | bytes 73732
  771.4 25.0 %copy-start.78 = (f32[2,3,1024]{2,1,0:T(4,128)S(1)}, f32[2,3,1024]{2,1,0:T(4,128)}, u32[]{:S(2)}) copy-start(f32[2,3,1024]{2,1,0:T(4,128)} %copy-done.77) | copy-start | bytes 73732
  771.4 25.1 %copy-start.22 = (bf16[256,1536]{1,0:T(8,128)(2,1)S(1)}, bf16[256,1536]{1,0:T(8,128)(2,1)}, u32[]{:S(2)}) copy-start(bf16[256,1536]{1,0:T(8,128)(2,1)} %copy-done.21) | copy-start | bytes 2359300
  771.4 18.5 %collective-permute-start.29 = (bf16[256,1536]{1,0:T(8,128)(2,1)S(1)}, bf16[256,1536]{1,0:T(8,128)(2,1)S(1)}, u32[]{:S(2)}, u32[]{:S(2)}) collective-permute-start(bf16[256,1536]{1,0:T(8,128)(2,1)S(1)} %fusion.99), channel_id=1, source_target_pairs={{0,2},{1,3},{2,0},{3,1},{4,6},{5,7},{6,4},{7,5},{8,10},{9,11},{10,... | collective-permute-start | bytes 2359304 | tf_op jit(solution)/shard_map/ppermute | solution.py:95
  773.0 23.3 %collective-permute-start.30 = (bf16[192,1280]{1,0:T(8,128)(2,1)S(1)}, bf16[192,1280]{1,0:T(8,128)(2,1)S(1)}, u32[]{:S(2)}, u32[]{:S(2)}) collective-permute-start(bf16[192,1280]{1,0:T(8,128)(2,1)S(1)} %get-tuple-element.213), channel_id=1, source_target_pairs={{0,16},{8,24},{16,0},{24,8},{1,17},{9,25},{17,1},{25,9},{2,18},{10... | collective-permute-start | bytes 1474568 | tf_op jit(solution)/shard_map/ppermute | solution.py:236
  796.3 3.4 collective-permute-start.31
  798.0 25.1 %collective-permute-start.32 = (bf16[192,1280]{1,0:T(8,128)(2,1)S(1)}, bf16[192,1280]{1,0:T(8,128)(2,1)S(1)}, u32[]{:S(2)}, u32[]{:S(2)}) collective-permute-start(bf16[192,1280]{1,0:T(8,128)(2,1)S(1)} %get-tuple-element.136), channel_id=1, source_target_pairs={{0,16},{8,24},{16,0},{24,8},{1,17},{9,25},{17,1},{25,9},{2,18},{10... | collective-permute-start | bytes 1474568 | tf_op jit(solution)/shard_map/ppermute | solution.py:236
  802.7 23.4 %copy-start.71 = (bf16[1024,128]{0,1:T(8,128)(2,1)S(1)}, bf16[1024,128]{0,1:T(8,128)(2,1)}, u32[]{:S(2)}) copy-start(bf16[1024,128]{0,1:T(8,128)(2,1)} %slice.338) | copy-start | bytes 786436
  826.0 46.0 %collective-permute-start.33 = (bf16[192,2560]{1,0:T(8,128)(2,1)}, bf16[192,2560]{1,0:T(8,128)(2,1)}, u32[]{:S(2)}, u32[]{:S(2)}) collective-permute-start(bf16[192,2560]{1,0:T(8,128)(2,1)} %get-tuple-element.138), channel_id=1, source_target_pairs={{0,8},{8,16},{16,24},{24,0},{1,9},{9,17},{17,25},{25,1},{2,10},{10... | collective-permute-start | bytes 2949128 | tf_op jit(solution)/shard_map/ppermute | solution.py:236
  872.0 24.8 %collective-permute-start.34 = (bf16[192,2560]{1,0:T(8,128)(2,1)}, bf16[192,2560]{1,0:T(8,128)(2,1)}, u32[]{:S(2)}, u32[]{:S(2)}) collective-permute-start(bf16[192,2560]{1,0:T(8,128)(2,1)} %get-tuple-element.141), channel_id=1, source_target_pairs={{0,24},{8,0},{16,8},{24,16},{1,25},{9,1},{17,9},{25,17},{2,26},{10... | collective-permute-start | bytes 2949128 | tf_op jit(solution)/shard_map/ppermute | solution.py:236
  914.3 24.1 %collective-permute-start.35 = (bf16[2,256,1536]{2,1,0:T(8,128)(2,1)}, bf16[2,256,1536]{2,1,0:T(8,128)(2,1)}, u32[]{:S(2)}, u32[]{:S(2)}) collective-permute-start(bf16[2,256,1536]{2,1,0:T(8,128)(2,1)} %dynamic-slice_bitcast_fusion), channel_id=1, source_target_pairs={{0,1},{1,0},{2,3},{3,2},{4,5},{5,4},{6,7},{7,6},{8,9},{9,8},{10,11... | collective-permute-start | bytes 4718600 | tf_op jit(solution)/shard_map/ppermute | solution.py:95
  940.9 20.1 %copy-start.11 = (bf16[256,1536]{1,0:T(8,128)(2,1)S(1)}, bf16[256,1536]{1,0:T(8,128)(2,1)}, u32[]{:S(2)}) copy-start(bf16[256,1536]{1,0:T(8,128)(2,1)} %param.14) | copy-start | bytes 2359300
  941.0 20.0 %collective-permute-start.36 = (bf16[256,1536]{1,0:T(8,128)(2,1)S(1)}, bf16[256,1536]{1,0:T(8,128)(2,1)S(1)}, u32[]{:S(2)}, u32[]{:S(2)}) collective-permute-start(bf16[256,1536]{1,0:T(8,128)(2,1)S(1)} %fusion.77), channel_id=1, source_target_pairs={{0,2},{1,3},{2,0},{3,1},{4,6},{5,7},{6,4},{7,5},{8,10},{9,11},{10,... | collective-permute-start | bytes 2359304 | tf_op jit(solution)/shard_map/ppermute | solution.py:95
  992.5 17.7 %copy-start.1 = (s32[1024,8]{0,1:T(8,128)S(1)}, s32[1024,8]{0,1:T(8,128)}, u32[]{:S(2)}) copy-start(s32[1024,8]{0,1:T(8,128)} %param.17) | copy-start | bytes 98308
  995.8 8.4 collective-permute-start.37
  995.9 8.4 collective-permute-start.38
  997.3 10.1 collective-permute-start.39
  (75 other events, 416.7 us)
Sparse Core Ops, SparseCore 0:
  11.7 67.3 all-gather.3
  218.1 134.7 all-gather.5
  355.1 98.5 all-gather.7
  457.7 151.0 reduce-scatter.3
  612.7 146.2 reduce-scatter.5
  911.8 81.1 reduce-scatter.7

commit v6 on v5

--- a/solution.py
+++ b/solution.py
@@ -229,7 +229,7 @@
             gate_up = jnp.concatenate(
                 [gate.reshape(depth, own_hidden), up.reshape(depth, own_hidden)], axis=1
             )
-            return gate_up, down.reshape(depth, own_hidden)
+            return by_rows(gate_up), by_rows(down.reshape(depth, own_hidden))
 
         def to_owner(piece, shift):
             pairs = [(m, (m + shift) % inner) for m in range(inner)]
@@ -257,15 +257,15 @@
         ).astype(bf16)
         values = qkv[:, q_cols + k_cols :].astype(bf16).reshape(group, -1, HEAD_DIM)
         attended, log_total = attend_forward(query, keys, values, prefix[0])
-        far_down, near, far_gate_up, owned[0], attended = tie(
-            pieces[2][1], pieces[1], far_gate_up, owned[0], attended
-        )
-        far_down, near = to_owner(far_down, 2), to_owner(near, 1)
+        far_down, far_gate_up, owned[0], attended = tie(
+            pieces[2][1], far_gate_up, owned[0], attended
+        )
+        far_down = to_owner(far_down, 2)
         branch = lax.dot_general(
             attended, w_out_t, (((1,), (1,)), ((), ())), preferred_element_type=f32
         ).astype(bf16)
         tokens_f = tokens.astype(f32)
-        branch, far_down = tie(scatter_t(branch), far_down)
+        branch = scatter_t(branch)
         middle = tokens_f + branch
         scale_two = rms_scale(middle)
         normed_two = (middle * scale_two * gain_two).astype(bf16)
@@ -286,8 +286,8 @@
             ],
             axis=1,
         )
-        last, near, shipped = tie(pieces[3], near, shipped)
-        last = to_owner(last, 3)
+        last, near, far_down, shipped = tie(pieces[3], pieces[1], far_down, shipped)
+        last, near = to_owner(last, 3), to_owner(near, 1)
         owned += [pass_on(near), pass_on((far_gate_up, far_down)), pass_on(last)]
         shared_all = by_rows(lax.all_gather(by_rows(shipped), shared, axis=0, tiled=True))
         w_gate_up = jnp.zeros((outer, inner, depth, 2 * own_hidden), bf16)
@@ -356,9 +356,7 @@
             ],
             axis=1,
         )
-        products, grad_gate_up, down_sums = tie(
-            (silu_g * up_part * cot_part).astype(bf16), grad_gate_up, down_sums
-        )
+        products, down_sums = tie((silu_g * up_part * cot_part).astype(bf16), down_sums)
         sent_down = down_sums[:1] + [to_owner(down_sums[s], s) for s in range(1, inner)]
         chosen = (jnp.arange(side_cols, dtype=jnp.int32)[None, :] == owner.T).astype(bf16)
         gate_block = jnp.dot(products, chosen, preferred_element_type=f32)
@@ -408,26 +406,23 @@
         grad_out_part = lax.dot_general(
             grad_branch, attended, contract_rows, preferred_element_type=f32
         ).astype(bf16)
-        grad_out_part, grad_branch, near_sum, sent_up = tie(
-            grad_out_part, grad_branch, gate_up_sums[1], sent_up
-        )
-        sent_gate_up[2] = (sent_gate, sent_up)
-        sent_gate_up[1] = to_owner(near_sum, 1)
+        grad_out_part, grad_branch = tie(grad_out_part, grad_branch)
         grad_attended = jnp.dot(
             grad_branch, w_out_t, preferred_element_type=f32
         ).astype(bf16)
-        grad_query, grad_keys, grad_values, (sent_gate_up[1], last_sum) = attend_backward(
+        grad_query, grad_keys, grad_values, (sent_up, near_sum, last_sum) = attend_backward(
             query,
             keys,
             values,
             grad_attended,
             log_total,
             prefix[0],
-            (sent_gate_up[1], gate_up_sums[3]),
-        )
-        sent_gate_up[3] = to_owner(last_sum, 3)
-        grad_query, grad_keys, grad_values, sent_gate_up[3] = tie(
-            grad_query, grad_keys, grad_values, sent_gate_up[3]
+            (sent_up, gate_up_sums[1], gate_up_sums[3]),
+        )
+        sent_gate_up[2] = (sent_gate, sent_up)
+        sent_gate_up[1], sent_gate_up[3] = to_owner(near_sum, 1), to_owner(last_sum, 3)
+        grad_query, grad_keys, grad_values, sent_gate_up[1] = tie(
+            grad_query, grad_keys, grad_values, sent_gate_up[1]
         )
         for shift in (1, 3):
             sent_gate_up[shift] = jnp.split(sent_gate_up[shift], 2, axis=1)

time: 1030 us -> 1030 us (level)
  waiting for transfers between devices: 355 us -> 393 us
  other arithmetic: 107 us -> 87.4 us
  local copies, waits for them, and re-layouts: 178 us -> 159 us
    ppermute x13, waiting for transfers between devices: 123 us -> 188 us  [to_owner(): return jax.tree.map(lambda part: lax.ppermute(part, 'i', pairs), piece)]
    optimization_barrier x9 -> x1, local copies, waits for them, and re-layouts: 23.5 us -> 1.15 us  [tie(): return lax.optimization_barrier(values)]
    all_gather x1, waiting for transfers between devices: 28.9 us -> 7.59 us  [on_device(): lax.all_gather(by_rows(shipped), shared, axis=0, tiled=True)]
    concatenate x1 -> x0, other arithmetic: 19.3 us -> none  [on_device(): jnp.concatenate([(grad_act * up_part * sigmoid_g * (1.0 + gate_part * (1....]
    reshape x0 -> x12, local copies, waits for them, and re-layouts: none -> 11.4 us  [the longest x4 4.05 us: expert_piece(): gate.reshape(depth, own_hidden)]
    sub x1, matrix products: 35 us -> 24.1 us  [attend_backward(): grad_weights - jnp.sum(weights * grad_weights, axis=-1, keepdims=True)]
    unnamed x188 -> x180, local copies, waits for them, and re-layouts: 23.1 us -> 19.8 us
  transfers between devices with their start and end apart: 46 -> 46, of which waited for: 24 -> 27; matrix products, arithmetic and copies ran while one was open for 52% -> 47% of each run, Pallas kernels for 0% -> 0%
where the time goes in v6:
time: 1030 us; the launch traced here: 1010 us
  waiting for transfers between devices  393 us (38%)
  matrix products  314 us (30%)
  local copies, waits for them, and re-layouts  159 us (15%)
  other arithmetic  87.4 us (8%)
  starting transfers between devices  42.6 us (4%)
  between operations  16.6 us (2%)
    ppermute x13, waiting for transfers between devices, to_owner(): return jax.tree.map(lambda part: lax.ppermute(part, 'i', pairs), piece)  188 us
    ppermute x24, waiting for transfers between devices, swap(): return lax.ppermute(values, axis, [(m, m ^ bit) for m in range(size)])  131 us
    dot_general x1, matrix products, on_device(): jnp.dot(normed_all, w_gate_up, preferred_element_type=f32).astype(bf16)  43.3 us
    dot_general x1, matrix products, on_device(): lax.dot_general(shared_rows[:, :width], grad_gate_up, contract_rows, pref...  41.3 us
    dot_general x1, matrix products, on_device(): lax.dot_general(grad_gate_up, w_gate_up, (((1,), (1,)), ((), ())), prefer...  40 us
    dot_general x1, matrix products, on_device(): cot_part = jnp.dot(cot_all, w_down_t, preferred_element_type=f32)  37.9 us
    convert_element_type x16, local copies, waits for them, and re-layouts, on_device(): jnp.swapaxes(part.reshape(depth, own_experts, hidden), 0, 1).astype(f32)  30.4 us
    all_gather x1, waiting for transfers between devices, on_device(): packed = lax.all_gather(pack, dp, axis=0, tiled=True)  26.1 us
  transfers between devices with their start and end apart: 46, of which 27 were waited for; matrix products, arithmetic and copies ran while one was open for 47% of the time, Pallas kernels for 0%

profile of v6, /device:TPU:0, one launch (start us, length us, event | category | flops | bytes accessed | tf_op | source)
XLA Modules:
  0.0 1012.8 jit_solution(5868481575581223403)
XLA Ops:
  11.6 3.1 collective-permute-start.3
  14.7 3.9 dynamic-slice_bitcast_fusion.19
  52.9 26.1 %all-gather.4.cloned.1.call-done = bf16[1536,1152]{1,0:T(8,128)(2,1)} async-done(((bf16[192,1152]{1,0:T(8,128)(2,1)}), bf16[1536,1152]{1,0:T(8,128)(2,1)}) %all-gather.4.cloned.1.call-update) | async-done | bytes 3538960 | tf_op jit(solution)/shard_map/all_gather | solution.py:219
  80.9 4.3 fusion.50
  92.1 5.7 fusion.107
  97.9 3.8 fusion.3
  101.6 4.6 copy-done.2
  106.7 10.5 %fusion.57 = bf16[2,64,3,1024]{3,1,2,0:T(8,128)(2,1)S(1)} fusion(bf16[1024,2,64,1]{0,2,3,1:T(8,128)(2,1)S(1)} %bitcast.396, f32[2,3,1024,1024]{2,3,1,0:T(8,128)} %copy-done.2, f32[2,3,1024]{2,1,0:T(4,128)S(1)} %fusion.3, f32[2,3,1024]{2,1,0:T(4,128)S(1)} %get-tuple-element.216), kind=kOutput, calls=%fused_computation.114 | convolution fusion | flops 824573952 | bytes 26263552 | tf_op jit(solution)/shard_map/hgqk,khd->qhgd/dot_general | solution.py:65
  122.4 11.2 %collective-permute-done = bf16[192,2560]{1,0:T(8,128)(2,1)} collective-permute-done((bf16[192,2560]{1,0:T(8,128)(2,1)}, bf16[192,2560]{1,0:T(8,128)(2,1)}, u32[]{:S(2)}, u32[]{:S(2)}) %collective-permute-start) | collective-permute-done | bytes 983072 | tf_op jit(solution)/shard_map/ppermute | solution.py:236
  133.6 3.1 convolution_convert_fusion.6
  139.7 3.7 collective-permute-done.5
  150.1 18.2 %collective-permute-done.6 = bf16[256,1536]{1,0:T(8,128)(2,1)} collective-permute-done((bf16[256,1536]{1,0:T(8,128)(2,1)}, bf16[256,1536]{1,0:T(8,128)(2,1)}, u32[]{:S(2)}, u32[]{:S(2)}) %collective-permute-start.6) | collective-permute-done | bytes 786464 | tf_op jit(solution)/shard_map/ppermute | solution.py:95
  168.3 2.7 multiply_reduce_fusion.2
  186.5 3.8 broadcast_in_dim.123
  192.3 3.9 collective-permute-start.16
  197.5 49.5 %collective-permute-done.13 = bf16[192,1280]{1,0:T(8,128)(2,1)S(1)} collective-permute-done((bf16[192,1280]{1,0:T(8,128)(2,1)S(1)}, bf16[192,1280]{1,0:T(8,128)(2,1)S(1)}, u32[]{:S(2)}, u32[]{:S(2)}) %collective-permute-start.13) | collective-permute-done | bytes 491552 | tf_op jit(solution)/shard_map/ppermute | solution.py:236
  249.4 4.3 collective-permute-done.16
  254.1 7.0 collective-permute-done.14
  262.4 41.6 %collective-permute-done.11 = bf16[192,2560]{1,0:T(8,128)(2,1)S(1)} collective-permute-done((bf16[192,2560]{1,0:T(8,128)(2,1)S(1)}, bf16[192,2560]{1,0:T(8,128)(2,1)S(1)}, u32[]{:S(2)}, u32[]{:S(2)}) %collective-permute-start.11) | collective-permute-done | bytes 983072 | tf_op jit(solution)/shard_map/ppermute | solution.py:236
  306.4 3.4 fusion.39
  312.4 14.8 %collective-permute-done.12 = bf16[192,2560]{1,0:T(8,128)(2,1)S(1)} collective-permute-done((bf16[192,2560]{1,0:T(8,128)(2,1)S(1)}, bf16[192,2560]{1,0:T(8,128)(2,1)S(1)}, u32[]{:S(2)}, u32[]{:S(2)}) %collective-permute-start.12) | collective-permute-done | bytes 983072 | tf_op jit(solution)/shard_map/ppermute | solution.py:95
  328.6 7.6 all-gather.6.cloned.1.call-done
  336.5 4.1 convolution_convert_fusion.2
  340.6 43.3 %convolution_convert_fusion = bf16[4096,2560]{1,0:T(8,128)(2,1)} fusion(bf16[1536,2560]{1,0:T(8,128)(2,1)} %bitcast.70, bf16[4096,1664]{1,0:T(8,128)(2,1)} %all-gather.6.cloned.1.call-done), kind=kOutput, calls=%fused_computation.16 | convolution fusion | flops 32222740480 | bytes 41418752 | tf_op jit(solution)/shard_map/dot_general | solution.py:313
  383.9 12.6 %fusion.18 = bf16[4096,1280]{1,0:T(8,128)(2,1)S(1)} fusion(bf16[4096,1280]{1,0:T(8,128)(2,1)S(1)} %convolution_convert_fusion.2, bf16[4096,2560]{1,0:T(8,128)(2,1)} %convolution_convert_fusion), kind=kLoop, calls=%fused_computation.35 | loop fusion | flops 52428800 | bytes 41943040 | tf_op jit(solution)/shard_map/convert_element_type | solution.py:323
  396.5 3.9 copy-done.14
  400.5 20.9 %convolution_convert_fusion.1 = bf16[4096,1536]{1,0:T(8,128)(2,1)} fusion(bf16[4096,1280]{1,0:T(8,128)(2,1)S(1)} %fusion.18, bf16[1536,1280]{1,0:T(8,128)(2,1)} %bitcast.351), kind=kOutput, calls=%fused_computation.37 | convolution fusion | flops 16112418816 | bytes 27000832 | tf_op jit(solution)/shard_map/dot_general | solution.py:324
  421.4 25.7 %all-gather.8.cloned.1.call-done = bf16[4096,1536]{1,0:T(8,128)(2,1)} async-done(((bf16[256,1536]{1,0:T(8,128)(2,1)}), bf16[4096,1536]{1,0:T(8,128)(2,1)}) %all-gather.8.cloned.1.call-update) | async-done | bytes 12582928 | tf_op jit(solution)/shard_map/all_gather | solution.py:305
  447.4 22.3 %convolution_convert_fusion.4 = bf16[1536,1280]{1,0:T(8,128)(2,1)S(1)} fusion(bf16[4096,1536]{1,0:T(8,128)(2,1)} %all-gather.8.cloned.1.call-done, bf16[4096,1280]{1,0:T(8,128)(2,1)} %copy-done.14), kind=kOutput, calls=%fused_computation.52 | convolution fusion | flops 16108093440 | bytes 27000832 | tf_op jit(solution)/shard_map/dot_general | solution.py:332
  475.1 37.9 %fusion.11 = (bf16[4096,1280]{1,0:T(8,128)(2,1)}, bf16[4096,1280]{1,0:T(8,128)(2,1)}, bf16[4096,1280]{1,0:T(8,128)(2,1)}) fusion(bf16[4096,1280]{1,0:T(8,128)(2,1)} %copy-done.3, bf16[4096,2560]{1,0:T(8,128)(2,1)} %convolution_convert_fusion, bf16[4096,1536]{1,0:T(8,128)(2,1)} %all-gather.8.cloned.1.call-done, bf16[1536,1280]{1,0:T(8,128)(2,1)S(1)} %bitcast.352), kind=kOutput, calls=%fused_computation.25 | convolution fusion | flops 16210984960 | bytes 79429632 | tf_op jit(solution)/shard_map/dot_general | solution.py:347
  513.0 40.0 %convolution_convert_fusion.3 = bf16[4096,1536]{1,0:T(8,128)(2,1)} fusion(bf16[1536,2560]{1,0:T(8,128)(2,1)} %bitcast.70, bf16[4096,1280]{1,0:T(8,128)(2,1)} %get-tuple-element.158, bf16[4096,1280]{1,0:T(8,128)(2,1)} %get-tuple-element.157), kind=kOutput, calls=%fused_computation.39 | convolution fusion | flops 32260489216 | bytes 41418752 | tf_op jit(solution)/shard_map/dot_general | solution.py:363
  553.1 3.3 fusion.69
  561.0 7.0 convolution_convert_fusion.5
  568.0 5.8 pad_maximum_fusion.1
  573.8 9.2 collective-permute-done.22
  583.0 31.6 %collective-permute-done.23 = bf16[192,1280]{1,0:T(8,128)(2,1)S(1)} collective-permute-done((bf16[192,1280]{1,0:T(8,128)(2,1)}, bf16[192,1280]{1,0:T(8,128)(2,1)S(1)}, u32[]{:S(2)}, u32[]{:S(2)}) %collective-permute-start.23) | collective-permute-done | bytes 491552 | tf_op jit(solution)/shard_map/ppermute | solution.py:236
  617.1 41.3 %fusion.27 = bf16[1536,2560]{1,0:T(8,128)(2,1)} fusion(bf16[4096,1280]{1,0:T(8,128)(2,1)} %get-tuple-element.158, bf16[4096,1280]{1,0:T(8,128)(2,1)} %get-tuple-element.157, bf16[4096,1664]{1,0:T(8,128)(2,1)} %all-gather.6.cloned.1.call-done), kind=kOutput, calls=%fused_computation.47 | convolution fusion | flops 32258129920 | bytes 41418752 | tf_op jit(solution)/shard_map/dot_general | solution.py:370
  658.4 5.3 dynamic-slice_bitcast_fusion.2
  680.9 7.8 collective-permute-done.25
  688.7 21.1 %collective-permute-done.26 = bf16[192,2560]{1,0:T(8,128)(2,1)} collective-permute-done((bf16[192,2560]{1,0:T(8,128)(2,1)}, bf16[192,2560]{1,0:T(8,128)(2,1)}, u32[]{:S(2)}, u32[]{:S(2)}) %collective-permute-start.26) | collective-permute-done | bytes 983072 | tf_op jit(solution)/shard_map/ppermute | solution.py:95
  709.7 21.1 %collective-permute-done.27 = bf16[192,2560]{1,0:T(8,128)(2,1)} collective-permute-done((bf16[192,2560]{1,0:T(8,128)(2,1)}, bf16[192,2560]{1,0:T(8,128)(2,1)}, u32[]{:S(2)}, u32[]{:S(2)}) %collective-permute-start.27) | collective-permute-done | bytes 983072 | tf_op jit(solution)/shard_map/ppermute | solution.py:95
  730.8 18.1 %collective-permute-done.28 = bf16[192,2560]{1,0:T(8,128)(2,1)} collective-permute-done((bf16[192,2560]{1,0:T(8,128)(2,1)}, bf16[192,2560]{1,0:T(8,128)(2,1)}, u32[]{:S(2)}, u32[]{:S(2)}) %collective-permute-start.28) | collective-permute-done | bytes 983072 | tf_op jit(solution)/shard_map/ppermute | solution.py:95
  748.9 6.1 fusion.42
  754.9 11.8 %reduce-scatter.6.cloned.1.call-done = bf16[256,1664]{1,0:T(8,128)(2,1)} async-done(((bf16[4096,1664]{1,0:T(8,128)(2,1)}), bf16[256,1664]{1,0:T(8,128)(2,1)}) %reduce-scatter.6.cloned.1.call-update) | async-done | bytes 851984 | tf_op jit(solution)/shard_map/reduce_scatter | solution.py:368
  771.5 3.0 copy.389
  775.6 2.9 multiply_reduce_fusion
  783.1 14.5 %collective-permute-done.29 = bf16[256,1536]{1,0:T(8,128)(2,1)S(1)} collective-permute-done((bf16[256,1536]{1,0:T(8,128)(2,1)S(1)}, bf16[256,1536]{1,0:T(8,128)(2,1)S(1)}, u32[]{:S(2)}, u32[]{:S(2)}) %collective-permute-start.29) | collective-permute-done | bytes 786464 | tf_op jit(solution)/shard_map/ppermute | solution.py:95
  797.7 7.0 collective-permute-done.30
  808.3 2.9 convolution_convert_fusion.8
  811.2 2.8 convolution_convert_fusion.9
  814.8 24.1 %fusion.2 = bf16[2,3,1024,1024]{2,3,1,0:T(8,128)(2,1)} fusion(f32[2,3,1024,1024]{2,3,1,0:T(8,128)} %copy-done.2, f32[2,3,1024]{2,1,0:T(4,128)S(1)} %log_add_fusion, bf16[1024,2,64,1]{0,2,3,1:T(8,128)(2,1)S(1)} %bitcast.397, bf16[1024,2,3,64]{0,3,2,1:T(8,128)(2,1)S(1)} %bitcast.385), kind=kOutput, calls=%fused_computation.11 | convolution fusion | flops 1648368640 | bytes 38821888 | tf_op jit(solution)/shard_map/sub | solution.py:78
  839.0 9.7 fusion.62
  848.6 4.3 convolution_multiply_fusion
  853.0 2.8 collective-permute-start.33
  855.8 13.1 %fusion.58 = bf16[1024,2,64]{0,2,1:T(8,128)(2,1)} fusion(bf16[1024,2,3,64]{0,3,2,1:T(8,128)(2,1)} %bitcast.386, f32[2,3,1024,1024]{2,3,1,0:T(8,128)} %copy-done.2, f32[2,3,1024]{2,1,0:T(4,128)S(1)} %log_add_fusion), kind=kOutput, calls=%fused_computation.117 | convolution fusion | flops 817889280 | bytes 26238976 | tf_op jit(solution)/shard_map/hgqk,qhgd->khd/dot_general | solution.py:88
  868.9 10.0 collective-permute-done.33
  880.7 6.5 fusion.36
  887.3 4.3 convolution_convert_fusion.7
  893.8 3.0 pad_maximum_fusion.6
  896.9 2.7 dynamic-slice_bitcast_fusion
  903.3 3.1 copy.377
  931.6 23.1 %collective-permute-done.39 = bf16[192,2560]{1,0:T(8,128)(2,1)} collective-permute-done((bf16[192,2560]{1,0:T(8,128)(2,1)}, bf16[192,2560]{1,0:T(8,128)(2,1)}, u32[]{:S(2)}, u32[]{:S(2)}) %collective-permute-start.39) | collective-permute-done | bytes 983072 | tf_op jit(solution)/shard_map/ppermute | solution.py:236
  969.9 2.7 copy.405
  975.0 2.7 copy.409
  (437 shorter events, 214.0 us)
Async XLA Ops:
  7.2 142.7 %copy-start = (s32[1024,8]{0,1:T(8,128)S(1)}, s32[1024,8]{0,1:T(8,128)}, u32[]{:S(2)}) copy-start(s32[1024,8]{0,1:T(8,128)} %param.17) | copy-start | bytes 98308
  7.2 71.8 %all-gather.4.cloned.1.call-start = ((), (), s32[]{:S(2)}) async-start(), calls=%async_computation.3 | async-start | bytes 3981312 | tf_op jit(solution)/shard_map/all_gather | solution.py:219
  11.6 324.7 %all-gather.6.cloned.1.call-start = ((), (), s32[]{:S(2)}) async-start(), calls=%async_computation.4 | async-start | bytes 14483456 | tf_op jit(solution)/shard_map/all_gather | solution.py:292
  11.6 35.8 %collective-permute-start.3 = (bf16[256,1536]{1,0:T(8,128)(2,1)}, bf16[256,1536]{1,0:T(8,128)(2,1)}, u32[]{:S(2)}, u32[]{:S(2)}) collective-permute-start(bf16[256,1536]{1,0:T(8,128)(2,1)} %param.14), channel_id=1, source_target_pairs={{0,2},{1,3},{2,0},{3,1},{4,6},{5,7},{6,4},{7,5},{8,10},{9,11},{10,... | collective-permute-start | bytes 2359304 | tf_op jit(solution)/shard_map/ppermute | solution.py:95
  48.6 3.5 collective-permute-start.4
  49.9 37.4 %copy-start.37 = (f32[1024,32]{0,1:T(8,128)}, f32[1024,32]{0,1:T(8,128)S(1)}, u32[]{:S(2)}) copy-start(f32[1024,32]{0,1:T(8,128)S(1)} %get-tuple-element.215) | copy-start | bytes 393220
  52.2 33.0 %copy-start.12 = (bf16[1024,1536]{1,0:T(8,128)(2,1)}, bf16[1024,1536]{1,0:T(8,128)(2,1)S(1)}, u32[]{:S(2)}) copy-start(bf16[1024,1536]{1,0:T(8,128)(2,1)S(1)} %slice_dynamic-update-slice_fusion.2) | copy-start | bytes 9437188
  52.9 32.3 %copy-start.82 = (f32[1024]{0:T(1024)}, f32[1024]{0:T(1024)S(1)}, u32[]{:S(2)}) copy-start(f32[1024]{0:T(1024)S(1)} %add_rsqrt_fusion) | copy-start | bytes 12292
  80.9 90.1 %copy-start.69 = (f32[1536]{0:T(1024)}, f32[1536]{0:T(1024)S(1)}, u32[]{:S(2)}) copy-start(f32[1536]{0:T(1024)S(1)} %get-tuple-element.148) | copy-start | bytes 18436
  88.0 29.3 %collective-permute-start.2 = (bf16[192,1280]{1,0:T(8,128)(2,1)}, bf16[192,1280]{1,0:T(8,128)(2,1)}, u32[]{:S(2)}, u32[]{:S(2)}) collective-permute-start(bf16[192,1280]{1,0:T(8,128)(2,1)} %copy.329), channel_id=1, source_target_pairs={{0,4},{4,0},{1,5},{5,1},{2,6},{6,2},{3,7},{7,3},{8,12},{12,8},{9,1... | collective-permute-start | bytes 1474568 | tf_op jit(solution)/shard_map/ppermute | solution.py:95
  88.5 32.2 %collective-permute-start.1 = (bf16[192,2560]{1,0:T(8,128)(2,1)}, bf16[192,2560]{1,0:T(8,128)(2,1)}, u32[]{:S(2)}, u32[]{:S(2)}) collective-permute-start(bf16[192,2560]{1,0:T(8,128)(2,1)} %pad_maximum_fusion.11), channel_id=1, source_target_pairs={{0,4},{4,0},{1,5},{5,1},{2,6},{6,2},{3,7},{7,3},{8,12},{12,8},{9,1... | collective-permute-start | bytes 2949128 | tf_op jit(solution)/shard_map/ppermute | solution.py:95
  90.0 43.6 %collective-permute-start = (bf16[192,2560]{1,0:T(8,128)(2,1)}, bf16[192,2560]{1,0:T(8,128)(2,1)}, u32[]{:S(2)}, u32[]{:S(2)}) collective-permute-start(bf16[192,2560]{1,0:T(8,128)(2,1)} %pad_maximum_fusion.13), channel_id=1, source_target_pairs={{0,16},{8,24},{16,0},{24,8},{1,17},{9,25},{17,1},{25,9},{2,18},{10... | collective-permute-start | bytes 2949128 | tf_op jit(solution)/shard_map/ppermute | solution.py:236
  117.3 19.5 %copy-start.84 = (bf16[2,64,3,1024]{3,1,2,0:T(8,128)(2,1)}, bf16[2,64,3,1024]{3,1,2,0:T(8,128)(2,1)S(1)}, u32[]{:S(2)}) copy-start(bf16[2,64,3,1024]{3,1,2,0:T(8,128)(2,1)S(1)} %fusion.57) | copy-start | bytes 2359300
  139.7 3.8 collective-permute-start.5
  139.7 28.6 %copy-start.10 = (bf16[256,1536]{1,0:T(8,128)(2,1)S(1)}, bf16[256,1536]{1,0:T(8,128)(2,1)}, u32[]{:S(2)}) copy-start(bf16[256,1536]{1,0:T(8,128)(2,1)} %param.14) | copy-start | bytes 2359300
  148.4 19.9 %collective-permute-start.6 = (bf16[256,1536]{1,0:T(8,128)(2,1)}, bf16[256,1536]{1,0:T(8,128)(2,1)}, u32[]{:S(2)}, u32[]{:S(2)}) collective-permute-start(bf16[256,1536]{1,0:T(8,128)(2,1)} %fusion.76), channel_id=1, source_target_pairs={{0,2},{1,3},{2,0},{3,1},{4,6},{5,7},{6,4},{7,5},{8,10},{9,11},{10,... | collective-permute-start | bytes 2359304 | tf_op jit(solution)/shard_map/ppermute | solution.py:95
  150.1 32.8 %collective-permute-start.7 = (bf16[192,1280]{1,0:T(8,128)(2,1)}, bf16[192,1280]{1,0:T(8,128)(2,1)}, u32[]{:S(2)}, u32[]{:S(2)}) collective-permute-start(bf16[192,1280]{1,0:T(8,128)(2,1)} %copy.341), channel_id=1, source_target_pairs={{0,16},{8,24},{16,0},{24,8},{1,17},{9,25},{17,1},{25,9},{2,18},{10... | collective-permute-start | bytes 1474568 | tf_op jit(solution)/shard_map/ppermute | solution.py:236
  182.9 264.2 %all-gather.8.cloned.1.call-start = ((), (), s32[]{:S(2)}) async-start(), calls=%async_computation.5 | async-start | bytes 13369344 | tf_op jit(solution)/shard_map/all_gather | solution.py:305
  184.5 62.5 %collective-permute-start.8 = (bf16[192,2560]{1,0:T(8,128)(2,1)}, bf16[192,2560]{1,0:T(8,128)(2,1)}, u32[]{:S(2)}, u32[]{:S(2)}) collective-permute-start(bf16[192,2560]{1,0:T(8,128)(2,1)} %pad_maximum_fusion.12), channel_id=1, source_target_pairs={{0,8},{8,16},{16,24},{24,0},{1,9},{9,17},{17,25},{25,1},{2,10},{10... | collective-permute-start | bytes 2949128 | tf_op jit(solution)/shard_map/ppermute | solution.py:236
  186.5 60.5 %collective-permute-start.13 = (bf16[192,1280]{1,0:T(8,128)(2,1)S(1)}, bf16[192,1280]{1,0:T(8,128)(2,1)S(1)}, u32[]{:S(2)}, u32[]{:S(2)}) collective-permute-start(bf16[192,1280]{1,0:T(8,128)(2,1)S(1)} %copy-done.62), channel_id=1, source_target_pairs={{0,8},{8,16},{16,24},{24,0},{1,9},{9,17},{17,25},{25,1},{2,10},{10... | collective-permute-start | bytes 1474568 | tf_op jit(solution)/shard_map/ppermute | solution.py:236
  190.3 59.0 %copy-start.28 = (bf16[2,192,1280]{2,1,0:T(8,128)(2,1)S(1)}, bf16[2,192,1280]{2,1,0:T(8,128)(2,1)}, u32[]{:S(2)}) copy-start(bf16[2,192,1280]{2,1,0:T(8,128)(2,1)} %pad_maximum_fusion.15) | copy-start | bytes 2949124
  191.7 69.6 %collective-permute-start.15 = (bf16[192,1280]{1,0:T(8,128)(2,1)}, bf16[192,1280]{1,0:T(8,128)(2,1)S(1)}, u32[]{:S(2)}, u32[]{:S(2)}) collective-permute-start(bf16[192,1280]{1,0:T(8,128)(2,1)} %collective-permute-done.7), channel_id=1, source_target_pairs={{0,4},{4,0},{1,5},{5,1},{2,6},{6,2},{3,7},{7,3},{8,12},{12,8},{9,1... | collective-permute-start | bytes 1474568 | tf_op jit(solution)/shard_map/ppermute | solution.py:95
  192.3 61.3 %collective-permute-start.16 = (bf16[192,1280]{1,0:T(8,128)(2,1)S(1)}, bf16[192,1280]{1,0:T(8,128)(2,1)S(1)}, u32[]{:S(2)}, u32[]{:S(2)}) collective-permute-start(bf16[192,1280]{1,0:T(8,128)(2,1)S(1)} %copy-done.61), channel_id=1, source_target_pairs={{0,24},{8,0},{16,8},{24,16},{1,25},{9,1},{17,9},{25,17},{2,26},{10... | collective-permute-start | bytes 1474568 | tf_op jit(solution)/shard_map/ppermute | solution.py:236
  196.2 107.8 %collective-permute-start.11 = (bf16[192,2560]{1,0:T(8,128)(2,1)S(1)}, bf16[192,2560]{1,0:T(8,128)(2,1)S(1)}, u32[]{:S(2)}, u32[]{:S(2)}) collective-permute-start(bf16[192,2560]{1,0:T(8,128)(2,1)S(1)} %copy-done.56), channel_id=1, source_target_pairs={{0,24},{8,0},{16,8},{24,16},{1,25},{9,1},{17,9},{25,17},{2,26},{10... | collective-permute-start | bytes 2949128 | tf_op jit(solution)/shard_map/ppermute | solution.py:236
  247.0 14.1 %collective-permute-start.14 = (bf16[192,1280]{1,0:T(8,128)(2,1)S(1)}, bf16[192,1280]{1,0:T(8,128)(2,1)S(1)}, u32[]{:S(2)}, u32[]{:S(2)}) collective-permute-start(bf16[192,1280]{1,0:T(8,128)(2,1)S(1)} %collective-permute-done.13), channel_id=1, source_target_pairs={{0,4},{4,0},{1,5},{5,1},{2,6},{6,2},{3,7},{7,3},{8,12},{12,8},{9,1... | collective-permute-start | bytes 1474568 | tf_op jit(solution)/shard_map/ppermute | solution.py:95
  247.0 59.3 %collective-permute-start.9 = (bf16[192,2560]{1,0:T(8,128)(2,1)}, bf16[192,2560]{1,0:T(8,128)(2,1)S(1)}, u32[]{:S(2)}, u32[]{:S(2)}) collective-permute-start(bf16[192,2560]{1,0:T(8,128)(2,1)} %collective-permute-done.8), channel_id=1, source_target_pairs={{0,4},{4,0},{1,5},{5,1},{2,6},{6,2},{3,7},{7,3},{8,12},{12,8},{9,1... | collective-permute-start | bytes 2949128 | tf_op jit(solution)/shard_map/ppermute | solution.py:95
  253.7 56.1 %collective-permute-start.10 = (bf16[192,2560]{1,0:T(8,128)(2,1)}, bf16[192,2560]{1,0:T(8,128)(2,1)S(1)}, u32[]{:S(2)}, u32[]{:S(2)}) collective-permute-start(bf16[192,2560]{1,0:T(8,128)(2,1)} %collective-permute-done), channel_id=1, source_target_pairs={{0,4},{4,0},{1,5},{5,1},{2,6},{6,2},{3,7},{7,3},{8,12},{12,8},{9,1... | collective-permute-start | bytes 2949128 | tf_op jit(solution)/shard_map/ppermute | solution.py:95
  261.1 45.1 %collective-permute-start.17 = (bf16[192,1280]{1,0:T(8,128)(2,1)S(1)}, bf16[192,1280]{1,0:T(8,128)(2,1)S(1)}, u32[]{:S(2)}, u32[]{:S(2)}) collective-permute-start(bf16[192,1280]{1,0:T(8,128)(2,1)S(1)} %collective-permute-done.16), channel_id=1, source_target_pairs={{0,4},{4,0},{1,5},{5,1},{2,6},{6,2},{3,7},{7,3},{8,12},{12,8},{9,1... | collective-permute-start | bytes 1474568 | tf_op jit(solution)/shard_map/ppermute | solution.py:95
  304.0 23.3 %collective-permute-start.12 = (bf16[192,2560]{1,0:T(8,128)(2,1)S(1)}, bf16[192,2560]{1,0:T(8,128)(2,1)S(1)}, u32[]{:S(2)}, u32[]{:S(2)}) collective-permute-start(bf16[192,2560]{1,0:T(8,128)(2,1)S(1)} %collective-permute-done.11), channel_id=1, source_target_pairs={{0,4},{4,0},{1,5},{5,1},{2,6},{6,2},{3,7},{7,3},{8,12},{12,8},{9,1... | collective-permute-start | bytes 2949128 | tf_op jit(solution)/shard_map/ppermute | solution.py:95
  336.3 280.7 %reduce-scatter.4.cloned.1.call-start = ((), (), s32[]{:S(2)}) async-start(), calls=%async_computation.6 | async-start | bytes 13369344 | tf_op jit(solution)/shard_map/reduce_scatter | solution.py:330
  340.6 43.3 %copy-start.3 = (bf16[4096,1280]{1,0:T(8,128)(2,1)}, bf16[4096,1280]{1,0:T(8,128)(2,1)S(1)}, u32[]{:S(2)}) copy-start(bf16[4096,1280]{1,0:T(8,128)(2,1)S(1)} %convolution_convert_fusion.2) | copy-start | bytes 31457284
  447.1 319.6 %reduce-scatter.6.cloned.1.call-start = ((), (), s32[]{:S(2)}) async-start(), calls=%async_computation.7 | async-start | bytes 14483456 | tf_op jit(solution)/shard_map/reduce_scatter | solution.py:368
  471.0 82.0 %collective-permute-start.18 = (bf16[192,1280]{1,0:T(8,128)(2,1)}, bf16[192,1280]{1,0:T(8,128)(2,1)}, u32[]{:S(2)}, u32[]{:S(2)}) collective-permute-start(bf16[192,1280]{1,0:T(8,128)(2,1)} %get-tuple-element.177), channel_id=1, source_target_pairs={{0,4},{4,0},{1,5},{5,1},{2,6},{6,2},{3,7},{7,3},{8,12},{12,8},{9,1... | collective-permute-start | bytes 1474568 | tf_op jit(solution)/shard_map/ppermute | solution.py:95
  472.5 80.6 %collective-permute-start.19 = (bf16[192,1280]{1,0:T(8,128)(2,1)}, bf16[192,1280]{1,0:T(8,128)(2,1)}, u32[]{:S(2)}, u32[]{:S(2)}) collective-permute-start(bf16[192,1280]{1,0:T(8,128)(2,1)} %get-tuple-element.176), channel_id=1, source_target_pairs={{0,4},{4,0},{1,5},{5,1},{2,6},{6,2},{3,7},{7,3},{8,12},{12,8},{9,1... | collective-permute-start | bytes 1474568 | tf_op jit(solution)/shard_map/ppermute | solution.py:95
  473.1 80.0 %collective-permute-start.20 = (bf16[192,1280]{1,0:T(8,128)(2,1)}, bf16[192,1280]{1,0:T(8,128)(2,1)}, u32[]{:S(2)}, u32[]{:S(2)}) collective-permute-start(bf16[192,1280]{1,0:T(8,128)(2,1)} %get-tuple-element.175), channel_id=1, source_target_pairs={{0,4},{4,0},{1,5},{5,1},{2,6},{6,2},{3,7},{7,3},{8,12},{12,8},{9,1... | collective-permute-start | bytes 1474568 | tf_op jit(solution)/shard_map/ppermute | solution.py:95
  474.5 78.5 %collective-permute-start.21 = (bf16[192,1280]{1,0:T(8,128)(2,1)}, bf16[192,1280]{1,0:T(8,128)(2,1)}, u32[]{:S(2)}, u32[]{:S(2)}) collective-permute-start(bf16[192,1280]{1,0:T(8,128)(2,1)} %get-tuple-element.174), channel_id=1, source_target_pairs={{0,4},{4,0},{1,5},{5,1},{2,6},{6,2},{3,7},{7,3},{8,12},{12,8},{9,1... | collective-permute-start | bytes 1474568 | tf_op jit(solution)/shard_map/ppermute | solution.py:95
  556.4 26.6 %collective-permute-start.22 = (bf16[192,1280]{1,0:T(8,128)(2,1)}, bf16[192,1280]{1,0:T(8,128)(2,1)S(1)}, u32[]{:S(2)}, u32[]{:S(2)}) collective-permute-start(bf16[192,1280]{1,0:T(8,128)(2,1)} %get-tuple-element.112), channel_id=1, source_target_pairs={{0,8},{8,16},{16,24},{24,0},{1,9},{9,17},{17,25},{25,1},{2,10},{10... | collective-permute-start | bytes 1474568 | tf_op jit(solution)/shard_map/ppermute | solution.py:236
  557.1 57.5 %collective-permute-start.23 = (bf16[192,1280]{1,0:T(8,128)(2,1)}, bf16[192,1280]{1,0:T(8,128)(2,1)S(1)}, u32[]{:S(2)}, u32[]{:S(2)}) collective-permute-start(bf16[192,1280]{1,0:T(8,128)(2,1)} %get-tuple-element.113), channel_id=1, source_target_pairs={{0,16},{8,24},{16,0},{24,8},{1,17},{9,25},{17,1},{25,9},{2,18},{10... | collective-permute-start | bytes 1474568 | tf_op jit(solution)/shard_map/ppermute | solution.py:236
  558.8 55.8 %collective-permute-start.24 = (bf16[192,1280]{1,0:T(8,128)(2,1)}, bf16[192,1280]{1,0:T(8,128)(2,1)S(1)}, u32[]{:S(2)}, u32[]{:S(2)}) collective-permute-start(bf16[192,1280]{1,0:T(8,128)(2,1)} %get-tuple-element.114), channel_id=1, source_target_pairs={{0,24},{8,0},{16,8},{24,16},{1,25},{9,1},{17,9},{25,17},{2,26},{10... | collective-permute-start | bytes 1474568 | tf_op jit(solution)/shard_map/ppermute | solution.py:236
  617.0 373.2 %reduce-scatter.8.cloned.1.call-start = ((), (), s32[]{:S(2)}) async-start(), calls=%async_computation.8 | async-start | bytes 3981312 | tf_op jit(solution)/shard_map/reduce_scatter | solution.py:460
  663.7 24.9 %collective-permute-start.25 = (bf16[192,2560]{1,0:T(8,128)(2,1)}, bf16[192,2560]{1,0:T(8,128)(2,1)}, u32[]{:S(2)}, u32[]{:S(2)}) collective-permute-start(bf16[192,2560]{1,0:T(8,128)(2,1)} %get-tuple-element.167), channel_id=1, source_target_pairs={{0,4},{4,0},{1,5},{5,1},{2,6},{6,2},{3,7},{7,3},{8,12},{12,8},{9,1... | collective-permute-start | bytes 2949128 | tf_op jit(solution)/shard_map/ppermute | solution.py:95
  665.0 44.8 %collective-permute-start.26 = (bf16[192,2560]{1,0:T(8,128)(2,1)}, bf16[192,2560]{1,0:T(8,128)(2,1)}, u32[]{:S(2)}, u32[]{:S(2)}) collective-permute-start(bf16[192,2560]{1,0:T(8,128)(2,1)} %get-tuple-element.166), channel_id=1, source_target_pairs={{0,4},{4,0},{1,5},{5,1},{2,6},{6,2},{3,7},{7,3},{8,12},{12,8},{9,1... | collective-permute-start | bytes 2949128 | tf_op jit(solution)/shard_map/ppermute | solution.py:95
  665.7 65.0 %collective-permute-start.27 = (bf16[192,2560]{1,0:T(8,128)(2,1)}, bf16[192,2560]{1,0:T(8,128)(2,1)}, u32[]{:S(2)}, u32[]{:S(2)}) collective-permute-start(bf16[192,2560]{1,0:T(8,128)(2,1)} %get-tuple-element.165), channel_id=1, source_target_pairs={{0,4},{4,0},{1,5},{5,1},{2,6},{6,2},{3,7},{7,3},{8,12},{12,8},{9,1... | collective-permute-start | bytes 2949128 | tf_op jit(solution)/shard_map/ppermute | solution.py:95
  667.0 81.9 %collective-permute-start.28 = (bf16[192,2560]{1,0:T(8,128)(2,1)}, bf16[192,2560]{1,0:T(8,128)(2,1)}, u32[]{:S(2)}, u32[]{:S(2)}) collective-permute-start(bf16[192,2560]{1,0:T(8,128)(2,1)} %get-tuple-element.164), channel_id=1, source_target_pairs={{0,4},{4,0},{1,5},{5,1},{2,6},{6,2},{3,7},{7,3},{8,12},{12,8},{9,1... | collective-permute-start | bytes 2949128 | tf_op jit(solution)/shard_map/ppermute | solution.py:95
  778.5 19.2 %copy-start.7 = (f32[256,1536]{1,0:T(8,128)}, f32[256,1536]{1,0:T(8,128)S(1)}, u32[]{:S(2)}) copy-start(f32[256,1536]{1,0:T(8,128)S(1)} %get-tuple-element.220) | copy-start | bytes 4718596
  779.1 25.8 %copy-start.72 = (f32[2,3,1024]{2,1,0:T(4,128)S(1)}, f32[2,3,1024]{2,1,0:T(4,128)}, u32[]{:S(2)}) copy-start(f32[2,3,1024]{2,1,0:T(4,128)} %copy-done.71) | copy-start | bytes 73732
  779.1 25.7 %copy-start.74 = (f32[2,3,1024]{2,1,0:T(4,128)S(1)}, f32[2,3,1024]{2,1,0:T(4,128)}, u32[]{:S(2)}) copy-start(f32[2,3,1024]{2,1,0:T(4,128)} %copy-done.73) | copy-start | bytes 73732
  779.1 25.8 %copy-start.17 = (bf16[256,1536]{1,0:T(8,128)(2,1)S(1)}, bf16[256,1536]{1,0:T(8,128)(2,1)}, u32[]{:S(2)}) copy-start(bf16[256,1536]{1,0:T(8,128)(2,1)} %copy-done.16) | copy-start | bytes 2359300
  779.1 18.5 %collective-permute-start.29 = (bf16[256,1536]{1,0:T(8,128)(2,1)S(1)}, bf16[256,1536]{1,0:T(8,128)(2,1)S(1)}, u32[]{:S(2)}, u32[]{:S(2)}) collective-permute-start(bf16[256,1536]{1,0:T(8,128)(2,1)S(1)} %fusion.101), channel_id=1, source_target_pairs={{0,2},{1,3},{2,0},{3,1},{4,6},{5,7},{6,4},{7,5},{8,10},{9,11},{10,... | collective-permute-start | bytes 2359304 | tf_op jit(solution)/shard_map/ppermute | solution.py:95
  781.5 23.3 %collective-permute-start.30 = (bf16[192,1280]{1,0:T(8,128)(2,1)S(1)}, bf16[192,1280]{1,0:T(8,128)(2,1)S(1)}, u32[]{:S(2)}, u32[]{:S(2)}) collective-permute-start(bf16[192,1280]{1,0:T(8,128)(2,1)S(1)} %get-tuple-element.203), channel_id=1, source_target_pairs={{0,16},{8,24},{16,0},{24,8},{1,17},{9,25},{17,1},{25,9},{2,18},{10... | collective-permute-start | bytes 1474568 | tf_op jit(solution)/shard_map/ppermute | solution.py:236
  804.7 3.4 collective-permute-start.31
  806.4 32.5 %collective-permute-start.32 = (bf16[192,1280]{1,0:T(8,128)(2,1)}, bf16[192,1280]{1,0:T(8,128)(2,1)}, u32[]{:S(2)}, u32[]{:S(2)}) collective-permute-start(bf16[192,1280]{1,0:T(8,128)(2,1)} %get-tuple-element.127), channel_id=1, source_target_pairs={{0,16},{8,24},{16,0},{24,8},{1,17},{9,25},{17,1},{25,9},{2,18},{10... | collective-permute-start | bytes 1474568 | tf_op jit(solution)/shard_map/ppermute | solution.py:236
  853.0 25.9 %copy-start.38 = (f32[1024,32]{0,1:T(8,128)S(1)}, f32[1024,32]{0,1:T(8,128)}, u32[]{:S(2)}) copy-start(f32[1024,32]{0,1:T(8,128)} %copy-done.37) | copy-start | bytes 393220
  853.0 25.9 %copy-start.55 = (f32[1024,32]{0,1:T(8,128)S(1)}, f32[1024,32]{0,1:T(8,128)}, u32[]{:S(2)}) copy-start(f32[1024,32]{0,1:T(8,128)} %get-tuple-element.213) | copy-start | bytes 393220
  853.0 27.5 %copy-start.23 = (f32[1024,2,64]{0,2,1:T(8,128)S(1)}, f32[1024,2,64]{0,2,1:T(8,128)}, u32[]{:S(2)}) copy-start(f32[1024,2,64]{0,2,1:T(8,128)} %fusion.62) | copy-start | bytes 1572868
  853.0 25.9 %collective-permute-start.33 = (bf16[192,2560]{1,0:T(8,128)(2,1)}, bf16[192,2560]{1,0:T(8,128)(2,1)}, u32[]{:S(2)}, u32[]{:S(2)}) collective-permute-start(bf16[192,2560]{1,0:T(8,128)(2,1)} %get-tuple-element.131), channel_id=1, source_target_pairs={{0,8},{8,16},{16,24},{24,0},{1,9},{9,17},{17,25},{25,1},{2,10},{10... | collective-permute-start | bytes 2949128 | tf_op jit(solution)/shard_map/ppermute | solution.py:236
  899.6 26.0 %collective-permute-start.34 = (bf16[2,256,1536]{2,1,0:T(8,128)(2,1)}, bf16[2,256,1536]{2,1,0:T(8,128)(2,1)}, u32[]{:S(2)}, u32[]{:S(2)}) collective-permute-start(bf16[2,256,1536]{2,1,0:T(8,128)(2,1)} %dynamic-slice_bitcast_fusion), channel_id=1, source_target_pairs={{0,1},{1,0},{2,3},{3,2},{4,5},{5,4},{6,7},{7,6},{8,9},{9,8},{10,11... | collective-permute-start | bytes 4718600 | tf_op jit(solution)/shard_map/ppermute | solution.py:95
  921.9 32.7 %collective-permute-start.39 = (bf16[192,2560]{1,0:T(8,128)(2,1)}, bf16[192,2560]{1,0:T(8,128)(2,1)}, u32[]{:S(2)}, u32[]{:S(2)}) collective-permute-start(bf16[192,2560]{1,0:T(8,128)(2,1)} %get-tuple-element.138), channel_id=1, source_target_pairs={{0,24},{8,0},{16,8},{24,16},{1,25},{9,1},{17,9},{25,17},{2,26},{10... | collective-permute-start | bytes 2949128 | tf_op jit(solution)/shard_map/ppermute | solution.py:236
  927.9 28.9 %copy-start.11 = (bf16[256,1536]{1,0:T(8,128)(2,1)S(1)}, bf16[256,1536]{1,0:T(8,128)(2,1)}, u32[]{:S(2)}) copy-start(bf16[256,1536]{1,0:T(8,128)(2,1)} %param.14) | copy-start | bytes 2359300
  928.0 28.8 %collective-permute-start.35 = (bf16[256,1536]{1,0:T(8,128)(2,1)S(1)}, bf16[256,1536]{1,0:T(8,128)(2,1)S(1)}, u32[]{:S(2)}, u32[]{:S(2)}) collective-permute-start(bf16[256,1536]{1,0:T(8,128)(2,1)S(1)} %fusion.77), channel_id=1, source_target_pairs={{0,2},{1,3},{2,0},{3,1},{4,6},{5,7},{6,4},{7,5},{8,10},{9,11},{10,... | collective-permute-start | bytes 2359304 | tf_op jit(solution)/shard_map/ppermute | solution.py:95
  987.9 17.9 %copy-start.1 = (s32[1024,8]{0,1:T(8,128)S(1)}, s32[1024,8]{0,1:T(8,128)}, u32[]{:S(2)}) copy-start(s32[1024,8]{0,1:T(8,128)} %param.17) | copy-start | bytes 98308
  991.2 8.6 collective-permute-start.36
  991.3 8.6 collective-permute-start.37
  992.9 10.1 collective-permute-start.38
  (71 other events, 400.3 us)
Sparse Core Ops, SparseCore 0:
  11.7 67.3 all-gather.3
  183.0 153.1 all-gather.5
  339.1 107.9 all-gather.7
  451.0 165.9 reduce-scatter.3
  620.9 145.7 reduce-scatter.5
  897.0 86.3 reduce-scatter.7

commit v7 on v6

--- a/solution.py
+++ b/solution.py
@@ -257,10 +257,10 @@
         ).astype(bf16)
         values = qkv[:, q_cols + k_cols :].astype(bf16).reshape(group, -1, HEAD_DIM)
         attended, log_total = attend_forward(query, keys, values, prefix[0])
-        far_down, far_gate_up, owned[0], attended = tie(
-            pieces[2][1], far_gate_up, owned[0], attended
-        )
-        far_down = to_owner(far_down, 2)
+        far_down, near, far_gate_up, owned[0], attended = tie(
+            pieces[2][1], pieces[1], far_gate_up, owned[0], attended
+        )
+        far_down, near = to_owner(far_down, 2), to_owner(near, 1)
         branch = lax.dot_general(
             attended, w_out_t, (((1,), (1,)), ((), ())), preferred_element_type=f32
         ).astype(bf16)
@@ -286,8 +286,8 @@
             ],
             axis=1,
         )
-        last, near, far_down, shipped = tie(pieces[3], pieces[1], far_down, shipped)
-        last, near = to_owner(last, 3), to_owner(near, 1)
+        last, near, far_down, shipped = tie(pieces[3], near, far_down, shipped)
+        last = to_owner(last, 3)
         owned += [pass_on(near), pass_on((far_gate_up, far_down)), pass_on(last)]
         shared_all = by_rows(lax.all_gather(by_rows(shipped), shared, axis=0, tiled=True))
         w_gate_up = jnp.zeros((outer, inner, depth, 2 * own_hidden), bf16)
@@ -356,7 +356,9 @@
             ],
             axis=1,
         )
-        products, down_sums = tie((silu_g * up_part * cot_part).astype(bf16), down_sums)
+        products, down_sums, w_gate_up = tie(
+            (silu_g * up_part * cot_part).astype(bf16), down_sums, w_gate_up
+        )
         sent_down = down_sums[:1] + [to_owner(down_sums[s], s) for s in range(1, inner)]
         chosen = (jnp.arange(side_cols, dtype=jnp.int32)[None, :] == owner.T).astype(bf16)
         gate_block = jnp.dot(products, chosen, preferred_element_type=f32)

time: 1030 us -> 1010 us (0.981)
  waiting for transfers between devices: 393 us -> 362 us
  starting transfers between devices: 42.6 us -> 54.6 us
    ppermute x13, waiting for transfers between devices: 188 us -> 117 us  [to_owner(): return jax.tree.map(lambda part: lax.ppermute(part, 'i', pairs), piece)]
    reduce_scatter x1, waiting for transfers between devices: 2.41 us -> 27.4 us  [on_device(): lax.psum_scatter(expert_part, shared, scatter_dimension=0, tiled=True)]
    all_gather x1, waiting for transfers between devices: 7.59 us -> 27.7 us  [on_device(): lax.all_gather(by_rows(shipped), shared, axis=0, tiled=True)]
  transfers between devices with their start and end apart: 46 -> 46, of which waited for: 27 -> 27; matrix products, arithmetic and copies ran while one was open for 47% -> 48% of each run, Pallas kernels for 0% -> 0%
where the time goes in v7:
time: 1010 us; the launch traced here: 999 us
  waiting for transfers between devices  362 us (36%)
  matrix products  314 us (31%)
  local copies, waits for them, and re-layouts  158 us (16%)
  other arithmetic  93.7 us (9%)
  starting transfers between devices  54.6 us (5%)
  between operations  16.6 us (2%)
    ppermute x24, waiting for transfers between devices, swap(): return lax.ppermute(values, axis, [(m, m ^ bit) for m in range(size)])  139 us
    ppermute x13, waiting for transfers between devices, to_owner(): return jax.tree.map(lambda part: lax.ppermute(part, 'i', pairs), piece)  117 us
    dot_general x1, matrix products, on_device(): jnp.dot(normed_all, w_gate_up, preferred_element_type=f32).astype(bf16)  43.6 us
    dot_general x1, matrix products, on_device(): lax.dot_general(shared_rows[:, :width], grad_gate_up, contract_rows, pref...  41.3 us
    dot_general x1, matrix products, on_device(): lax.dot_general(grad_gate_up, w_gate_up, (((1,), (1,)), ((), ())), prefer...  39.8 us
    dot_general x1, matrix products, on_device(): cot_part = jnp.dot(cot_all, w_down_t, preferred_element_type=f32)  37.9 us
    convert_element_type x16, local copies, waits for them, and re-layouts, on_device(): jnp.swapaxes(part.reshape(depth, own_experts, hidden), 0, 1).astype(f32)  30.4 us
    ppermute x13, starting transfers between devices, to_owner(): return jax.tree.map(lambda part: lax.ppermute(part, 'i', pairs), piece)  28.1 us
  transfers between devices with their start and end apart: 46, of which 27 were waited for; matrix products, arithmetic and copies ran while one was open for 48% of the time, Pallas kernels for 0%

profile of v7, /device:TPU:0, one launch (start us, length us, event | category | flops | bytes accessed | tf_op | source)
XLA Modules:
  0.0 998.8 jit_solution(7197861579110892965)
XLA Ops:
  11.6 3.1 collective-permute-start.3
  14.7 3.9 dynamic-slice_bitcast_fusion.19
  52.9 26.1 %all-gather.4.cloned.1.call-done = bf16[1536,1152]{1,0:T(8,128)(2,1)} async-done(((bf16[192,1152]{1,0:T(8,128)(2,1)}), bf16[1536,1152]{1,0:T(8,128)(2,1)}) %all-gather.4.cloned.1.call-update) | async-done | bytes 3538960 | tf_op jit(solution)/shard_map/all_gather | solution.py:219
  80.9 4.2 fusion.50
  92.0 5.7 fusion.107
  97.7 3.8 fusion.3
  101.5 4.6 copy-done.2
  106.6 10.5 %fusion.57 = bf16[2,64,3,1024]{3,1,2,0:T(8,128)(2,1)S(1)} fusion(bf16[1024,2,64,1]{0,2,3,1:T(8,128)(2,1)S(1)} %bitcast.393, f32[2,3,1024,1024]{2,3,1,0:T(8,128)} %copy-done.2, f32[2,3,1024]{2,1,0:T(4,128)S(1)} %fusion.3, f32[2,3,1024]{2,1,0:T(4,128)S(1)} %get-tuple-element.222), kind=kOutput, calls=%fused_computation.114 | convolution fusion | flops 824573952 | bytes 26263552 | tf_op jit(solution)/shard_map/hgqk,khd->qhgd/dot_general | solution.py:65
  122.3 11.2 %collective-permute-done = bf16[192,2560]{1,0:T(8,128)(2,1)} collective-permute-done((bf16[192,2560]{1,0:T(8,128)(2,1)}, bf16[192,2560]{1,0:T(8,128)(2,1)}, u32[]{:S(2)}, u32[]{:S(2)}) %collective-permute-start) | collective-permute-done | bytes 983072 | tf_op jit(solution)/shard_map/ppermute | solution.py:236
  133.5 3.1 convolution_convert_fusion.6
  139.6 3.7 collective-permute-done.5
  150.7 11.0 %collective-permute-start.8 = (bf16[192,1280]{1,0:T(8,128)(2,1)S(1)}, bf16[192,1280]{1,0:T(8,128)(2,1)}, u32[]{:S(2)}, u32[]{:S(2)}) collective-permute-start(bf16[192,1280]{1,0:T(8,128)(2,1)S(1)} %copy-done.63), channel_id=1, source_target_pairs={{0,8},{8,16},{16,24},{24,0},{1,9},{9,17},{17,25},{25,1},{2,10},{10... | collective-permute-start | bytes 1474568 | tf_op jit(solution)/shard_map/ppermute | solution.py:236
  161.7 3.4 collective-permute-start.9
  165.1 3.1 collective-permute-done.6
  182.8 4.6 collective-permute-done.8
  187.4 19.9 %collective-permute-done.9 = bf16[192,1280]{1,0:T(8,128)(2,1)} collective-permute-done((bf16[192,1280]{1,0:T(8,128)(2,1)}, bf16[192,1280]{1,0:T(8,128)(2,1)}, u32[]{:S(2)}, u32[]{:S(2)}) %collective-permute-start.9) | collective-permute-done | bytes 491552 | tf_op jit(solution)/shard_map/ppermute | solution.py:236
  210.2 3.9 broadcast_in_dim.123
  219.3 10.4 %collective-permute-done.14 = bf16[192,1280]{1,0:T(8,128)(2,1)S(1)} collective-permute-done((bf16[192,1280]{1,0:T(8,128)(2,1)}, bf16[192,1280]{1,0:T(8,128)(2,1)S(1)}, u32[]{:S(2)}, u32[]{:S(2)}) %collective-permute-start.14) | collective-permute-done | bytes 491552 | tf_op jit(solution)/shard_map/ppermute | solution.py:95
  230.4 20.4 %collective-permute-done.16 = bf16[192,1280]{1,0:T(8,128)(2,1)S(1)} collective-permute-done((bf16[192,1280]{1,0:T(8,128)(2,1)S(1)}, bf16[192,1280]{1,0:T(8,128)(2,1)S(1)}, u32[]{:S(2)}, u32[]{:S(2)}) %collective-permute-start.16) | collective-permute-done | bytes 491552 | tf_op jit(solution)/shard_map/ppermute | solution.py:236
  253.4 20.7 %collective-permute-done.12 = bf16[192,2560]{1,0:T(8,128)(2,1)S(1)} collective-permute-done((bf16[192,2560]{1,0:T(8,128)(2,1)S(1)}, bf16[192,2560]{1,0:T(8,128)(2,1)S(1)}, u32[]{:S(2)}, u32[]{:S(2)}) %collective-permute-start.12) | collective-permute-done | bytes 983072 | tf_op jit(solution)/shard_map/ppermute | solution.py:236
  275.6 17.4 %collective-permute-done.17 = bf16[192,1280]{1,0:T(8,128)(2,1)S(1)} collective-permute-done((bf16[192,1280]{1,0:T(8,128)(2,1)S(1)}, bf16[192,1280]{1,0:T(8,128)(2,1)S(1)}, u32[]{:S(2)}, u32[]{:S(2)}) %collective-permute-start.17) | collective-permute-done | bytes 491552 | tf_op jit(solution)/shard_map/ppermute | solution.py:95
  293.0 3.5 fusion.39
  299.1 14.0 %collective-permute-done.13 = bf16[192,2560]{1,0:T(8,128)(2,1)S(1)} collective-permute-done((bf16[192,2560]{1,0:T(8,128)(2,1)S(1)}, bf16[192,2560]{1,0:T(8,128)(2,1)S(1)}, u32[]{:S(2)}, u32[]{:S(2)}) %collective-permute-start.13) | collective-permute-done | bytes 983072 | tf_op jit(solution)/shard_map/ppermute | solution.py:95
  314.5 27.7 %all-gather.6.cloned.1.call-done = bf16[4096,1664]{1,0:T(8,128)(2,1)} async-done(((bf16[256,1664]{1,0:T(8,128)(2,1)}), bf16[4096,1664]{1,0:T(8,128)(2,1)}) %all-gather.6.cloned.1.call-update) | async-done | bytes 13631504 | tf_op jit(solution)/shard_map/all_gather | solution.py:292
  342.3 4.1 convolution_convert_fusion.2
  346.5 43.6 %convolution_convert_fusion = bf16[4096,2560]{1,0:T(8,128)(2,1)} fusion(bf16[1536,2560]{1,0:T(8,128)(2,1)} %bitcast.70, bf16[4096,1664]{1,0:T(8,128)(2,1)} %all-gather.6.cloned.1.call-done), kind=kOutput, calls=%fused_computation.16 | convolution fusion | flops 32222740480 | bytes 41418752 | tf_op jit(solution)/shard_map/dot_general | solution.py:313
  390.1 11.6 %fusion.18 = bf16[4096,1280]{1,0:T(8,128)(2,1)S(1)} fusion(bf16[4096,1280]{1,0:T(8,128)(2,1)S(1)} %convolution_convert_fusion.2, bf16[4096,2560]{1,0:T(8,128)(2,1)} %convolution_convert_fusion), kind=kLoop, calls=%fused_computation.35 | loop fusion | flops 52428800 | bytes 41943040 | tf_op jit(solution)/shard_map/convert_element_type | solution.py:323
  401.7 3.9 copy-done.14
  405.7 20.9 %convolution_convert_fusion.1 = bf16[4096,1536]{1,0:T(8,128)(2,1)} fusion(bf16[4096,1280]{1,0:T(8,128)(2,1)S(1)} %fusion.18, bf16[1536,1280]{1,0:T(8,128)(2,1)} %bitcast.349), kind=kOutput, calls=%fused_computation.37 | convolution fusion | flops 16112418816 | bytes 27000832 | tf_op jit(solution)/shard_map/dot_general | solution.py:324
  426.5 17.2 %all-gather.8.cloned.1.call-done = bf16[4096,1536]{1,0:T(8,128)(2,1)} async-done(((bf16[256,1536]{1,0:T(8,128)(2,1)}), bf16[4096,1536]{1,0:T(8,128)(2,1)}) %all-gather.8.cloned.1.call-update) | async-done | bytes 12582928 | tf_op jit(solution)/shard_map/all_gather | solution.py:305
  444.2 22.3 %convolution_convert_fusion.4 = bf16[1536,1280]{1,0:T(8,128)(2,1)S(1)} fusion(bf16[4096,1536]{1,0:T(8,128)(2,1)} %all-gather.8.cloned.1.call-done, bf16[4096,1280]{1,0:T(8,128)(2,1)} %copy-done.14), kind=kOutput, calls=%fused_computation.52 | convolution fusion | flops 16108093440 | bytes 27000832 | tf_op jit(solution)/shard_map/dot_general | solution.py:332
  472.0 37.9 %fusion.11 = (bf16[4096,1280]{1,0:T(8,128)(2,1)}, bf16[4096,1280]{1,0:T(8,128)(2,1)}, bf16[4096,1280]{1,0:T(8,128)(2,1)}) fusion(bf16[4096,1280]{1,0:T(8,128)(2,1)} %copy-done.3, bf16[4096,2560]{1,0:T(8,128)(2,1)} %convolution_convert_fusion, bf16[4096,1536]{1,0:T(8,128)(2,1)} %all-gather.8.cloned.1.call-done, bf16[1536,1280]{1,0:T(8,128)(2,1)S(1)} %bitcast.350), kind=kOutput, calls=%fused_computation.25 | convolution fusion | flops 16210984960 | bytes 79429632 | tf_op jit(solution)/shard_map/dot_general | solution.py:347
  509.9 3.3 collective-permute-done.21
  513.2 3.1 fusion.69
  520.9 7.0 convolution_convert_fusion.5
  527.9 39.8 %convolution_convert_fusion.3 = bf16[4096,1536]{1,0:T(8,128)(2,1)} fusion(bf16[1536,2560]{1,0:T(8,128)(2,1)} %bitcast.70, bf16[4096,1280]{1,0:T(8,128)(2,1)} %get-tuple-element.164, bf16[4096,1280]{1,0:T(8,128)(2,1)} %get-tuple-element.163), kind=kOutput, calls=%fused_computation.39 | convolution fusion | flops 32260489216 | bytes 41418752 | tf_op jit(solution)/shard_map/dot_general | solution.py:365
  567.7 12.1 %pad_maximum_fusion.1 = bf16[4096,1664]{1,0:T(8,128)(2,1)} fusion(bf16[4096,128]{1,0:T(8,128)(2,1)S(1)} %convolution_convert_fusion.5, bf16[4096,1536]{1,0:T(8,128)(2,1)} %convolution_convert_fusion.3), kind=kLoop, calls=%fused_computation.40 | loop fusion | flops 27262976 | bytes 27262976 | tf_op jit(solution)/shard_map/concatenate | solution.py:368
  579.9 27.4 %reduce-scatter.4.cloned.1.call-done = bf16[256,1536]{1,0:T(8,128)(2,1)} async-done(((bf16[4096,1536]{1,0:T(8,128)(2,1)}), bf16[256,1536]{1,0:T(8,128)(2,1)}) %reduce-scatter.4.cloned.1.call-update) | async-done | bytes 786448 | tf_op jit(solution)/shard_map/reduce_scatter | solution.py:330
  607.4 41.3 %fusion.27 = bf16[1536,2560]{1,0:T(8,128)(2,1)} fusion(bf16[4096,1280]{1,0:T(8,128)(2,1)} %get-tuple-element.164, bf16[4096,1280]{1,0:T(8,128)(2,1)} %get-tuple-element.163, bf16[4096,1664]{1,0:T(8,128)(2,1)} %all-gather.6.cloned.1.call-done), kind=kOutput, calls=%fused_computation.47 | convolution fusion | flops 32258129920 | bytes 41418752 | tf_op jit(solution)/shard_map/dot_general | solution.py:372
  648.7 4.1 dynamic-slice_bitcast_fusion.2
  670.0 7.8 collective-permute-done.25
  677.8 21.1 %collective-permute-done.26 = bf16[192,2560]{1,0:T(8,128)(2,1)} collective-permute-done((bf16[192,2560]{1,0:T(8,128)(2,1)}, bf16[192,2560]{1,0:T(8,128)(2,1)}, u32[]{:S(2)}, u32[]{:S(2)}) %collective-permute-start.26) | collective-permute-done | bytes 983072 | tf_op jit(solution)/shard_map/ppermute | solution.py:95
  698.9 21.1 %collective-permute-done.27 = bf16[192,2560]{1,0:T(8,128)(2,1)} collective-permute-done((bf16[192,2560]{1,0:T(8,128)(2,1)}, bf16[192,2560]{1,0:T(8,128)(2,1)}, u32[]{:S(2)}, u32[]{:S(2)}) %collective-permute-start.27) | collective-permute-done | bytes 983072 | tf_op jit(solution)/shard_map/ppermute | solution.py:95
  719.9 19.1 %collective-permute-done.28 = bf16[192,2560]{1,0:T(8,128)(2,1)} collective-permute-done((bf16[192,2560]{1,0:T(8,128)(2,1)}, bf16[192,2560]{1,0:T(8,128)(2,1)}, u32[]{:S(2)}, u32[]{:S(2)}) %collective-permute-start.28) | collective-permute-done | bytes 983072 | tf_op jit(solution)/shard_map/ppermute | solution.py:95
  739.1 6.1 fusion.42
  745.2 7.6 reduce-scatter.6.cloned.1.call-done
  757.5 3.0 copy.389
  761.6 2.9 multiply_reduce_fusion
  769.1 14.5 %collective-permute-done.29 = bf16[256,1536]{1,0:T(8,128)(2,1)S(1)} collective-permute-done((bf16[256,1536]{1,0:T(8,128)(2,1)S(1)}, bf16[256,1536]{1,0:T(8,128)(2,1)S(1)}, u32[]{:S(2)}, u32[]{:S(2)}) %collective-permute-start.29) | collective-permute-done | bytes 786464 | tf_op jit(solution)/shard_map/ppermute | solution.py:95
  783.7 7.0 collective-permute-done.30
  794.3 2.9 convolution_convert_fusion.8
  797.2 2.8 convolution_convert_fusion.9
  800.8 24.3 %fusion.2 = bf16[2,3,1024,1024]{2,3,1,0:T(8,128)(2,1)} fusion(f32[2,3,1024,1024]{2,3,1,0:T(8,128)} %copy-done.2, f32[2,3,1024]{2,1,0:T(4,128)S(1)} %log_add_fusion, bf16[1024,2,64,1]{0,2,3,1:T(8,128)(2,1)S(1)} %bitcast.394, bf16[1024,2,3,64]{0,3,2,1:T(8,128)(2,1)S(1)} %bitcast.383), kind=kOutput, calls=%fused_computation.11 | convolution fusion | flops 1648368640 | bytes 38821888 | tf_op jit(solution)/shard_map/sub | solution.py:78
  825.2 9.7 fusion.62
  834.8 4.3 convolution_multiply_fusion
  839.2 2.8 collective-permute-start.33
  842.0 13.1 %fusion.58 = bf16[1024,2,64]{0,2,1:T(8,128)(2,1)} fusion(bf16[1024,2,3,64]{0,3,2,1:T(8,128)(2,1)} %bitcast.384, f32[2,3,1024,1024]{2,3,1,0:T(8,128)} %copy-done.2, f32[2,3,1024]{2,1,0:T(4,128)S(1)} %log_add_fusion), kind=kOutput, calls=%fused_computation.117 | convolution fusion | flops 817889280 | bytes 26238976 | tf_op jit(solution)/shard_map/hgqk,qhgd->khd/dot_general | solution.py:88
  855.1 10.0 %collective-permute-done.33 = bf16[192,2560]{1,0:T(8,128)(2,1)} collective-permute-done((bf16[192,2560]{1,0:T(8,128)(2,1)}, bf16[192,2560]{1,0:T(8,128)(2,1)}, u32[]{:S(2)}, u32[]{:S(2)}) %collective-permute-start.33) | collective-permute-done | bytes 983072 | tf_op jit(solution)/shard_map/ppermute | solution.py:236
  866.9 6.3 fusion.36
  873.2 4.3 convolution_convert_fusion.7
  879.7 3.0 pad_maximum_fusion.6
  882.8 2.7 dynamic-slice_bitcast_fusion
  889.3 3.1 copy.377
  917.5 23.1 %collective-permute-done.39 = bf16[192,2560]{1,0:T(8,128)(2,1)} collective-permute-done((bf16[192,2560]{1,0:T(8,128)(2,1)}, bf16[192,2560]{1,0:T(8,128)(2,1)}, u32[]{:S(2)}, u32[]{:S(2)}) %collective-permute-start.39) | collective-permute-done | bytes 983072 | tf_op jit(solution)/shard_map/ppermute | solution.py:236
  (430 shorter events, 219.8 us)
Async XLA Ops:
  7.2 142.6 %copy-start = (s32[1024,8]{0,1:T(8,128)S(1)}, s32[1024,8]{0,1:T(8,128)}, u32[]{:S(2)}) copy-start(s32[1024,8]{0,1:T(8,128)} %param.17) | copy-start | bytes 98308
  7.2 71.8 %all-gather.4.cloned.1.call-start = ((), (), s32[]{:S(2)}) async-start(), calls=%async_computation.3 | async-start | bytes 3981312 | tf_op jit(solution)/shard_map/all_gather | solution.py:219
  11.5 330.7 %all-gather.6.cloned.1.call-start = ((), (), s32[]{:S(2)}) async-start(), calls=%async_computation.4 | async-start | bytes 14483456 | tf_op jit(solution)/shard_map/all_gather | solution.py:292
  11.6 35.7 %collective-permute-start.3 = (bf16[256,1536]{1,0:T(8,128)(2,1)}, bf16[256,1536]{1,0:T(8,128)(2,1)}, u32[]{:S(2)}, u32[]{:S(2)}) collective-permute-start(bf16[256,1536]{1,0:T(8,128)(2,1)} %param.14), channel_id=1, source_target_pairs={{0,2},{1,3},{2,0},{3,1},{4,6},{5,7},{6,4},{7,5},{8,10},{9,11},{10,... | collective-permute-start | bytes 2359304 | tf_op jit(solution)/shard_map/ppermute | solution.py:95
  48.6 3.5 collective-permute-start.4
  49.8 37.3 %copy-start.37 = (f32[1024,32]{0,1:T(8,128)}, f32[1024,32]{0,1:T(8,128)S(1)}, u32[]{:S(2)}) copy-start(f32[1024,32]{0,1:T(8,128)S(1)} %get-tuple-element.221) | copy-start | bytes 393220
  52.2 33.0 %copy-start.12 = (bf16[1024,1536]{1,0:T(8,128)(2,1)}, bf16[1024,1536]{1,0:T(8,128)(2,1)S(1)}, u32[]{:S(2)}) copy-start(bf16[1024,1536]{1,0:T(8,128)(2,1)S(1)} %slice_dynamic-update-slice_fusion.2) | copy-start | bytes 9437188
  52.9 32.3 %copy-start.82 = (f32[1024]{0:T(1024)}, f32[1024]{0:T(1024)S(1)}, u32[]{:S(2)}) copy-start(f32[1024]{0:T(1024)S(1)} %add_rsqrt_fusion) | copy-start | bytes 12292
  80.9 90.0 %copy-start.69 = (f32[1536]{0:T(1024)}, f32[1536]{0:T(1024)S(1)}, u32[]{:S(2)}) copy-start(f32[1536]{0:T(1024)S(1)} %get-tuple-element.154) | copy-start | bytes 18436
  87.9 29.3 %collective-permute-start.2 = (bf16[192,1280]{1,0:T(8,128)(2,1)}, bf16[192,1280]{1,0:T(8,128)(2,1)}, u32[]{:S(2)}, u32[]{:S(2)}) collective-permute-start(bf16[192,1280]{1,0:T(8,128)(2,1)} %copy.329), channel_id=1, source_target_pairs={{0,4},{4,0},{1,5},{5,1},{2,6},{6,2},{3,7},{7,3},{8,12},{12,8},{9,1... | collective-permute-start | bytes 1474568 | tf_op jit(solution)/shard_map/ppermute | solution.py:95
  88.4 32.2 %collective-permute-start.1 = (bf16[192,2560]{1,0:T(8,128)(2,1)}, bf16[192,2560]{1,0:T(8,128)(2,1)}, u32[]{:S(2)}, u32[]{:S(2)}) collective-permute-start(bf16[192,2560]{1,0:T(8,128)(2,1)} %pad_maximum_fusion.11), channel_id=1, source_target_pairs={{0,4},{4,0},{1,5},{5,1},{2,6},{6,2},{3,7},{7,3},{8,12},{12,8},{9,1... | collective-permute-start | bytes 2949128 | tf_op jit(solution)/shard_map/ppermute | solution.py:95
  89.9 43.6 %collective-permute-start = (bf16[192,2560]{1,0:T(8,128)(2,1)}, bf16[192,2560]{1,0:T(8,128)(2,1)}, u32[]{:S(2)}, u32[]{:S(2)}) collective-permute-start(bf16[192,2560]{1,0:T(8,128)(2,1)} %pad_maximum_fusion.13), channel_id=1, source_target_pairs={{0,16},{8,24},{16,0},{24,8},{1,17},{9,25},{17,1},{25,9},{2,18},{10... | collective-permute-start | bytes 2949128 | tf_op jit(solution)/shard_map/ppermute | solution.py:236
  117.1 19.5 %copy-start.84 = (bf16[2,64,3,1024]{3,1,2,0:T(8,128)(2,1)}, bf16[2,64,3,1024]{3,1,2,0:T(8,128)(2,1)S(1)}, u32[]{:S(2)}) copy-start(bf16[2,64,3,1024]{3,1,2,0:T(8,128)(2,1)S(1)} %fusion.57) | copy-start | bytes 2359300
  139.6 3.8 collective-permute-start.5
  139.6 28.6 %copy-start.10 = (bf16[256,1536]{1,0:T(8,128)(2,1)S(1)}, bf16[256,1536]{1,0:T(8,128)(2,1)}, u32[]{:S(2)}) copy-start(bf16[256,1536]{1,0:T(8,128)(2,1)} %param.14) | copy-start | bytes 2359300
  148.3 19.9 %collective-permute-start.6 = (bf16[256,1536]{1,0:T(8,128)(2,1)}, bf16[256,1536]{1,0:T(8,128)(2,1)}, u32[]{:S(2)}, u32[]{:S(2)}) collective-permute-start(bf16[256,1536]{1,0:T(8,128)(2,1)} %fusion.76), channel_id=1, source_target_pairs={{0,2},{1,3},{2,0},{3,1},{4,6},{5,7},{6,4},{7,5},{8,10},{9,11},{10,... | collective-permute-start | bytes 2359304 | tf_op jit(solution)/shard_map/ppermute | solution.py:95
  150.0 57.3 %collective-permute-start.7 = (bf16[192,2560]{1,0:T(8,128)(2,1)}, bf16[192,2560]{1,0:T(8,128)(2,1)}, u32[]{:S(2)}, u32[]{:S(2)}) collective-permute-start(bf16[192,2560]{1,0:T(8,128)(2,1)} %pad_maximum_fusion.12), channel_id=1, source_target_pairs={{0,8},{8,16},{16,24},{24,0},{1,9},{9,17},{17,25},{25,1},{2,10},{10... | collective-permute-start | bytes 2949128 | tf_op jit(solution)/shard_map/ppermute | solution.py:236
  150.7 36.7 %collective-permute-start.8 = (bf16[192,1280]{1,0:T(8,128)(2,1)S(1)}, bf16[192,1280]{1,0:T(8,128)(2,1)}, u32[]{:S(2)}, u32[]{:S(2)}) collective-permute-start(bf16[192,1280]{1,0:T(8,128)(2,1)S(1)} %copy-done.63), channel_id=1, source_target_pairs={{0,8},{8,16},{16,24},{24,0},{1,9},{9,17},{17,25},{25,1},{2,10},{10... | collective-permute-start | bytes 1474568 | tf_op jit(solution)/shard_map/ppermute | solution.py:236
  161.7 45.6 %collective-permute-start.9 = (bf16[192,1280]{1,0:T(8,128)(2,1)}, bf16[192,1280]{1,0:T(8,128)(2,1)}, u32[]{:S(2)}, u32[]{:S(2)}) collective-permute-start(bf16[192,1280]{1,0:T(8,128)(2,1)} %copy.341), channel_id=1, source_target_pairs={{0,16},{8,24},{16,0},{24,8},{1,17},{9,25},{17,1},{25,9},{2,18},{10... | collective-permute-start | bytes 1474568 | tf_op jit(solution)/shard_map/ppermute | solution.py:236
  207.3 236.5 %all-gather.8.cloned.1.call-start = ((), (), s32[]{:S(2)}) async-start(), calls=%async_computation.5 | async-start | bytes 13369344 | tf_op jit(solution)/shard_map/all_gather | solution.py:305
  215.4 14.3 %collective-permute-start.14 = (bf16[192,1280]{1,0:T(8,128)(2,1)}, bf16[192,1280]{1,0:T(8,128)(2,1)S(1)}, u32[]{:S(2)}, u32[]{:S(2)}) collective-permute-start(bf16[192,1280]{1,0:T(8,128)(2,1)} %collective-permute-done.8), channel_id=1, source_target_pairs={{0,4},{4,0},{1,5},{5,1},{2,6},{6,2},{3,7},{7,3},{8,12},{12,8},{9,1... | collective-permute-start | bytes 1474568 | tf_op jit(solution)/shard_map/ppermute | solution.py:95
  216.1 36.1 %collective-permute-start.15 = (bf16[192,1280]{1,0:T(8,128)(2,1)}, bf16[192,1280]{1,0:T(8,128)(2,1)S(1)}, u32[]{:S(2)}, u32[]{:S(2)}) collective-permute-start(bf16[192,1280]{1,0:T(8,128)(2,1)} %collective-permute-done.9), channel_id=1, source_target_pairs={{0,4},{4,0},{1,5},{5,1},{2,6},{6,2},{3,7},{7,3},{8,12},{12,8},{9,1... | collective-permute-start | bytes 1474568 | tf_op jit(solution)/shard_map/ppermute | solution.py:95
  217.5 33.3 %collective-permute-start.16 = (bf16[192,1280]{1,0:T(8,128)(2,1)S(1)}, bf16[192,1280]{1,0:T(8,128)(2,1)S(1)}, u32[]{:S(2)}, u32[]{:S(2)}) collective-permute-start(bf16[192,1280]{1,0:T(8,128)(2,1)S(1)} %copy-done.61), channel_id=1, source_target_pairs={{0,24},{8,0},{16,8},{24,16},{1,25},{9,1},{17,9},{25,17},{2,26},{10... | collective-permute-start | bytes 1474568 | tf_op jit(solution)/shard_map/ppermute | solution.py:236
  217.5 75.6 %collective-permute-start.10 = (bf16[192,2560]{1,0:T(8,128)(2,1)}, bf16[192,2560]{1,0:T(8,128)(2,1)S(1)}, u32[]{:S(2)}, u32[]{:S(2)}) collective-permute-start(bf16[192,2560]{1,0:T(8,128)(2,1)} %collective-permute-done.7), channel_id=1, source_target_pairs={{0,4},{4,0},{1,5},{5,1},{2,6},{6,2},{3,7},{7,3},{8,12},{12,8},{9,1... | collective-permute-start | bytes 2949128 | tf_op jit(solution)/shard_map/ppermute | solution.py:95
  218.2 55.9 %collective-permute-start.12 = (bf16[192,2560]{1,0:T(8,128)(2,1)S(1)}, bf16[192,2560]{1,0:T(8,128)(2,1)S(1)}, u32[]{:S(2)}, u32[]{:S(2)}) collective-permute-start(bf16[192,2560]{1,0:T(8,128)(2,1)S(1)} %copy-done.56), channel_id=1, source_target_pairs={{0,24},{8,0},{16,8},{24,16},{1,25},{9,1},{17,9},{25,17},{2,26},{10... | collective-permute-start | bytes 2949128 | tf_op jit(solution)/shard_map/ppermute | solution.py:236
  229.7 66.8 %collective-permute-start.11 = (bf16[192,2560]{1,0:T(8,128)(2,1)}, bf16[192,2560]{1,0:T(8,128)(2,1)S(1)}, u32[]{:S(2)}, u32[]{:S(2)}) collective-permute-start(bf16[192,2560]{1,0:T(8,128)(2,1)} %collective-permute-done), channel_id=1, source_target_pairs={{0,4},{4,0},{1,5},{5,1},{2,6},{6,2},{3,7},{7,3},{8,12},{12,8},{9,1... | collective-permute-start | bytes 2949128 | tf_op jit(solution)/shard_map/ppermute | solution.py:95
  250.8 42.1 %collective-permute-start.17 = (bf16[192,1280]{1,0:T(8,128)(2,1)S(1)}, bf16[192,1280]{1,0:T(8,128)(2,1)S(1)}, u32[]{:S(2)}, u32[]{:S(2)}) collective-permute-start(bf16[192,1280]{1,0:T(8,128)(2,1)S(1)} %collective-permute-done.16), channel_id=1, source_target_pairs={{0,4},{4,0},{1,5},{5,1},{2,6},{6,2},{3,7},{7,3},{8,12},{12,8},{9,1... | collective-permute-start | bytes 1474568 | tf_op jit(solution)/shard_map/ppermute | solution.py:95
  274.1 39.0 %collective-permute-start.13 = (bf16[192,2560]{1,0:T(8,128)(2,1)S(1)}, bf16[192,2560]{1,0:T(8,128)(2,1)S(1)}, u32[]{:S(2)}, u32[]{:S(2)}) collective-permute-start(bf16[192,2560]{1,0:T(8,128)(2,1)S(1)} %collective-permute-done.12), channel_id=1, source_target_pairs={{0,4},{4,0},{1,5},{5,1},{2,6},{6,2},{3,7},{7,3},{8,12},{12,8},{9,1... | collective-permute-start | bytes 2949128 | tf_op jit(solution)/shard_map/ppermute | solution.py:95
  342.3 265.1 %reduce-scatter.4.cloned.1.call-start = ((), (), s32[]{:S(2)}) async-start(), calls=%async_computation.6 | async-start | bytes 13369344 | tf_op jit(solution)/shard_map/reduce_scatter | solution.py:330
  346.5 43.6 %copy-start.3 = (bf16[4096,1280]{1,0:T(8,128)(2,1)}, bf16[4096,1280]{1,0:T(8,128)(2,1)S(1)}, u32[]{:S(2)}) copy-start(bf16[4096,1280]{1,0:T(8,128)(2,1)S(1)} %convolution_convert_fusion.2) | copy-start | bytes 31457284
  443.8 309.0 %reduce-scatter.6.cloned.1.call-start = ((), (), s32[]{:S(2)}) async-start(), calls=%async_computation.7 | async-start | bytes 14483456 | tf_op jit(solution)/shard_map/reduce_scatter | solution.py:370
  467.9 42.0 %collective-permute-start.18 = (bf16[192,1280]{1,0:T(8,128)(2,1)}, bf16[192,1280]{1,0:T(8,128)(2,1)}, u32[]{:S(2)}, u32[]{:S(2)}) collective-permute-start(bf16[192,1280]{1,0:T(8,128)(2,1)} %get-tuple-element.183), channel_id=1, source_target_pairs={{0,4},{4,0},{1,5},{5,1},{2,6},{6,2},{3,7},{7,3},{8,12},{12,8},{9,1... | collective-permute-start | bytes 1474568 | tf_op jit(solution)/shard_map/ppermute | solution.py:95
  469.4 40.5 %collective-permute-start.19 = (bf16[192,1280]{1,0:T(8,128)(2,1)}, bf16[192,1280]{1,0:T(8,128)(2,1)}, u32[]{:S(2)}, u32[]{:S(2)}) collective-permute-start(bf16[192,1280]{1,0:T(8,128)(2,1)} %get-tuple-element.182), channel_id=1, source_target_pairs={{0,4},{4,0},{1,5},{5,1},{2,6},{6,2},{3,7},{7,3},{8,12},{12,8},{9,1... | collective-permute-start | bytes 1474568 | tf_op jit(solution)/shard_map/ppermute | solution.py:95
  469.9 40.0 %collective-permute-start.20 = (bf16[192,1280]{1,0:T(8,128)(2,1)}, bf16[192,1280]{1,0:T(8,128)(2,1)}, u32[]{:S(2)}, u32[]{:S(2)}) collective-permute-start(bf16[192,1280]{1,0:T(8,128)(2,1)} %get-tuple-element.181), channel_id=1, source_target_pairs={{0,4},{4,0},{1,5},{5,1},{2,6},{6,2},{3,7},{7,3},{8,12},{12,8},{9,1... | collective-permute-start | bytes 1474568 | tf_op jit(solution)/shard_map/ppermute | solution.py:95
  471.4 41.8 %collective-permute-start.21 = (bf16[192,1280]{1,0:T(8,128)(2,1)}, bf16[192,1280]{1,0:T(8,128)(2,1)}, u32[]{:S(2)}, u32[]{:S(2)}) collective-permute-start(bf16[192,1280]{1,0:T(8,128)(2,1)} %get-tuple-element.180), channel_id=1, source_target_pairs={{0,4},{4,0},{1,5},{5,1},{2,6},{6,2},{3,7},{7,3},{8,12},{12,8},{9,1... | collective-permute-start | bytes 1474568 | tf_op jit(solution)/shard_map/ppermute | solution.py:95
  516.3 63.5 %collective-permute-start.22 = (bf16[192,1280]{1,0:T(8,128)(2,1)}, bf16[192,1280]{1,0:T(8,128)(2,1)S(1)}, u32[]{:S(2)}, u32[]{:S(2)}) collective-permute-start(bf16[192,1280]{1,0:T(8,128)(2,1)} %get-tuple-element.118), channel_id=1, source_target_pairs={{0,8},{8,16},{16,24},{24,0},{1,9},{9,17},{17,25},{25,1},{2,10},{10... | collective-permute-start | bytes 1474568 | tf_op jit(solution)/shard_map/ppermute | solution.py:236
  516.8 63.1 %collective-permute-start.23 = (bf16[192,1280]{1,0:T(8,128)(2,1)}, bf16[192,1280]{1,0:T(8,128)(2,1)S(1)}, u32[]{:S(2)}, u32[]{:S(2)}) collective-permute-start(bf16[192,1280]{1,0:T(8,128)(2,1)} %get-tuple-element.119), channel_id=1, source_target_pairs={{0,16},{8,24},{16,0},{24,8},{1,17},{9,25},{17,1},{25,9},{2,18},{10... | collective-permute-start | bytes 1474568 | tf_op jit(solution)/shard_map/ppermute | solution.py:236
  518.5 61.4 %collective-permute-start.24 = (bf16[192,1280]{1,0:T(8,128)(2,1)}, bf16[192,1280]{1,0:T(8,128)(2,1)S(1)}, u32[]{:S(2)}, u32[]{:S(2)}) collective-permute-start(bf16[192,1280]{1,0:T(8,128)(2,1)} %get-tuple-element.120), channel_id=1, source_target_pairs={{0,24},{8,0},{16,8},{24,16},{1,25},{9,1},{17,9},{25,17},{2,26},{10... | collective-permute-start | bytes 1474568 | tf_op jit(solution)/shard_map/ppermute | solution.py:236
  579.9 27.5 %copy-start.64 = (bf16[192,1280]{1,0:T(8,128)(2,1)}, bf16[192,1280]{1,0:T(8,128)(2,1)S(1)}, u32[]{:S(2)}) copy-start(bf16[192,1280]{1,0:T(8,128)(2,1)S(1)} %collective-permute-done.23) | copy-start | bytes 1474564
  579.9 27.5 %copy-start.65 = (bf16[192,1280]{1,0:T(8,128)(2,1)}, bf16[192,1280]{1,0:T(8,128)(2,1)S(1)}, u32[]{:S(2)}) copy-start(bf16[192,1280]{1,0:T(8,128)(2,1)S(1)} %collective-permute-done.24) | copy-start | bytes 1474564
  607.4 368.8 %reduce-scatter.8.cloned.1.call-start = ((), (), s32[]{:S(2)}) async-start(), calls=%async_computation.8 | async-start | bytes 3981312 | tf_op jit(solution)/shard_map/reduce_scatter | solution.py:462
  652.9 24.9 %collective-permute-start.25 = (bf16[192,2560]{1,0:T(8,128)(2,1)}, bf16[192,2560]{1,0:T(8,128)(2,1)}, u32[]{:S(2)}, u32[]{:S(2)}) collective-permute-start(bf16[192,2560]{1,0:T(8,128)(2,1)} %get-tuple-element.173), channel_id=1, source_target_pairs={{0,4},{4,0},{1,5},{5,1},{2,6},{6,2},{3,7},{7,3},{8,12},{12,8},{9,1... | collective-permute-start | bytes 2949128 | tf_op jit(solution)/shard_map/ppermute | solution.py:95
  654.3 44.6 %collective-permute-start.26 = (bf16[192,2560]{1,0:T(8,128)(2,1)}, bf16[192,2560]{1,0:T(8,128)(2,1)}, u32[]{:S(2)}, u32[]{:S(2)}) collective-permute-start(bf16[192,2560]{1,0:T(8,128)(2,1)} %get-tuple-element.172), channel_id=1, source_target_pairs={{0,4},{4,0},{1,5},{5,1},{2,6},{6,2},{3,7},{7,3},{8,12},{12,8},{9,1... | collective-permute-start | bytes 2949128 | tf_op jit(solution)/shard_map/ppermute | solution.py:95
  654.9 65.0 %collective-permute-start.27 = (bf16[192,2560]{1,0:T(8,128)(2,1)}, bf16[192,2560]{1,0:T(8,128)(2,1)}, u32[]{:S(2)}, u32[]{:S(2)}) collective-permute-start(bf16[192,2560]{1,0:T(8,128)(2,1)} %get-tuple-element.171), channel_id=1, source_target_pairs={{0,4},{4,0},{1,5},{5,1},{2,6},{6,2},{3,7},{7,3},{8,12},{12,8},{9,1... | collective-permute-start | bytes 2949128 | tf_op jit(solution)/shard_map/ppermute | solution.py:95
  656.3 82.7 %collective-permute-start.28 = (bf16[192,2560]{1,0:T(8,128)(2,1)}, bf16[192,2560]{1,0:T(8,128)(2,1)}, u32[]{:S(2)}, u32[]{:S(2)}) collective-permute-start(bf16[192,2560]{1,0:T(8,128)(2,1)} %get-tuple-element.170), channel_id=1, source_target_pairs={{0,4},{4,0},{1,5},{5,1},{2,6},{6,2},{3,7},{7,3},{8,12},{12,8},{9,1... | collective-permute-start | bytes 2949128 | tf_op jit(solution)/shard_map/ppermute | solution.py:95
  764.5 19.1 %copy-start.7 = (f32[256,1536]{1,0:T(8,128)}, f32[256,1536]{1,0:T(8,128)S(1)}, u32[]{:S(2)}) copy-start(f32[256,1536]{1,0:T(8,128)S(1)} %get-tuple-element.226) | copy-start | bytes 4718596
  765.1 25.8 %copy-start.72 = (f32[2,3,1024]{2,1,0:T(4,128)S(1)}, f32[2,3,1024]{2,1,0:T(4,128)}, u32[]{:S(2)}) copy-start(f32[2,3,1024]{2,1,0:T(4,128)} %copy-done.71) | copy-start | bytes 73732
  765.1 25.7 %copy-start.74 = (f32[2,3,1024]{2,1,0:T(4,128)S(1)}, f32[2,3,1024]{2,1,0:T(4,128)}, u32[]{:S(2)}) copy-start(f32[2,3,1024]{2,1,0:T(4,128)} %copy-done.73) | copy-start | bytes 73732
  765.1 25.8 %copy-start.17 = (bf16[256,1536]{1,0:T(8,128)(2,1)S(1)}, bf16[256,1536]{1,0:T(8,128)(2,1)}, u32[]{:S(2)}) copy-start(bf16[256,1536]{1,0:T(8,128)(2,1)} %copy-done.16) | copy-start | bytes 2359300
  765.1 18.5 %collective-permute-start.29 = (bf16[256,1536]{1,0:T(8,128)(2,1)S(1)}, bf16[256,1536]{1,0:T(8,128)(2,1)S(1)}, u32[]{:S(2)}, u32[]{:S(2)}) collective-permute-start(bf16[256,1536]{1,0:T(8,128)(2,1)S(1)} %fusion.101), channel_id=1, source_target_pairs={{0,2},{1,3},{2,0},{3,1},{4,6},{5,7},{6,4},{7,5},{8,10},{9,11},{10,... | collective-permute-start | bytes 2359304 | tf_op jit(solution)/shard_map/ppermute | solution.py:95
  767.5 23.2 %collective-permute-start.30 = (bf16[192,1280]{1,0:T(8,128)(2,1)S(1)}, bf16[192,1280]{1,0:T(8,128)(2,1)S(1)}, u32[]{:S(2)}, u32[]{:S(2)}) collective-permute-start(bf16[192,1280]{1,0:T(8,128)(2,1)S(1)} %get-tuple-element.209), channel_id=1, source_target_pairs={{0,16},{8,24},{16,0},{24,8},{1,17},{9,25},{17,1},{25,9},{2,18},{10... | collective-permute-start | bytes 1474568 | tf_op jit(solution)/shard_map/ppermute | solution.py:236
  790.7 3.4 collective-permute-start.31
  792.4 32.7 %collective-permute-start.32 = (bf16[192,1280]{1,0:T(8,128)(2,1)}, bf16[192,1280]{1,0:T(8,128)(2,1)}, u32[]{:S(2)}, u32[]{:S(2)}) collective-permute-start(bf16[192,1280]{1,0:T(8,128)(2,1)} %get-tuple-element.133), channel_id=1, source_target_pairs={{0,16},{8,24},{16,0},{24,8},{1,17},{9,25},{17,1},{25,9},{2,18},{10... | collective-permute-start | bytes 1474568 | tf_op jit(solution)/shard_map/ppermute | solution.py:236
  839.2 25.9 %copy-start.38 = (f32[1024,32]{0,1:T(8,128)S(1)}, f32[1024,32]{0,1:T(8,128)}, u32[]{:S(2)}) copy-start(f32[1024,32]{0,1:T(8,128)} %copy-done.37) | copy-start | bytes 393220
  839.2 25.9 %copy-start.55 = (f32[1024,32]{0,1:T(8,128)S(1)}, f32[1024,32]{0,1:T(8,128)}, u32[]{:S(2)}) copy-start(f32[1024,32]{0,1:T(8,128)} %get-tuple-element.219) | copy-start | bytes 393220
  839.2 27.5 %copy-start.23 = (f32[1024,2,64]{0,2,1:T(8,128)S(1)}, f32[1024,2,64]{0,2,1:T(8,128)}, u32[]{:S(2)}) copy-start(f32[1024,2,64]{0,2,1:T(8,128)} %fusion.62) | copy-start | bytes 1572868
  839.2 25.9 %collective-permute-start.33 = (bf16[192,2560]{1,0:T(8,128)(2,1)}, bf16[192,2560]{1,0:T(8,128)(2,1)}, u32[]{:S(2)}, u32[]{:S(2)}) collective-permute-start(bf16[192,2560]{1,0:T(8,128)(2,1)} %get-tuple-element.137), channel_id=1, source_target_pairs={{0,8},{8,16},{16,24},{24,0},{1,9},{9,17},{17,25},{25,1},{2,10},{10... | collective-permute-start | bytes 2949128 | tf_op jit(solution)/shard_map/ppermute | solution.py:236
  885.5 26.0 %collective-permute-start.34 = (bf16[2,256,1536]{2,1,0:T(8,128)(2,1)}, bf16[2,256,1536]{2,1,0:T(8,128)(2,1)}, u32[]{:S(2)}, u32[]{:S(2)}) collective-permute-start(bf16[2,256,1536]{2,1,0:T(8,128)(2,1)} %dynamic-slice_bitcast_fusion), channel_id=1, source_target_pairs={{0,1},{1,0},{2,3},{3,2},{4,5},{5,4},{6,7},{7,6},{8,9},{9,8},{10,11... | collective-permute-start | bytes 4718600 | tf_op jit(solution)/shard_map/ppermute | solution.py:95
  907.9 32.7 %collective-permute-start.39 = (bf16[192,2560]{1,0:T(8,128)(2,1)}, bf16[192,2560]{1,0:T(8,128)(2,1)}, u32[]{:S(2)}, u32[]{:S(2)}) collective-permute-start(bf16[192,2560]{1,0:T(8,128)(2,1)} %get-tuple-element.144), channel_id=1, source_target_pairs={{0,24},{8,0},{16,8},{24,16},{1,25},{9,1},{17,9},{25,17},{2,26},{10... | collective-permute-start | bytes 2949128 | tf_op jit(solution)/shard_map/ppermute | solution.py:236
  913.9 28.9 %copy-start.11 = (bf16[256,1536]{1,0:T(8,128)(2,1)S(1)}, bf16[256,1536]{1,0:T(8,128)(2,1)}, u32[]{:S(2)}) copy-start(bf16[256,1536]{1,0:T(8,128)(2,1)} %param.14) | copy-start | bytes 2359300
  914.0 28.8 %collective-permute-start.35 = (bf16[256,1536]{1,0:T(8,128)(2,1)S(1)}, bf16[256,1536]{1,0:T(8,128)(2,1)S(1)}, u32[]{:S(2)}, u32[]{:S(2)}) collective-permute-start(bf16[256,1536]{1,0:T(8,128)(2,1)S(1)} %fusion.77), channel_id=1, source_target_pairs={{0,2},{1,3},{2,0},{3,1},{4,6},{5,7},{6,4},{7,5},{8,10},{9,11},{10,... | collective-permute-start | bytes 2359304 | tf_op jit(solution)/shard_map/ppermute | solution.py:95
  977.2 8.6 collective-permute-start.36
  977.3 8.6 collective-permute-start.37
  978.8 10.1 %collective-permute-start.38 = (f32[42,192]{1,0:T(8,128)S(1)}, f32[42,192]{1,0:T(8,128)S(1)}, u32[]{:S(2)}, u32[]{:S(2)}) collective-permute-start(f32[42,192]{1,0:T(8,128)S(1)} %bitcast.399), channel_id=1, source_target_pairs={{0,3},{1,0},{2,1},{3,2},{4,7},{5,4},{6,5},{7,6},{8,11},{9,8},{10,9... | collective-permute-start | bytes 96776 | tf_op jit(solution)/shard_map/ppermute | solution.py:177
  (68 other events, 388.8 us)
Sparse Core Ops, SparseCore 0:
  11.7 67.3 all-gather.3
  207.4 134.7 all-gather.5
  345.1 98.5 all-gather.7
  447.6 159.6 reduce-scatter.3
  611.3 141.4 reduce-scatter.5
  882.9 86.2 reduce-scatter.7

commit v8 on v7

--- a/solution.py
+++ b/solution.py
@@ -169,6 +169,22 @@
             send = lax.dynamic_index_in_dim(block, 1 - own, axis, keepdims=False)
             block = keep.astype(f32) + swap(send.astype(bf16), "t", n_tensor, bit).astype(f32)
         return block
+
+    def scatter_small(values):
+        if n_tensor != 4:
+            return lax.psum_scatter(values, shared, scatter_dimension=0, tiled=True).astype(f32)
+        me_i, me_t = lax.axis_index("i"), lax.axis_index("t")
+        block = values.reshape(inner, 2, 2, -1, values.shape[1])
+        for axis, bit, own in ((2, 1, me_t % 2), (1, 2, me_t // 2)):
+            keep = lax.dynamic_index_in_dim(block, own, axis, keepdims=False)
+            send = lax.dynamic_index_in_dim(block, 1 - own, axis, keepdims=False)
+            block = (keep.astype(f32) + swap(send, "t", n_tensor, bit).astype(f32)).astype(bf16)
+        total = lax.dynamic_index_in_dim(block, me_i, 0, keepdims=False).astype(f32)
+        for shift in range(1, inner):
+            send = lax.dynamic_index_in_dim(block, (me_i + shift) % inner, 0, keepdims=False)
+            pairs = [(m, (m + shift) % inner) for m in range(inner)]
+            total = total + lax.ppermute(send, "i", pairs).astype(f32)
+        return total
 
     def sum_tensor(values):
         me_t = lax.axis_index("t")
@@ -365,8 +381,12 @@
         grad_normed_part = lax.dot_general(
             grad_gate_up, w_gate_up, (((1,), (1,)), ((), ())), preferred_element_type=f32
         )
-        grad_shipped = jnp.concatenate([grad_normed_part, gate_block], axis=1).astype(bf16)
-        grad_shipped, sent_down, expert_share = tie(by_rows(grad_shipped), sent_down, expert_share)
+        gate_block, grad_shipped, sent_down, expert_share = tie(
+            gate_block.astype(bf16),
+            by_rows(grad_normed_part.astype(bf16)),
+            sent_down,
+            expert_share,
+        )
         grad_back = lax.psum_scatter(grad_shipped, shared, scatter_dimension=0, tiled=True)
         shared_rows, _ = tie(shared_all, grad_shipped)
         grad_w_gate_up = lax.dot_general(
@@ -379,17 +399,20 @@
             grad_down = put(
                 grad_down, part.astype(f32), (me_i - shift) % inner * own_experts, 0, 0
             )
-        gate_up_sums, grad_down, grad_back = tie(gate_up_sums, grad_down, grad_back)
+        gates_back = scatter_small(gate_block)
+        gate_up_sums, grad_down, gates_back, grad_back = tie(
+            gate_up_sums, grad_down, gates_back, grad_back
+        )
         far_sum_gate, far_sum_up = jnp.split(gate_up_sums[2], 2, axis=1)
         sent_gate_up = {0: jnp.split(gate_up_sums[0], 2, axis=1)}
         mixed = (middle + from_owner_order(expert_share).astype(f32)).astype(bf16)
 
         grad_back = grad_back.astype(f32)
-        grad_chosen = grad_back[:, width : width + n_experts]
+        grad_chosen = gates_back[:, :n_experts]
         grad_logits = gates * (
             grad_chosen - jnp.sum(gates * grad_chosen, axis=-1, keepdims=True)
         )
-        grad_normed_two = from_owner_order(grad_back[:, :width]) + jnp.dot(
+        grad_normed_two = from_owner_order(grad_back) + jnp.dot(
             grad_logits, router.astype(f32).T, precision=HIGHEST
         )
         grad_middle_part, normal_two = norm_backward(

time: 1010 us -> 1010 us (level)
  other arithmetic: 93.7 us -> 78.9 us
    ppermute x0 -> x3, waiting for transfers between devices: none -> 17.7 us  [scatter_small(): total = total + lax.ppermute(send, 'i', pairs).astype(f32)]
    ppermute x24 -> x26, waiting for transfers between devices: 139 us -> 123 us  [swap(): return lax.ppermute(values, axis, [(m, m ^ bit) for m in range(size)])]
    reduce_scatter x1, waiting for transfers between devices: 27.4 us -> 39.8 us  [on_device(): lax.psum_scatter(expert_part, shared, scatter_dimension=0, tiled=True)]
    concatenate x1 -> x0, other arithmetic: 12.1 us -> none  [on_device(): jnp.concatenate([grad_normed_part, gate_block], axis=1).astype(bf16)]
    ppermute x24 -> x26, starting transfers between devices: 22.9 us -> 24.6 us  [swap(): return lax.ppermute(values, axis, [(m, m ^ bit) for m in range(size)])]
    unnamed x174 -> x178, local copies, waits for them, and re-layouts: 19.7 us -> 20.9 us
  transfers between devices with their start and end apart: 46 -> 51, of which waited for: 27 -> 30; matrix products, arithmetic and copies ran while one was open for 48% -> 47% of each run, Pallas kernels for 0% -> 0%
where the time goes in v8:
time: 1010 us; the launch traced here: 996 us
  waiting for transfers between devices  371 us (37%)
  matrix products  313 us (31%)
  local copies, waits for them, and re-layouts  158 us (16%)
  other arithmetic  78.9 us (8%)
  starting transfers between devices  59 us (6%)
  between operations  17 us (2%)
    ppermute x26, waiting for transfers between devices, swap(): return lax.ppermute(values, axis, [(m, m ^ bit) for m in range(size)])  123 us
    ppermute x13, waiting for transfers between devices, to_owner(): return jax.tree.map(lambda part: lax.ppermute(part, 'i', pairs), piece)  117 us
    dot_general x1, matrix products, on_device(): jnp.dot(normed_all, w_gate_up, preferred_element_type=f32).astype(bf16)  43.6 us
    dot_general x1, matrix products, on_device(): lax.dot_general(shared_rows[:, :width], grad_gate_up, contract_rows, pref...  41.2 us
    reduce_scatter x1, waiting for transfers between devices, on_device(): lax.psum_scatter(expert_part, shared, scatter_dimension=0, tiled=True)  39.8 us
    dot_general x1, matrix products, on_device(): lax.dot_general(grad_gate_up, w_gate_up, (((1,), (1,)), ((), ())), prefer...  39.5 us
    dot_general x1, matrix products, on_device(): cot_part = jnp.dot(cot_all, w_down_t, preferred_element_type=f32)  37.8 us
    convert_element_type x16, local copies, waits for them, and re-layouts, on_device(): jnp.swapaxes(part.reshape(depth, own_experts, hidden), 0, 1).astype(f32)  30.6 us
  transfers between devices with their start and end apart: 51, of which 30 were waited for; matrix products, arithmetic and copies ran while one was open for 47% of the time, Pallas kernels for 0%

profile of v8, /device:TPU:0, one launch (start us, length us, event | category | flops | bytes accessed | tf_op | source)
XLA Modules:
  0.0 995.9 jit_solution(17240461701612078918)
XLA Ops:
  11.6 3.1 collective-permute-start.3
  14.7 3.9 dynamic-slice_bitcast_fusion.19
  52.9 26.1 %all-gather.4.cloned.1.call-done = bf16[1536,1152]{1,0:T(8,128)(2,1)} async-done(((bf16[192,1152]{1,0:T(8,128)(2,1)}), bf16[1536,1152]{1,0:T(8,128)(2,1)}) %all-gather.4.cloned.1.call-update) | async-done | bytes 3538960 | tf_op jit(solution)/shard_map/all_gather | solution.py:235
  80.9 4.2 fusion.50
  92.0 5.7 fusion.111
  97.8 3.8 fusion.3
  101.5 4.6 copy-done.2
  106.6 10.5 %fusion.57 = bf16[2,64,3,1024]{3,1,2,0:T(8,128)(2,1)S(1)} fusion(bf16[1024,2,64,1]{0,2,3,1:T(8,128)(2,1)S(1)} %bitcast.418, f32[2,3,1024,1024]{2,3,1,0:T(8,128)} %copy-done.2, f32[2,3,1024]{2,1,0:T(4,128)S(1)} %fusion.3, f32[2,3,1024]{2,1,0:T(4,128)S(1)} %get-tuple-element.231), kind=kOutput, calls=%fused_computation.113 | convolution fusion | flops 824573952 | bytes 26263552 | tf_op jit(solution)/shard_map/hgqk,khd->qhgd/dot_general | solution.py:65
  122.3 11.2 %collective-permute-done = bf16[192,2560]{1,0:T(8,128)(2,1)} collective-permute-done((bf16[192,2560]{1,0:T(8,128)(2,1)}, bf16[192,2560]{1,0:T(8,128)(2,1)}, u32[]{:S(2)}, u32[]{:S(2)}) %collective-permute-start) | collective-permute-done | bytes 983072 | tf_op jit(solution)/shard_map/ppermute | solution.py:252
  133.5 3.1 convolution_convert_fusion.6
  139.6 3.7 collective-permute-done.5
  150.7 11.0 %collective-permute-start.8 = (bf16[192,1280]{1,0:T(8,128)(2,1)S(1)}, bf16[192,1280]{1,0:T(8,128)(2,1)}, u32[]{:S(2)}, u32[]{:S(2)}) collective-permute-start(bf16[192,1280]{1,0:T(8,128)(2,1)S(1)} %copy-done.62), channel_id=1, source_target_pairs={{0,8},{8,16},{16,24},{24,0},{1,9},{9,17},{17,25},{25,1},{2,10},{10... | collective-permute-start | bytes 1474568 | tf_op jit(solution)/shard_map/ppermute | solution.py:252
  161.7 3.4 collective-permute-start.9
  165.1 3.1 collective-permute-done.6
  182.8 4.6 collective-permute-done.8
  187.4 19.9 %collective-permute-done.9 = bf16[192,1280]{1,0:T(8,128)(2,1)} collective-permute-done((bf16[192,1280]{1,0:T(8,128)(2,1)}, bf16[192,1280]{1,0:T(8,128)(2,1)}, u32[]{:S(2)}, u32[]{:S(2)}) %collective-permute-start.9) | collective-permute-done | bytes 491552 | tf_op jit(solution)/shard_map/ppermute | solution.py:252
  210.2 3.9 broadcast_in_dim.123
  219.3 10.4 %collective-permute-done.14 = bf16[192,1280]{1,0:T(8,128)(2,1)S(1)} collective-permute-done((bf16[192,1280]{1,0:T(8,128)(2,1)}, bf16[192,1280]{1,0:T(8,128)(2,1)S(1)}, u32[]{:S(2)}, u32[]{:S(2)}) %collective-permute-start.14) | collective-permute-done | bytes 491552 | tf_op jit(solution)/shard_map/ppermute | solution.py:95
  230.4 20.3 %collective-permute-done.16 = bf16[192,1280]{1,0:T(8,128)(2,1)S(1)} collective-permute-done((bf16[192,1280]{1,0:T(8,128)(2,1)S(1)}, bf16[192,1280]{1,0:T(8,128)(2,1)S(1)}, u32[]{:S(2)}, u32[]{:S(2)}) %collective-permute-start.16) | collective-permute-done | bytes 491552 | tf_op jit(solution)/shard_map/ppermute | solution.py:252
  253.4 20.7 %collective-permute-done.12 = bf16[192,2560]{1,0:T(8,128)(2,1)S(1)} collective-permute-done((bf16[192,2560]{1,0:T(8,128)(2,1)S(1)}, bf16[192,2560]{1,0:T(8,128)(2,1)S(1)}, u32[]{:S(2)}, u32[]{:S(2)}) %collective-permute-start.12) | collective-permute-done | bytes 983072 | tf_op jit(solution)/shard_map/ppermute | solution.py:252
  275.6 17.3 %collective-permute-done.17 = bf16[192,1280]{1,0:T(8,128)(2,1)S(1)} collective-permute-done((bf16[192,1280]{1,0:T(8,128)(2,1)S(1)}, bf16[192,1280]{1,0:T(8,128)(2,1)S(1)}, u32[]{:S(2)}, u32[]{:S(2)}) %collective-permute-start.17) | collective-permute-done | bytes 491552 | tf_op jit(solution)/shard_map/ppermute | solution.py:95
  293.0 3.4 fusion.39
  299.1 14.0 %collective-permute-done.13 = bf16[192,2560]{1,0:T(8,128)(2,1)S(1)} collective-permute-done((bf16[192,2560]{1,0:T(8,128)(2,1)S(1)}, bf16[192,2560]{1,0:T(8,128)(2,1)S(1)}, u32[]{:S(2)}, u32[]{:S(2)}) %collective-permute-start.13) | collective-permute-done | bytes 983072 | tf_op jit(solution)/shard_map/ppermute | solution.py:95
  314.5 27.7 %all-gather.6.cloned.1.call-done = bf16[4096,1664]{1,0:T(8,128)(2,1)} async-done(((bf16[256,1664]{1,0:T(8,128)(2,1)}), bf16[4096,1664]{1,0:T(8,128)(2,1)}) %all-gather.6.cloned.1.call-update) | async-done | bytes 13631504 | tf_op jit(solution)/shard_map/all_gather | solution.py:308
  342.3 4.1 convolution_convert_fusion.2
  346.5 43.6 %convolution_convert_fusion = bf16[4096,2560]{1,0:T(8,128)(2,1)} fusion(bf16[1536,2560]{1,0:T(8,128)(2,1)} %bitcast.70, bf16[4096,1664]{1,0:T(8,128)(2,1)} %all-gather.6.cloned.1.call-done), kind=kOutput, calls=%fused_computation.16 | convolution fusion | flops 32222740480 | bytes 41418752 | tf_op jit(solution)/shard_map/dot_general | solution.py:329
  390.1 11.6 %fusion.18 = bf16[4096,1280]{1,0:T(8,128)(2,1)S(1)} fusion(bf16[4096,1280]{1,0:T(8,128)(2,1)S(1)} %convolution_convert_fusion.2, bf16[4096,2560]{1,0:T(8,128)(2,1)} %convolution_convert_fusion), kind=kLoop, calls=%fused_computation.35 | loop fusion | flops 52428800 | bytes 41943040 | tf_op jit(solution)/shard_map/convert_element_type | solution.py:339
  401.7 4.0 copy-done.14
  405.7 20.9 %convolution_convert_fusion.1 = bf16[4096,1536]{1,0:T(8,128)(2,1)} fusion(bf16[4096,1280]{1,0:T(8,128)(2,1)S(1)} %fusion.18, bf16[1536,1280]{1,0:T(8,128)(2,1)} %bitcast.372), kind=kOutput, calls=%fused_computation.37 | convolution fusion | flops 16112418816 | bytes 27000832 | tf_op jit(solution)/shard_map/dot_general | solution.py:340
  426.6 17.1 %all-gather.8.cloned.1.call-done = bf16[4096,1536]{1,0:T(8,128)(2,1)} async-done(((bf16[256,1536]{1,0:T(8,128)(2,1)}), bf16[4096,1536]{1,0:T(8,128)(2,1)}) %all-gather.8.cloned.1.call-update) | async-done | bytes 12582928 | tf_op jit(solution)/shard_map/all_gather | solution.py:321
  444.2 22.3 %convolution_convert_fusion.4 = bf16[1536,1280]{1,0:T(8,128)(2,1)S(1)} fusion(bf16[4096,1536]{1,0:T(8,128)(2,1)} %all-gather.8.cloned.1.call-done, bf16[4096,1280]{1,0:T(8,128)(2,1)} %copy-done.14), kind=kOutput, calls=%fused_computation.51 | convolution fusion | flops 16108093440 | bytes 27000832 | tf_op jit(solution)/shard_map/dot_general | solution.py:348
  472.0 37.8 %fusion.13 = (bf16[4096,1280]{1,0:T(8,128)(2,1)}, bf16[4096,1280]{1,0:T(8,128)(2,1)}, bf16[4096,1280]{1,0:T(8,128)(2,1)}) fusion(bf16[4096,1280]{1,0:T(8,128)(2,1)} %copy-done.3, bf16[4096,2560]{1,0:T(8,128)(2,1)} %convolution_convert_fusion, bf16[4096,1536]{1,0:T(8,128)(2,1)} %all-gather.8.cloned.1.call-done, bf16[1536,1280]{1,0:T(8,128)(2,1)S(1)} %bitcast.373), kind=kOutput, calls=%fused_computation.27 | convolution fusion | flops 16210984960 | bytes 79429632 | tf_op jit(solution)/shard_map/dot_general | solution.py:363
  509.8 3.4 collective-permute-done.21
  513.2 3.1 fusion.70
  520.9 39.5 %convolution_convert_fusion.3 = bf16[4096,1536]{1,0:T(8,128)(2,1)} fusion(bf16[1536,2560]{1,0:T(8,128)(2,1)} %bitcast.70, bf16[4096,1280]{1,0:T(8,128)(2,1)} %get-tuple-element.168, bf16[4096,1280]{1,0:T(8,128)(2,1)} %get-tuple-element.167), kind=kOutput, calls=%fused_computation.39 | convolution fusion | flops 32260489216 | bytes 41418752 | tf_op jit(solution)/shard_map/dot_general | solution.py:381
  560.4 7.0 convolution_convert_fusion.5
  567.5 39.8 %reduce-scatter.4.cloned.1.call-done = bf16[256,1536]{1,0:T(8,128)(2,1)} async-done(((bf16[4096,1536]{1,0:T(8,128)(2,1)}), bf16[256,1536]{1,0:T(8,128)(2,1)}) %reduce-scatter.4.cloned.1.call-update) | async-done | bytes 786448 | tf_op jit(solution)/shard_map/reduce_scatter | solution.py:346
  607.7 41.2 %fusion.27 = bf16[1536,2560]{1,0:T(8,128)(2,1)} fusion(bf16[4096,1280]{1,0:T(8,128)(2,1)} %get-tuple-element.168, bf16[4096,1280]{1,0:T(8,128)(2,1)} %get-tuple-element.167, bf16[4096,1664]{1,0:T(8,128)(2,1)} %all-gather.6.cloned.1.call-done), kind=kOutput, calls=%fused_computation.46 | convolution fusion | flops 32258129920 | bytes 41418752 | tf_op jit(solution)/shard_map/dot_general | solution.py:392
  652.0 4.1 dynamic-slice_bitcast_fusion.2
  670.3 4.2 collective-permute-done.31
  676.4 8.1 collective-permute-done.32
  687.6 5.4 collective-permute-done.33
  693.1 10.8 %collective-permute-done.26 = bf16[192,2560]{1,0:T(8,128)(2,1)} collective-permute-done((bf16[192,2560]{1,0:T(8,128)(2,1)}, bf16[192,2560]{1,0:T(8,128)(2,1)}, u32[]{:S(2)}, u32[]{:S(2)}) %collective-permute-start.26) | collective-permute-done | bytes 983072 | tf_op jit(solution)/shard_map/ppermute | solution.py:95
  703.9 21.1 %collective-permute-done.27 = bf16[192,2560]{1,0:T(8,128)(2,1)} collective-permute-done((bf16[192,2560]{1,0:T(8,128)(2,1)}, bf16[192,2560]{1,0:T(8,128)(2,1)}, u32[]{:S(2)}, u32[]{:S(2)}) %collective-permute-start.27) | collective-permute-done | bytes 983072 | tf_op jit(solution)/shard_map/ppermute | solution.py:95
  725.0 20.3 %collective-permute-done.28 = bf16[192,2560]{1,0:T(8,128)(2,1)} collective-permute-done((bf16[192,2560]{1,0:T(8,128)(2,1)}, bf16[192,2560]{1,0:T(8,128)(2,1)}, u32[]{:S(2)}, u32[]{:S(2)}) %collective-permute-start.28) | collective-permute-done | bytes 983072 | tf_op jit(solution)/shard_map/ppermute | solution.py:95
  745.3 5.8 fusion.42
  755.5 3.0 copy.387
  758.7 2.9 multiply_reduce_fusion
  766.2 14.5 %collective-permute-done.34 = bf16[256,1536]{1,0:T(8,128)(2,1)S(1)} collective-permute-done((bf16[256,1536]{1,0:T(8,128)(2,1)S(1)}, bf16[256,1536]{1,0:T(8,128)(2,1)S(1)}, u32[]{:S(2)}, u32[]{:S(2)}) %collective-permute-start.34) | collective-permute-done | bytes 786464 | tf_op jit(solution)/shard_map/ppermute | solution.py:95
  780.8 7.0 collective-permute-done.35
  791.4 2.9 convolution_convert_fusion.8
  794.3 2.8 convolution_convert_fusion.9
  798.0 24.1 %fusion.2 = bf16[2,3,1024,1024]{2,3,1,0:T(8,128)(2,1)} fusion(f32[2,3,1024,1024]{2,3,1,0:T(8,128)} %copy-done.2, f32[2,3,1024]{2,1,0:T(4,128)S(1)} %log_add_fusion, bf16[1024,2,64,1]{0,2,3,1:T(8,128)(2,1)S(1)} %bitcast.419, bf16[1024,2,3,64]{0,3,2,1:T(8,128)(2,1)S(1)} %bitcast.407), kind=kOutput, calls=%fused_computation.11 | convolution fusion | flops 1648368640 | bytes 38821888 | tf_op jit(solution)/shard_map/sub | solution.py:78
  822.1 9.7 fusion.62
  831.8 4.3 convolution_multiply_fusion
  838.0 13.1 %fusion.58 = bf16[1024,2,64]{0,2,1:T(8,128)(2,1)} fusion(bf16[1024,2,3,64]{0,3,2,1:T(8,128)(2,1)} %bitcast.408, f32[2,3,1024,1024]{2,3,1,0:T(8,128)} %copy-done.2, f32[2,3,1024]{2,1,0:T(4,128)S(1)} %log_add_fusion), kind=kOutput, calls=%fused_computation.116 | convolution fusion | flops 817889280 | bytes 26238976 | tf_op jit(solution)/shard_map/hgqk,qhgd->khd/dot_general | solution.py:88
  851.1 11.0 %collective-permute-done.38 = bf16[192,2560]{1,0:T(8,128)(2,1)} collective-permute-done((bf16[192,2560]{1,0:T(8,128)(2,1)}, bf16[192,2560]{1,0:T(8,128)(2,1)}, u32[]{:S(2)}, u32[]{:S(2)}) %collective-permute-start.38) | collective-permute-done | bytes 983072 | tf_op jit(solution)/shard_map/ppermute | solution.py:252
  863.9 6.4 fusion.36
  870.2 4.3 convolution_convert_fusion.7
  876.7 3.1 pad_maximum_fusion.5
  879.8 2.7 dynamic-slice_bitcast_fusion
  886.3 3.1 copy.373
  914.8 22.6 %collective-permute-done.44 = bf16[192,2560]{1,0:T(8,128)(2,1)} collective-permute-done((bf16[192,2560]{1,0:T(8,128)(2,1)}, bf16[192,2560]{1,0:T(8,128)(2,1)}, u32[]{:S(2)}, u32[]{:S(2)}) %collective-permute-start.44) | collective-permute-done | bytes 983072 | tf_op jit(solution)/shard_map/ppermute | solution.py:252
  948.6 2.7 copy.415
  (448 shorter events, 223.4 us)
Async XLA Ops:
  7.2 142.6 %copy-start = (s32[1024,8]{0,1:T(8,128)S(1)}, s32[1024,8]{0,1:T(8,128)}, u32[]{:S(2)}) copy-start(s32[1024,8]{0,1:T(8,128)} %param.17) | copy-start | bytes 98308
  7.2 71.8 %all-gather.4.cloned.1.call-start = ((), (), s32[]{:S(2)}) async-start(), calls=%async_computation.3 | async-start | bytes 3981312 | tf_op jit(solution)/shard_map/all_gather | solution.py:235
  11.6 330.7 %all-gather.6.cloned.1.call-start = ((), (), s32[]{:S(2)}) async-start(), calls=%async_computation.4 | async-start | bytes 14483456 | tf_op jit(solution)/shard_map/all_gather | solution.py:308
  11.6 35.7 %collective-permute-start.3 = (bf16[256,1536]{1,0:T(8,128)(2,1)}, bf16[256,1536]{1,0:T(8,128)(2,1)}, u32[]{:S(2)}, u32[]{:S(2)}) collective-permute-start(bf16[256,1536]{1,0:T(8,128)(2,1)} %param.14), channel_id=1, source_target_pairs={{0,2},{1,3},{2,0},{3,1},{4,6},{5,7},{6,4},{7,5},{8,10},{9,11},{10,... | collective-permute-start | bytes 2359304 | tf_op jit(solution)/shard_map/ppermute | solution.py:95
  48.6 3.5 collective-permute-start.4
  49.9 37.3 %copy-start.34 = (f32[1024,32]{0,1:T(8,128)}, f32[1024,32]{0,1:T(8,128)S(1)}, u32[]{:S(2)}) copy-start(f32[1024,32]{0,1:T(8,128)S(1)} %get-tuple-element.230) | copy-start | bytes 393220
  52.2 32.9 %copy-start.12 = (bf16[1024,1536]{1,0:T(8,128)(2,1)}, bf16[1024,1536]{1,0:T(8,128)(2,1)S(1)}, u32[]{:S(2)}) copy-start(bf16[1024,1536]{1,0:T(8,128)(2,1)S(1)} %slice_dynamic-update-slice_fusion.2) | copy-start | bytes 9437188
  52.9 32.2 %copy-start.84 = (f32[1024]{0:T(1024)}, f32[1024]{0:T(1024)S(1)}, u32[]{:S(2)}) copy-start(f32[1024]{0:T(1024)S(1)} %add_rsqrt_fusion) | copy-start | bytes 12292
  80.9 90.0 %copy-start.71 = (f32[1536]{0:T(1024)}, f32[1536]{0:T(1024)S(1)}, u32[]{:S(2)}) copy-start(f32[1536]{0:T(1024)S(1)} %get-tuple-element.158) | copy-start | bytes 18436
  87.9 29.3 %collective-permute-start.2 = (bf16[192,1280]{1,0:T(8,128)(2,1)}, bf16[192,1280]{1,0:T(8,128)(2,1)}, u32[]{:S(2)}, u32[]{:S(2)}) collective-permute-start(bf16[192,1280]{1,0:T(8,128)(2,1)} %copy.327), channel_id=1, source_target_pairs={{0,4},{4,0},{1,5},{5,1},{2,6},{6,2},{3,7},{7,3},{8,12},{12,8},{9,1... | collective-permute-start | bytes 1474568 | tf_op jit(solution)/shard_map/ppermute | solution.py:95
  88.5 32.2 %collective-permute-start.1 = (bf16[192,2560]{1,0:T(8,128)(2,1)}, bf16[192,2560]{1,0:T(8,128)(2,1)}, u32[]{:S(2)}, u32[]{:S(2)}) collective-permute-start(bf16[192,2560]{1,0:T(8,128)(2,1)} %pad_maximum_fusion.10), channel_id=1, source_target_pairs={{0,4},{4,0},{1,5},{5,1},{2,6},{6,2},{3,7},{7,3},{8,12},{12,8},{9,1... | collective-permute-start | bytes 2949128 | tf_op jit(solution)/shard_map/ppermute | solution.py:95
  89.9 43.6 %collective-permute-start = (bf16[192,2560]{1,0:T(8,128)(2,1)}, bf16[192,2560]{1,0:T(8,128)(2,1)}, u32[]{:S(2)}, u32[]{:S(2)}) collective-permute-start(bf16[192,2560]{1,0:T(8,128)(2,1)} %pad_maximum_fusion.12), channel_id=1, source_target_pairs={{0,16},{8,24},{16,0},{24,8},{1,17},{9,25},{17,1},{25,9},{2,18},{10... | collective-permute-start | bytes 2949128 | tf_op jit(solution)/shard_map/ppermute | solution.py:252
  139.6 3.8 collective-permute-start.5
  139.6 28.6 %copy-start.10 = (bf16[256,1536]{1,0:T(8,128)(2,1)S(1)}, bf16[256,1536]{1,0:T(8,128)(2,1)}, u32[]{:S(2)}) copy-start(bf16[256,1536]{1,0:T(8,128)(2,1)} %param.14) | copy-start | bytes 2359300
  148.3 19.9 %collective-permute-start.6 = (bf16[256,1536]{1,0:T(8,128)(2,1)}, bf16[256,1536]{1,0:T(8,128)(2,1)}, u32[]{:S(2)}, u32[]{:S(2)}) collective-permute-start(bf16[256,1536]{1,0:T(8,128)(2,1)} %fusion.77), channel_id=1, source_target_pairs={{0,2},{1,3},{2,0},{3,1},{4,6},{5,7},{6,4},{7,5},{8,10},{9,11},{10,... | collective-permute-start | bytes 2359304 | tf_op jit(solution)/shard_map/ppermute | solution.py:95
  150.0 57.3 %collective-permute-start.7 = (bf16[192,2560]{1,0:T(8,128)(2,1)}, bf16[192,2560]{1,0:T(8,128)(2,1)}, u32[]{:S(2)}, u32[]{:S(2)}) collective-permute-start(bf16[192,2560]{1,0:T(8,128)(2,1)} %pad_maximum_fusion.11), channel_id=1, source_target_pairs={{0,8},{8,16},{16,24},{24,0},{1,9},{9,17},{17,25},{25,1},{2,10},{10... | collective-permute-start | bytes 2949128 | tf_op jit(solution)/shard_map/ppermute | solution.py:252
  150.7 36.7 %collective-permute-start.8 = (bf16[192,1280]{1,0:T(8,128)(2,1)S(1)}, bf16[192,1280]{1,0:T(8,128)(2,1)}, u32[]{:S(2)}, u32[]{:S(2)}) collective-permute-start(bf16[192,1280]{1,0:T(8,128)(2,1)S(1)} %copy-done.62), channel_id=1, source_target_pairs={{0,8},{8,16},{16,24},{24,0},{1,9},{9,17},{17,25},{25,1},{2,10},{10... | collective-permute-start | bytes 1474568 | tf_op jit(solution)/shard_map/ppermute | solution.py:252
  161.7 45.6 %collective-permute-start.9 = (bf16[192,1280]{1,0:T(8,128)(2,1)}, bf16[192,1280]{1,0:T(8,128)(2,1)}, u32[]{:S(2)}, u32[]{:S(2)}) collective-permute-start(bf16[192,1280]{1,0:T(8,128)(2,1)} %copy.339), channel_id=1, source_target_pairs={{0,16},{8,24},{16,0},{24,8},{1,17},{9,25},{17,1},{25,9},{2,18},{10... | collective-permute-start | bytes 1474568 | tf_op jit(solution)/shard_map/ppermute | solution.py:252
  207.3 236.5 %all-gather.8.cloned.1.call-start = ((), (), s32[]{:S(2)}) async-start(), calls=%async_computation.5 | async-start | bytes 13369344 | tf_op jit(solution)/shard_map/all_gather | solution.py:321
  215.4 14.3 %collective-permute-start.14 = (bf16[192,1280]{1,0:T(8,128)(2,1)}, bf16[192,1280]{1,0:T(8,128)(2,1)S(1)}, u32[]{:S(2)}, u32[]{:S(2)}) collective-permute-start(bf16[192,1280]{1,0:T(8,128)(2,1)} %collective-permute-done.8), channel_id=1, source_target_pairs={{0,4},{4,0},{1,5},{5,1},{2,6},{6,2},{3,7},{7,3},{8,12},{12,8},{9,1... | collective-permute-start | bytes 1474568 | tf_op jit(solution)/shard_map/ppermute | solution.py:95
  216.1 36.1 %collective-permute-start.15 = (bf16[192,1280]{1,0:T(8,128)(2,1)}, bf16[192,1280]{1,0:T(8,128)(2,1)S(1)}, u32[]{:S(2)}, u32[]{:S(2)}) collective-permute-start(bf16[192,1280]{1,0:T(8,128)(2,1)} %collective-permute-done.9), channel_id=1, source_target_pairs={{0,4},{4,0},{1,5},{5,1},{2,6},{6,2},{3,7},{7,3},{8,12},{12,8},{9,1... | collective-permute-start | bytes 1474568 | tf_op jit(solution)/shard_map/ppermute | solution.py:95
  217.4 33.3 %collective-permute-start.16 = (bf16[192,1280]{1,0:T(8,128)(2,1)S(1)}, bf16[192,1280]{1,0:T(8,128)(2,1)S(1)}, u32[]{:S(2)}, u32[]{:S(2)}) collective-permute-start(bf16[192,1280]{1,0:T(8,128)(2,1)S(1)} %copy-done.60), channel_id=1, source_target_pairs={{0,24},{8,0},{16,8},{24,16},{1,25},{9,1},{17,9},{25,17},{2,26},{10... | collective-permute-start | bytes 1474568 | tf_op jit(solution)/shard_map/ppermute | solution.py:252
  217.5 75.6 %collective-permute-start.10 = (bf16[192,2560]{1,0:T(8,128)(2,1)}, bf16[192,2560]{1,0:T(8,128)(2,1)S(1)}, u32[]{:S(2)}, u32[]{:S(2)}) collective-permute-start(bf16[192,2560]{1,0:T(8,128)(2,1)} %collective-permute-done.7), channel_id=1, source_target_pairs={{0,4},{4,0},{1,5},{5,1},{2,6},{6,2},{3,7},{7,3},{8,12},{12,8},{9,1... | collective-permute-start | bytes 2949128 | tf_op jit(solution)/shard_map/ppermute | solution.py:95
  218.2 56.0 %collective-permute-start.12 = (bf16[192,2560]{1,0:T(8,128)(2,1)S(1)}, bf16[192,2560]{1,0:T(8,128)(2,1)S(1)}, u32[]{:S(2)}, u32[]{:S(2)}) collective-permute-start(bf16[192,2560]{1,0:T(8,128)(2,1)S(1)} %copy-done.55), channel_id=1, source_target_pairs={{0,24},{8,0},{16,8},{24,16},{1,25},{9,1},{17,9},{25,17},{2,26},{10... | collective-permute-start | bytes 2949128 | tf_op jit(solution)/shard_map/ppermute | solution.py:252
  229.7 66.7 %collective-permute-start.11 = (bf16[192,2560]{1,0:T(8,128)(2,1)}, bf16[192,2560]{1,0:T(8,128)(2,1)S(1)}, u32[]{:S(2)}, u32[]{:S(2)}) collective-permute-start(bf16[192,2560]{1,0:T(8,128)(2,1)} %collective-permute-done), channel_id=1, source_target_pairs={{0,4},{4,0},{1,5},{5,1},{2,6},{6,2},{3,7},{7,3},{8,12},{12,8},{9,1... | collective-permute-start | bytes 2949128 | tf_op jit(solution)/shard_map/ppermute | solution.py:95
  250.8 42.2 %collective-permute-start.17 = (bf16[192,1280]{1,0:T(8,128)(2,1)S(1)}, bf16[192,1280]{1,0:T(8,128)(2,1)S(1)}, u32[]{:S(2)}, u32[]{:S(2)}) collective-permute-start(bf16[192,1280]{1,0:T(8,128)(2,1)S(1)} %collective-permute-done.16), channel_id=1, source_target_pairs={{0,4},{4,0},{1,5},{5,1},{2,6},{6,2},{3,7},{7,3},{8,12},{12,8},{9,1... | collective-permute-start | bytes 1474568 | tf_op jit(solution)/shard_map/ppermute | solution.py:95
  274.1 39.0 %collective-permute-start.13 = (bf16[192,2560]{1,0:T(8,128)(2,1)S(1)}, bf16[192,2560]{1,0:T(8,128)(2,1)S(1)}, u32[]{:S(2)}, u32[]{:S(2)}) collective-permute-start(bf16[192,2560]{1,0:T(8,128)(2,1)S(1)} %collective-permute-done.12), channel_id=1, source_target_pairs={{0,4},{4,0},{1,5},{5,1},{2,6},{6,2},{3,7},{7,3},{8,12},{12,8},{9,1... | collective-permute-start | bytes 2949128 | tf_op jit(solution)/shard_map/ppermute | solution.py:95
  342.3 265.1 %reduce-scatter.4.cloned.1.call-start = ((), (), s32[]{:S(2)}) async-start(), calls=%async_computation.6 | async-start | bytes 13369344 | tf_op jit(solution)/shard_map/reduce_scatter | solution.py:346
  346.5 43.6 %copy-start.3 = (bf16[4096,1280]{1,0:T(8,128)(2,1)}, bf16[4096,1280]{1,0:T(8,128)(2,1)S(1)}, u32[]{:S(2)}) copy-start(bf16[4096,1280]{1,0:T(8,128)(2,1)S(1)} %convolution_convert_fusion.2) | copy-start | bytes 31457284
  443.8 308.9 %reduce-scatter.6.cloned.1.call-start = ((), (), s32[]{:S(2)}) async-start(), calls=%async_computation.7 | async-start | bytes 13369344 | tf_op jit(solution)/shard_map/reduce_scatter | solution.py:390
  467.9 41.9 %collective-permute-start.18 = (bf16[192,1280]{1,0:T(8,128)(2,1)}, bf16[192,1280]{1,0:T(8,128)(2,1)}, u32[]{:S(2)}, u32[]{:S(2)}) collective-permute-start(bf16[192,1280]{1,0:T(8,128)(2,1)} %get-tuple-element.187), channel_id=1, source_target_pairs={{0,4},{4,0},{1,5},{5,1},{2,6},{6,2},{3,7},{7,3},{8,12},{12,8},{9,1... | collective-permute-start | bytes 1474568 | tf_op jit(solution)/shard_map/ppermute | solution.py:95
  469.4 40.4 %collective-permute-start.19 = (bf16[192,1280]{1,0:T(8,128)(2,1)}, bf16[192,1280]{1,0:T(8,128)(2,1)}, u32[]{:S(2)}, u32[]{:S(2)}) collective-permute-start(bf16[192,1280]{1,0:T(8,128)(2,1)} %get-tuple-element.186), channel_id=1, source_target_pairs={{0,4},{4,0},{1,5},{5,1},{2,6},{6,2},{3,7},{7,3},{8,12},{12,8},{9,1... | collective-permute-start | bytes 1474568 | tf_op jit(solution)/shard_map/ppermute | solution.py:95
  469.9 39.9 %collective-permute-start.20 = (bf16[192,1280]{1,0:T(8,128)(2,1)}, bf16[192,1280]{1,0:T(8,128)(2,1)}, u32[]{:S(2)}, u32[]{:S(2)}) collective-permute-start(bf16[192,1280]{1,0:T(8,128)(2,1)} %get-tuple-element.185), channel_id=1, source_target_pairs={{0,4},{4,0},{1,5},{5,1},{2,6},{6,2},{3,7},{7,3},{8,12},{12,8},{9,1... | collective-permute-start | bytes 1474568 | tf_op jit(solution)/shard_map/ppermute | solution.py:95
  471.4 41.8 %collective-permute-start.21 = (bf16[192,1280]{1,0:T(8,128)(2,1)}, bf16[192,1280]{1,0:T(8,128)(2,1)}, u32[]{:S(2)}, u32[]{:S(2)}) collective-permute-start(bf16[192,1280]{1,0:T(8,128)(2,1)} %get-tuple-element.184), channel_id=1, source_target_pairs={{0,4},{4,0},{1,5},{5,1},{2,6},{6,2},{3,7},{7,3},{8,12},{12,8},{9,1... | collective-permute-start | bytes 1474568 | tf_op jit(solution)/shard_map/ppermute | solution.py:95
  516.3 51.2 %collective-permute-start.22 = (bf16[192,1280]{1,0:T(8,128)(2,1)}, bf16[192,1280]{1,0:T(8,128)(2,1)S(1)}, u32[]{:S(2)}, u32[]{:S(2)}) collective-permute-start(bf16[192,1280]{1,0:T(8,128)(2,1)} %get-tuple-element.120), channel_id=1, source_target_pairs={{0,8},{8,16},{16,24},{24,0},{1,9},{9,17},{17,25},{25,1},{2,10},{10... | collective-permute-start | bytes 1474568 | tf_op jit(solution)/shard_map/ppermute | solution.py:252
  516.8 50.7 %collective-permute-start.23 = (bf16[192,1280]{1,0:T(8,128)(2,1)}, bf16[192,1280]{1,0:T(8,128)(2,1)S(1)}, u32[]{:S(2)}, u32[]{:S(2)}) collective-permute-start(bf16[192,1280]{1,0:T(8,128)(2,1)} %get-tuple-element.121), channel_id=1, source_target_pairs={{0,16},{8,24},{16,0},{24,8},{1,17},{9,25},{17,1},{25,9},{2,18},{10... | collective-permute-start | bytes 1474568 | tf_op jit(solution)/shard_map/ppermute | solution.py:252
  518.4 49.1 %collective-permute-start.24 = (bf16[192,1280]{1,0:T(8,128)(2,1)}, bf16[192,1280]{1,0:T(8,128)(2,1)S(1)}, u32[]{:S(2)}, u32[]{:S(2)}) collective-permute-start(bf16[192,1280]{1,0:T(8,128)(2,1)} %get-tuple-element.122), channel_id=1, source_target_pairs={{0,24},{8,0},{16,8},{24,16},{1,25},{9,1},{17,9},{25,17},{2,26},{10... | collective-permute-start | bytes 1474568 | tf_op jit(solution)/shard_map/ppermute | solution.py:252
  520.9 39.6 %copy-start.80 = (s32[1280]{0:T(1024)S(1)}, s32[1280]{0:T(1024)}, u32[]{:S(2)}) copy-start(s32[1280]{0:T(1024)} %copy-done.79) | copy-start | bytes 15364
  567.5 39.9 %copy-start.66 = (bf16[192,1280]{1,0:T(8,128)(2,1)}, bf16[192,1280]{1,0:T(8,128)(2,1)S(1)}, u32[]{:S(2)}) copy-start(bf16[192,1280]{1,0:T(8,128)(2,1)S(1)} %collective-permute-done.22) | copy-start | bytes 1474564
  567.5 39.9 %copy-start.65 = (bf16[192,1280]{1,0:T(8,128)(2,1)}, bf16[192,1280]{1,0:T(8,128)(2,1)S(1)}, u32[]{:S(2)}) copy-start(bf16[192,1280]{1,0:T(8,128)(2,1)S(1)} %collective-permute-done.23) | copy-start | bytes 1474564
  567.5 39.9 %copy-start.63 = (bf16[192,1280]{1,0:T(8,128)(2,1)}, bf16[192,1280]{1,0:T(8,128)(2,1)S(1)}, u32[]{:S(2)}) copy-start(bf16[192,1280]{1,0:T(8,128)(2,1)S(1)} %collective-permute-done.24) | copy-start | bytes 1474564
  607.4 365.5 %reduce-scatter.8.cloned.1.call-start = ((), (), s32[]{:S(2)}) async-start(), calls=%async_computation.8 | async-start | bytes 3981312 | tf_op jit(solution)/shard_map/reduce_scatter | solution.py:485
  607.6 41.3 %collective-permute-start.29 = (bf16[4,2,256,128]{3,2,0,1:T(8,128)(2,1)S(1)}, bf16[4,2,256,128]{3,2,0,1:T(8,128)(2,1)S(1)}, u32[]{:S(2)}, u32[]{:S(2)}) collective-permute-start(bf16[4,2,256,128]{3,2,0,1:T(8,128)(2,1)S(1)} %bitcast.411), channel_id=1, source_target_pairs={{0,1},{1,0},{2,3},{3,2},{4,5},{5,4},{6,7},{7,6},{8,9},{9,8},{10,11... | collective-permute-start | bytes 1572872 | tf_op jit(solution)/shard_map/ppermute | solution.py:95
  650.5 15.0 %collective-permute-start.30 = (bf16[4,256,128]{2,1,0:T(8,128)(2,1)}, bf16[4,256,128]{2,1,0:T(8,128)(2,1)}, u32[]{:S(2)}, u32[]{:S(2)}) collective-permute-start(bf16[4,256,128]{2,1,0:T(8,128)(2,1)} %dynamic-slice_bitcast_fusion.30), channel_id=1, source_target_pairs={{0,2},{1,3},{2,0},{3,1},{4,6},{5,7},{6,4},{7,5},{8,10},{9,11},{10,... | collective-permute-start | bytes 786440 | tf_op jit(solution)/shard_map/ppermute | solution.py:95
  657.8 35.2 %collective-permute-start.25 = (bf16[192,2560]{1,0:T(8,128)(2,1)}, bf16[192,2560]{1,0:T(8,128)(2,1)}, u32[]{:S(2)}, u32[]{:S(2)}) collective-permute-start(bf16[192,2560]{1,0:T(8,128)(2,1)} %get-tuple-element.177), channel_id=1, source_target_pairs={{0,4},{4,0},{1,5},{5,1},{2,6},{6,2},{3,7},{7,3},{8,12},{12,8},{9,1... | collective-permute-start | bytes 2949128 | tf_op jit(solution)/shard_map/ppermute | solution.py:95
  659.4 44.5 %collective-permute-start.26 = (bf16[192,2560]{1,0:T(8,128)(2,1)}, bf16[192,2560]{1,0:T(8,128)(2,1)}, u32[]{:S(2)}, u32[]{:S(2)}) collective-permute-start(bf16[192,2560]{1,0:T(8,128)(2,1)} %get-tuple-element.176), channel_id=1, source_target_pairs={{0,4},{4,0},{1,5},{5,1},{2,6},{6,2},{3,7},{7,3},{8,12},{12,8},{9,1... | collective-permute-start | bytes 2949128 | tf_op jit(solution)/shard_map/ppermute | solution.py:95
  659.9 65.0 %collective-permute-start.27 = (bf16[192,2560]{1,0:T(8,128)(2,1)}, bf16[192,2560]{1,0:T(8,128)(2,1)}, u32[]{:S(2)}, u32[]{:S(2)}) collective-permute-start(bf16[192,2560]{1,0:T(8,128)(2,1)} %get-tuple-element.175), channel_id=1, source_target_pairs={{0,4},{4,0},{1,5},{5,1},{2,6},{6,2},{3,7},{7,3},{8,12},{12,8},{9,1... | collective-permute-start | bytes 2949128 | tf_op jit(solution)/shard_map/ppermute | solution.py:95
  661.4 83.9 %collective-permute-start.28 = (bf16[192,2560]{1,0:T(8,128)(2,1)}, bf16[192,2560]{1,0:T(8,128)(2,1)}, u32[]{:S(2)}, u32[]{:S(2)}) collective-permute-start(bf16[192,2560]{1,0:T(8,128)(2,1)} %get-tuple-element.174), channel_id=1, source_target_pairs={{0,4},{4,0},{1,5},{5,1},{2,6},{6,2},{3,7},{7,3},{8,12},{12,8},{9,1... | collective-permute-start | bytes 2949128 | tf_op jit(solution)/shard_map/ppermute | solution.py:95
  666.6 7.9 collective-permute-start.31
  674.4 10.1 %collective-permute-start.32 = (bf16[256,128]{1,0:T(8,128)(2,1)S(1)}, bf16[256,128]{1,0:T(8,128)(2,1)S(1)}, u32[]{:S(2)}, u32[]{:S(2)}) collective-permute-start(bf16[256,128]{1,0:T(8,128)(2,1)S(1)} %get-tuple-element.225), channel_id=1, source_target_pairs={{0,16},{8,24},{16,0},{24,8},{1,17},{9,25},{17,1},{25,9},{2,18},{10... | collective-permute-start | bytes 196616 | tf_op jit(solution)/shard_map/ppermute | solution.py:186
  684.5 8.5 collective-permute-start.33
  762.2 18.6 %collective-permute-start.34 = (bf16[256,1536]{1,0:T(8,128)(2,1)S(1)}, bf16[256,1536]{1,0:T(8,128)(2,1)S(1)}, u32[]{:S(2)}, u32[]{:S(2)}) collective-permute-start(bf16[256,1536]{1,0:T(8,128)(2,1)S(1)} %fusion.105), channel_id=1, source_target_pairs={{0,2},{1,3},{2,0},{3,1},{4,6},{5,7},{6,4},{7,5},{8,10},{9,11},{10,... | collective-permute-start | bytes 2359304 | tf_op jit(solution)/shard_map/ppermute | solution.py:95
  764.5 23.3 %collective-permute-start.35 = (bf16[192,1280]{1,0:T(8,128)(2,1)S(1)}, bf16[192,1280]{1,0:T(8,128)(2,1)S(1)}, u32[]{:S(2)}, u32[]{:S(2)}) collective-permute-start(bf16[192,1280]{1,0:T(8,128)(2,1)S(1)} %get-tuple-element.215), channel_id=1, source_target_pairs={{0,16},{8,24},{16,0},{24,8},{1,17},{9,25},{17,1},{25,9},{2,18},{10... | collective-permute-start | bytes 1474568 | tf_op jit(solution)/shard_map/ppermute | solution.py:252
  787.9 3.4 collective-permute-start.36
  788.6 33.5 %collective-permute-start.37 = (bf16[192,1280]{1,0:T(8,128)(2,1)}, bf16[192,1280]{1,0:T(8,128)(2,1)}, u32[]{:S(2)}, u32[]{:S(2)}) collective-permute-start(bf16[192,1280]{1,0:T(8,128)(2,1)} %get-tuple-element.137), channel_id=1, source_target_pairs={{0,16},{8,24},{16,0},{24,8},{1,17},{9,25},{17,1},{25,9},{2,18},{10... | collective-permute-start | bytes 1474568 | tf_op jit(solution)/shard_map/ppermute | solution.py:252
  836.1 27.5 %copy-start.22 = (f32[1024,2,64]{0,2,1:T(8,128)S(1)}, f32[1024,2,64]{0,2,1:T(8,128)}, u32[]{:S(2)}) copy-start(f32[1024,2,64]{0,2,1:T(8,128)} %fusion.62) | copy-start | bytes 1572868
  836.1 25.9 %collective-permute-start.38 = (bf16[192,2560]{1,0:T(8,128)(2,1)}, bf16[192,2560]{1,0:T(8,128)(2,1)}, u32[]{:S(2)}, u32[]{:S(2)}) collective-permute-start(bf16[192,2560]{1,0:T(8,128)(2,1)} %get-tuple-element.141), channel_id=1, source_target_pairs={{0,8},{8,16},{16,24},{24,0},{1,9},{9,17},{17,25},{25,1},{2,10},{10... | collective-permute-start | bytes 2949128 | tf_op jit(solution)/shard_map/ppermute | solution.py:252
  882.5 26.2 %collective-permute-start.39 = (bf16[2,256,1536]{2,1,0:T(8,128)(2,1)}, bf16[2,256,1536]{2,1,0:T(8,128)(2,1)}, u32[]{:S(2)}, u32[]{:S(2)}) collective-permute-start(bf16[2,256,1536]{2,1,0:T(8,128)(2,1)} %dynamic-slice_bitcast_fusion), channel_id=1, source_target_pairs={{0,1},{1,0},{2,3},{3,2},{4,5},{5,4},{6,7},{7,6},{8,9},{9,8},{10,11... | collective-permute-start | bytes 4718600 | tf_op jit(solution)/shard_map/ppermute | solution.py:95
  905.0 32.4 %collective-permute-start.44 = (bf16[192,2560]{1,0:T(8,128)(2,1)}, bf16[192,2560]{1,0:T(8,128)(2,1)}, u32[]{:S(2)}, u32[]{:S(2)}) collective-permute-start(bf16[192,2560]{1,0:T(8,128)(2,1)} %get-tuple-element.148), channel_id=1, source_target_pairs={{0,24},{8,0},{16,8},{24,16},{1,25},{9,1},{17,9},{25,17},{2,26},{10... | collective-permute-start | bytes 2949128 | tf_op jit(solution)/shard_map/ppermute | solution.py:252
  911.2 28.5 %copy-start.11 = (bf16[256,1536]{1,0:T(8,128)(2,1)S(1)}, bf16[256,1536]{1,0:T(8,128)(2,1)}, u32[]{:S(2)}) copy-start(bf16[256,1536]{1,0:T(8,128)(2,1)} %param.14) | copy-start | bytes 2359300
  911.3 28.3 %collective-permute-start.40 = (bf16[256,1536]{1,0:T(8,128)(2,1)S(1)}, bf16[256,1536]{1,0:T(8,128)(2,1)S(1)}, u32[]{:S(2)}, u32[]{:S(2)}) collective-permute-start(bf16[256,1536]{1,0:T(8,128)(2,1)S(1)} %fusion.78), channel_id=1, source_target_pairs={{0,2},{1,3},{2,0},{3,1},{4,6},{5,7},{6,4},{7,5},{8,10},{9,11},{10,... | collective-permute-start | bytes 2359304 | tf_op jit(solution)/shard_map/ppermute | solution.py:95
  973.9 8.8 collective-permute-start.41
  974.2 8.6 collective-permute-start.42
  975.7 10.0 %collective-permute-start.43 = (f32[42,192]{1,0:T(8,128)S(1)}, f32[42,192]{1,0:T(8,128)S(1)}, u32[]{:S(2)}, u32[]{:S(2)}) collective-permute-start(f32[42,192]{1,0:T(8,128)S(1)} %bitcast.424), channel_id=1, source_target_pairs={{0,3},{1,0},{2,1},{3,2},{4,7},{5,4},{6,5},{7,6},{8,11},{9,8},{10,9... | collective-permute-start | bytes 96776 | tf_op jit(solution)/shard_map/ppermute | solution.py:193
  (75 other events, 549.4 us)
Sparse Core Ops, SparseCore 0:
  11.7 67.3 all-gather.3
  207.4 134.7 all-gather.5
  345.1 98.5 all-gather.7
  447.6 159.6 reduce-scatter.3
  611.2 141.4 reduce-scatter.5
  879.9 86.8 reduce-scatter.7
